TPU v7x, 512 devices: a whole 4x4x16 slice. The times are simulated.
512 devices in a mesh: blk: 32 (over z_lo, x, core), group: 16 (over y, z_hi).
Axes of the slice: x: 4, y: 4, z: 16 (z_hi: 4, z_lo: 4; z = z_hi * 4 + z_lo), core: 2. Of those that a mesh axis runs over, the one named last changes fastest.
Arguments:
- queries: bfloat16 [16, 8192, 4096], P('group', 'blk'), may hold values from -30 to 30
- passages: bfloat16 [16, 512, 4096], P('group', 'blk'), may hold values from -7 to 7
- positives: int32 [16, 8192], P('group', 'blk'), may hold values from 0 to 511
- hard_rows: bfloat16 [16, 512, 4096], P('group', 'blk'), may hold values from -6 to 6
- hard_dest: int32 [16, 512, 1], P('group', 'blk'), may hold values from 0 to 15; in each aligned block of 16 rows (0 to 15, 16 to 31, ..., all dimensions but the last counted through in order) at most 2 rows name the same one
Outputs:
- loss_rows: float32 [16, 8192], P('group', 'blk')
- d_queries: bfloat16 [16, 8192, 4096], P('group', 'blk')
- d_passages: bfloat16 [16, 512, 4096], P('group', 'blk')
- d_hard: bfloat16 [16, 512, 4096], P('group', 'blk')
Inputs may be any that keep to these rules, and one draw needn't show every extreme that they name: `hard_dest`: among the 16 hard rows of one device, at most 2 name the same group, and some device reaches 2.
All inputs are finite; a program needn't handle non-finite values.
Results may differ from a plain program's by a relative error of at most 0.0048.
Values may be sent and summed in bfloat16 or wider, within the bound.
No kernel may reach another device: no remote copies, remote signals or barrier semaphores. Data moves between devices by JAX's collectives and lax.ppermute only.
A program may use at most 64 MiB of HBM per device.

v0:
```python
import jax
import jax.numpy as jnp
from jax import lax
from jax.sharding import PartitionSpec as P


def from_behind(x, axis, by):
    count = lax.axis_size(axis)
    return lax.ppermute(x, axis, [(i, (i + by) % count) for i in range(count)])


def body(queries, passages, positives, hard_rows, hard_dest):
    query_rows = queries[0]
    own_passages = passages[0]
    targets = positives[0]
    owned_hard = hard_rows[0]
    routes = hard_dest[0, :, 0]
    groups = lax.axis_size("group")
    blocks = lax.axis_size("blk")
    blk_index = lax.axis_index("blk")
    feat_width = query_rows.shape[1]
    passage_count = own_passages.shape[0]
    hard_count = owned_hard.shape[0]
    total_rows = passage_count * blocks
    score_multiplier = feat_width ** (-0.5)
    largest_score = lax.Precision.HIGHEST
    slot_count = max(2, 2 * hard_count // groups)
    onehot_dest = (routes[:, None] == jnp.arange(groups, dtype=jnp.int32)[None, :]).astype(
        jnp.int32
    )
    ranking = jnp.sum((jnp.cumsum(onehot_dest, axis=0) - onehot_dest) * onehot_dest, axis=1)
    slot_of = routes * slot_count + ranking
    placing = (
        slot_of[None, :] == jnp.arange(groups * slot_count, dtype=jnp.int32)[:, None]
    ).astype(jnp.bfloat16)
    packed = jnp.dot(placing, owned_hard, preferred_element_type=jnp.float32).astype(jnp.bfloat16)
    packed = packed.reshape(groups, slot_count, feat_width)
    live_flags = jnp.sum(placing, axis=1).reshape(groups, slot_count)
    arrived, arrived_flags = (
        lax.all_to_all(packed, "group", split_axis=0, concat_axis=0, tiled=True),
        lax.all_to_all(live_flags, "group", split_axis=0, concat_axis=0, tiled=True),
    )
    received = arrived.reshape(groups * slot_count, feat_width)
    is_live = arrived_flags.reshape(groups * slot_count) > 0.5
    raw_hard = score_multiplier * jnp.einsum(
        "qd,hd->qh", query_rows, received, preferred_element_type=jnp.float32
    )
    negative_scores = jnp.where(is_live[None, :], raw_hard, -jnp.inf)
    hard_top = jnp.max(negative_scores, axis=1)
    received_wide = received.astype(jnp.float32)
    target_hot = (targets[:, None] == jnp.arange(total_rows, dtype=jnp.int32)[None, :]).astype(
        jnp.float32
    )
    gathered = lax.all_gather(own_passages, "blk", axis=0, tiled=True)
    in_scores = score_multiplier * jnp.einsum(
        "qd,pd->qp", query_rows, gathered, preferred_element_type=jnp.float32
    )
    run_top = jnp.maximum(jnp.max(in_scores, axis=1), hard_top)
    run_total = jnp.sum(jnp.exp(in_scores - run_top[:, None]), axis=1) + jnp.sum(
        jnp.exp(negative_scores - run_top[:, None]), axis=1
    )
    log_total = run_top + jnp.log(run_total)
    prob_in = jnp.exp(in_scores - log_total[:, None])
    hard_probability = jnp.exp(negative_scores - log_total[:, None])
    coef_in = prob_in - target_hot
    d_query = score_multiplier * (
        jnp.dot(coef_in, gathered.astype(jnp.float32), precision=largest_score)
        + jnp.dot(hard_probability, received_wide, precision=largest_score)
    )
    loss_rows = log_total - jnp.sum(in_scores * target_hot, axis=1)
    coef_round = coef_in.astype(jnp.bfloat16)

    def contrib(col_start, row_count):
        coef_cols = lax.dynamic_slice_in_dim(coef_round, col_start, row_count, 1)
        return jnp.einsum("qp,qd->pd", coef_cols, query_rows, preferred_element_type=jnp.float32)

    def owner_col(turn_index):
        return (blk_index - turn_index - 1) % blocks * passage_count

    def advance(turn_index, running):
        running = from_behind(running, "blk", 1)
        return running + contrib(owner_col(turn_index), passage_count)

    summed = lax.fori_loop(1, blocks, advance, contrib(owner_col(0), passage_count))
    d_passage = (score_multiplier * summed).astype(jnp.bfloat16)
    hard_exchange_round = hard_probability.astype(jnp.bfloat16)
    slot_grads = (
        score_multiplier
        * jnp.einsum(
            "qh,qd->hd", hard_exchange_round, query_rows, preferred_element_type=jnp.float32
        )
    ).astype(jnp.bfloat16)
    slot_grads = slot_grads.reshape(groups, slot_count, feat_width)
    returned = lax.all_to_all(slot_grads, "group", split_axis=0, concat_axis=0, tiled=True).reshape(
        groups * slot_count, feat_width
    )
    d_owned = jnp.einsum("sh,sd->hd", placing, returned, preferred_element_type=jnp.float32).astype(
        jnp.bfloat16
    )
    return (loss_rows[None], d_query.astype(jnp.bfloat16)[None], d_passage[None], d_owned[None])


def solution(mesh):
    return jax.shard_map(
        body,
        mesh=mesh,
        in_specs=(
            P("group", "blk", None),
            P("group", "blk", None),
            P("group", "blk"),
            P("group", "blk", None),
            P("group", "blk", None),
        ),
        out_specs=(
            P("group", "blk"),
            P("group", "blk", None),
            P("group", "blk", None),
            P("group", "blk", None),
        ),
        check_vma=False,
    )
```

profile of v0, /device:TPU:1, one launch (start us, length us, event | category | flops | bytes accessed | tf_op | source)
XLA Modules:
  0.0 499.8 jit_solution(9961726672704951241)
XLA Ops:
  11.0 18.4 %all-to-all-start = ((bf16[16,1,2]{2,1,0:T(2,128)(2,1)}), bf16[16,1,2]{2,1,0:T(2,128)(2,1)S(1)}, u32[]{:S(2)}, u32[]{:S(2)}) async-start(bf16[16,1,2]{2,1,0:T(2,128)(2,1)} %all_to_all.16), calls=%async_computation | async-start | bytes 16384 | tf_op jit(solution)/shard_map/all_to_all | solution.py:41
  30.6 12.3 %all-to-all-done = bf16[16,1,2]{2,1,0:T(2,128)(2,1)S(1)} async-done(((bf16[16,1,2]{2,1,0:T(2,128)(2,1)}), bf16[16,1,2]{2,1,0:T(2,128)(2,1)S(1)}, u32[]{:S(2)}, u32[]{:S(2)}) %all-to-all-start) | async-done | bytes 96 | tf_op jit(solution)/shard_map/all_to_all | solution.py:41
  42.9 3.5 all-to-all-start.1
  46.6 25.0 %all-to-all-done.1 = bf16[16,2,4096]{2,1,0:T(2,128)(2,1)S(1)} async-done(((bf16[16,2,4096]{2,1,0:T(2,128)(2,1)}), bf16[16,2,4096]{2,1,0:T(2,128)(2,1)S(1)}, u32[]{:S(2)}, u32[]{:S(2)}) %all-to-all-start.1) | async-done | bytes 262176 | tf_op jit(solution)/shard_map/all_to_all | solution.py:40
  72.5 19.9 %all-gather.3.cloned.1.call-done = bf16[1,512,4096]{2,1,0:T(8,128)(2,1)} async-done(((bf16[1,16,4096]{2,1,0:T(8,128)(2,1)}), bf16[1,512,4096]{2,1,0:T(8,128)(2,1)}) %all-gather.3.cloned.1.call-update) | async-done | bytes 4194320 | tf_op jit(solution)/shard_map/all_gather | solution.py:54
  92.4 3.7 fusion.37
  97.7 3.8 fusion.7
  101.5 3.3 fusion.4
  105.7 14.8 %all-to-all-start.2 = ((bf16[16,2,4096]{2,1,0:T(2,128)(2,1)}), bf16[16,2,4096]{2,1,0:T(2,128)(2,1)S(1)}, u32[]{:S(2)}, u32[]{:S(2)}) async-start(bf16[16,2,4096]{2,1,0:T(2,128)(2,1)} %reshape.101), calls=%async_computation.2 | async-start | bytes 524288 | tf_op jit(solution)/shard_map/all_to_all | solution.py:94
  121.0 370.3 %while.15 = (s32[]{:T(128)}, f32[16,4096]{1,0:T(8,128)S(1)}, s32[]{:T(128)}, bf16[256,512]{1,0:T(8,128)(2,1)S(1)}, bf16[256,4096]{1,0:T(8,128)(2,1)S(1)}, /*inde...) while((s32[]{:T(128)}, f32[16,4096]{1,0:T(8,128)S(1)}, ...), condition=%wide.region_9.10_spmd, body=%wide.region_8.9_spmd.sunk | while | flops 33619984 | bytes 3735892 | solution.py:84
  121.0 3.1 collective-permute-start
  124.1 3.3 collective-permute-done
  127.9 4.4 collective-permute-start
  132.3 8.0 %collective-permute-done = f32[16,4096]{1,0:T(8,128)S(1)} collective-permute-done((f32[16,4096]{1,0:T(8,128)S(1)}, f32[16,4096]{1,0:T(8,128)S(1)}, u32[]{:S(2)}, u32[]{:S(2)}) %collective-permute-start) | collective-permute-done | bytes 262176 | tf_op jit(solution)/shard_map/while/body/eval_jaxpr/ppermute | solution.py:9
  142.7 10.0 %collective-permute-done = f32[16,4096]{1,0:T(8,128)S(1)} collective-permute-done((f32[16,4096]{1,0:T(8,128)S(1)}, f32[16,4096]{1,0:T(8,128)S(1)}, u32[]{:S(2)}, u32[]{:S(2)}) %collective-permute-start) | collective-permute-done | bytes 262176 | tf_op jit(solution)/shard_map/while/body/eval_jaxpr/ppermute | solution.py:9
  153.2 1.9 collective-permute-start
  155.1 9.6 %collective-permute-done = f32[16,4096]{1,0:T(8,128)S(1)} collective-permute-done((f32[16,4096]{1,0:T(8,128)S(1)}, f32[16,4096]{1,0:T(8,128)S(1)}, u32[]{:S(2)}, u32[]{:S(2)}) %collective-permute-start) | collective-permute-done | bytes 262176 | tf_op jit(solution)/shard_map/while/body/eval_jaxpr/ppermute | solution.py:9
  165.3 1.9 collective-permute-start
  167.2 9.6 %collective-permute-done = f32[16,4096]{1,0:T(8,128)S(1)} collective-permute-done((f32[16,4096]{1,0:T(8,128)S(1)}, f32[16,4096]{1,0:T(8,128)S(1)}, u32[]{:S(2)}, u32[]{:S(2)}) %collective-permute-start) | collective-permute-done | bytes 262176 | tf_op jit(solution)/shard_map/while/body/eval_jaxpr/ppermute | solution.py:9
  177.3 1.9 collective-permute-start
  179.3 9.6 %collective-permute-done = f32[16,4096]{1,0:T(8,128)S(1)} collective-permute-done((f32[16,4096]{1,0:T(8,128)S(1)}, f32[16,4096]{1,0:T(8,128)S(1)}, u32[]{:S(2)}, u32[]{:S(2)}) %collective-permute-start) | collective-permute-done | bytes 262176 | tf_op jit(solution)/shard_map/while/body/eval_jaxpr/ppermute | solution.py:9
  189.4 1.9 collective-permute-start
  191.4 9.6 %collective-permute-done = f32[16,4096]{1,0:T(8,128)S(1)} collective-permute-done((f32[16,4096]{1,0:T(8,128)S(1)}, f32[16,4096]{1,0:T(8,128)S(1)}, u32[]{:S(2)}, u32[]{:S(2)}) %collective-permute-start) | collective-permute-done | bytes 262176 | tf_op jit(solution)/shard_map/while/body/eval_jaxpr/ppermute | solution.py:9
  203.4 9.6 %collective-permute-done = f32[16,4096]{1,0:T(8,128)S(1)} collective-permute-done((f32[16,4096]{1,0:T(8,128)S(1)}, f32[16,4096]{1,0:T(8,128)S(1)}, u32[]{:S(2)}, u32[]{:S(2)}) %collective-permute-start) | collective-permute-done | bytes 262176 | tf_op jit(solution)/shard_map/while/body/eval_jaxpr/ppermute | solution.py:9
  215.5 9.6 %collective-permute-done = f32[16,4096]{1,0:T(8,128)S(1)} collective-permute-done((f32[16,4096]{1,0:T(8,128)S(1)}, f32[16,4096]{1,0:T(8,128)S(1)}, u32[]{:S(2)}, u32[]{:S(2)}) %collective-permute-start) | collective-permute-done | bytes 262176 | tf_op jit(solution)/shard_map/while/body/eval_jaxpr/ppermute | solution.py:9
  225.6 1.9 collective-permute-start
  227.6 9.6 %collective-permute-done = f32[16,4096]{1,0:T(8,128)S(1)} collective-permute-done((f32[16,4096]{1,0:T(8,128)S(1)}, f32[16,4096]{1,0:T(8,128)S(1)}, u32[]{:S(2)}, u32[]{:S(2)}) %collective-permute-start) | collective-permute-done | bytes 262176 | tf_op jit(solution)/shard_map/while/body/eval_jaxpr/ppermute | solution.py:9
  237.7 1.9 collective-permute-start
  239.7 9.6 %collective-permute-done = f32[16,4096]{1,0:T(8,128)S(1)} collective-permute-done((f32[16,4096]{1,0:T(8,128)S(1)}, f32[16,4096]{1,0:T(8,128)S(1)}, u32[]{:S(2)}, u32[]{:S(2)}) %collective-permute-start) | collective-permute-done | bytes 262176 | tf_op jit(solution)/shard_map/while/body/eval_jaxpr/ppermute | solution.py:9
  249.8 1.9 collective-permute-start
  251.7 9.6 %collective-permute-done = f32[16,4096]{1,0:T(8,128)S(1)} collective-permute-done((f32[16,4096]{1,0:T(8,128)S(1)}, f32[16,4096]{1,0:T(8,128)S(1)}, u32[]{:S(2)}, u32[]{:S(2)}) %collective-permute-start) | collective-permute-done | bytes 262176 | tf_op jit(solution)/shard_map/while/body/eval_jaxpr/ppermute | solution.py:9
  261.9 1.9 collective-permute-start
  263.8 9.6 %collective-permute-done = f32[16,4096]{1,0:T(8,128)S(1)} collective-permute-done((f32[16,4096]{1,0:T(8,128)S(1)}, f32[16,4096]{1,0:T(8,128)S(1)}, u32[]{:S(2)}, u32[]{:S(2)}) %collective-permute-start) | collective-permute-done | bytes 262176 | tf_op jit(solution)/shard_map/while/body/eval_jaxpr/ppermute | solution.py:9
  273.9 1.9 collective-permute-start
  275.9 9.6 %collective-permute-done = f32[16,4096]{1,0:T(8,128)S(1)} collective-permute-done((f32[16,4096]{1,0:T(8,128)S(1)}, f32[16,4096]{1,0:T(8,128)S(1)}, u32[]{:S(2)}, u32[]{:S(2)}) %collective-permute-start) | collective-permute-done | bytes 262176 | tf_op jit(solution)/shard_map/while/body/eval_jaxpr/ppermute | solution.py:9
  288.0 9.6 %collective-permute-done = f32[16,4096]{1,0:T(8,128)S(1)} collective-permute-done((f32[16,4096]{1,0:T(8,128)S(1)}, f32[16,4096]{1,0:T(8,128)S(1)}, u32[]{:S(2)}, u32[]{:S(2)}) %collective-permute-start) | collective-permute-done | bytes 262176 | tf_op jit(solution)/shard_map/while/body/eval_jaxpr/ppermute | solution.py:9
  298.1 1.9 collective-permute-start
  300.0 9.6 %collective-permute-done = f32[16,4096]{1,0:T(8,128)S(1)} collective-permute-done((f32[16,4096]{1,0:T(8,128)S(1)}, f32[16,4096]{1,0:T(8,128)S(1)}, u32[]{:S(2)}, u32[]{:S(2)}) %collective-permute-start) | collective-permute-done | bytes 262176 | tf_op jit(solution)/shard_map/while/body/eval_jaxpr/ppermute | solution.py:9
  310.2 1.9 collective-permute-start
  312.1 9.6 %collective-permute-done = f32[16,4096]{1,0:T(8,128)S(1)} collective-permute-done((f32[16,4096]{1,0:T(8,128)S(1)}, f32[16,4096]{1,0:T(8,128)S(1)}, u32[]{:S(2)}, u32[]{:S(2)}) %collective-permute-start) | collective-permute-done | bytes 262176 | tf_op jit(solution)/shard_map/while/body/eval_jaxpr/ppermute | solution.py:9
  322.2 1.9 collective-permute-start
  324.2 9.6 %collective-permute-done = f32[16,4096]{1,0:T(8,128)S(1)} collective-permute-done((f32[16,4096]{1,0:T(8,128)S(1)}, f32[16,4096]{1,0:T(8,128)S(1)}, u32[]{:S(2)}, u32[]{:S(2)}) %collective-permute-start) | collective-permute-done | bytes 262176 | tf_op jit(solution)/shard_map/while/body/eval_jaxpr/ppermute | solution.py:9
  334.3 1.9 collective-permute-start
  336.3 9.6 %collective-permute-done = f32[16,4096]{1,0:T(8,128)S(1)} collective-permute-done((f32[16,4096]{1,0:T(8,128)S(1)}, f32[16,4096]{1,0:T(8,128)S(1)}, u32[]{:S(2)}, u32[]{:S(2)}) %collective-permute-start) | collective-permute-done | bytes 262176 | tf_op jit(solution)/shard_map/while/body/eval_jaxpr/ppermute | solution.py:9
  346.4 1.9 collective-permute-start
  348.3 9.6 %collective-permute-done = f32[16,4096]{1,0:T(8,128)S(1)} collective-permute-done((f32[16,4096]{1,0:T(8,128)S(1)}, f32[16,4096]{1,0:T(8,128)S(1)}, u32[]{:S(2)}, u32[]{:S(2)}) %collective-permute-start) | collective-permute-done | bytes 262176 | tf_op jit(solution)/shard_map/while/body/eval_jaxpr/ppermute | solution.py:9
  360.4 9.6 %collective-permute-done = f32[16,4096]{1,0:T(8,128)S(1)} collective-permute-done((f32[16,4096]{1,0:T(8,128)S(1)}, f32[16,4096]{1,0:T(8,128)S(1)}, u32[]{:S(2)}, u32[]{:S(2)}) %collective-permute-start) | collective-permute-done | bytes 262176 | tf_op jit(solution)/shard_map/while/body/eval_jaxpr/ppermute | solution.py:9
  370.5 1.9 collective-permute-start
  372.5 9.6 %collective-permute-done = f32[16,4096]{1,0:T(8,128)S(1)} collective-permute-done((f32[16,4096]{1,0:T(8,128)S(1)}, f32[16,4096]{1,0:T(8,128)S(1)}, u32[]{:S(2)}, u32[]{:S(2)}) %collective-permute-start) | collective-permute-done | bytes 262176 | tf_op jit(solution)/shard_map/while/body/eval_jaxpr/ppermute | solution.py:9
  382.6 1.9 collective-permute-start
  384.6 9.6 %collective-permute-done = f32[16,4096]{1,0:T(8,128)S(1)} collective-permute-done((f32[16,4096]{1,0:T(8,128)S(1)}, f32[16,4096]{1,0:T(8,128)S(1)}, u32[]{:S(2)}, u32[]{:S(2)}) %collective-permute-start) | collective-permute-done | bytes 262176 | tf_op jit(solution)/shard_map/while/body/eval_jaxpr/ppermute | solution.py:9
  394.7 1.9 collective-permute-start
  396.6 9.6 %collective-permute-done = f32[16,4096]{1,0:T(8,128)S(1)} collective-permute-done((f32[16,4096]{1,0:T(8,128)S(1)}, f32[16,4096]{1,0:T(8,128)S(1)}, u32[]{:S(2)}, u32[]{:S(2)}) %collective-permute-start) | collective-permute-done | bytes 262176 | tf_op jit(solution)/shard_map/while/body/eval_jaxpr/ppermute | solution.py:9
  406.8 1.9 collective-permute-start
  408.7 9.6 %collective-permute-done = f32[16,4096]{1,0:T(8,128)S(1)} collective-permute-done((f32[16,4096]{1,0:T(8,128)S(1)}, f32[16,4096]{1,0:T(8,128)S(1)}, u32[]{:S(2)}, u32[]{:S(2)}) %collective-permute-start) | collective-permute-done | bytes 262176 | tf_op jit(solution)/shard_map/while/body/eval_jaxpr/ppermute | solution.py:9
  418.8 1.9 collective-permute-start
  420.8 9.6 %collective-permute-done = f32[16,4096]{1,0:T(8,128)S(1)} collective-permute-done((f32[16,4096]{1,0:T(8,128)S(1)}, f32[16,4096]{1,0:T(8,128)S(1)}, u32[]{:S(2)}, u32[]{:S(2)}) %collective-permute-start) | collective-permute-done | bytes 262176 | tf_op jit(solution)/shard_map/while/body/eval_jaxpr/ppermute | solution.py:9
  432.9 9.6 %collective-permute-done = f32[16,4096]{1,0:T(8,128)S(1)} collective-permute-done((f32[16,4096]{1,0:T(8,128)S(1)}, f32[16,4096]{1,0:T(8,128)S(1)}, u32[]{:S(2)}, u32[]{:S(2)}) %collective-permute-start) | collective-permute-done | bytes 262176 | tf_op jit(solution)/shard_map/while/body/eval_jaxpr/ppermute | solution.py:9
  443.0 1.9 collective-permute-start
  444.9 9.6 %collective-permute-done = f32[16,4096]{1,0:T(8,128)S(1)} collective-permute-done((f32[16,4096]{1,0:T(8,128)S(1)}, f32[16,4096]{1,0:T(8,128)S(1)}, u32[]{:S(2)}, u32[]{:S(2)}) %collective-permute-start) | collective-permute-done | bytes 262176 | tf_op jit(solution)/shard_map/while/body/eval_jaxpr/ppermute | solution.py:9
  457.0 9.6 %collective-permute-done = f32[16,4096]{1,0:T(8,128)S(1)} collective-permute-done((f32[16,4096]{1,0:T(8,128)S(1)}, f32[16,4096]{1,0:T(8,128)S(1)}, u32[]{:S(2)}, u32[]{:S(2)}) %collective-permute-start) | collective-permute-done | bytes 262176 | tf_op jit(solution)/shard_map/while/body/eval_jaxpr/ppermute | solution.py:9
  467.1 1.9 collective-permute-start
  469.1 9.6 %collective-permute-done = f32[16,4096]{1,0:T(8,128)S(1)} collective-permute-done((f32[16,4096]{1,0:T(8,128)S(1)}, f32[16,4096]{1,0:T(8,128)S(1)}, u32[]{:S(2)}, u32[]{:S(2)}) %collective-permute-start) | collective-permute-done | bytes 262176 | tf_op jit(solution)/shard_map/while/body/eval_jaxpr/ppermute | solution.py:9
  481.2 9.6 %collective-permute-done = f32[16,4096]{1,0:T(8,128)S(1)} collective-permute-done((f32[16,4096]{1,0:T(8,128)S(1)}, f32[16,4096]{1,0:T(8,128)S(1)}, u32[]{:S(2)}, u32[]{:S(2)}) %collective-permute-start) | collective-permute-done | bytes 262176 | tf_op jit(solution)/shard_map/while/body/eval_jaxpr/ppermute | solution.py:9
  (73 shorter events, 40.8 us)
Async XLA Ops:
  7.2 22.2 %copy-start = (bf16[1,16,4096]{2,1,0:T(8,128)(2,1)S(1)}, bf16[1,16,4096]{2,1,0:T(8,128)(2,1)}, u32[]{:S(2)}) copy-start(bf16[1,16,4096]{2,1,0:T(8,128)(2,1)} %param.10) | copy-start | bytes 393220
  7.2 64.5 %copy-start.1 = (bf16[1,256,4096]{2,1,0:T(8,128)(2,1)S(1)}, bf16[1,256,4096]{2,1,0:T(8,128)(2,1)}, u32[]{:S(2)}) copy-start(bf16[1,256,4096]{2,1,0:T(8,128)(2,1)} %param.7) | copy-start | bytes 6291460
  7.2 85.2 %all-gather.3.cloned.1.call-start = ((), (), s32[]{:S(2)}) async-start(), calls=%async_computation.3 | async-start | bytes 4325376 | tf_op jit(solution)/shard_map/all_gather | solution.py:54
  11.0 31.9 %all-to-all-start = ((bf16[16,1,2]{2,1,0:T(2,128)(2,1)}), bf16[16,1,2]{2,1,0:T(2,128)(2,1)S(1)}, u32[]{:S(2)}, u32[]{:S(2)}) async-start(bf16[16,1,2]{2,1,0:T(2,128)(2,1)} %all_to_all.16), calls=%async_computation | async-start | bytes 16384 | tf_op jit(solution)/shard_map/all_to_all | solution.py:41
  42.9 28.7 %all-to-all-start.1 = ((bf16[16,2,4096]{2,1,0:T(2,128)(2,1)}), bf16[16,2,4096]{2,1,0:T(2,128)(2,1)S(1)}, u32[]{:S(2)}, u32[]{:S(2)}) async-start(bf16[16,2,4096]{2,1,0:T(2,128)(2,1)} %reshape.99), calls=%async_computation.1 | async-start | bytes 524288 | tf_op jit(solution)/shard_map/all_to_all | solution.py:40
  72.5 23.6 %copy-start.3 = (s32[1,256]{1,0:T(1,128)S(1)}, s32[1,256]{1,0:T(1,128)}, u32[]{:S(2)}) copy-start(s32[1,256]{1,0:T(1,128)} %param.9) | copy-start | bytes 3076
  92.4 5.3 %copy-start.2 = (bf16[1,512,4096]{2,1,0:T(8,128)(2,1)S(1)}, bf16[1,512,4096]{2,1,0:T(8,128)(2,1)}, u32[]{:S(2)}) copy-start(bf16[1,512,4096]{2,1,0:T(8,128)(2,1)} %all-gather.3.cloned.1.call-done) | copy-start | bytes 12582916
  105.7 386.3 %all-to-all-start.2 = ((bf16[16,2,4096]{2,1,0:T(2,128)(2,1)}), bf16[16,2,4096]{2,1,0:T(2,128)(2,1)S(1)}, u32[]{:S(2)}, u32[]{:S(2)}) async-start(bf16[16,2,4096]{2,1,0:T(2,128)(2,1)} %reshape.101), calls=%async_computation.2 | async-start | bytes 524288 | tf_op jit(solution)/shard_map/all_to_all | solution.py:94
  121.0 6.4 %collective-permute-start = (f32[16,4096]{1,0:T(8,128)S(1)}, f32[16,4096]{1,0:T(8,128)S(1)}, u32[]{:S(2)}, u32[]{:S(2)}) collective-permute-start(f32[16,4096]{1,0:T(8,128)S(1)} %get-tuple-element.201), channel_id=1, source_target_pairs={{0,16},{16,32},{32,48},{48,64},{64,80},{80,96},{96,112},{112,128},... | collective-permute-start | bytes 786440 | tf_op jit(solution)/shard_map/while/body/eval_jaxpr/ppermute | solution.py:9
  127.9 12.4 %collective-permute-start = (f32[16,4096]{1,0:T(8,128)S(1)}, f32[16,4096]{1,0:T(8,128)S(1)}, u32[]{:S(2)}, u32[]{:S(2)}) collective-permute-start(f32[16,4096]{1,0:T(8,128)S(1)} %get-tuple-element.201), channel_id=1, source_target_pairs={{0,16},{16,32},{32,48},{48,64},{64,80},{80,96},{96,112},{112,128},... | collective-permute-start | bytes 786440 | tf_op jit(solution)/shard_map/while/body/eval_jaxpr/ppermute | solution.py:9
  140.8 11.9 %collective-permute-start = (f32[16,4096]{1,0:T(8,128)S(1)}, f32[16,4096]{1,0:T(8,128)S(1)}, u32[]{:S(2)}, u32[]{:S(2)}) collective-permute-start(f32[16,4096]{1,0:T(8,128)S(1)} %get-tuple-element.201), channel_id=1, source_target_pairs={{0,16},{16,32},{32,48},{48,64},{64,80},{80,96},{96,112},{112,128},... | collective-permute-start | bytes 786440 | tf_op jit(solution)/shard_map/while/body/eval_jaxpr/ppermute | solution.py:9
  153.2 11.6 %collective-permute-start = (f32[16,4096]{1,0:T(8,128)S(1)}, f32[16,4096]{1,0:T(8,128)S(1)}, u32[]{:S(2)}, u32[]{:S(2)}) collective-permute-start(f32[16,4096]{1,0:T(8,128)S(1)} %get-tuple-element.201), channel_id=1, source_target_pairs={{0,16},{16,32},{32,48},{48,64},{64,80},{80,96},{96,112},{112,128},... | collective-permute-start | bytes 786440 | tf_op jit(solution)/shard_map/while/body/eval_jaxpr/ppermute | solution.py:9
  165.3 11.6 %collective-permute-start = (f32[16,4096]{1,0:T(8,128)S(1)}, f32[16,4096]{1,0:T(8,128)S(1)}, u32[]{:S(2)}, u32[]{:S(2)}) collective-permute-start(f32[16,4096]{1,0:T(8,128)S(1)} %get-tuple-element.201), channel_id=1, source_target_pairs={{0,16},{16,32},{32,48},{48,64},{64,80},{80,96},{96,112},{112,128},... | collective-permute-start | bytes 786440 | tf_op jit(solution)/shard_map/while/body/eval_jaxpr/ppermute | solution.py:9
  177.3 11.6 %collective-permute-start = (f32[16,4096]{1,0:T(8,128)S(1)}, f32[16,4096]{1,0:T(8,128)S(1)}, u32[]{:S(2)}, u32[]{:S(2)}) collective-permute-start(f32[16,4096]{1,0:T(8,128)S(1)} %get-tuple-element.201), channel_id=1, source_target_pairs={{0,16},{16,32},{32,48},{48,64},{64,80},{80,96},{96,112},{112,128},... | collective-permute-start | bytes 786440 | tf_op jit(solution)/shard_map/while/body/eval_jaxpr/ppermute | solution.py:9
  189.4 11.6 %collective-permute-start = (f32[16,4096]{1,0:T(8,128)S(1)}, f32[16,4096]{1,0:T(8,128)S(1)}, u32[]{:S(2)}, u32[]{:S(2)}) collective-permute-start(f32[16,4096]{1,0:T(8,128)S(1)} %get-tuple-element.201), channel_id=1, source_target_pairs={{0,16},{16,32},{32,48},{48,64},{64,80},{80,96},{96,112},{112,128},... | collective-permute-start | bytes 786440 | tf_op jit(solution)/shard_map/while/body/eval_jaxpr/ppermute | solution.py:9
  201.5 11.6 %collective-permute-start = (f32[16,4096]{1,0:T(8,128)S(1)}, f32[16,4096]{1,0:T(8,128)S(1)}, u32[]{:S(2)}, u32[]{:S(2)}) collective-permute-start(f32[16,4096]{1,0:T(8,128)S(1)} %get-tuple-element.201), channel_id=1, source_target_pairs={{0,16},{16,32},{32,48},{48,64},{64,80},{80,96},{96,112},{112,128},... | collective-permute-start | bytes 786440 | tf_op jit(solution)/shard_map/while/body/eval_jaxpr/ppermute | solution.py:9
  213.6 11.6 %collective-permute-start = (f32[16,4096]{1,0:T(8,128)S(1)}, f32[16,4096]{1,0:T(8,128)S(1)}, u32[]{:S(2)}, u32[]{:S(2)}) collective-permute-start(f32[16,4096]{1,0:T(8,128)S(1)} %get-tuple-element.201), channel_id=1, source_target_pairs={{0,16},{16,32},{32,48},{48,64},{64,80},{80,96},{96,112},{112,128},... | collective-permute-start | bytes 786440 | tf_op jit(solution)/shard_map/while/body/eval_jaxpr/ppermute | solution.py:9
  225.6 11.6 %collective-permute-start = (f32[16,4096]{1,0:T(8,128)S(1)}, f32[16,4096]{1,0:T(8,128)S(1)}, u32[]{:S(2)}, u32[]{:S(2)}) collective-permute-start(f32[16,4096]{1,0:T(8,128)S(1)} %get-tuple-element.201), channel_id=1, source_target_pairs={{0,16},{16,32},{32,48},{48,64},{64,80},{80,96},{96,112},{112,128},... | collective-permute-start | bytes 786440 | tf_op jit(solution)/shard_map/while/body/eval_jaxpr/ppermute | solution.py:9
  237.7 11.6 %collective-permute-start = (f32[16,4096]{1,0:T(8,128)S(1)}, f32[16,4096]{1,0:T(8,128)S(1)}, u32[]{:S(2)}, u32[]{:S(2)}) collective-permute-start(f32[16,4096]{1,0:T(8,128)S(1)} %get-tuple-element.201), channel_id=1, source_target_pairs={{0,16},{16,32},{32,48},{48,64},{64,80},{80,96},{96,112},{112,128},... | collective-permute-start | bytes 786440 | tf_op jit(solution)/shard_map/while/body/eval_jaxpr/ppermute | solution.py:9
  249.8 11.6 %collective-permute-start = (f32[16,4096]{1,0:T(8,128)S(1)}, f32[16,4096]{1,0:T(8,128)S(1)}, u32[]{:S(2)}, u32[]{:S(2)}) collective-permute-start(f32[16,4096]{1,0:T(8,128)S(1)} %get-tuple-element.201), channel_id=1, source_target_pairs={{0,16},{16,32},{32,48},{48,64},{64,80},{80,96},{96,112},{112,128},... | collective-permute-start | bytes 786440 | tf_op jit(solution)/shard_map/while/body/eval_jaxpr/ppermute | solution.py:9
  261.9 11.6 %collective-permute-start = (f32[16,4096]{1,0:T(8,128)S(1)}, f32[16,4096]{1,0:T(8,128)S(1)}, u32[]{:S(2)}, u32[]{:S(2)}) collective-permute-start(f32[16,4096]{1,0:T(8,128)S(1)} %get-tuple-element.201), channel_id=1, source_target_pairs={{0,16},{16,32},{32,48},{48,64},{64,80},{80,96},{96,112},{112,128},... | collective-permute-start | bytes 786440 | tf_op jit(solution)/shard_map/while/body/eval_jaxpr/ppermute | solution.py:9
  273.9 11.6 %collective-permute-start = (f32[16,4096]{1,0:T(8,128)S(1)}, f32[16,4096]{1,0:T(8,128)S(1)}, u32[]{:S(2)}, u32[]{:S(2)}) collective-permute-start(f32[16,4096]{1,0:T(8,128)S(1)} %get-tuple-element.201), channel_id=1, source_target_pairs={{0,16},{16,32},{32,48},{48,64},{64,80},{80,96},{96,112},{112,128},... | collective-permute-start | bytes 786440 | tf_op jit(solution)/shard_map/while/body/eval_jaxpr/ppermute | solution.py:9
  286.0 11.6 %collective-permute-start = (f32[16,4096]{1,0:T(8,128)S(1)}, f32[16,4096]{1,0:T(8,128)S(1)}, u32[]{:S(2)}, u32[]{:S(2)}) collective-permute-start(f32[16,4096]{1,0:T(8,128)S(1)} %get-tuple-element.201), channel_id=1, source_target_pairs={{0,16},{16,32},{32,48},{48,64},{64,80},{80,96},{96,112},{112,128},... | collective-permute-start | bytes 786440 | tf_op jit(solution)/shard_map/while/body/eval_jaxpr/ppermute | solution.py:9
  298.1 11.6 %collective-permute-start = (f32[16,4096]{1,0:T(8,128)S(1)}, f32[16,4096]{1,0:T(8,128)S(1)}, u32[]{:S(2)}, u32[]{:S(2)}) collective-permute-start(f32[16,4096]{1,0:T(8,128)S(1)} %get-tuple-element.201), channel_id=1, source_target_pairs={{0,16},{16,32},{32,48},{48,64},{64,80},{80,96},{96,112},{112,128},... | collective-permute-start | bytes 786440 | tf_op jit(solution)/shard_map/while/body/eval_jaxpr/ppermute | solution.py:9
  310.2 11.6 %collective-permute-start = (f32[16,4096]{1,0:T(8,128)S(1)}, f32[16,4096]{1,0:T(8,128)S(1)}, u32[]{:S(2)}, u32[]{:S(2)}) collective-permute-start(f32[16,4096]{1,0:T(8,128)S(1)} %get-tuple-element.201), channel_id=1, source_target_pairs={{0,16},{16,32},{32,48},{48,64},{64,80},{80,96},{96,112},{112,128},... | collective-permute-start | bytes 786440 | tf_op jit(solution)/shard_map/while/body/eval_jaxpr/ppermute | solution.py:9
  322.2 11.6 %collective-permute-start = (f32[16,4096]{1,0:T(8,128)S(1)}, f32[16,4096]{1,0:T(8,128)S(1)}, u32[]{:S(2)}, u32[]{:S(2)}) collective-permute-start(f32[16,4096]{1,0:T(8,128)S(1)} %get-tuple-element.201), channel_id=1, source_target_pairs={{0,16},{16,32},{32,48},{48,64},{64,80},{80,96},{96,112},{112,128},... | collective-permute-start | bytes 786440 | tf_op jit(solution)/shard_map/while/body/eval_jaxpr/ppermute | solution.py:9
  334.3 11.6 %collective-permute-start = (f32[16,4096]{1,0:T(8,128)S(1)}, f32[16,4096]{1,0:T(8,128)S(1)}, u32[]{:S(2)}, u32[]{:S(2)}) collective-permute-start(f32[16,4096]{1,0:T(8,128)S(1)} %get-tuple-element.201), channel_id=1, source_target_pairs={{0,16},{16,32},{32,48},{48,64},{64,80},{80,96},{96,112},{112,128},... | collective-permute-start | bytes 786440 | tf_op jit(solution)/shard_map/while/body/eval_jaxpr/ppermute | solution.py:9
  346.4 11.6 %collective-permute-start = (f32[16,4096]{1,0:T(8,128)S(1)}, f32[16,4096]{1,0:T(8,128)S(1)}, u32[]{:S(2)}, u32[]{:S(2)}) collective-permute-start(f32[16,4096]{1,0:T(8,128)S(1)} %get-tuple-element.201), channel_id=1, source_target_pairs={{0,16},{16,32},{32,48},{48,64},{64,80},{80,96},{96,112},{112,128},... | collective-permute-start | bytes 786440 | tf_op jit(solution)/shard_map/while/body/eval_jaxpr/ppermute | solution.py:9
  358.5 11.6 %collective-permute-start = (f32[16,4096]{1,0:T(8,128)S(1)}, f32[16,4096]{1,0:T(8,128)S(1)}, u32[]{:S(2)}, u32[]{:S(2)}) collective-permute-start(f32[16,4096]{1,0:T(8,128)S(1)} %get-tuple-element.201), channel_id=1, source_target_pairs={{0,16},{16,32},{32,48},{48,64},{64,80},{80,96},{96,112},{112,128},... | collective-permute-start | bytes 786440 | tf_op jit(solution)/shard_map/while/body/eval_jaxpr/ppermute | solution.py:9
  370.5 11.6 %collective-permute-start = (f32[16,4096]{1,0:T(8,128)S(1)}, f32[16,4096]{1,0:T(8,128)S(1)}, u32[]{:S(2)}, u32[]{:S(2)}) collective-permute-start(f32[16,4096]{1,0:T(8,128)S(1)} %get-tuple-element.201), channel_id=1, source_target_pairs={{0,16},{16,32},{32,48},{48,64},{64,80},{80,96},{96,112},{112,128},... | collective-permute-start | bytes 786440 | tf_op jit(solution)/shard_map/while/body/eval_jaxpr/ppermute | solution.py:9
  382.6 11.6 %collective-permute-start = (f32[16,4096]{1,0:T(8,128)S(1)}, f32[16,4096]{1,0:T(8,128)S(1)}, u32[]{:S(2)}, u32[]{:S(2)}) collective-permute-start(f32[16,4096]{1,0:T(8,128)S(1)} %get-tuple-element.201), channel_id=1, source_target_pairs={{0,16},{16,32},{32,48},{48,64},{64,80},{80,96},{96,112},{112,128},... | collective-permute-start | bytes 786440 | tf_op jit(solution)/shard_map/while/body/eval_jaxpr/ppermute | solution.py:9
  394.7 11.6 %collective-permute-start = (f32[16,4096]{1,0:T(8,128)S(1)}, f32[16,4096]{1,0:T(8,128)S(1)}, u32[]{:S(2)}, u32[]{:S(2)}) collective-permute-start(f32[16,4096]{1,0:T(8,128)S(1)} %get-tuple-element.201), channel_id=1, source_target_pairs={{0,16},{16,32},{32,48},{48,64},{64,80},{80,96},{96,112},{112,128},... | collective-permute-start | bytes 786440 | tf_op jit(solution)/shard_map/while/body/eval_jaxpr/ppermute | solution.py:9
  406.8 11.6 %collective-permute-start = (f32[16,4096]{1,0:T(8,128)S(1)}, f32[16,4096]{1,0:T(8,128)S(1)}, u32[]{:S(2)}, u32[]{:S(2)}) collective-permute-start(f32[16,4096]{1,0:T(8,128)S(1)} %get-tuple-element.201), channel_id=1, source_target_pairs={{0,16},{16,32},{32,48},{48,64},{64,80},{80,96},{96,112},{112,128},... | collective-permute-start | bytes 786440 | tf_op jit(solution)/shard_map/while/body/eval_jaxpr/ppermute | solution.py:9
  418.8 11.6 %collective-permute-start = (f32[16,4096]{1,0:T(8,128)S(1)}, f32[16,4096]{1,0:T(8,128)S(1)}, u32[]{:S(2)}, u32[]{:S(2)}) collective-permute-start(f32[16,4096]{1,0:T(8,128)S(1)} %get-tuple-element.201), channel_id=1, source_target_pairs={{0,16},{16,32},{32,48},{48,64},{64,80},{80,96},{96,112},{112,128},... | collective-permute-start | bytes 786440 | tf_op jit(solution)/shard_map/while/body/eval_jaxpr/ppermute | solution.py:9
  430.9 11.6 %collective-permute-start = (f32[16,4096]{1,0:T(8,128)S(1)}, f32[16,4096]{1,0:T(8,128)S(1)}, u32[]{:S(2)}, u32[]{:S(2)}) collective-permute-start(f32[16,4096]{1,0:T(8,128)S(1)} %get-tuple-element.201), channel_id=1, source_target_pairs={{0,16},{16,32},{32,48},{48,64},{64,80},{80,96},{96,112},{112,128},... | collective-permute-start | bytes 786440 | tf_op jit(solution)/shard_map/while/body/eval_jaxpr/ppermute | solution.py:9
  443.0 11.6 %collective-permute-start = (f32[16,4096]{1,0:T(8,128)S(1)}, f32[16,4096]{1,0:T(8,128)S(1)}, u32[]{:S(2)}, u32[]{:S(2)}) collective-permute-start(f32[16,4096]{1,0:T(8,128)S(1)} %get-tuple-element.201), channel_id=1, source_target_pairs={{0,16},{16,32},{32,48},{48,64},{64,80},{80,96},{96,112},{112,128},... | collective-permute-start | bytes 786440 | tf_op jit(solution)/shard_map/while/body/eval_jaxpr/ppermute | solution.py:9
  455.1 11.6 %collective-permute-start = (f32[16,4096]{1,0:T(8,128)S(1)}, f32[16,4096]{1,0:T(8,128)S(1)}, u32[]{:S(2)}, u32[]{:S(2)}) collective-permute-start(f32[16,4096]{1,0:T(8,128)S(1)} %get-tuple-element.201), channel_id=1, source_target_pairs={{0,16},{16,32},{32,48},{48,64},{64,80},{80,96},{96,112},{112,128},... | collective-permute-start | bytes 786440 | tf_op jit(solution)/shard_map/while/body/eval_jaxpr/ppermute | solution.py:9
  467.1 11.6 %collective-permute-start = (f32[16,4096]{1,0:T(8,128)S(1)}, f32[16,4096]{1,0:T(8,128)S(1)}, u32[]{:S(2)}, u32[]{:S(2)}) collective-permute-start(f32[16,4096]{1,0:T(8,128)S(1)} %get-tuple-element.201), channel_id=1, source_target_pairs={{0,16},{16,32},{32,48},{48,64},{64,80},{80,96},{96,112},{112,128},... | collective-permute-start | bytes 786440 | tf_op jit(solution)/shard_map/while/body/eval_jaxpr/ppermute | solution.py:9
  479.2 11.6 %collective-permute-start = (f32[16,4096]{1,0:T(8,128)S(1)}, f32[16,4096]{1,0:T(8,128)S(1)}, u32[]{:S(2)}, u32[]{:S(2)}) collective-permute-start(f32[16,4096]{1,0:T(8,128)S(1)} %get-tuple-element.201), channel_id=1, source_target_pairs={{0,16},{16,32},{32,48},{48,64},{64,80},{80,96},{96,112},{112,128},... | collective-permute-start | bytes 786440 | tf_op jit(solution)/shard_map/while/body/eval_jaxpr/ppermute | solution.py:9
Sparse Core Ops, SparseCore 0:
  10.2 82.1 all-gather.2
where the time goes:
time: 509 us; the launch traced here: 500 us
  waiting for transfers between devices  349 us (69%)
  starting transfers between devices  99.8 us (20%)
  matrix products  28.6 us (6%)
  between operations  14.2 us (3%)
    ppermute x31, waiting for transfers between devices, from_behind(): return lax.ppermute(x, axis, [(i, (i + by) % count) for i in range(count)])  291 us
    ppermute x31, starting transfers between devices, from_behind(): return lax.ppermute(x, axis, [(i, (i + by) % count) for i in range(count)])  63.1 us
    all_to_all x1, waiting for transfers between devices, body(): lax.all_to_all(packed, 'group', split_axis=0, concat_axis=0, tiled=True)  25 us
    all_gather x1, waiting for transfers between devices, body(): gathered = lax.all_gather(own_passages, 'blk', axis=0, tiled=True)  19.9 us
    all_to_all x1, starting transfers between devices, body(): lax.all_to_all(live_flags, 'group', split_axis=0, concat_axis=0, tiled=True)  18.4 us
    dot_general x32, matrix products, contrib(): jnp.einsum('qp,qd->pd', coef_cols, query_rows, preferred_element_type=jnp...  15.4 us
    all_to_all x1, starting transfers between devices, body(): lax.all_to_all(slot_grads, 'group', split_axis=0, concat_axis=0, tiled=True)  14.8 us
    all_to_all x1, waiting for transfers between devices, body(): lax.all_to_all(live_flags, 'group', split_axis=0, concat_axis=0, tiled=True)  12.3 us
  transfers between devices with their start and end apart: 35, of which 34 were waited for; matrix products, arithmetic and copies ran while one was open for 4% of the time, Pallas kernels for 0%

commit v1 on v0

v1 whole, which is shorter than its diff:
```python
import jax
import jax.numpy as jnp
from jax import lax
from jax.sharding import PartitionSpec as P

NZ, NX, NC = 4, 4, 2
NY, NH = 4, 4
FLAG = 128
BF16, F32 = jnp.bfloat16, jnp.float32


def blk_perm(dz=0, dx=0, dc=0):
    out = []
    for z in range(NZ):
        for x in range(NX):
            for c in range(NC):
                to = (((z + dz) % NZ) * NX + (x + dx) % NX) * NC + (c + dc) % NC
                out.append(((z * NX + x) * NC + c, to))
    return out


def group_perm(dy=0, dh=0):
    return [
        (y * NH + h, ((y + dy) % NY) * NH + (h + dh) % NH) for y in range(NY) for h in range(NH)
    ]


def dot_t(a, b):
    return lax.dot_general(a, b, (((1,), (1,)), ((), ())), preferred_element_type=F32)


def t_dot(a, b):
    return lax.dot_general(a, b, (((0,), (0,)), ((), ())), preferred_element_type=F32)


def dot(a, b):
    return jnp.dot(a, b, preferred_element_type=F32)


def split(a):
    hi = a.astype(BF16)
    return hi, (a - hi.astype(F32)).astype(BF16)


def body(queries, passages, positives, hard_rows, hard_dest):
    q = queries[0]
    own = passages[0]
    targets = positives[0]
    owned_hard = hard_rows[0]
    routes = hard_dest[0, :, 0]
    width = q.shape[1]
    rows = own.shape[0]
    hard_count = owned_hard.shape[0]
    groups = NY * NH
    slots = max(2, 2 * hard_count // groups)
    scale = width ** (-0.5)
    blk = lax.axis_index("blk")
    grp = lax.axis_index("group")
    my_z, my_x, my_c = blk // (NX * NC), blk // NC % NX, blk % NC
    my_y, my_h = grp // NH, grp % NH

    rel = ((routes // NH - my_y) % NY) * NH + (routes % NH - my_h) % NH
    same = (rel[:, None] == rel[None, :]) & (
        jnp.arange(hard_count)[:, None] > jnp.arange(hard_count)[None, :]
    )
    slot_of = rel * slots + jnp.sum(same.astype(jnp.int32), axis=1)
    placing = (slot_of[None, :] == jnp.arange(groups * slots)[:, None]).astype(BF16)
    wide = jnp.concatenate([owned_hard, jnp.ones((hard_count, FLAG), BF16)], axis=1)
    packed = dot(placing, wide).astype(BF16)
    per_y = NH * slots

    with jax.named_scope("gather_z"):
        parts = [own] + [lax.ppermute(own, "blk", blk_perm(dz=d)) for d in range(1, NZ)]
        z_rows = jnp.concatenate(parts, axis=0)
    with jax.named_scope("hard_y"):
        from_y = [
            packed[d * per_y : (d + 1) * per_y]
            if d == 0
            else lax.ppermute(packed[d * per_y : (d + 1) * per_y], "group", group_perm(dy=d))
            for d in range(NY)
        ]
    with jax.named_scope("gather_x"):
        parts = [z_rows] + [lax.ppermute(z_rows, "blk", blk_perm(dx=d)) for d in range(1, NX)]
        half0 = jnp.concatenate(parts, axis=0)
    with jax.named_scope("hard_h"):
        to_h = [
            jnp.concatenate([f[d * slots : (d + 1) * slots] for f in from_y], axis=0)
            for d in range(NH)
        ]
        received = jnp.concatenate(
            [
                to_h[d] if d == 0 else lax.ppermute(to_h[d], "group", group_perm(dh=d))
                for d in range(NH)
            ],
            axis=0,
        )
    with jax.named_scope("gather_core"):
        half1 = lax.ppermute(half0, "blk", blk_perm(dc=1))

    hard = received[:, :width]
    live = received[:, width] > 0.5
    half = half0.shape[0]

    owner = targets // rows
    o_z, o_x, o_c = owner // (NX * NC), owner // NC % NX, owner % NC
    column = (
        ((my_c - o_c) % NC) * half
        + (((my_x - o_x) % NX) * NZ + (my_z - o_z) % NZ) * rows
        + targets % rows
    )
    hot0 = column[:, None] == jnp.arange(half)[None, :]
    hot1 = column[:, None] == (jnp.arange(half) + half)[None, :]

    with jax.named_scope("scores"):
        s0 = scale * dot_t(q, half0)
        s1 = scale * dot_t(q, half1)
        sh = jnp.where(live[None, :], scale * dot_t(q, hard), -jnp.inf)
        top = jnp.maximum(
            jnp.maximum(jnp.max(s0, axis=1), jnp.max(s1, axis=1)), jnp.max(sh, axis=1)
        )
        total = (
            jnp.sum(jnp.exp(s0 - top[:, None]), axis=1)
            + jnp.sum(jnp.exp(s1 - top[:, None]), axis=1)
            + jnp.sum(jnp.exp(sh - top[:, None]), axis=1)
        )
        log_total = top + jnp.log(total)
        c0 = jnp.exp(s0 - log_total[:, None]) - hot0.astype(F32)
        c1 = jnp.exp(s1 - log_total[:, None]) - hot1.astype(F32)
        ph = jnp.exp(sh - log_total[:, None])
        at_target = jnp.sum(jnp.where(hot0, s0, 0.0), axis=1) + jnp.sum(
            jnp.where(hot1, s1, 0.0), axis=1
        )
        loss_rows = log_total - at_target

    c0_hi, c0_lo = split(c0)
    c1_hi, c1_lo = split(c1)
    ph_hi, ph_lo = split(ph)
    with jax.named_scope("scatter_core"):
        away = t_dot(c1_hi, q).astype(BF16)
        away = lax.ppermute(away, "blk", blk_perm(dc=1))
    with jax.named_scope("hard_grad"):
        g = (scale * t_dot(ph_hi, q)).astype(BF16)
    with jax.named_scope("scatter_x"):
        total0 = t_dot(c0_hi, q) + away.astype(F32)
        n = half // NX
        acc = total0[:n]
        for d in range(1, NX):
            acc = acc + lax.ppermute(
                total0[d * n : (d + 1) * n].astype(BF16), "blk", blk_perm(dx=-d)
            ).astype(F32)
    with jax.named_scope("hard_grad_h"):
        per_h = NY * slots
        back_h = [
            g[d * per_h : (d + 1) * per_h]
            if d == 0
            else lax.ppermute(g[d * per_h : (d + 1) * per_h], "group", group_perm(dh=-d))
            for d in range(NH)
        ]
    with jax.named_scope("scatter_z"):
        fin = acc[:rows]
        for d in range(1, NZ):
            fin = fin + lax.ppermute(
                acc[d * rows : (d + 1) * rows].astype(BF16), "blk", blk_perm(dz=-d)
            ).astype(F32)
        d_passage = (scale * fin).astype(BF16)
    with jax.named_scope("hard_grad_y"):
        to_y = [
            jnp.concatenate([b[d * slots : (d + 1) * slots] for b in back_h], axis=0)
            for d in range(NY)
        ]
        returned = jnp.concatenate(
            [
                to_y[d] if d == 0 else lax.ppermute(to_y[d], "group", group_perm(dy=-d))
                for d in range(NY)
            ],
            axis=0,
        )
        d_owned = t_dot(placing, returned).astype(BF16)

    with jax.named_scope("d_query"):
        d_query = scale * (
            (dot(c0_hi, half0) + dot(c1_hi, half1) + dot(ph_hi, hard))
            + (dot(c0_lo, half0) + dot(c1_lo, half1) + dot(ph_lo, hard))
        )
    return (loss_rows[None], d_query.astype(BF16)[None], d_passage[None], d_owned[None])


def solution(mesh):
    return jax.shard_map(
        body,
        mesh=mesh,
        in_specs=(
            P("group", "blk", None),
            P("group", "blk", None),
            P("group", "blk"),
            P("group", "blk", None),
            P("group", "blk", None),
        ),
        out_specs=(
            P("group", "blk"),
            P("group", "blk", None),
            P("group", "blk", None),
            P("group", "blk", None),
        ),
        check_vma=False,
    )
```

time: 509 us -> 191 us (0.38); the launches traced: 500 us -> 188 us
  waiting for transfers between devices: 349 us -> 41.2 us
  between operations: 14.2 us -> 1.17 us
  local copies, waits for them, and re-layouts: 2.78 us -> 14.1 us
  matrix products: 28.6 us -> 18.5 us
  starting transfers between devices: 99.8 us -> 107 us
    ppermute x31 -> x26, waiting for transfers between devices: 291 us -> 41.2 us  [the longest x3 15.4 us: body(): lax.ppermute(z_rows, 'blk', blk_perm(dx=d))]
    ppermute x31 -> x26, starting transfers between devices: 63.1 us -> 107 us  [the longest x3 22.5 us: body(): lax.ppermute(to_h[d], 'group', group_perm(dh=d))]
    all_to_all x3 -> x0, waiting for transfers between devices: 37.3 us -> none  [the longest x1 25 us: body(): lax.all_to_all(packed, 'group', split_axis=0, concat_axis=0, tiled=True)]
    all_to_all x3 -> x0, starting transfers between devices: 36.7 us -> none  [the longest x1 18.4 us: body(): lax.all_to_all(live_flags, 'group', split_axis=0, concat_axis=0, tiled=True)]
    all_gather x1 -> x0, waiting for transfers between devices: 19.9 us -> none  [body(): gathered = lax.all_gather(own_passages, 'blk', axis=0, tiled=True)]
    dot_general x39 -> x14, matrix products: 28.6 us -> 18.5 us  [the longest x7 11 us: dot(): return jnp.dot(a, b, preferred_element_type=F32)]
    unnamed x8 -> x20, local copies, waits for them, and re-layouts: 0.02 us -> 6.61 us
  transfers between devices with their start and end apart: 35 -> 26, of which waited for: 34 -> 9; matrix products, arithmetic and copies ran while one was open for 4% -> 15% of each run, Pallas kernels for 0% -> 0%
where the time goes in v1:
time: 191 us; the launch traced here: 188 us
  starting transfers between devices  107 us (56%)
  waiting for transfers between devices  41.2 us (22%)
  matrix products  18.5 us (10%)
  local copies, waits for them, and re-layouts  14.1 us (7%)
  other arithmetic  5.91 us (3%)
    ppermute x3, starting transfers between devices, body(): lax.ppermute(to_h[d], 'group', group_perm(dh=d))  22.5 us
    ppermute x3, starting transfers between devices, body(): lax.ppermute(g[d * per_h:(d + 1) * per_h], 'group', group_perm(dh=-d))  17.1 us
    ppermute x3, waiting for transfers between devices, body(): lax.ppermute(z_rows, 'blk', blk_perm(dx=d))  15.4 us
    ppermute x3, waiting for transfers between devices, body(): lax.ppermute(total0[d * n:(d + 1) * n].astype(BF16), 'blk', blk_perm(dx=-d))  15.1 us
    ppermute x3, starting transfers between devices, body(): lax.ppermute(own, 'blk', blk_perm(dz=d))  12 us
    dot_general x7, matrix products, dot(): return jnp.dot(a, b, preferred_element_type=F32)  11 us
    ppermute x3, starting transfers between devices, body(): lax.ppermute(packed[d * per_y:(d + 1) * per_y], 'group', group_perm(dy=d))  10.7 us
    ppermute x3, starting transfers between devices, body(): lax.ppermute(total0[d * n:(d + 1) * n].astype(BF16), 'blk', blk_perm(dx=-d))  10.5 us
  transfers between devices with their start and end apart: 26, of which 9 were waited for; matrix products, arithmetic and copies ran while one was open for 15% of the time, Pallas kernels for 0%

profile of v1, /device:TPU:1, one launch (start us, length us, event | category | flops | bytes accessed | tf_op | source)
XLA Modules:
  0.0 188.2 jit_solution(4056006420258641907)
XLA Ops:
  0.6 4.5 %collective-permute-start = (bf16[16,4096]{1,0:T(8,128)(2,1)}, bf16[16,4096]{1,0:T(8,128)(2,1)S(1)}, u32[]{:S(2)}, u32[]{:S(2)}) collective-permute-start(bf16[16,4096]{1,0:T(8,128)(2,1)} %bitcast.121), channel_id=1, source_target_pairs={{0,128},{16,144},{32,160},{48,176},{64,192},{80,208},{96,224},{112... | collective-permute-start | bytes 393224 | tf_op jit(solution)/shard_map/gather_z/ppermute | solution.py:73
  5.2 4.9 %collective-permute-start.1 = (bf16[16,4096]{1,0:T(8,128)(2,1)}, bf16[16,4096]{1,0:T(8,128)(2,1)S(1)}, u32[]{:S(2)}, u32[]{:S(2)}) collective-permute-start(bf16[16,4096]{1,0:T(8,128)(2,1)} %bitcast.122), channel_id=1, source_target_pairs={{0,256},{16,272},{32,288},{48,304},{64,320},{80,336},{96,352},{112... | collective-permute-start | bytes 393224 | tf_op jit(solution)/shard_map/gather_z/ppermute | solution.py:73
  10.1 2.6 %collective-permute-start.2 = (bf16[16,4096]{1,0:T(8,128)(2,1)}, bf16[16,4096]{1,0:T(8,128)(2,1)S(1)}, u32[]{:S(2)}, u32[]{:S(2)}) collective-permute-start(bf16[16,4096]{1,0:T(8,128)(2,1)} %bitcast.123), channel_id=1, source_target_pairs={{0,384},{16,400},{32,416},{48,432},{64,448},{80,464},{96,480},{112... | collective-permute-start | bytes 393224 | tf_op jit(solution)/shard_map/gather_z/ppermute | solution.py:73
  12.7 0.7 fusion.82
  13.6 0.7 multiply_add_fusion
  14.3 1.1 convolution_convert_fusion
  15.4 3.2 %collective-permute-start.7 = (bf16[8,4224]{1,0:T(8,128)(2,1)S(1)}, bf16[8,4224]{1,0:T(8,128)(2,1)S(1)}, u32[]{:S(2)}, u32[]{:S(2)}) collective-permute-start(bf16[8,4224]{1,0:T(8,128)(2,1)S(1)} %get-tuple-element.26), channel_id=1, source_target_pairs={{0,4},{1,5},{2,6},{3,7},{4,8},{5,9},{6,10},{7,11},{8,12},{9,13},{1... | collective-permute-start | bytes 202760 | tf_op jit(solution)/shard_map/hard_y/ppermute | solution.py:79
  18.7 4.5 %collective-permute-start.8 = (bf16[8,4224]{1,0:T(8,128)(2,1)S(1)}, bf16[8,4224]{1,0:T(8,128)(2,1)S(1)}, u32[]{:S(2)}, u32[]{:S(2)}) collective-permute-start(bf16[8,4224]{1,0:T(8,128)(2,1)S(1)} %get-tuple-element.25), channel_id=1, source_target_pairs={{0,8},{1,9},{2,10},{3,11},{4,12},{5,13},{6,14},{7,15},{8,0},{9,1},... | collective-permute-start | bytes 202760 | tf_op jit(solution)/shard_map/hard_y/ppermute | solution.py:79
  23.3 1.6 constant_dynamic-update-slice_fusion.6
  24.8 3.0 %collective-permute-start.9 = (bf16[8,4224]{1,0:T(8,128)(2,1)S(1)}, bf16[8,4224]{1,0:T(8,128)(2,1)S(1)}, u32[]{:S(2)}, u32[]{:S(2)}) collective-permute-start(bf16[8,4224]{1,0:T(8,128)(2,1)S(1)} %get-tuple-element.24), channel_id=1, source_target_pairs={{0,12},{1,13},{2,14},{3,15},{4,0},{5,1},{6,2},{7,3},{8,4},{9,5},{1... | collective-permute-start | bytes 202760 | tf_op jit(solution)/shard_map/hard_y/ppermute | solution.py:79
  27.9 2.2 %collective-permute-done.9 = bf16[8,4224]{1,0:T(8,128)(2,1)S(1)} collective-permute-done((bf16[8,4224]{1,0:T(8,128)(2,1)S(1)}, bf16[8,4224]{1,0:T(8,128)(2,1)S(1)}, u32[]{:S(2)}, u32[]{:S(2)}) %collective-permute-start.9) | collective-permute-done | bytes 67616 | tf_op jit(solution)/shard_map/hard_y/ppermute | solution.py:79
  30.3 0.9 pad_maximum_fusion
  31.2 2.8 %collective-permute-start.3 = (bf16[64,4096]{1,0:T(8,128)(2,1)S(1)}, bf16[64,4096]{1,0:T(8,128)(2,1)S(1)}, u32[]{:S(2)}, u32[]{:S(2)}) collective-permute-start(bf16[64,4096]{1,0:T(8,128)(2,1)S(1)} %pad_maximum_fusion), channel_id=1, source_target_pairs={{0,32},{16,48},{32,64},{48,80},{64,96},{80,112},{96,0},{112,16},{1... | collective-permute-start | bytes 1572872 | tf_op jit(solution)/shard_map/gather_x/ppermute | solution.py:83
  34.0 4.4 %collective-permute-start.4 = (bf16[64,4096]{1,0:T(8,128)(2,1)S(1)}, bf16[64,4096]{1,0:T(8,128)(2,1)S(1)}, u32[]{:S(2)}, u32[]{:S(2)}) collective-permute-start(bf16[64,4096]{1,0:T(8,128)(2,1)S(1)} %pad_maximum_fusion), channel_id=1, source_target_pairs={{0,64},{16,80},{32,96},{48,112},{64,0},{80,16},{96,32},{112,48},{1... | collective-permute-start | bytes 1572872 | tf_op jit(solution)/shard_map/gather_x/ppermute | solution.py:83
  38.4 3.1 %collective-permute-start.5 = (bf16[64,4096]{1,0:T(8,128)(2,1)S(1)}, bf16[64,4096]{1,0:T(8,128)(2,1)S(1)}, u32[]{:S(2)}, u32[]{:S(2)}) collective-permute-start(bf16[64,4096]{1,0:T(8,128)(2,1)S(1)} %pad_maximum_fusion), channel_id=1, source_target_pairs={{0,96},{16,112},{32,0},{48,16},{64,32},{80,48},{96,64},{112,80},{1... | collective-permute-start | bytes 1572872 | tf_op jit(solution)/shard_map/gather_x/ppermute | solution.py:83
  41.4 0.7 constant_dynamic-update-slice_fusion.5
  42.1 0.7 constant_dynamic-update-slice_fusion.4
  42.8 0.7 constant_dynamic-update-slice_fusion.3
  43.4 0.8 collective-permute-done.3
  44.2 0.8 constant_dynamic-update-slice_fusion.2
  45.0 11.4 %collective-permute-done.4 = bf16[64,4096]{1,0:T(8,128)(2,1)S(1)} collective-permute-done((bf16[64,4096]{1,0:T(8,128)(2,1)S(1)}, bf16[64,4096]{1,0:T(8,128)(2,1)S(1)}, u32[]{:S(2)}, u32[]{:S(2)}) %collective-permute-start.4) | collective-permute-done | bytes 524320 | tf_op jit(solution)/shard_map/gather_x/ppermute | solution.py:83
  56.4 0.8 constant_dynamic-update-slice_fusion.1
  57.2 3.2 %collective-permute-done.5 = bf16[64,4096]{1,0:T(8,128)(2,1)S(1)} collective-permute-done((bf16[64,4096]{1,0:T(8,128)(2,1)S(1)}, bf16[64,4096]{1,0:T(8,128)(2,1)S(1)}, u32[]{:S(2)}, u32[]{:S(2)}) %collective-permute-start.5) | collective-permute-done | bytes 524320 | tf_op jit(solution)/shard_map/gather_x/ppermute | solution.py:83
  60.5 0.8 constant_dynamic-update-slice_fusion
  61.3 3.8 %collective-permute-start.6 = (bf16[256,4096]{1,0:T(8,128)(2,1)}, bf16[256,4096]{1,0:T(8,128)(2,1)}, u32[]{:S(2)}, u32[]{:S(2)}) collective-permute-start(bf16[256,4096]{1,0:T(8,128)(2,1)} %constant_dynamic-update-slice_fusion), channel_id=1, source_target_pairs={{0,16},{16,0},{32,48},{48,32},{64,80},{80,64},{96,112},{112,96},{1... | collective-permute-start | bytes 6291464 | tf_op jit(solution)/shard_map/gather_core/ppermute | solution.py:98
  65.2 8.5 %collective-permute-start.10 = (bf16[8,4224]{1,0:T(8,128)(2,1)S(1)}, bf16[8,4224]{1,0:T(8,128)(2,1)S(1)}, u32[]{:S(2)}, u32[]{:S(2)}) collective-permute-start(bf16[8,4224]{1,0:T(8,128)(2,1)S(1)} %pad_maximum_fusion.1), channel_id=1, source_target_pairs={{0,1},{1,2},{2,3},{3,0},{4,5},{5,6},{6,7},{7,4},{8,9},{9,10},{10,1... | collective-permute-start | bytes 202760 | tf_op jit(solution)/shard_map/hard_h/ppermute | solution.py:92
  73.8 8.8 %collective-permute-start.11 = (bf16[8,4224]{1,0:T(8,128)(2,1)S(1)}, bf16[8,4224]{1,0:T(8,128)(2,1)S(1)}, u32[]{:S(2)}, u32[]{:S(2)}) collective-permute-start(bf16[8,4224]{1,0:T(8,128)(2,1)S(1)} %pad_maximum_fusion.2), channel_id=1, source_target_pairs={{0,2},{1,3},{2,0},{3,1},{4,6},{5,7},{6,4},{7,5},{8,10},{9,11},{10,... | collective-permute-start | bytes 202760 | tf_op jit(solution)/shard_map/hard_h/ppermute | solution.py:92
  82.8 5.2 %collective-permute-start.12 = (bf16[8,4224]{1,0:T(8,128)(2,1)S(1)}, bf16[8,4224]{1,0:T(8,128)(2,1)S(1)}, u32[]{:S(2)}, u32[]{:S(2)}) collective-permute-start(bf16[8,4224]{1,0:T(8,128)(2,1)S(1)} %pad_maximum_fusion.3), channel_id=1, source_target_pairs={{0,3},{1,0},{2,1},{3,2},{4,7},{5,4},{6,5},{7,6},{8,11},{9,8},{10,9... | collective-permute-start | bytes 202760 | tf_op jit(solution)/shard_map/hard_h/ppermute | solution.py:92
  88.0 3.9 %collective-permute-done.11 = bf16[8,4224]{1,0:T(8,128)(2,1)S(1)} collective-permute-done((bf16[8,4224]{1,0:T(8,128)(2,1)S(1)}, bf16[8,4224]{1,0:T(8,128)(2,1)S(1)}, u32[]{:S(2)}, u32[]{:S(2)}) %collective-permute-start.11) | collective-permute-done | bytes 67616 | tf_op jit(solution)/shard_map/hard_h/ppermute | solution.py:92
  92.0 4.5 %collective-permute-done.12 = bf16[8,4224]{1,0:T(8,128)(2,1)S(1)} collective-permute-done((bf16[8,4224]{1,0:T(8,128)(2,1)S(1)}, bf16[8,4224]{1,0:T(8,128)(2,1)S(1)}, u32[]{:S(2)}, u32[]{:S(2)}) %collective-permute-start.12) | collective-permute-done | bytes 67616 | tf_op jit(solution)/shard_map/hard_h/ppermute | solution.py:92
  96.8 0.8 select_reduce_fusion
  97.5 0.7 copy-done.1
  98.2 0.8 fusion.107
  99.0 2.4 %fusion.108 = (f32[256]{0:T(256)S(1)}, f32[256,256]{1,0:T(8,128)S(1)}) fusion(bf16[256,4096]{1,0:T(8,128)(2,1)} %collective-permute-done.6, bf16[1,256,4096]{2,1,0:T(8,128)(2,1)S(1)} %copy-done), kind=kOutput, calls=%fused_computation.176 | convolution fusion | flops 537001728 | bytes 4457472 | tf_op jit(solution)/shard_map/scores/dot_general | solution.py:29
  102.2 0.8 fusion.47
  103.0 0.8 fusion.49
  103.8 0.8 convolution_convert_fusion.1
  105.2 2.4 %collective-permute-start.13 = (bf16[256,4096]{1,0:T(8,128)(2,1)S(1)}, bf16[256,4096]{1,0:T(8,128)(2,1)S(1)}, u32[]{:S(2)}, u32[]{:S(2)}) collective-permute-start(bf16[256,4096]{1,0:T(8,128)(2,1)S(1)} %convolution_convert_fusion.1), channel_id=1, source_target_pairs={{0,16},{16,0},{32,48},{48,32},{64,80},{80,64},{96,112},{112,96},{1... | collective-permute-start | bytes 6291464 | tf_op jit(solution)/shard_map/scatter_core/ppermute | solution.py:140
  107.6 4.7 %collective-permute-start.20 = (bf16[8,4096]{1,0:T(8,128)(2,1)S(1)}, bf16[8,4096]{1,0:T(8,128)(2,1)S(1)}, u32[]{:S(2)}, u32[]{:S(2)}) collective-permute-start(bf16[8,4096]{1,0:T(8,128)(2,1)S(1)} %get-tuple-element.33), channel_id=1, source_target_pairs={{0,3},{1,0},{2,1},{3,2},{4,7},{5,4},{6,5},{7,6},{8,11},{9,8},{10,9... | collective-permute-start | bytes 196616 | tf_op jit(solution)/shard_map/hard_grad_h/ppermute | solution.py:156
  112.3 7.2 %collective-permute-start.21 = (bf16[8,4096]{1,0:T(8,128)(2,1)S(1)}, bf16[8,4096]{1,0:T(8,128)(2,1)S(1)}, u32[]{:S(2)}, u32[]{:S(2)}) collective-permute-start(bf16[8,4096]{1,0:T(8,128)(2,1)S(1)} %get-tuple-element.32), channel_id=1, source_target_pairs={{0,2},{1,3},{2,0},{3,1},{4,6},{5,7},{6,4},{7,5},{8,10},{9,11},{10,... | collective-permute-start | bytes 196616 | tf_op jit(solution)/shard_map/hard_grad_h/ppermute | solution.py:156
  119.5 5.2 %collective-permute-start.22 = (bf16[8,4096]{1,0:T(8,128)(2,1)S(1)}, bf16[8,4096]{1,0:T(8,128)(2,1)S(1)}, u32[]{:S(2)}, u32[]{:S(2)}) collective-permute-start(bf16[8,4096]{1,0:T(8,128)(2,1)S(1)} %get-tuple-element.31), channel_id=1, source_target_pairs={{0,1},{1,2},{2,3},{3,0},{4,5},{5,6},{6,7},{7,4},{8,9},{9,10},{10,1... | collective-permute-start | bytes 196616 | tf_op jit(solution)/shard_map/hard_grad_h/ppermute | solution.py:156
  124.8 2.4 %fusion.53 = f32[256,4096]{1,0:T(8,128)S(1)} fusion(bf16[256,4096]{1,0:T(8,128)(2,1)} %collective-permute-done.6, f32[256,256]{1,0:T(8,128)S(1)} %get-tuple-element.63, f32[256]{0:T(256)S(1)} %get-tuple-element.13, s32[256]{0:T(256)S(1)} %get-tuple-element.66, s32[256]{0:T(256)S(1)} %get-tuple-element.67), kind=kOutput, calls=%fused_computation.65 | convolution fusion | flops 537395200 | bytes 6556672 | tf_op jit(solution)/shard_map/d_query/dot_general | solution.py:37
  127.2 0.9 fusion
  128.2 2.4 %fusion.91 = f32[256,4096]{1,0:T(8,128)S(1)} fusion(bf16[256,4096]{1,0:T(8,128)(2,1)} %collective-permute-done.6, f32[256,256]{1,0:T(8,128)S(1)} %get-tuple-element.63, f32[256]{0:T(256)S(1)} %get-tuple-element.13, s32[256]{0:T(256)S(1)} %get-tuple-element.66, s32[256]{0:T(256)S(1)} %get-tuple-element.67), kind=kOutput, calls=%fused_computation.161 | convolution fusion | flops 537198592 | bytes 6556672 | tf_op jit(solution)/shard_map/d_query/dot_general | solution.py:37
  130.6 0.6 fusion.104
  131.9 0.6 fusion.106
  132.6 4.2 %collective-permute-start.23 = (bf16[8,4096]{1,0:T(8,128)(2,1)S(1)}, bf16[8,4096]{1,0:T(8,128)(2,1)S(1)}, u32[]{:S(2)}, u32[]{:S(2)}) collective-permute-start(bf16[8,4096]{1,0:T(8,128)(2,1)S(1)} %pad_maximum_fusion.4), channel_id=1, source_target_pairs={{0,12},{1,13},{2,14},{3,15},{4,0},{5,1},{6,2},{7,3},{8,4},{9,5},{1... | collective-permute-start | bytes 196616 | tf_op jit(solution)/shard_map/hard_grad_y/ppermute | solution.py:173
  136.8 0.8 fusion.109
  137.8 4.0 %collective-permute-start.16 = (bf16[64,4096]{1,0:T(8,128)(2,1)S(1)}, bf16[64,4096]{1,0:T(8,128)(2,1)S(1)}, u32[]{:S(2)}, u32[]{:S(2)}) collective-permute-start(bf16[64,4096]{1,0:T(8,128)(2,1)S(1)} %get-tuple-element.15), channel_id=1, source_target_pairs={{0,32},{16,48},{32,64},{48,80},{64,96},{80,112},{96,0},{112,16},{1... | collective-permute-start | bytes 1572872 | tf_op jit(solution)/shard_map/scatter_x/ppermute | solution.py:148
  141.7 3.4 %collective-permute-start.15 = (bf16[64,4096]{1,0:T(8,128)(2,1)S(1)}, bf16[64,4096]{1,0:T(8,128)(2,1)S(1)}, u32[]{:S(2)}, u32[]{:S(2)}) collective-permute-start(bf16[64,4096]{1,0:T(8,128)(2,1)S(1)} %get-tuple-element.16), channel_id=1, source_target_pairs={{0,64},{16,80},{32,96},{48,112},{64,0},{80,16},{96,32},{112,48},{1... | collective-permute-start | bytes 1572872 | tf_op jit(solution)/shard_map/scatter_x/ppermute | solution.py:148
  145.1 3.2 %collective-permute-start.14 = (bf16[64,4096]{1,0:T(8,128)(2,1)S(1)}, bf16[64,4096]{1,0:T(8,128)(2,1)S(1)}, u32[]{:S(2)}, u32[]{:S(2)}) collective-permute-start(bf16[64,4096]{1,0:T(8,128)(2,1)S(1)} %get-tuple-element.14), channel_id=1, source_target_pairs={{0,96},{16,112},{32,0},{48,16},{64,32},{80,48},{96,64},{112,80},{1... | collective-permute-start | bytes 1572872 | tf_op jit(solution)/shard_map/scatter_x/ppermute | solution.py:148
  148.4 1.9 %collective-permute-start.24 = (bf16[8,4096]{1,0:T(8,128)(2,1)S(1)}, bf16[8,4096]{1,0:T(8,128)(2,1)S(1)}, u32[]{:S(2)}, u32[]{:S(2)}) collective-permute-start(bf16[8,4096]{1,0:T(8,128)(2,1)S(1)} %pad_maximum_fusion.5), channel_id=1, source_target_pairs={{0,8},{1,9},{2,10},{3,11},{4,12},{5,13},{6,14},{7,15},{8,0},{9,1},... | collective-permute-start | bytes 196616 | tf_op jit(solution)/shard_map/hard_grad_y/ppermute | solution.py:173
  150.4 2.8 %collective-permute-done.16 = bf16[64,4096]{1,0:T(8,128)(2,1)S(1)} collective-permute-done((bf16[64,4096]{1,0:T(8,128)(2,1)S(1)}, bf16[64,4096]{1,0:T(8,128)(2,1)S(1)}, u32[]{:S(2)}, u32[]{:S(2)}) %collective-permute-start.16) | collective-permute-done | bytes 524320 | tf_op jit(solution)/shard_map/scatter_x/ppermute | solution.py:148
  153.1 1.9 %collective-permute-start.25 = (bf16[8,4096]{1,0:T(8,128)(2,1)S(1)}, bf16[8,4096]{1,0:T(8,128)(2,1)S(1)}, u32[]{:S(2)}, u32[]{:S(2)}) collective-permute-start(bf16[8,4096]{1,0:T(8,128)(2,1)S(1)} %pad_maximum_fusion.6), channel_id=1, source_target_pairs={{0,4},{1,5},{2,6},{3,7},{4,8},{5,9},{6,10},{7,11},{8,12},{9,13},{1... | collective-permute-start | bytes 196616 | tf_op jit(solution)/shard_map/hard_grad_y/ppermute | solution.py:173
  155.1 10.2 %collective-permute-done.15 = bf16[64,4096]{1,0:T(8,128)(2,1)S(1)} collective-permute-done((bf16[64,4096]{1,0:T(8,128)(2,1)S(1)}, bf16[64,4096]{1,0:T(8,128)(2,1)S(1)}, u32[]{:S(2)}, u32[]{:S(2)}) %collective-permute-start.15) | collective-permute-done | bytes 524320 | tf_op jit(solution)/shard_map/scatter_x/ppermute | solution.py:148
  165.2 2.2 %collective-permute-done.14 = bf16[64,4096]{1,0:T(8,128)(2,1)S(1)} collective-permute-done((bf16[64,4096]{1,0:T(8,128)(2,1)S(1)}, bf16[64,4096]{1,0:T(8,128)(2,1)S(1)}, u32[]{:S(2)}, u32[]{:S(2)}) %collective-permute-start.14) | collective-permute-done | bytes 524320 | tf_op jit(solution)/shard_map/scatter_x/ppermute | solution.py:148
  167.7 0.7 fusion.96
  168.4 1.9 %collective-permute-start.19 = (bf16[16,4096]{1,0:T(8,128)(2,1)}, bf16[16,4096]{1,0:T(8,128)(2,1)S(1)}, u32[]{:S(2)}, u32[]{:S(2)}) collective-permute-start(bf16[16,4096]{1,0:T(8,128)(2,1)} %get-tuple-element.18), channel_id=1, source_target_pairs={{0,128},{16,144},{32,160},{48,176},{64,192},{80,208},{96,224},{112... | collective-permute-start | bytes 393224 | tf_op jit(solution)/shard_map/scatter_z/ppermute | solution.py:162
  170.3 6.1 %collective-permute-start.18 = (bf16[16,4096]{1,0:T(8,128)(2,1)}, bf16[16,4096]{1,0:T(8,128)(2,1)}, u32[]{:S(2)}, u32[]{:S(2)}) collective-permute-start(bf16[16,4096]{1,0:T(8,128)(2,1)} %get-tuple-element.19), channel_id=1, source_target_pairs={{0,256},{16,272},{32,288},{48,304},{64,320},{80,336},{96,352},{112... | collective-permute-start | bytes 393224 | tf_op jit(solution)/shard_map/scatter_z/ppermute | solution.py:162
  176.5 1.9 %collective-permute-start.17 = (bf16[16,4096]{1,0:T(8,128)(2,1)}, bf16[16,4096]{1,0:T(8,128)(2,1)}, u32[]{:S(2)}, u32[]{:S(2)}) collective-permute-start(bf16[16,4096]{1,0:T(8,128)(2,1)} %get-tuple-element.17), channel_id=1, source_target_pairs={{0,384},{16,400},{32,416},{48,432},{64,448},{80,464},{96,480},{112... | collective-permute-start | bytes 393224 | tf_op jit(solution)/shard_map/scatter_z/ppermute | solution.py:162
  178.4 2.5 %fusion.5 = bf16[1,256,4096]{2,1,0:T(8,128)(2,1)} fusion(f32[256,4096]{1,0:T(8,128)S(1)} %fusion, f32[256,4096]{1,0:T(8,128)S(1)} %fusion.49, f32[256,4096]{1,0:T(8,128)S(1)} %fusion.91, bf16[256,4096]{1,0:T(8,128)(2,1)S(1)} %copy-done.1, f32[256,256]{1,0:T(8,128)S(1)} %get-tuple-element.61, f32[256]{0:T(256)S(1)} %get-tuple-element.13, ...), kind=kOutput, calls=%fused_computation.9 | convolution fusion | flops 542441472 | bytes 17041408 | tf_op jit(solution)/shard_map/d_query/dot_general | solution.py:37
  181.6 3.4 %concatenate.44 = bf16[32,4096]{1,0:T(8,128)(2,1)S(1)} concatenate(bf16[2,4096]{1,0:T(2,128)(2,1)S(1)} %get-tuple-element.30, bf16[2,4096]{1,0:T(2,128)(2,1)} %get-tuple-element.49, bf16[2,4096]{1,0:T(2,128)(2,1)} %get-tuple-element.53, bf16[2,4096]{1,0:T(2,128)(2,1)} %get-tuple-element.57, bf16[8,4096]{1,0:T(8,128)(2,1)} %copy-done.2, bf16[8,4096]{1,0:T(8,128)(2,1)} %copy-done.3, ...), dimensions={0} | concatenate | bytes 524288 | tf_op jit(solution)/shard_map/hard_grad_y/concatenate | solution.py:171
  185.0 1.5 fusion.7
  186.5 1.7 fusion.54
  (55 shorter events, 4.4 us)
Async XLA Ops:
  0.6 96.1 %copy-start = (bf16[1,256,4096]{2,1,0:T(8,128)(2,1)S(1)}, bf16[1,256,4096]{2,1,0:T(8,128)(2,1)}, u32[]{:S(2)}) copy-start(bf16[1,256,4096]{2,1,0:T(8,128)(2,1)} %param.5) | copy-start | bytes 6291460
  0.6 29.6 %collective-permute-start = (bf16[16,4096]{1,0:T(8,128)(2,1)}, bf16[16,4096]{1,0:T(8,128)(2,1)S(1)}, u32[]{:S(2)}, u32[]{:S(2)}) collective-permute-start(bf16[16,4096]{1,0:T(8,128)(2,1)} %bitcast.121), channel_id=1, source_target_pairs={{0,128},{16,144},{32,160},{48,176},{64,192},{80,208},{96,224},{112... | collective-permute-start | bytes 393224 | tf_op jit(solution)/shard_map/gather_z/ppermute | solution.py:73
  5.2 25.1 %collective-permute-start.1 = (bf16[16,4096]{1,0:T(8,128)(2,1)}, bf16[16,4096]{1,0:T(8,128)(2,1)S(1)}, u32[]{:S(2)}, u32[]{:S(2)}) collective-permute-start(bf16[16,4096]{1,0:T(8,128)(2,1)} %bitcast.122), channel_id=1, source_target_pairs={{0,256},{16,272},{32,288},{48,304},{64,320},{80,336},{96,352},{112... | collective-permute-start | bytes 393224 | tf_op jit(solution)/shard_map/gather_z/ppermute | solution.py:73
  10.1 20.2 %collective-permute-start.2 = (bf16[16,4096]{1,0:T(8,128)(2,1)}, bf16[16,4096]{1,0:T(8,128)(2,1)S(1)}, u32[]{:S(2)}, u32[]{:S(2)}) collective-permute-start(bf16[16,4096]{1,0:T(8,128)(2,1)} %bitcast.123), channel_id=1, source_target_pairs={{0,384},{16,400},{32,416},{48,432},{64,448},{80,464},{96,480},{112... | collective-permute-start | bytes 393224 | tf_op jit(solution)/shard_map/gather_z/ppermute | solution.py:73
  14.3 9.0 %copy-start.5 = (s32[16]{0:T(128)}, s32[16]{0:T(128)S(1)}, u32[]{:S(2)}) copy-start(s32[16]{0:T(128)S(1)} %multiply_add_fusion) | copy-start | bytes 196
  15.4 9.4 %collective-permute-start.7 = (bf16[8,4224]{1,0:T(8,128)(2,1)S(1)}, bf16[8,4224]{1,0:T(8,128)(2,1)S(1)}, u32[]{:S(2)}, u32[]{:S(2)}) collective-permute-start(bf16[8,4224]{1,0:T(8,128)(2,1)S(1)} %get-tuple-element.26), channel_id=1, source_target_pairs={{0,4},{1,5},{2,6},{3,7},{4,8},{5,9},{6,10},{7,11},{8,12},{9,13},{1... | collective-permute-start | bytes 202760 | tf_op jit(solution)/shard_map/hard_y/ppermute | solution.py:79
  18.7 9.2 %collective-permute-start.8 = (bf16[8,4224]{1,0:T(8,128)(2,1)S(1)}, bf16[8,4224]{1,0:T(8,128)(2,1)S(1)}, u32[]{:S(2)}, u32[]{:S(2)}) collective-permute-start(bf16[8,4224]{1,0:T(8,128)(2,1)S(1)} %get-tuple-element.25), channel_id=1, source_target_pairs={{0,8},{1,9},{2,10},{3,11},{4,12},{5,13},{6,14},{7,15},{8,0},{9,1},... | collective-permute-start | bytes 202760 | tf_op jit(solution)/shard_map/hard_y/ppermute | solution.py:79
  24.8 5.3 %collective-permute-start.9 = (bf16[8,4224]{1,0:T(8,128)(2,1)S(1)}, bf16[8,4224]{1,0:T(8,128)(2,1)S(1)}, u32[]{:S(2)}, u32[]{:S(2)}) collective-permute-start(bf16[8,4224]{1,0:T(8,128)(2,1)S(1)} %get-tuple-element.24), channel_id=1, source_target_pairs={{0,12},{1,13},{2,14},{3,15},{4,0},{5,1},{6,2},{7,3},{8,4},{9,5},{1... | collective-permute-start | bytes 202760 | tf_op jit(solution)/shard_map/hard_y/ppermute | solution.py:79
  31.2 13.0 %collective-permute-start.3 = (bf16[64,4096]{1,0:T(8,128)(2,1)S(1)}, bf16[64,4096]{1,0:T(8,128)(2,1)S(1)}, u32[]{:S(2)}, u32[]{:S(2)}) collective-permute-start(bf16[64,4096]{1,0:T(8,128)(2,1)S(1)} %pad_maximum_fusion), channel_id=1, source_target_pairs={{0,32},{16,48},{32,64},{48,80},{64,96},{80,112},{96,0},{112,16},{1... | collective-permute-start | bytes 1572872 | tf_op jit(solution)/shard_map/gather_x/ppermute | solution.py:83
  34.0 22.4 %collective-permute-start.4 = (bf16[64,4096]{1,0:T(8,128)(2,1)S(1)}, bf16[64,4096]{1,0:T(8,128)(2,1)S(1)}, u32[]{:S(2)}, u32[]{:S(2)}) collective-permute-start(bf16[64,4096]{1,0:T(8,128)(2,1)S(1)} %pad_maximum_fusion), channel_id=1, source_target_pairs={{0,64},{16,80},{32,96},{48,112},{64,0},{80,16},{96,32},{112,48},{1... | collective-permute-start | bytes 1572872 | tf_op jit(solution)/shard_map/gather_x/ppermute | solution.py:83
  38.4 22.1 %collective-permute-start.5 = (bf16[64,4096]{1,0:T(8,128)(2,1)S(1)}, bf16[64,4096]{1,0:T(8,128)(2,1)S(1)}, u32[]{:S(2)}, u32[]{:S(2)}) collective-permute-start(bf16[64,4096]{1,0:T(8,128)(2,1)S(1)} %pad_maximum_fusion), channel_id=1, source_target_pairs={{0,96},{16,112},{32,0},{48,16},{64,32},{80,48},{96,64},{112,80},{1... | collective-permute-start | bytes 1572872 | tf_op jit(solution)/shard_map/gather_x/ppermute | solution.py:83
  42.1 45.9 %copy-start.6 = (s32[1,256]{1,0:T(1,128)S(1)}, s32[1,256]{1,0:T(1,128)}, u32[]{:S(2)}) copy-start(s32[1,256]{1,0:T(1,128)} %param.7) | copy-start | bytes 3076
  61.3 37.7 %collective-permute-start.6 = (bf16[256,4096]{1,0:T(8,128)(2,1)}, bf16[256,4096]{1,0:T(8,128)(2,1)}, u32[]{:S(2)}, u32[]{:S(2)}) collective-permute-start(bf16[256,4096]{1,0:T(8,128)(2,1)} %constant_dynamic-update-slice_fusion), channel_id=1, source_target_pairs={{0,16},{16,0},{32,48},{48,32},{64,80},{80,64},{96,112},{112,96},{1... | collective-permute-start | bytes 6291464 | tf_op jit(solution)/shard_map/gather_core/ppermute | solution.py:98
  65.2 22.8 %collective-permute-start.10 = (bf16[8,4224]{1,0:T(8,128)(2,1)S(1)}, bf16[8,4224]{1,0:T(8,128)(2,1)S(1)}, u32[]{:S(2)}, u32[]{:S(2)}) collective-permute-start(bf16[8,4224]{1,0:T(8,128)(2,1)S(1)} %pad_maximum_fusion.1), channel_id=1, source_target_pairs={{0,1},{1,2},{2,3},{3,0},{4,5},{5,6},{6,7},{7,4},{8,9},{9,10},{10,1... | collective-permute-start | bytes 202760 | tf_op jit(solution)/shard_map/hard_h/ppermute | solution.py:92
  73.8 18.1 %collective-permute-start.11 = (bf16[8,4224]{1,0:T(8,128)(2,1)S(1)}, bf16[8,4224]{1,0:T(8,128)(2,1)S(1)}, u32[]{:S(2)}, u32[]{:S(2)}) collective-permute-start(bf16[8,4224]{1,0:T(8,128)(2,1)S(1)} %pad_maximum_fusion.2), channel_id=1, source_target_pairs={{0,2},{1,3},{2,0},{3,1},{4,6},{5,7},{6,4},{7,5},{8,10},{9,11},{10,... | collective-permute-start | bytes 202760 | tf_op jit(solution)/shard_map/hard_h/ppermute | solution.py:92
  82.8 13.7 %collective-permute-start.12 = (bf16[8,4224]{1,0:T(8,128)(2,1)S(1)}, bf16[8,4224]{1,0:T(8,128)(2,1)S(1)}, u32[]{:S(2)}, u32[]{:S(2)}) collective-permute-start(bf16[8,4224]{1,0:T(8,128)(2,1)S(1)} %pad_maximum_fusion.3), channel_id=1, source_target_pairs={{0,3},{1,0},{2,1},{3,2},{4,7},{5,4},{6,5},{7,6},{8,11},{9,8},{10,9... | collective-permute-start | bytes 202760 | tf_op jit(solution)/shard_map/hard_h/ppermute | solution.py:92
  96.6 1.6 copy-start.1
  105.2 31.6 %collective-permute-start.13 = (bf16[256,4096]{1,0:T(8,128)(2,1)S(1)}, bf16[256,4096]{1,0:T(8,128)(2,1)S(1)}, u32[]{:S(2)}, u32[]{:S(2)}) collective-permute-start(bf16[256,4096]{1,0:T(8,128)(2,1)S(1)} %convolution_convert_fusion.1), channel_id=1, source_target_pairs={{0,16},{16,0},{32,48},{48,32},{64,80},{80,64},{96,112},{112,96},{1... | collective-permute-start | bytes 6291464 | tf_op jit(solution)/shard_map/scatter_core/ppermute | solution.py:140
  107.6 22.9 %collective-permute-start.20 = (bf16[8,4096]{1,0:T(8,128)(2,1)S(1)}, bf16[8,4096]{1,0:T(8,128)(2,1)S(1)}, u32[]{:S(2)}, u32[]{:S(2)}) collective-permute-start(bf16[8,4096]{1,0:T(8,128)(2,1)S(1)} %get-tuple-element.33), channel_id=1, source_target_pairs={{0,3},{1,0},{2,1},{3,2},{4,7},{5,4},{6,5},{7,6},{8,11},{9,8},{10,9... | collective-permute-start | bytes 196616 | tf_op jit(solution)/shard_map/hard_grad_h/ppermute | solution.py:156
  112.3 18.9 %collective-permute-start.21 = (bf16[8,4096]{1,0:T(8,128)(2,1)S(1)}, bf16[8,4096]{1,0:T(8,128)(2,1)S(1)}, u32[]{:S(2)}, u32[]{:S(2)}) collective-permute-start(bf16[8,4096]{1,0:T(8,128)(2,1)S(1)} %get-tuple-element.32), channel_id=1, source_target_pairs={{0,2},{1,3},{2,0},{3,1},{4,6},{5,7},{6,4},{7,5},{8,10},{9,11},{10,... | collective-permute-start | bytes 196616 | tf_op jit(solution)/shard_map/hard_grad_h/ppermute | solution.py:156
  119.5 12.3 %collective-permute-start.22 = (bf16[8,4096]{1,0:T(8,128)(2,1)S(1)}, bf16[8,4096]{1,0:T(8,128)(2,1)S(1)}, u32[]{:S(2)}, u32[]{:S(2)}) collective-permute-start(bf16[8,4096]{1,0:T(8,128)(2,1)S(1)} %get-tuple-element.31), channel_id=1, source_target_pairs={{0,1},{1,2},{2,3},{3,0},{4,5},{5,6},{6,7},{7,4},{8,9},{9,10},{10,1... | collective-permute-start | bytes 196616 | tf_op jit(solution)/shard_map/hard_grad_h/ppermute | solution.py:156
  132.6 43.8 %collective-permute-start.23 = (bf16[8,4096]{1,0:T(8,128)(2,1)S(1)}, bf16[8,4096]{1,0:T(8,128)(2,1)S(1)}, u32[]{:S(2)}, u32[]{:S(2)}) collective-permute-start(bf16[8,4096]{1,0:T(8,128)(2,1)S(1)} %pad_maximum_fusion.4), channel_id=1, source_target_pairs={{0,12},{1,13},{2,14},{3,15},{4,0},{5,1},{6,2},{7,3},{8,4},{9,5},{1... | collective-permute-start | bytes 196616 | tf_op jit(solution)/shard_map/hard_grad_y/ppermute | solution.py:173
  137.8 15.4 %collective-permute-start.16 = (bf16[64,4096]{1,0:T(8,128)(2,1)S(1)}, bf16[64,4096]{1,0:T(8,128)(2,1)S(1)}, u32[]{:S(2)}, u32[]{:S(2)}) collective-permute-start(bf16[64,4096]{1,0:T(8,128)(2,1)S(1)} %get-tuple-element.15), channel_id=1, source_target_pairs={{0,32},{16,48},{32,64},{48,80},{64,96},{80,112},{96,0},{112,16},{1... | collective-permute-start | bytes 1572872 | tf_op jit(solution)/shard_map/scatter_x/ppermute | solution.py:148
  141.7 23.5 %collective-permute-start.15 = (bf16[64,4096]{1,0:T(8,128)(2,1)S(1)}, bf16[64,4096]{1,0:T(8,128)(2,1)S(1)}, u32[]{:S(2)}, u32[]{:S(2)}) collective-permute-start(bf16[64,4096]{1,0:T(8,128)(2,1)S(1)} %get-tuple-element.16), channel_id=1, source_target_pairs={{0,64},{16,80},{32,96},{48,112},{64,0},{80,16},{96,32},{112,48},{1... | collective-permute-start | bytes 1572872 | tf_op jit(solution)/shard_map/scatter_x/ppermute | solution.py:148
  145.1 22.3 %collective-permute-start.14 = (bf16[64,4096]{1,0:T(8,128)(2,1)S(1)}, bf16[64,4096]{1,0:T(8,128)(2,1)S(1)}, u32[]{:S(2)}, u32[]{:S(2)}) collective-permute-start(bf16[64,4096]{1,0:T(8,128)(2,1)S(1)} %get-tuple-element.14), channel_id=1, source_target_pairs={{0,96},{16,112},{32,0},{48,16},{64,32},{80,48},{96,64},{112,80},{1... | collective-permute-start | bytes 1572872 | tf_op jit(solution)/shard_map/scatter_x/ppermute | solution.py:148
  148.4 32.6 %collective-permute-start.24 = (bf16[8,4096]{1,0:T(8,128)(2,1)S(1)}, bf16[8,4096]{1,0:T(8,128)(2,1)S(1)}, u32[]{:S(2)}, u32[]{:S(2)}) collective-permute-start(bf16[8,4096]{1,0:T(8,128)(2,1)S(1)} %pad_maximum_fusion.5), channel_id=1, source_target_pairs={{0,8},{1,9},{2,10},{3,11},{4,12},{5,13},{6,14},{7,15},{8,0},{9,1},... | collective-permute-start | bytes 196616 | tf_op jit(solution)/shard_map/hard_grad_y/ppermute | solution.py:173
  153.1 27.8 %collective-permute-start.25 = (bf16[8,4096]{1,0:T(8,128)(2,1)S(1)}, bf16[8,4096]{1,0:T(8,128)(2,1)S(1)}, u32[]{:S(2)}, u32[]{:S(2)}) collective-permute-start(bf16[8,4096]{1,0:T(8,128)(2,1)S(1)} %pad_maximum_fusion.6), channel_id=1, source_target_pairs={{0,4},{1,5},{2,6},{3,7},{4,8},{5,9},{6,10},{7,11},{8,12},{9,13},{1... | collective-permute-start | bytes 196616 | tf_op jit(solution)/shard_map/hard_grad_y/ppermute | solution.py:173
  168.4 18.1 %collective-permute-start.19 = (bf16[16,4096]{1,0:T(8,128)(2,1)}, bf16[16,4096]{1,0:T(8,128)(2,1)S(1)}, u32[]{:S(2)}, u32[]{:S(2)}) collective-permute-start(bf16[16,4096]{1,0:T(8,128)(2,1)} %get-tuple-element.18), channel_id=1, source_target_pairs={{0,128},{16,144},{32,160},{48,176},{64,192},{80,208},{96,224},{112... | collective-permute-start | bytes 393224 | tf_op jit(solution)/shard_map/scatter_z/ppermute | solution.py:162
  170.3 16.2 %collective-permute-start.18 = (bf16[16,4096]{1,0:T(8,128)(2,1)}, bf16[16,4096]{1,0:T(8,128)(2,1)}, u32[]{:S(2)}, u32[]{:S(2)}) collective-permute-start(bf16[16,4096]{1,0:T(8,128)(2,1)} %get-tuple-element.19), channel_id=1, source_target_pairs={{0,256},{16,272},{32,288},{48,304},{64,320},{80,336},{96,352},{112... | collective-permute-start | bytes 393224 | tf_op jit(solution)/shard_map/scatter_z/ppermute | solution.py:162
  176.4 4.5 %copy-start.2 = (bf16[8,4096]{1,0:T(8,128)(2,1)}, bf16[8,4096]{1,0:T(8,128)(2,1)S(1)}, u32[]{:S(2)}) copy-start(bf16[8,4096]{1,0:T(8,128)(2,1)S(1)} %collective-permute-done.23) | copy-start | bytes 196612
  176.5 10.1 %collective-permute-start.17 = (bf16[16,4096]{1,0:T(8,128)(2,1)}, bf16[16,4096]{1,0:T(8,128)(2,1)}, u32[]{:S(2)}, u32[]{:S(2)}) collective-permute-start(bf16[16,4096]{1,0:T(8,128)(2,1)} %get-tuple-element.17), channel_id=1, source_target_pairs={{0,384},{16,400},{32,416},{48,432},{64,448},{80,464},{96,480},{112... | collective-permute-start | bytes 393224 | tf_op jit(solution)/shard_map/scatter_z/ppermute | solution.py:162
  180.9 0.6 copy-start.3
  180.9 0.7 copy-start.4

commit v2 on v1

--- a/solution.py
+++ b/solution.py
@@ -1,10 +1,13 @@
 import jax
 import jax.numpy as jnp
+import numpy as np
 from jax import lax
 from jax.sharding import PartitionSpec as P
 
 NZ, NX, NC = 4, 4, 2
 NY, NH = 4, 4
+Y_GROUPS = [[y * NH + h for y in range(NY)] for h in range(NH)]
+H_GROUPS = [[y * NH + h for h in range(NH)] for y in range(NY)]
 FLAG = 128
 BF16, F32 = jnp.bfloat16, jnp.float32
 
@@ -17,12 +20,6 @@
                 to = (((z + dz) % NZ) * NX + (x + dx) % NX) * NC + (c + dc) % NC
                 out.append(((z * NX + x) * NC + c, to))
     return out
-
-
-def group_perm(dy=0, dh=0):
-    return [
-        (y * NH + h, ((y + dy) % NY) * NH + (h + dh) % NH) for y in range(NY) for h in range(NH)
-    ]
 
 
 def dot_t(a, b):
@@ -51,49 +48,39 @@
     width = q.shape[1]
     rows = own.shape[0]
     hard_count = owned_hard.shape[0]
-    groups = NY * NH
+    groups = lax.axis_size("group")
     slots = max(2, 2 * hard_count // groups)
     scale = width ** (-0.5)
     blk = lax.axis_index("blk")
-    grp = lax.axis_index("group")
     my_z, my_x, my_c = blk // (NX * NC), blk // NC % NX, blk % NC
-    my_y, my_h = grp // NH, grp % NH
 
-    rel = ((routes // NH - my_y) % NY) * NH + (routes % NH - my_h) % NH
-    same = (rel[:, None] == rel[None, :]) & (
+    same = (routes[:, None] == routes[None, :]) & (
         jnp.arange(hard_count)[:, None] > jnp.arange(hard_count)[None, :]
     )
-    slot_of = rel * slots + jnp.sum(same.astype(jnp.int32), axis=1)
+    slot_of = routes * slots + jnp.sum(same.astype(jnp.int32), axis=1)
     placing = (slot_of[None, :] == jnp.arange(groups * slots)[:, None]).astype(BF16)
     wide = jnp.concatenate([owned_hard, jnp.ones((hard_count, FLAG), BF16)], axis=1)
     packed = dot(placing, wide).astype(BF16)
-    per_y = NH * slots
 
     with jax.named_scope("gather_z"):
         parts = [own] + [lax.ppermute(own, "blk", blk_perm(dz=d)) for d in range(1, NZ)]
         z_rows = jnp.concatenate(parts, axis=0)
     with jax.named_scope("hard_y"):
-        from_y = [
-            packed[d * per_y : (d + 1) * per_y]
-            if d == 0
-            else lax.ppermute(packed[d * per_y : (d + 1) * per_y], "group", group_perm(dy=d))
-            for d in range(NY)
-        ]
+        from_y = lax.all_to_all(
+            packed, "group", split_axis=0, concat_axis=0, axis_index_groups=Y_GROUPS, tiled=True
+        )
+        order = np.arange(groups * slots).reshape(NY, NH, slots).transpose(1, 0, 2).reshape(-1)
+        turn = jnp.asarray(order[:, None] == np.arange(groups * slots)[None, :], BF16)
+        to_h = dot(turn, from_y).astype(BF16)
+        z_rows, to_h = lax.optimization_barrier((z_rows, to_h))
+    with jax.named_scope("hard_h"):
+        received = lax.all_to_all(
+            to_h, "group", split_axis=0, concat_axis=0, axis_index_groups=H_GROUPS, tiled=True
+        )
     with jax.named_scope("gather_x"):
         parts = [z_rows] + [lax.ppermute(z_rows, "blk", blk_perm(dx=d)) for d in range(1, NX)]
+        *parts, received = lax.optimization_barrier((*parts, received))
         half0 = jnp.concatenate(parts, axis=0)
-    with jax.named_scope("hard_h"):
-        to_h = [
-            jnp.concatenate([f[d * slots : (d + 1) * slots] for f in from_y], axis=0)
-            for d in range(NH)
-        ]
-        received = jnp.concatenate(
-            [
-                to_h[d] if d == 0 else lax.ppermute(to_h[d], "group", group_perm(dh=d))
-                for d in range(NH)
-            ],
-            axis=0,
-        )
     with jax.named_scope("gather_core"):
         half1 = lax.ppermute(half0, "blk", blk_perm(dc=1))
 
@@ -139,7 +126,8 @@
         away = t_dot(c1_hi, q).astype(BF16)
         away = lax.ppermute(away, "blk", blk_perm(dc=1))
     with jax.named_scope("hard_grad"):
-        g = (scale * t_dot(ph_hi, q)).astype(BF16)
+        ph_late, _ = lax.optimization_barrier((ph_hi, away))
+        g = (scale * t_dot(dot(ph_late, turn).astype(BF16), q)).astype(BF16)
     with jax.named_scope("scatter_x"):
         total0 = t_dot(c0_hi, q) + away.astype(F32)
         n = half // NX
@@ -148,14 +136,13 @@
             acc = acc + lax.ppermute(
                 total0[d * n : (d + 1) * n].astype(BF16), "blk", blk_perm(dx=-d)
             ).astype(F32)
-    with jax.named_scope("hard_grad_h"):
-        per_h = NY * slots
-        back_h = [
-            g[d * per_h : (d + 1) * per_h]
-            if d == 0
-            else lax.ppermute(g[d * per_h : (d + 1) * per_h], "group", group_perm(dh=-d))
-            for d in range(NH)
-        ]
+    with jax.named_scope("hard_back"):
+        returned = lax.all_to_all(
+            g.reshape(groups, slots, width), "group", split_axis=0, concat_axis=0, tiled=True
+        ).reshape(groups * slots, width)
+    c0_hi, c0_lo, c1_hi, c1_lo, ph_hi, ph_lo, _ = lax.optimization_barrier(
+        (c0_hi, c0_lo, c1_hi, c1_lo, ph_hi, ph_lo, away)
+    )
     with jax.named_scope("scatter_z"):
         fin = acc[:rows]
         for d in range(1, NZ):
@@ -163,18 +150,7 @@
                 acc[d * rows : (d + 1) * rows].astype(BF16), "blk", blk_perm(dz=-d)
             ).astype(F32)
         d_passage = (scale * fin).astype(BF16)
-    with jax.named_scope("hard_grad_y"):
-        to_y = [
-            jnp.concatenate([b[d * slots : (d + 1) * slots] for b in back_h], axis=0)
-            for d in range(NY)
-        ]
-        returned = jnp.concatenate(
-            [
-                to_y[d] if d == 0 else lax.ppermute(to_y[d], "group", group_perm(dy=-d))
-                for d in range(NY)
-            ],
-            axis=0,
-        )
+    with jax.named_scope("hard_own"):
         d_owned = t_dot(placing, returned).astype(BF16)
 
     with jax.named_scope("d_query"):

time: 191 us -> 155 us (0.81); the launches traced: 188 us -> 154 us
  starting transfers between devices: 107 us -> 76.5 us
  matrix products: 18.5 us -> 30.7 us
  waiting for transfers between devices: 41.2 us -> 32 us
  local copies, waits for them, and re-layouts: 14.1 us -> 7.65 us
    ppermute x12 -> x0, starting transfers between devices: 58.4 us -> none  [the longest x3 22.5 us: body(): lax.ppermute(to_h[d], 'group', group_perm(dh=d))]
    all_to_all x0 -> x3, starting transfers between devices: none -> 29.4 us  [the longest x1 13 us: body(): lax.all_to_all(to_h, 'group', split_axis=0, concat_axis=0, axis_index_gro...]
    ppermute x3, waiting for transfers between devices: 15.1 us -> 0.01 us  [body(): lax.ppermute(total0[d * n:(d + 1) * n].astype(BF16), 'blk', blk_perm(dx=-d))]
    ppermute x12 -> x0, waiting for transfers between devices: 10.7 us -> none  [the longest x3 8.45 us: body(): lax.ppermute(to_h[d], 'group', group_perm(dh=d))]
    dot_general x7 -> x8, matrix products: 11 us -> 20.3 us  [dot(): return jnp.dot(a, b, preferred_element_type=F32)]
    ppermute x3, waiting for transfers between devices: 0.01 us -> 4.98 us  [body(): lax.ppermute(acc[d * rows:(d + 1) * rows].astype(BF16), 'blk', blk_perm(d...]
    all_to_all x0 -> x3, waiting for transfers between devices: none -> 4.61 us  [the longest x1 4.61 us: body(): lax.all_to_all(packed, 'group', split_axis=0, concat_axis=0, axis_index_g...]
    ppermute x1, waiting for transfers between devices: 0.01 us -> 3.72 us  [body(): away = lax.ppermute(away, 'blk', blk_perm(dc=1))]
  transfers between devices with their start and end apart: 26 -> 17, of which waited for: 9 -> 7; matrix products, arithmetic and copies ran while one was open for 15% -> 19% of each run, Pallas kernels for 0% -> 0%
where the time goes in v2:
time: 155 us; the launch traced here: 154 us
  starting transfers between devices  76.5 us (49%)
  waiting for transfers between devices  32 us (21%)
  matrix products  30.7 us (20%)
  local copies, waits for them, and re-layouts  7.65 us (5%)
  other arithmetic  6.44 us (4%)
    dot_general x8, matrix products, dot(): return jnp.dot(a, b, preferred_element_type=F32)  20.3 us
    ppermute x3, waiting for transfers between devices, body(): lax.ppermute(z_rows, 'blk', blk_perm(dx=d))  17.9 us
    all_to_all x1, starting transfers between devices, body(): lax.all_to_all(to_h, 'group', split_axis=0, concat_axis=0, axis_index_gro...  13 us
    all_to_all x1, starting transfers between devices, body(): lax.all_to_all(g.reshape(groups, slots, width), 'group', split_axis=0, co...  12.2 us
    ppermute x3, starting transfers between devices, body(): lax.ppermute(own, 'blk', blk_perm(dz=d))  12 us
    ppermute x3, starting transfers between devices, body(): lax.ppermute(z_rows, 'blk', blk_perm(dx=d))  10.5 us
    ppermute x3, starting transfers between devices, body(): lax.ppermute(total0[d * n:(d + 1) * n].astype(BF16), 'blk', blk_perm(dx=-d))  9.93 us
    ppermute x3, starting transfers between devices, body(): lax.ppermute(acc[d * rows:(d + 1) * rows].astype(BF16), 'blk', blk_perm(d...  8.37 us
  transfers between devices with their start and end apart: 17, of which 7 were waited for; matrix products, arithmetic and copies ran while one was open for 19% of the time, Pallas kernels for 0%

profile of v2, /device:TPU:1, one launch (start us, length us, event | category | flops | bytes accessed | tf_op | source)
XLA Modules:
  0.0 154.3 jit_solution(18333537303005918772)
XLA Ops:
  0.6 0.0 copy-start
  0.6 4.5 %collective-permute-start = (bf16[16,4096]{1,0:T(8,128)(2,1)}, bf16[16,4096]{1,0:T(8,128)(2,1)S(1)}, u32[]{:S(2)}, u32[]{:S(2)}) collective-permute-start(bf16[16,4096]{1,0:T(8,128)(2,1)} %bitcast.118), channel_id=1, source_target_pairs={{0,128},{16,144},{32,160},{48,176},{64,192},{80,208},{96,224},{112... | collective-permute-start | bytes 393224 | tf_op jit(solution)/shard_map/gather_z/ppermute | solution.py:66
  5.2 4.9 %collective-permute-start.1 = (bf16[16,4096]{1,0:T(8,128)(2,1)}, bf16[16,4096]{1,0:T(8,128)(2,1)S(1)}, u32[]{:S(2)}, u32[]{:S(2)}) collective-permute-start(bf16[16,4096]{1,0:T(8,128)(2,1)} %bitcast.119), channel_id=1, source_target_pairs={{0,256},{16,272},{32,288},{48,304},{64,320},{80,336},{96,352},{112... | collective-permute-start | bytes 393224 | tf_op jit(solution)/shard_map/gather_z/ppermute | solution.py:66
  10.1 2.6 %collective-permute-start.2 = (bf16[16,4096]{1,0:T(8,128)(2,1)}, bf16[16,4096]{1,0:T(8,128)(2,1)S(1)}, u32[]{:S(2)}, u32[]{:S(2)}) collective-permute-start(bf16[16,4096]{1,0:T(8,128)(2,1)} %bitcast.120), channel_id=1, source_target_pairs={{0,384},{16,400},{32,416},{48,432},{64,448},{80,464},{96,480},{112... | collective-permute-start | bytes 393224 | tf_op jit(solution)/shard_map/gather_z/ppermute | solution.py:66
  12.7 0.9 convert_reduce_fusion
  13.6 0.7 multiply_add_fusion
  14.3 1.8 %fusion = bf16[4,8,4224]{2,1,0:T(8,128)(2,1)} fusion(bf16[16,4096]{1,0:T(8,128)(2,1)} %bitcast.117, s32[16]{0:T(128)S(1)} %multiply_add_fusion), kind=kOutput, calls=%fused_computation.2 | convolution fusion | flops 4461056 | bytes 401472 | tf_op jit(solution)/shard_map/dot_general | solution.py:34
  16.1 4.2 %all-to-all-start = ((bf16[4,8,4224]{2,1,0:T(8,128)(2,1)}), bf16[4,8,4224]{2,1,0:T(8,128)(2,1)S(1)}, u32[]{:S(2)}, u32[]{:S(2)}) async-start(bf16[4,8,4224]{2,1,0:T(8,128)(2,1)} %fusion), calls=%async_computation | async-start | bytes 540672 | tf_op jit(solution)/shard_map/hard_y/all_to_all | solution.py:69
  20.3 0.0 collective-permute-done
  20.3 0.0 collective-permute-done.1
  20.3 0.0 collective-permute-done.2
  20.3 0.9 pad_maximum_fusion
  21.3 4.6 %all-to-all-done = bf16[4,8,4224]{2,1,0:T(8,128)(2,1)S(1)} async-done(((bf16[4,8,4224]{2,1,0:T(8,128)(2,1)}), bf16[4,8,4224]{2,1,0:T(8,128)(2,1)S(1)}, u32[]{:S(2)}, u32[]{:S(2)}) %all-to-all-start) | async-done | bytes 270368 | tf_op jit(solution)/shard_map/hard_y/all_to_all | solution.py:69
  25.9 1.6 %fusion.1 = bf16[32,4224]{1,0:T(8,128)(2,1)} fusion(bf16[32,32]{1,0:T(8,128)(2,1)} %constant.135.clone, bf16[4,8,4224]{2,1,0:T(8,128)(2,1)S(1)} %all-to-all-done), kind=kOutput, calls=%fused_computation.3 | convolution fusion | flops 8785920 | bytes 542720 | tf_op jit(solution)/shard_map/hard_y/dot_general | solution.py:34
  27.5 13.0 %all-to-all-start.1 = ((bf16[4,8,4224]{2,1,0:T(8,128)(2,1)}), bf16[4,8,4224]{2,1,0:T(8,128)(2,1)S(1)}, u32[]{:S(2)}, u32[]{:S(2)}) async-start(bf16[4,8,4224]{2,1,0:T(8,128)(2,1)} %bitcast.6), calls=%async_computation.1 | async-start | bytes 540672 | tf_op jit(solution)/shard_map/hard_h/all_to_all | solution.py:77
  40.5 3.1 %collective-permute-start.3 = (bf16[64,4096]{1,0:T(8,128)(2,1)S(1)}, bf16[64,4096]{1,0:T(8,128)(2,1)S(1)}, u32[]{:S(2)}, u32[]{:S(2)}) collective-permute-start(bf16[64,4096]{1,0:T(8,128)(2,1)S(1)} %pad_maximum_fusion), channel_id=1, source_target_pairs={{0,32},{16,48},{32,64},{48,80},{64,96},{80,112},{96,0},{112,16},{1... | collective-permute-start | bytes 1572872 | tf_op jit(solution)/shard_map/gather_x/ppermute | solution.py:81
  43.6 4.4 %collective-permute-start.4 = (bf16[64,4096]{1,0:T(8,128)(2,1)S(1)}, bf16[64,4096]{1,0:T(8,128)(2,1)S(1)}, u32[]{:S(2)}, u32[]{:S(2)}) collective-permute-start(bf16[64,4096]{1,0:T(8,128)(2,1)S(1)} %pad_maximum_fusion), channel_id=1, source_target_pairs={{0,64},{16,80},{32,96},{48,112},{64,0},{80,16},{96,32},{112,48},{1... | collective-permute-start | bytes 1572872 | tf_op jit(solution)/shard_map/gather_x/ppermute | solution.py:81
  48.0 3.1 %collective-permute-start.5 = (bf16[64,4096]{1,0:T(8,128)(2,1)S(1)}, bf16[64,4096]{1,0:T(8,128)(2,1)}, u32[]{:S(2)}, u32[]{:S(2)}) collective-permute-start(bf16[64,4096]{1,0:T(8,128)(2,1)S(1)} %pad_maximum_fusion), channel_id=1, source_target_pairs={{0,96},{16,112},{32,0},{48,16},{64,32},{80,48},{96,64},{112,80},{1... | collective-permute-start | bytes 1572872 | tf_op jit(solution)/shard_map/gather_x/ppermute | solution.py:81
  51.0 2.7 %collective-permute-done.3 = bf16[64,4096]{1,0:T(8,128)(2,1)S(1)} collective-permute-done((bf16[64,4096]{1,0:T(8,128)(2,1)S(1)}, bf16[64,4096]{1,0:T(8,128)(2,1)S(1)}, u32[]{:S(2)}, u32[]{:S(2)}) %collective-permute-start.3) | collective-permute-done | bytes 524320 | tf_op jit(solution)/shard_map/gather_x/ppermute | solution.py:81
  53.8 12.2 %collective-permute-done.4 = bf16[64,4096]{1,0:T(8,128)(2,1)S(1)} collective-permute-done((bf16[64,4096]{1,0:T(8,128)(2,1)S(1)}, bf16[64,4096]{1,0:T(8,128)(2,1)S(1)}, u32[]{:S(2)}, u32[]{:S(2)}) %collective-permute-start.4) | collective-permute-done | bytes 524320 | tf_op jit(solution)/shard_map/gather_x/ppermute | solution.py:81
  66.0 0.8 copy-done.3
  66.8 3.0 %collective-permute-done.5 = bf16[64,4096]{1,0:T(8,128)(2,1)} collective-permute-done((bf16[64,4096]{1,0:T(8,128)(2,1)S(1)}, bf16[64,4096]{1,0:T(8,128)(2,1)}, u32[]{:S(2)}, u32[]{:S(2)}) %collective-permute-start.5) | collective-permute-done | bytes 524320 | tf_op jit(solution)/shard_map/gather_x/ppermute | solution.py:81
  69.7 0.0 all-to-all-done.1
  69.8 0.8 constant_dynamic-update-slice_fusion.3
  70.6 0.8 constant_dynamic-update-slice_fusion.2
  71.4 0.8 constant_dynamic-update-slice_fusion.1
  72.3 1.9 %constant_dynamic-update-slice_fusion = bf16[256,4096]{1,0:T(8,128)(2,1)} fusion(bf16[256,4096]{1,0:T(8,128)(2,1)} %constant_dynamic-update-slice_fusion.1, bf16[64,4096]{1,0:T(8,128)(2,1)} %collective-permute-done.5), kind=kLoop, calls=%fused_computation.79 | loop fusion | bytes 1048576 | tf_op jit(solution)/shard_map/gather_x/concatenate | solution.py:83
  74.1 4.0 %collective-permute-start.6 = (bf16[256,4096]{1,0:T(8,128)(2,1)}, bf16[256,4096]{1,0:T(8,128)(2,1)}, u32[]{:S(2)}, u32[]{:S(2)}) collective-permute-start(bf16[256,4096]{1,0:T(8,128)(2,1)} %constant_dynamic-update-slice_fusion), channel_id=1, source_target_pairs={{0,16},{16,0},{32,48},{48,32},{64,80},{80,64},{96,112},{112,96},{1... | collective-permute-start | bytes 6291464 | tf_op jit(solution)/shard_map/gather_core/ppermute | solution.py:85
  78.2 0.1 compare_reduce_fusion
  78.3 0.8 fusion.82
  79.1 2.3 %fusion.83 = (f32[256]{0:T(256)S(1)}, f32[256,256]{1,0:T(8,128)S(1)}) fusion(bf16[256,4096]{1,0:T(8,128)(2,1)} %constant_dynamic-update-slice_fusion, bf16[1,256,4096]{2,1,0:T(8,128)(2,1)S(1)} %copy-done), kind=kOutput, calls=%fused_computation.134 | convolution fusion | flops 537001728 | bytes 4457472 | tf_op jit(solution)/shard_map/scores/dot_general | solution.py:26
  81.4 0.8 collective-permute-done.6
  82.2 2.4 %fusion.84 = (f32[256]{0:T(256)S(1)}, f32[256,256]{1,0:T(8,128)S(1)}) fusion(bf16[256,4096]{1,0:T(8,128)(2,1)} %collective-permute-done.6, bf16[1,256,4096]{2,1,0:T(8,128)(2,1)S(1)} %copy-done), kind=kOutput, calls=%fused_computation.135 | convolution fusion | flops 537001728 | bytes 4457472 | tf_op jit(solution)/shard_map/scores/dot_general | solution.py:26
  84.6 0.2 fusion.48
  84.8 0.6 add_subtract_fusion
  85.3 0.2 subtract_convert_fusion
  85.5 0.7 convolution_convert_fusion.2
  86.2 2.3 %collective-permute-start.7 = (bf16[256,4096]{1,0:T(8,128)(2,1)S(1)}, bf16[256,4096]{1,0:T(8,128)(2,1)S(1)}, u32[]{:S(2)}, u32[]{:S(2)}) collective-permute-start(bf16[256,4096]{1,0:T(8,128)(2,1)S(1)} %convolution_convert_fusion.2), channel_id=1, source_target_pairs={{0,16},{16,0},{32,48},{48,32},{64,80},{80,64},{96,112},{112,96},{1... | collective-permute-start | bytes 6291464 | tf_op jit(solution)/shard_map/scatter_core/ppermute | solution.py:127
  88.6 3.7 %collective-permute-done.7 = bf16[256,4096]{1,0:T(8,128)(2,1)S(1)} collective-permute-done((bf16[256,4096]{1,0:T(8,128)(2,1)S(1)}, bf16[256,4096]{1,0:T(8,128)(2,1)S(1)}, u32[]{:S(2)}, u32[]{:S(2)}) %collective-permute-start.7) | collective-permute-done | bytes 2097184 | tf_op jit(solution)/shard_map/scatter_core/ppermute | solution.py:127
  92.3 2.7 %fusion.85 = (bf16[256,4096]{1,0:T(8,128)(2,1)S(1)}, f32[256,4096]{1,0:T(8,128)}) fusion(bf16[256,4096]{1,0:T(8,128)(2,1)S(1)} %collective-permute-done.7, bf16[256,256]{0,1:T(8,128)(2,1)S(1)} %get-tuple-element.25, bf16[1,256,4096]{2,1,0:T(8,128)(2,1)S(1)} %copy-done), kind=kOutput, calls=%fused_computation.136 | convolution fusion | flops 540016640 | bytes 10616832 | tf_op jit(solution)/shard_map/scatter_x/dot_general | solution.py:30
  95.0 1.1 fusion.80
  96.1 4.0 %collective-permute-start.10 = (bf16[64,4096]{1,0:T(8,128)(2,1)}, bf16[64,4096]{1,0:T(8,128)(2,1)}, u32[]{:S(2)}, u32[]{:S(2)}) collective-permute-start(bf16[64,4096]{1,0:T(8,128)(2,1)} %get-tuple-element.47), channel_id=1, source_target_pairs={{0,32},{16,48},{32,64},{48,80},{64,96},{80,112},{96,0},{112,16},{1... | collective-permute-start | bytes 1572872 | tf_op jit(solution)/shard_map/scatter_x/ppermute | solution.py:136
  100.1 2.5 %collective-permute-start.8 = (bf16[64,4096]{1,0:T(8,128)(2,1)}, bf16[64,4096]{1,0:T(8,128)(2,1)}, u32[]{:S(2)}, u32[]{:S(2)}) collective-permute-start(bf16[64,4096]{1,0:T(8,128)(2,1)} %get-tuple-element.46), channel_id=1, source_target_pairs={{0,96},{16,112},{32,0},{48,16},{64,32},{80,48},{96,64},{112,80},{1... | collective-permute-start | bytes 1572872 | tf_op jit(solution)/shard_map/scatter_x/ppermute | solution.py:136
  102.6 3.4 %collective-permute-start.9 = (bf16[64,4096]{1,0:T(8,128)(2,1)S(1)}, bf16[64,4096]{1,0:T(8,128)(2,1)}, u32[]{:S(2)}, u32[]{:S(2)}) collective-permute-start(bf16[64,4096]{1,0:T(8,128)(2,1)S(1)} %get-tuple-element.48), channel_id=1, source_target_pairs={{0,64},{16,80},{32,96},{48,112},{64,0},{80,16},{96,32},{112,48},{1... | collective-permute-start | bytes 1572872 | tf_op jit(solution)/shard_map/scatter_x/ppermute | solution.py:136
  106.0 2.7 %fusion.53 = f32[256,4096]{1,0:T(8,128)} fusion(bf16[256,32]{0,1:T(8,128)(2,1)S(1)} %fusion.60, bf16[32,4224]{1,0:T(8,128)(2,1)S(1)} %bitcast.115), kind=kOutput, calls=%fused_computation.65 | convolution fusion | flops 67108864 | bytes 4472832 | tf_op jit(solution)/shard_map/d_query/dot_general | solution.py:34
  108.7 2.7 %fusion.55 = f32[256,4096]{1,0:T(8,128)} fusion(bf16[256,32]{0,1:T(8,128)(2,1)S(1)} %bitcast_convert_fusion, bf16[32,4224]{1,0:T(8,128)(2,1)S(1)} %bitcast.116), kind=kOutput, calls=%fused_computation.67 | convolution fusion | flops 67108864 | bytes 4472832 | tf_op jit(solution)/shard_map/d_query/dot_general | solution.py:34
  111.4 0.6 fusion.8
  112.1 0.9 reshape.263
  113.0 12.2 %all-to-all-start.2 = ((bf16[16,2,4096]{2,1,0:T(2,128)(2,1)}), bf16[16,2,4096]{2,1,0:T(2,128)(2,1)S(1)}, u32[]{:S(2)}, u32[]{:S(2)}) async-start(bf16[16,2,4096]{2,1,0:T(2,128)(2,1)} %reshape.263), calls=%async_computation.2 | async-start | bytes 524288 | tf_op jit(solution)/shard_map/hard_back/all_to_all | solution.py:140
  125.2 2.3 %fusion.86 = f32[256,4096]{1,0:T(8,128)S(1)} fusion(bf16[256,256]{0,1:T(8,128)(2,1)S(1)} %get-tuple-element.26, bf16[256,4096]{1,0:T(8,128)(2,1)} %collective-permute-done.6), kind=kOutput, calls=%fused_computation.137 | convolution fusion | flops 536870912 | bytes 6422528 | tf_op jit(solution)/shard_map/d_query/dot_general | solution.py:34
  127.5 2.5 %fusion.87 = f32[256,4096]{1,0:T(8,128)S(1)} fusion(bf16[256,256]{0,1:T(8,128)(2,1)S(1)} %get-tuple-element.29, bf16[256,4096]{1,0:T(8,128)(2,1)} %collective-permute-done.6), kind=kOutput, calls=%fused_computation.138 | convolution fusion | flops 536870912 | bytes 6422528 | tf_op jit(solution)/shard_map/d_query/dot_general | solution.py:34
  130.0 0.3 copy-done.1
  130.4 2.5 %fusion.2 = f32[256,4096]{1,0:T(8,128)S(1)} fusion(f32[256,4096]{1,0:T(8,128)S(1)} %copy-done.1, f32[256,4096]{1,0:T(8,128)S(1)} %fusion.87, bf16[256,256]{0,1:T(8,128)(2,1)S(1)} %get-tuple-element.28, bf16[256,4096]{1,0:T(8,128)(2,1)} %constant_dynamic-update-slice_fusion), kind=kOutput, calls=%fused_computation.5 | convolution fusion | flops 538968064 | bytes 14811136 | tf_op jit(solution)/shard_map/d_query/dot_general | solution.py:34
  132.8 0.0 collective-permute-done.8
  132.9 2.1 %fusion.76 = (bf16[64,4096]{1,0:T(8,128)(2,1)S(1)}, f32[64,4096]{1,0:T(8,128)S(1)}) fusion(bf16[64,4096]{1,0:T(8,128)(2,1)} %collective-permute-done.10, bf16[64,4096]{1,0:T(8,128)(2,1)} %collective-permute-done.9, bf16[64,4096]{1,0:T(8,128)(2,1)} %collective-permute-done.8, f32[256,4096]{1,0:T(8,128)} %get-tuple-element.61), kind=kLoop, calls=%fused_computation.130 | loop fusion | flops 1835008 | bytes 4194304 | tf_op jit(solution)/shard_map/convert.2
  135.0 2.6 %collective-permute-start.11 = (bf16[16,4096]{1,0:T(8,128)(2,1)S(1)}, bf16[16,4096]{1,0:T(8,128)(2,1)S(1)}, u32[]{:S(2)}, u32[]{:S(2)}) collective-permute-start(bf16[16,4096]{1,0:T(8,128)(2,1)S(1)} %get-tuple-element.49), channel_id=1, source_target_pairs={{0,384},{16,400},{32,416},{48,432},{64,448},{80,464},{96,480},{112... | collective-permute-start | bytes 393224 | tf_op jit(solution)/shard_map/scatter_z/ppermute | solution.py:149
  137.6 2.4 %collective-permute-start.12 = (bf16[16,4096]{1,0:T(8,128)(2,1)S(1)}, bf16[16,4096]{1,0:T(8,128)(2,1)S(1)}, u32[]{:S(2)}, u32[]{:S(2)}) collective-permute-start(bf16[16,4096]{1,0:T(8,128)(2,1)S(1)} %get-tuple-element.51), channel_id=1, source_target_pairs={{0,256},{16,272},{32,288},{48,304},{64,320},{80,336},{96,352},{112... | collective-permute-start | bytes 393224 | tf_op jit(solution)/shard_map/scatter_z/ppermute | solution.py:149
  140.1 3.3 %collective-permute-start.13 = (bf16[16,4096]{1,0:T(8,128)(2,1)S(1)}, bf16[16,4096]{1,0:T(8,128)(2,1)S(1)}, u32[]{:S(2)}, u32[]{:S(2)}) collective-permute-start(bf16[16,4096]{1,0:T(8,128)(2,1)S(1)} %get-tuple-element.50), channel_id=1, source_target_pairs={{0,128},{16,144},{32,160},{48,176},{64,192},{80,208},{96,224},{112... | collective-permute-start | bytes 393224 | tf_op jit(solution)/shard_map/scatter_z/ppermute | solution.py:149
  143.4 4.2 %fusion.7 = bf16[1,256,4096]{2,1,0:T(8,128)(2,1)} fusion(f32[256,4096]{1,0:T(8,128)S(1)} %fusion.2, f32[256,4096]{1,0:T(8,128)S(1)} %copy-done.2, f32[256,4096]{1,0:T(8,128)S(1)} %fusion.86, bf16[256,256]{0,1:T(8,128)(2,1)S(1)} %get-tuple-element.25, bf16[256,4096]{1,0:T(8,128)(2,1)} %constant_dynamic-update-slice_fusion), kind=kOutput, calls=%fused_computation.12 | convolution fusion | flops 542113792 | bytes 16908288 | tf_op jit(solution)/shard_map/d_query/dot_general | solution.py:34
  147.6 0.0 collective-permute-done.11
  147.6 5.0 %collective-permute-done.12 = bf16[16,4096]{1,0:T(8,128)(2,1)S(1)} collective-permute-done((bf16[16,4096]{1,0:T(8,128)(2,1)S(1)}, bf16[16,4096]{1,0:T(8,128)(2,1)S(1)}, u32[]{:S(2)}, u32[]{:S(2)}) %collective-permute-start.12) | collective-permute-done | bytes 131104 | tf_op jit(solution)/shard_map/scatter_z/ppermute | solution.py:149
  152.5 0.7 fusion.59
  153.3 0.1 reshape.264
  153.4 0.9 fusion.9
  (21 shorter events, 0.2 us)
Async XLA Ops:
  0.6 77.7 %copy-start = (bf16[1,256,4096]{2,1,0:T(8,128)(2,1)S(1)}, bf16[1,256,4096]{2,1,0:T(8,128)(2,1)}, u32[]{:S(2)}) copy-start(bf16[1,256,4096]{2,1,0:T(8,128)(2,1)} %param.6) | copy-start | bytes 6291460
  0.6 19.7 %collective-permute-start = (bf16[16,4096]{1,0:T(8,128)(2,1)}, bf16[16,4096]{1,0:T(8,128)(2,1)S(1)}, u32[]{:S(2)}, u32[]{:S(2)}) collective-permute-start(bf16[16,4096]{1,0:T(8,128)(2,1)} %bitcast.118), channel_id=1, source_target_pairs={{0,128},{16,144},{32,160},{48,176},{64,192},{80,208},{96,224},{112... | collective-permute-start | bytes 393224 | tf_op jit(solution)/shard_map/gather_z/ppermute | solution.py:66
  5.2 15.1 %collective-permute-start.1 = (bf16[16,4096]{1,0:T(8,128)(2,1)}, bf16[16,4096]{1,0:T(8,128)(2,1)S(1)}, u32[]{:S(2)}, u32[]{:S(2)}) collective-permute-start(bf16[16,4096]{1,0:T(8,128)(2,1)} %bitcast.119), channel_id=1, source_target_pairs={{0,256},{16,272},{32,288},{48,304},{64,320},{80,336},{96,352},{112... | collective-permute-start | bytes 393224 | tf_op jit(solution)/shard_map/gather_z/ppermute | solution.py:66
  10.1 10.2 %collective-permute-start.2 = (bf16[16,4096]{1,0:T(8,128)(2,1)}, bf16[16,4096]{1,0:T(8,128)(2,1)S(1)}, u32[]{:S(2)}, u32[]{:S(2)}) collective-permute-start(bf16[16,4096]{1,0:T(8,128)(2,1)} %bitcast.120), channel_id=1, source_target_pairs={{0,384},{16,400},{32,416},{48,432},{64,448},{80,464},{96,480},{112... | collective-permute-start | bytes 393224 | tf_op jit(solution)/shard_map/gather_z/ppermute | solution.py:66
  16.1 9.8 %all-to-all-start = ((bf16[4,8,4224]{2,1,0:T(8,128)(2,1)}), bf16[4,8,4224]{2,1,0:T(8,128)(2,1)S(1)}, u32[]{:S(2)}, u32[]{:S(2)}) async-start(bf16[4,8,4224]{2,1,0:T(8,128)(2,1)} %fusion), calls=%async_computation | async-start | bytes 540672 | tf_op jit(solution)/shard_map/hard_y/all_to_all | solution.py:69
  27.5 42.3 %all-to-all-start.1 = ((bf16[4,8,4224]{2,1,0:T(8,128)(2,1)}), bf16[4,8,4224]{2,1,0:T(8,128)(2,1)S(1)}, u32[]{:S(2)}, u32[]{:S(2)}) async-start(bf16[4,8,4224]{2,1,0:T(8,128)(2,1)} %bitcast.6), calls=%async_computation.1 | async-start | bytes 540672 | tf_op jit(solution)/shard_map/hard_h/all_to_all | solution.py:77
  40.5 13.3 %collective-permute-start.3 = (bf16[64,4096]{1,0:T(8,128)(2,1)S(1)}, bf16[64,4096]{1,0:T(8,128)(2,1)S(1)}, u32[]{:S(2)}, u32[]{:S(2)}) collective-permute-start(bf16[64,4096]{1,0:T(8,128)(2,1)S(1)} %pad_maximum_fusion), channel_id=1, source_target_pairs={{0,32},{16,48},{32,64},{48,80},{64,96},{80,112},{96,0},{112,16},{1... | collective-permute-start | bytes 1572872 | tf_op jit(solution)/shard_map/gather_x/ppermute | solution.py:81
  43.6 22.4 %collective-permute-start.4 = (bf16[64,4096]{1,0:T(8,128)(2,1)S(1)}, bf16[64,4096]{1,0:T(8,128)(2,1)S(1)}, u32[]{:S(2)}, u32[]{:S(2)}) collective-permute-start(bf16[64,4096]{1,0:T(8,128)(2,1)S(1)} %pad_maximum_fusion), channel_id=1, source_target_pairs={{0,64},{16,80},{32,96},{48,112},{64,0},{80,16},{96,32},{112,48},{1... | collective-permute-start | bytes 1572872 | tf_op jit(solution)/shard_map/gather_x/ppermute | solution.py:81
  48.0 21.8 %collective-permute-start.5 = (bf16[64,4096]{1,0:T(8,128)(2,1)S(1)}, bf16[64,4096]{1,0:T(8,128)(2,1)}, u32[]{:S(2)}, u32[]{:S(2)}) collective-permute-start(bf16[64,4096]{1,0:T(8,128)(2,1)S(1)} %pad_maximum_fusion), channel_id=1, source_target_pairs={{0,96},{16,112},{32,0},{48,16},{64,32},{80,48},{96,64},{112,80},{1... | collective-permute-start | bytes 1572872 | tf_op jit(solution)/shard_map/gather_x/ppermute | solution.py:81
  66.0 0.8 copy-start.3
  69.7 1.7 %copy-start.4 = (bf16[64,4096]{1,0:T(8,128)(2,1)S(1)}, bf16[64,4096]{1,0:T(8,128)(2,1)}, u32[]{:S(2)}) copy-start(bf16[64,4096]{1,0:T(8,128)(2,1)} %copy-done.3) | copy-start | bytes 1572868
  69.7 8.4 %copy-start.6 = (s32[1,256]{1,0:T(1,128)S(1)}, s32[1,256]{1,0:T(1,128)}, u32[]{:S(2)}) copy-start(s32[1,256]{1,0:T(1,128)} %param.8) | copy-start | bytes 3076
  74.1 8.1 %collective-permute-start.6 = (bf16[256,4096]{1,0:T(8,128)(2,1)}, bf16[256,4096]{1,0:T(8,128)(2,1)}, u32[]{:S(2)}, u32[]{:S(2)}) collective-permute-start(bf16[256,4096]{1,0:T(8,128)(2,1)} %constant_dynamic-update-slice_fusion), channel_id=1, source_target_pairs={{0,16},{16,0},{32,48},{48,32},{64,80},{80,64},{96,112},{112,96},{1... | collective-permute-start | bytes 6291464 | tf_op jit(solution)/shard_map/gather_core/ppermute | solution.py:85
  86.2 6.1 %collective-permute-start.7 = (bf16[256,4096]{1,0:T(8,128)(2,1)S(1)}, bf16[256,4096]{1,0:T(8,128)(2,1)S(1)}, u32[]{:S(2)}, u32[]{:S(2)}) collective-permute-start(bf16[256,4096]{1,0:T(8,128)(2,1)S(1)} %convolution_convert_fusion.2), channel_id=1, source_target_pairs={{0,16},{16,0},{32,48},{48,32},{64,80},{80,64},{96,112},{112,96},{1... | collective-permute-start | bytes 6291464 | tf_op jit(solution)/shard_map/scatter_core/ppermute | solution.py:127
  96.1 36.7 %collective-permute-start.10 = (bf16[64,4096]{1,0:T(8,128)(2,1)}, bf16[64,4096]{1,0:T(8,128)(2,1)}, u32[]{:S(2)}, u32[]{:S(2)}) collective-permute-start(bf16[64,4096]{1,0:T(8,128)(2,1)} %get-tuple-element.47), channel_id=1, source_target_pairs={{0,32},{16,48},{32,64},{48,80},{64,96},{80,112},{96,0},{112,16},{1... | collective-permute-start | bytes 1572872 | tf_op jit(solution)/shard_map/scatter_x/ppermute | solution.py:136
  100.1 32.7 %collective-permute-start.8 = (bf16[64,4096]{1,0:T(8,128)(2,1)}, bf16[64,4096]{1,0:T(8,128)(2,1)}, u32[]{:S(2)}, u32[]{:S(2)}) collective-permute-start(bf16[64,4096]{1,0:T(8,128)(2,1)} %get-tuple-element.46), channel_id=1, source_target_pairs={{0,96},{16,112},{32,0},{48,16},{64,32},{80,48},{96,64},{112,80},{1... | collective-permute-start | bytes 1572872 | tf_op jit(solution)/shard_map/scatter_x/ppermute | solution.py:136
  102.6 30.3 %collective-permute-start.9 = (bf16[64,4096]{1,0:T(8,128)(2,1)S(1)}, bf16[64,4096]{1,0:T(8,128)(2,1)}, u32[]{:S(2)}, u32[]{:S(2)}) collective-permute-start(bf16[64,4096]{1,0:T(8,128)(2,1)S(1)} %get-tuple-element.48), channel_id=1, source_target_pairs={{0,64},{16,80},{32,96},{48,112},{64,0},{80,16},{96,32},{112,48},{1... | collective-permute-start | bytes 1572872 | tf_op jit(solution)/shard_map/scatter_x/ppermute | solution.py:136
  108.7 2.7 %copy-start.5 = (bf16[32,32]{1,0:T(8,128)(2,1)S(1)}, bf16[32,32]{1,0:T(8,128)(2,1)}, u32[]{:S(2)}) copy-start(bf16[32,32]{1,0:T(8,128)(2,1)} %constant.135.clone) | copy-start | bytes 6148
  113.0 40.3 %all-to-all-start.2 = ((bf16[16,2,4096]{2,1,0:T(2,128)(2,1)}), bf16[16,2,4096]{2,1,0:T(2,128)(2,1)S(1)}, u32[]{:S(2)}, u32[]{:S(2)}) async-start(bf16[16,2,4096]{2,1,0:T(2,128)(2,1)} %reshape.263), calls=%async_computation.2 | async-start | bytes 524288 | tf_op jit(solution)/shard_map/hard_back/all_to_all | solution.py:140
  127.5 2.8 %copy-start.1 = (f32[256,4096]{1,0:T(8,128)S(1)}, f32[256,4096]{1,0:T(8,128)}, u32[]{:S(2)}) copy-start(f32[256,4096]{1,0:T(8,128)} %fusion.53) | copy-start | bytes 12582916
  132.9 10.5 %copy-start.2 = (f32[256,4096]{1,0:T(8,128)S(1)}, f32[256,4096]{1,0:T(8,128)}, u32[]{:S(2)}) copy-start(f32[256,4096]{1,0:T(8,128)} %fusion.55) | copy-start | bytes 12582916
  135.0 12.6 %collective-permute-start.11 = (bf16[16,4096]{1,0:T(8,128)(2,1)S(1)}, bf16[16,4096]{1,0:T(8,128)(2,1)S(1)}, u32[]{:S(2)}, u32[]{:S(2)}) collective-permute-start(bf16[16,4096]{1,0:T(8,128)(2,1)S(1)} %get-tuple-element.49), channel_id=1, source_target_pairs={{0,384},{16,400},{32,416},{48,432},{64,448},{80,464},{96,480},{112... | collective-permute-start | bytes 393224 | tf_op jit(solution)/shard_map/scatter_z/ppermute | solution.py:149
  137.6 14.9 %collective-permute-start.12 = (bf16[16,4096]{1,0:T(8,128)(2,1)S(1)}, bf16[16,4096]{1,0:T(8,128)(2,1)S(1)}, u32[]{:S(2)}, u32[]{:S(2)}) collective-permute-start(bf16[16,4096]{1,0:T(8,128)(2,1)S(1)} %get-tuple-element.51), channel_id=1, source_target_pairs={{0,256},{16,272},{32,288},{48,304},{64,320},{80,336},{96,352},{112... | collective-permute-start | bytes 393224 | tf_op jit(solution)/shard_map/scatter_z/ppermute | solution.py:149
  140.1 12.5 %collective-permute-start.13 = (bf16[16,4096]{1,0:T(8,128)(2,1)S(1)}, bf16[16,4096]{1,0:T(8,128)(2,1)S(1)}, u32[]{:S(2)}, u32[]{:S(2)}) collective-permute-start(bf16[16,4096]{1,0:T(8,128)(2,1)S(1)} %get-tuple-element.50), channel_id=1, source_target_pairs={{0,128},{16,144},{32,160},{48,176},{64,192},{80,208},{96,224},{112... | collective-permute-start | bytes 393224 | tf_op jit(solution)/shard_map/scatter_z/ppermute | solution.py:149

commit v3 on v2

v3 whole, which is shorter than its diff:
```python
import functools

import jax
import jax.numpy as jnp
from jax import lax
from jax.experimental import pallas as pl
from jax.experimental.pallas import tpu as pltpu
from jax.sharding import PartitionSpec as P

NZ, NX, NC = 4, 4, 2
NY, NH = 4, 4
X_GROUPS = [
    [(z * NX + x) * NC + c for x in range(NX)] for z in range(NZ) for c in range(NC)
]
Y_GROUPS = [[y * NH + h for y in range(NY)] for h in range(NH)]
CORE_SWAP = [(i, i ^ 1) for i in range(NZ * NX * NC)]
FLAG = 128
BF16, F32 = jnp.bfloat16, jnp.float32


def z_shift(d):
    step = NX * NC
    return [(i, (i // step + d) % NZ * step + i % step) for i in range(NZ * step)]


def x_shift(d):
    step = NX * NC
    return [(i, i // step * step + (i + d * NC) % step) for i in range(NZ * step)]


def h_shift(d):
    return [(i, i // NH * NH + (i + d) % NH) for i in range(NY * NH)]


def exchange(parts, axis, perm, sign=1):
    return parts[:1] + [lax.ppermute(p, axis, perm(sign * d)) for d, p in enumerate(parts) if d]


def pieces(x, n):
    k = x.shape[0] // n
    return [x[i * k : (i + 1) * k] for i in range(n)]


def turn(parts, n):
    cut = [pieces(p, n) for p in parts]
    return [jnp.concatenate([c[i] for c in cut], axis=0) for i in range(n)]


def dot_t(a, b):
    return lax.dot_general(a, b, (((1,), (1,)), ((), ())), preferred_element_type=F32)


def t_dot(a, b):
    return lax.dot_general(a, b, (((0,), (0,)), ((), ())), preferred_element_type=F32)


def dot(a, b):
    return jnp.dot(a, b, preferred_element_type=F32)


def split(a):
    hi = a.astype(BF16)
    return hi, (a - hi.astype(F32)).astype(BF16)


def swap(x, axis, members):
    return lax.all_to_all(
        x, axis, split_axis=0, concat_axis=0, axis_index_groups=members, tiled=True
    )


def pack_kernel(slots, h_ref, dest_ref, rows_ref, packed_ref, placing_ref):
    dest = dest_ref[...]
    count, width = rows_ref.shape
    groups = NY * NH
    hot = (dest == lax.broadcasted_iota(jnp.int32, (count, groups), 1)).astype(F32)
    ahead = (
        lax.broadcasted_iota(jnp.int32, (count, count), 0)
        > lax.broadcasted_iota(jnp.int32, (count, count), 1)
    ).astype(F32)
    rank = jnp.sum(dot(ahead, hot) * hot, axis=1, keepdims=True).astype(jnp.int32)
    at = lax.broadcasted_iota(jnp.int32, (count, groups * slots), 1)
    h = dest % NH
    step = h - h_ref[0]
    step = jnp.where(step < 0, step + NH, step)
    send = ((dest - h + step) * slots + rank == at).astype(BF16)
    packed_ref[:, :width] = t_dot(send, rows_ref[...]).astype(BF16)
    packed_ref[:, width:] = t_dot(send, jnp.ones((count, FLAG), BF16)).astype(BF16)
    placing_ref[...] = (dest * slots + rank == at).astype(BF16)


def pack(dest, rows, my_h, slots):
    count, width = rows.shape
    places = NY * NH * slots
    return pl.pallas_call(
        functools.partial(pack_kernel, slots),
        in_specs=[
            pl.BlockSpec(memory_space=pltpu.SMEM),
            pl.BlockSpec(memory_space=pltpu.VMEM),
            pl.BlockSpec(memory_space=pltpu.VMEM),
        ],
        out_specs=[pl.BlockSpec(memory_space=pltpu.VMEM)] * 2,
        out_shape=[
            jax.ShapeDtypeStruct((places, width + FLAG), BF16),
            jax.ShapeDtypeStruct((count, places), BF16),
        ],
        cost_estimate=pl.CostEstimate(
            flops=2 * count * places * width, bytes_accessed=6 * places * width, transcendentals=0
        ),
        name="pack",
    )(my_h.reshape(1), dest, rows)


def core_sum_kernel(coef_ref, q_ref, away_ref, own_ref, *sent_refs):
    total = t_dot(coef_ref[...], q_ref[...]) + away_ref[...].astype(F32)
    n = own_ref.shape[0]
    own_ref[...] = total[:n]
    for d, ref in enumerate(sent_refs):
        ref[...] = total[(d + 1) * n : (d + 2) * n].astype(BF16)


def core_sum(coef, q, away, block=512):
    count, width = q.shape
    half = coef.shape[1]
    n = half // NX
    return pl.pallas_call(
        core_sum_kernel,
        grid=(width // block,),
        in_specs=[
            pl.BlockSpec((count, half), lambda i: (0, 0)),
            pl.BlockSpec((count, block), lambda i: (0, i)),
            pl.BlockSpec((half, block), lambda i: (0, i)),
        ],
        out_specs=[pl.BlockSpec((n, block), lambda i: (0, i))] * NX,
        out_shape=[jax.ShapeDtypeStruct((n, width), F32)]
        + [jax.ShapeDtypeStruct((n, width), BF16)] * (NX - 1),
        cost_estimate=pl.CostEstimate(
            flops=2 * count * half * width, bytes_accessed=6 * half * width, transcendentals=0
        ),
        compiler_params=pltpu.CompilerParams(vmem_limit_bytes=16 << 20),
        name="core_sum",
    )(coef, q, away)


def query_grad_kernel(scale, *refs):
    coefs, rows, out = refs[:6], refs[6:9], refs[9]
    total = dot(coefs[0][...], rows[0][...])
    for i in range(1, 6):
        total = total + dot(coefs[i][...], rows[i % 3][...])
    out[0] = (scale * total).astype(out.dtype)


def query_grad(coefs, rows, scale, block=512):
    count, width = coefs[0].shape[0], rows[0].shape[1]
    return pl.pallas_call(
        functools.partial(query_grad_kernel, scale),
        grid=(width // block,),
        in_specs=[pl.BlockSpec(c.shape, lambda i: (0, 0)) for c in coefs]
        + [pl.BlockSpec((r.shape[0], block), lambda i: (0, i)) for r in rows],
        out_specs=pl.BlockSpec((1, count, block), lambda i: (0, 0, i)),
        out_shape=jax.ShapeDtypeStruct((1, count, width), BF16),
        cost_estimate=pl.CostEstimate(
            flops=4 * count * width * sum(r.shape[0] for r in rows),
            bytes_accessed=2 * width * (count + sum(r.shape[0] for r in rows)),
            transcendentals=0,
        ),
        compiler_params=pltpu.CompilerParams(vmem_limit_bytes=16 << 20),
        name="query_grad",
    )(*coefs, *rows)


def body(queries, passages, positives, hard_rows, hard_dest):
    q = queries[0]
    own = passages[0]
    targets = positives[0]
    owned_hard = hard_rows[0]
    width = q.shape[1]
    rows = own.shape[0]
    groups = NY * NH
    slots = max(2, 2 * owned_hard.shape[0] // groups)
    scale = width ** (-0.5)
    blk = lax.axis_index("blk")
    my_z, my_x, my_c = blk // (NX * NC), blk // NC % NX, blk % NC
    my_h = lax.axis_index("group") % NH

    packed, placing = pack(hard_dest[0], owned_hard, my_h, slots)
    own, packed = lax.optimization_barrier((own, packed))

    with jax.named_scope("gather_z"):
        z_rows = jnp.concatenate(exchange([own] * NZ, "blk", z_shift), axis=0)
    with jax.named_scope("hard_y"):
        from_y = pieces(swap(packed, "group", Y_GROUPS), NY)
    with jax.named_scope("gather_x"):
        z_rows = lax.optimization_barrier(z_rows)
        spread = jnp.broadcast_to(z_rows, (NX, *z_rows.shape)).reshape(-1, width)
        half0 = swap(spread, "blk", X_GROUPS)
    with jax.named_scope("hard_h"):
        received = jnp.concatenate(exchange(turn(from_y, NH), "group", h_shift), axis=0)
    half0, received = lax.optimization_barrier((half0, received))
    with jax.named_scope("gather_core"):
        half1 = lax.ppermute(half0, "blk", CORE_SWAP)

    hard = received[:, :width]
    live = received[:, width] > 0.5
    half = half0.shape[0]

    owner = targets // rows
    o_z, o_x, o_c = owner // (NX * NC), owner // NC % NX, owner % NC
    column = (o_c != my_c).astype(jnp.int32) * half + (o_x * NZ + (my_z - o_z) % NZ) * rows + targets % rows
    hot0 = column[:, None] == jnp.arange(half)[None, :]
    hot1 = column[:, None] == (jnp.arange(half) + half)[None, :]

    with jax.named_scope("scores"):
        s0 = scale * dot_t(q, half0)
        s1 = scale * dot_t(q, half1)
        sh = jnp.where(live[None, :], scale * dot_t(q, hard), -jnp.inf)
        top = jnp.maximum(
            jnp.maximum(jnp.max(s0, axis=1), jnp.max(s1, axis=1)), jnp.max(sh, axis=1)
        )
        total = (
            jnp.sum(jnp.exp(s0 - top[:, None]), axis=1)
            + jnp.sum(jnp.exp(s1 - top[:, None]), axis=1)
            + jnp.sum(jnp.exp(sh - top[:, None]), axis=1)
        )
        log_total = top + jnp.log(total)
        c0 = jnp.exp(s0 - log_total[:, None]) - hot0.astype(F32)
        c1 = jnp.exp(s1 - log_total[:, None]) - hot1.astype(F32)
        ph = jnp.exp(sh - log_total[:, None])
        at_target = jnp.sum(jnp.where(hot0, s0, 0.0), axis=1) + jnp.sum(
            jnp.where(hot1, s1, 0.0), axis=1
        )
        loss_rows = log_total - at_target

    c0_hi, c0_lo = split(c0)
    c1_hi, c1_lo = split(c1)
    ph_hi, ph_lo = split(ph)
    n = half // NX
    col = jnp.arange(half)
    back_x = (my_x - col // n) % NX * n + col % n
    roll = (col[:, None] == back_x[None, :]).astype(BF16)
    with jax.named_scope("scatter_core"):
        away = t_dot(dot(c1_hi, roll).astype(BF16), q).astype(BF16)
        away = lax.ppermute(away, "blk", CORE_SWAP)
    with jax.named_scope("scatter_x"):
        mine = core_sum(dot(c0_hi, roll).astype(BF16), q, away)
        chunks = [c.astype(F32) for c in exchange(list(mine), "blk", x_shift, -1)]
        mine_x = pieces(functools.reduce(jnp.add, chunks), NZ)

    c0_hi, c0_lo, c1_hi, c1_lo, ph_hi, ph_lo, _ = lax.optimization_barrier(
        (c0_hi, c0_lo, c1_hi, c1_lo, ph_hi, ph_lo, away)
    )
    with jax.named_scope("hard_back"):
        at = jnp.arange(groups * slots)
        step, y, slot = at // (NY * slots), at // slots % NY, at % slots
        to = (y * NH + (my_h - step) % NH) * slots + slot
        order = (to[:, None] == at[None, :]).astype(BF16)
        g = (scale * t_dot(dot(ph_hi, order).astype(BF16), q)).astype(BF16)
        returned = lax.all_to_all(
            g.reshape(groups, slots, width), "group", split_axis=0, concat_axis=0, tiled=True
        ).reshape(groups * slots, width)
    with jax.named_scope("scatter_z"):
        sent = [mine_x[0]] + [m.astype(BF16) for m in mine_x[1:]]
        chunks = [c.astype(F32) for c in exchange(sent, "blk", z_shift, -1)]
        d_passage = (scale * functools.reduce(jnp.add, chunks)).astype(BF16)
    with jax.named_scope("hard_own"):
        d_owned = dot(placing, returned).astype(BF16)
    with jax.named_scope("d_query"):
        d_query = query_grad(
            (c0_hi, c1_hi, ph_hi, c0_lo, c1_lo, ph_lo), (half0, half1, hard), scale
        )
    return (loss_rows[None], d_query, d_passage[None], d_owned[None])


def solution(mesh):
    return jax.shard_map(
        body,
        mesh=mesh,
        in_specs=(
            P("group", "blk", None),
            P("group", "blk", None),
            P("group", "blk"),
            P("group", "blk", None),
            P("group", "blk", None),
        ),
        out_specs=(
            P("group", "blk"),
            P("group", "blk", None),
            P("group", "blk", None),
            P("group", "blk", None),
        ),
        check_vma=False,
    )
```

time: 155 us -> 145 us (0.935); the launches traced: 154 us -> 142 us
  matrix products: 30.7 us -> 10.3 us
  Pallas kernels: 0 us -> 14.6 us
  waiting for transfers between devices: 32 us -> 20.5 us
  starting transfers between devices: 76.5 us -> 82.7 us
    dot_general x8 -> x2, matrix products: 20.3 us -> 1.01 us  [dot(): return jnp.dot(a, b, preferred_element_type=F32)]
    ppermute x14, starting transfers between devices: 47.1 us -> 65.6 us  [the longest x12 54.2 us: exchange(): lax.ppermute(p, axis, perm(sign * d))]
    pallas_call x0 -> x3, Pallas kernels: none -> 14.6 us  [the longest x1 8.19 us: query_grad(): pl.pallas_call(functools.partial(query_grad_kernel, scale), grid=(width /...]
    ppermute x14, waiting for transfers between devices: 27.4 us -> 17.9 us  [the longest x12 14.2 us: exchange(): lax.ppermute(p, axis, perm(sign * d))]
    all_to_all x2, starting transfers between devices: 17.2 us -> 8.78 us  [swap(): lax.all_to_all(x, axis, split_axis=0, concat_axis=0, axis_index_groups=me...]
    all_to_all x1, starting transfers between devices: 12.2 us -> 8.33 us  [body(): lax.all_to_all(g.reshape(groups, slots, width), 'group', split_axis=0, co...]
    unnamed x17 -> x16, local copies, waits for them, and re-layouts: 3.67 us -> 0.03 us
    all_to_all x2, waiting for transfers between devices: 4.61 us -> 2.57 us  [swap(): lax.all_to_all(x, axis, split_axis=0, concat_axis=0, axis_index_groups=me...]
  transfers between devices with their start and end apart: 17 -> 17, of which waited for: 7 -> 8; matrix products, arithmetic and copies ran while one was open for 19% -> 8% of each run, Pallas kernels for 0% -> 6%
where the time goes in v3:
time: 145 us; the launch traced here: 142 us
  starting transfers between devices  82.7 us (57%)
  waiting for transfers between devices  20.5 us (14%)
  Pallas kernels  14.6 us (10%)
  matrix products  10.3 us (7%)
  local copies, waits for them, and re-layouts  6.94 us (5%)
  other arithmetic  5.96 us (4%)
    ppermute x12, starting transfers between devices, exchange(): lax.ppermute(p, axis, perm(sign * d))  54.2 us
    ppermute x12, waiting for transfers between devices, exchange(): lax.ppermute(p, axis, perm(sign * d))  14.2 us
    ppermute x1, starting transfers between devices, body(): half1 = lax.ppermute(half0, 'blk', CORE_SWAP)  9.15 us
    all_to_all x2, starting transfers between devices, swap(): lax.all_to_all(x, axis, split_axis=0, concat_axis=0, axis_index_groups=me...  8.78 us
    all_to_all x1, starting transfers between devices, body(): lax.all_to_all(g.reshape(groups, slots, width), 'group', split_axis=0, co...  8.33 us
    pallas_call x1, Pallas kernels, query_grad(): pl.pallas_call(functools.partial(query_grad_kernel, scale), grid=(width /...  8.19 us
    dot_general x3, matrix products, dot_t(): lax.dot_general(a, b, (((1,), (1,)), ((), ())), preferred_element_type=F32)  5.62 us
    pallas_call x1, Pallas kernels, core_sum(): pl.pallas_call(core_sum_kernel, grid=(width // block,), in_specs=[pl.Bloc...  4.24 us
  transfers between devices with their start and end apart: 17, of which 8 were waited for; matrix products, arithmetic and copies ran while one was open for 8% of the time, Pallas kernels for 6%

profile of v3, /device:TPU:1, one launch (start us, length us, event | category | flops | bytes accessed | tf_op | source)
XLA Modules:
  0.0 142.0 jit_solution(10066405188870199624)
XLA Ops:
  0.6 1.3 copy.13.dest_ref
  2.0 2.2 %pack.1 = (bf16[32,4224]{1,0:T(8,128)(2,1)}, bf16[16,32]{1,0:T(8,128)(2,1)}) custom-call(s32[1]{0:T(128)} %bitcast.1.h_ref, s32[16,1]{1,0:T(8,128)} %copy.13.dest_ref, bf16[16,4096]{1,0:T(8,128)(2,1)} %bitcast.83), custom_call_target="tpu_custom_call" | custom-call | flops 4194304 | bytes 786432 | tf_op jit(solution)/shard_map/pack/pallas_call | solution.py:95
  4.2 7.1 %collective-permute-start.2 = (bf16[16,4096]{1,0:T(8,128)(2,1)}, bf16[16,4096]{1,0:T(8,128)(2,1)S(1)}, u32[]{:S(2)}, u32[]{:S(2)}) collective-permute-start(bf16[16,4096]{1,0:T(8,128)(2,1)} %bitcast.84), channel_id=1, source_target_pairs={{0,384},{16,400},{32,416},{48,432},{64,448},{80,464},{96,480},{112... | collective-permute-start | bytes 393224 | tf_op jit(solution)/shard_map/gather_z/ppermute | solution.py:36
  11.3 1.9 %collective-permute-start.1 = (bf16[16,4096]{1,0:T(8,128)(2,1)}, bf16[16,4096]{1,0:T(8,128)(2,1)S(1)}, u32[]{:S(2)}, u32[]{:S(2)}) collective-permute-start(bf16[16,4096]{1,0:T(8,128)(2,1)} %bitcast.85), channel_id=1, source_target_pairs={{0,256},{16,272},{32,288},{48,304},{64,320},{80,336},{96,352},{112... | collective-permute-start | bytes 393224 | tf_op jit(solution)/shard_map/gather_z/ppermute | solution.py:36
  13.2 2.2 %collective-permute-start = (bf16[16,4096]{1,0:T(8,128)(2,1)}, bf16[16,4096]{1,0:T(8,128)(2,1)S(1)}, u32[]{:S(2)}, u32[]{:S(2)}) collective-permute-start(bf16[16,4096]{1,0:T(8,128)(2,1)} %bitcast.86), channel_id=1, source_target_pairs={{0,128},{16,144},{32,160},{48,176},{64,192},{80,208},{96,224},{112... | collective-permute-start | bytes 393224 | tf_op jit(solution)/shard_map/gather_z/ppermute | solution.py:36
  15.4 4.2 %all-to-all-start.1 = ((bf16[4,8,4224]{2,1,0:T(8,128)(2,1)}), bf16[4,8,4224]{2,1,0:T(8,128)(2,1)S(1)}, u32[]{:S(2)}, u32[]{:S(2)}) async-start(bf16[4,8,4224]{2,1,0:T(8,128)(2,1)} %bitcast.82), calls=%async_computation.1 | async-start | bytes 540672 | tf_op jit(solution)/shard_map/hard_y/all_to_all | solution.py:67
  19.6 0.0 collective-permute-done.2
  19.6 0.0 collective-permute-done.1
  19.6 2.1 %collective-permute-done = bf16[16,4096]{1,0:T(8,128)(2,1)S(1)} collective-permute-done((bf16[16,4096]{1,0:T(8,128)(2,1)}, bf16[16,4096]{1,0:T(8,128)(2,1)S(1)}, u32[]{:S(2)}, u32[]{:S(2)}) %collective-permute-start) | collective-permute-done | bytes 131104 | tf_op jit(solution)/shard_map/gather_z/ppermute | solution.py:36
  21.7 0.9 pad_maximum_fusion
  22.6 2.6 %all-to-all-done.1 = bf16[4,8,4224]{2,1,0:T(8,128)(2,1)S(1)} async-done(((bf16[4,8,4224]{2,1,0:T(8,128)(2,1)}), bf16[4,8,4224]{2,1,0:T(8,128)(2,1)S(1)}, u32[]{:S(2)}, u32[]{:S(2)}) %all-to-all-start.1) | async-done | bytes 270368 | tf_op jit(solution)/shard_map/hard_y/all_to_all | solution.py:67
  25.2 1.6 %broadcast_in_dim.23 = bf16[4,64,4096]{2,1,0:T(8,128)(2,1)} broadcast(bf16[64,4096]{1,0:T(8,128)(2,1)S(1)} %pad_maximum_fusion), dimensions={1,2} | broadcast | bytes 2621440 | tf_op jit(solution)/shard_map/gather_x/broadcast_in_dim | solution.py:195
  26.8 4.6 %all-to-all-start = ((bf16[4,64,4096]{2,1,0:T(8,128)(2,1)}), bf16[4,64,4096]{2,1,0:T(8,128)(2,1)}, u32[]{:S(2)}, u32[]{:S(2)}) async-start(bf16[4,64,4096]{2,1,0:T(8,128)(2,1)} %broadcast_in_dim.23), calls=%async_computation | async-start | bytes 4194304 | tf_op jit(solution)/shard_map/gather_x/all_to_all | solution.py:67
  31.3 0.2 fusion.55
  31.6 0.1 pad_maximum_fusion.1
  31.7 8.8 %collective-permute-start.3 = (bf16[8,4224]{1,0:T(8,128)(2,1)S(1)}, bf16[8,4224]{1,0:T(8,128)(2,1)S(1)}, u32[]{:S(2)}, u32[]{:S(2)}) collective-permute-start(bf16[8,4224]{1,0:T(8,128)(2,1)S(1)} %pad_maximum_fusion.1), channel_id=1, source_target_pairs={{0,1},{1,2},{2,3},{3,0},{4,5},{5,6},{6,7},{7,4},{8,9},{9,10},{10,1... | collective-permute-start | bytes 202760 | tf_op jit(solution)/shard_map/hard_h/ppermute | solution.py:36
  40.5 0.1 pad_maximum_fusion.2
  40.6 8.7 %collective-permute-start.4 = (bf16[8,4224]{1,0:T(8,128)(2,1)S(1)}, bf16[8,4224]{1,0:T(8,128)(2,1)S(1)}, u32[]{:S(2)}, u32[]{:S(2)}) collective-permute-start(bf16[8,4224]{1,0:T(8,128)(2,1)S(1)} %pad_maximum_fusion.2), channel_id=1, source_target_pairs={{0,2},{1,3},{2,0},{3,1},{4,6},{5,7},{6,4},{7,5},{8,10},{9,11},{10,... | collective-permute-start | bytes 202760 | tf_op jit(solution)/shard_map/hard_h/ppermute | solution.py:36
  49.2 0.1 pad_maximum_fusion.3
  49.3 5.2 %collective-permute-start.5 = (bf16[8,4224]{1,0:T(8,128)(2,1)S(1)}, bf16[8,4224]{1,0:T(8,128)(2,1)S(1)}, u32[]{:S(2)}, u32[]{:S(2)}) collective-permute-start(bf16[8,4224]{1,0:T(8,128)(2,1)S(1)} %pad_maximum_fusion.3), channel_id=1, source_target_pairs={{0,3},{1,0},{2,1},{3,2},{4,7},{5,4},{6,5},{7,6},{8,11},{9,8},{10,9... | collective-permute-start | bytes 202760 | tf_op jit(solution)/shard_map/hard_h/ppermute | solution.py:36
  54.5 0.0 collective-permute-done.3
  54.5 1.8 %collective-permute-done.4 = bf16[8,4224]{1,0:T(8,128)(2,1)S(1)} collective-permute-done((bf16[8,4224]{1,0:T(8,128)(2,1)S(1)}, bf16[8,4224]{1,0:T(8,128)(2,1)S(1)}, u32[]{:S(2)}, u32[]{:S(2)}) %collective-permute-start.4) | collective-permute-done | bytes 67616 | tf_op jit(solution)/shard_map/hard_h/ppermute | solution.py:36
  56.3 2.6 %collective-permute-done.5 = bf16[8,4224]{1,0:T(8,128)(2,1)S(1)} collective-permute-done((bf16[8,4224]{1,0:T(8,128)(2,1)S(1)}, bf16[8,4224]{1,0:T(8,128)(2,1)S(1)}, u32[]{:S(2)}, u32[]{:S(2)}) %collective-permute-start.5) | collective-permute-done | bytes 67616 | tf_op jit(solution)/shard_map/hard_h/ppermute | solution.py:36
  58.9 0.2 concatenate.19
  59.1 0.0 all-to-all-done
  59.1 9.1 %collective-permute-start.6 = (bf16[256,4096]{1,0:T(8,128)(2,1)}, bf16[256,4096]{1,0:T(8,128)(2,1)}, u32[]{:S(2)}, u32[]{:S(2)}) collective-permute-start(bf16[256,4096]{1,0:T(8,128)(2,1)} %bitcast.4.refs_6_), channel_id=1, source_target_pairs={{0,16},{16,0},{32,48},{48,32},{64,80},{80,64},{96,112},{112,96},{1... | collective-permute-start | bytes 6291464 | tf_op jit(solution)/shard_map/gather_core/ppermute | solution.py:201
  68.3 0.1 compare_reduce_fusion
  68.5 0.8 fusion.56
  69.2 2.5 %fusion.57 = (f32[256]{0:T(256)S(1)}, f32[256,256]{0,1:T(8,128)S(1)}) fusion(bf16[256,4096]{1,0:T(8,128)(2,1)} %bitcast.4.refs_6_, bf16[1,256,4096]{2,1,0:T(8,128)(2,1)S(1)} %copy-done), kind=kOutput, calls=%fused_computation.131 | convolution fusion | flops 537001728 | bytes 4457472 | tf_op jit(solution)/shard_map/scores/dot_general | solution.py:50
  71.7 0.7 collective-permute-done.6.refs_7_
  72.3 2.4 %fusion.58 = (f32[256]{0:T(256)S(1)}, f32[256,256]{0,1:T(8,128)S(1)}) fusion(bf16[256,4096]{1,0:T(8,128)(2,1)} %collective-permute-done.6.refs_7_, bf16[1,256,4096]{2,1,0:T(8,128)(2,1)S(1)} %copy-done), kind=kOutput, calls=%fused_computation.132 | convolution fusion | flops 537001728 | bytes 4457472 | tf_op jit(solution)/shard_map/scores/dot_general | solution.py:50
  74.8 0.2 exponential_reduce_fusion
  75.0 0.3 fusion.14
  75.3 0.6 add_subtract_fusion
  75.9 0.9 subtract_convert_fusion
  76.8 2.2 %convolution_convert_fusion = bf16[256,4096]{1,0:T(8,128)(2,1)} fusion(bf16[256,256]{1,0:T(8,128)(2,1)S(1)} %get-tuple-element.26.refs_1_, s32[256]{0:T(256)S(1)} %fusion.28, bf16[1,256,4096]{2,1,0:T(8,128)(2,1)S(1)} %copy-done), kind=kOutput, calls=%fused_computation | convolution fusion | flops 571604992 | bytes 4326400 | tf_op jit(solution)/shard_map/scatter_core/dot_general | solution.py:54
  79.0 2.3 %collective-permute-start.7 = (bf16[256,4096]{1,0:T(8,128)(2,1)}, bf16[256,4096]{1,0:T(8,128)(2,1)S(1)}, u32[]{:S(2)}, u32[]{:S(2)}) collective-permute-start(bf16[256,4096]{1,0:T(8,128)(2,1)} %convolution_convert_fusion), channel_id=1, source_target_pairs={{0,16},{16,0},{32,48},{48,32},{64,80},{80,64},{96,112},{112,96},{1... | collective-permute-start | bytes 6291464 | tf_op jit(solution)/shard_map/scatter_core/ppermute | solution.py:243
  81.3 0.7 slice.106.refs_8_
  82.0 0.2 convolution_convert_fusion.2.coef_ref
  82.2 3.0 %collective-permute-done.7.away_ref = bf16[256,4096]{1,0:T(8,128)(2,1)S(1)} collective-permute-done((bf16[256,4096]{1,0:T(8,128)(2,1)}, bf16[256,4096]{1,0:T(8,128)(2,1)S(1)}, u32[]{:S(2)}, u32[]{:S(2)}) %collective-permute-start.7) | collective-permute-done | bytes 2097184 | tf_op jit(solution)/shard_map/scatter_core/ppermute | solution.py:243
  85.3 4.2 %core_sum.1 = (f32[64,4096]{1,0:T(8,128)S(1)}, bf16[64,4096]{1,0:T(8,128)(2,1)}, bf16[64,4096]{1,0:T(8,128)(2,1)}, bf16[64,4096]{1,0:T(8,128)(2,1)}) custom-call(bf16[256,256]{1,0:T(8,128)(2,1)S(1)} %convolution_convert_fusion.2.coef_ref, bf16[256,4096]{1,0:T(8,128)(2,1)S(1)} %bitcast.80, bf16[256,4096]{1,0:T(8,128)(2,1)S(1)} %collective-permute-done.7.away_ref), custom_call_target="tpu_custom_call" | custom-call | flops 536870912 | bytes 6291456 | tf_op jit(solution)/shard_map/scatter_x/core_sum/pallas_call | solution.py:126
  89.5 3.9 %collective-permute-start.10 = (bf16[64,4096]{1,0:T(8,128)(2,1)}, bf16[64,4096]{1,0:T(8,128)(2,1)}, u32[]{:S(2)}, u32[]{:S(2)}) collective-permute-start(bf16[64,4096]{1,0:T(8,128)(2,1)} %get-tuple-element.34), channel_id=1, source_target_pairs={{0,32},{16,48},{32,64},{48,80},{64,96},{80,112},{96,0},{112,16},{1... | collective-permute-start | bytes 1572872 | tf_op jit(solution)/shard_map/scatter_x/ppermute | solution.py:36
  93.4 4.3 %collective-permute-start.9 = (bf16[64,4096]{1,0:T(8,128)(2,1)}, bf16[64,4096]{1,0:T(8,128)(2,1)}, u32[]{:S(2)}, u32[]{:S(2)}) collective-permute-start(bf16[64,4096]{1,0:T(8,128)(2,1)} %get-tuple-element.33), channel_id=1, source_target_pairs={{0,64},{16,80},{32,96},{48,112},{64,0},{80,16},{96,32},{112,48},{1... | collective-permute-start | bytes 1572872 | tf_op jit(solution)/shard_map/scatter_x/ppermute | solution.py:36
  97.8 3.1 %collective-permute-start.8 = (bf16[64,4096]{1,0:T(8,128)(2,1)}, bf16[64,4096]{1,0:T(8,128)(2,1)}, u32[]{:S(2)}, u32[]{:S(2)}) collective-permute-start(bf16[64,4096]{1,0:T(8,128)(2,1)} %get-tuple-element.32), channel_id=1, source_target_pairs={{0,96},{16,112},{32,0},{48,16},{64,32},{80,48},{96,64},{112,80},{1... | collective-permute-start | bytes 1572872 | tf_op jit(solution)/shard_map/scatter_x/ppermute | solution.py:36
  100.9 0.1 bitcast_convert_fusion.refs_2_
  101.0 0.1 fusion.20.refs_5_
  101.1 1.4 fusion
  102.5 1.8 %reshape.325 = bf16[16,2,4096]{2,1,0:T(2,128)(2,1)} reshape(bf16[32,4096]{1,0:T(8,128)(2,1)} %fusion) | data formatting | bytes 524288 | tf_op jit(solution)/shard_map/hard_back/reshape | solution.py:259
  104.3 8.3 %all-to-all-start.2 = ((bf16[16,2,4096]{2,1,0:T(2,128)(2,1)}), bf16[16,2,4096]{2,1,0:T(2,128)(2,1)}, u32[]{:S(2)}, u32[]{:S(2)}) async-start(bf16[16,2,4096]{2,1,0:T(2,128)(2,1)} %reshape.325), calls=%async_computation.2 | async-start | bytes 524288 | tf_op jit(solution)/shard_map/hard_back/all_to_all | solution.py:258
  112.7 0.0 collective-permute-done.10
  112.7 6.4 %collective-permute-done.9 = bf16[64,4096]{1,0:T(8,128)(2,1)} collective-permute-done((bf16[64,4096]{1,0:T(8,128)(2,1)}, bf16[64,4096]{1,0:T(8,128)(2,1)}, u32[]{:S(2)}, u32[]{:S(2)}) %collective-permute-start.9) | collective-permute-done | bytes 524320 | tf_op jit(solution)/shard_map/scatter_x/ppermute | solution.py:36
  119.1 1.4 collective-permute-done.8
  120.4 1.6 %fusion.51 = (bf16[64,4096]{1,0:T(8,128)(2,1)S(1)}, f32[64,4096]{1,0:T(8,128)S(1)}) fusion(bf16[64,4096]{1,0:T(8,128)(2,1)} %collective-permute-done.10, bf16[64,4096]{1,0:T(8,128)(2,1)} %collective-permute-done.9, f32[64,4096]{1,0:T(8,128)S(1)} %get-tuple-element.31, bf16[64,4096]{1,0:T(8,128)(2,1)} %collective-permute-done.8), kind=kLoop, calls=%fused_computation.127 | loop fusion | flops 1835008 | bytes 4194304 | tf_op jit(solution)/shard_map/convert.2
  122.1 1.9 %collective-permute-start.13 = (bf16[16,4096]{1,0:T(8,128)(2,1)S(1)}, bf16[16,4096]{1,0:T(8,128)(2,1)S(1)}, u32[]{:S(2)}, u32[]{:S(2)}) collective-permute-start(bf16[16,4096]{1,0:T(8,128)(2,1)S(1)} %get-tuple-element.51), channel_id=1, source_target_pairs={{0,128},{16,144},{32,160},{48,176},{64,192},{80,208},{96,224},{112... | collective-permute-start | bytes 393224 | tf_op jit(solution)/shard_map/scatter_z/ppermute | solution.py:36
  124.0 2.5 %collective-permute-start.12 = (bf16[16,4096]{1,0:T(8,128)(2,1)S(1)}, bf16[16,4096]{1,0:T(8,128)(2,1)S(1)}, u32[]{:S(2)}, u32[]{:S(2)}) collective-permute-start(bf16[16,4096]{1,0:T(8,128)(2,1)S(1)} %get-tuple-element.52), channel_id=1, source_target_pairs={{0,256},{16,272},{32,288},{48,304},{64,320},{80,336},{96,352},{112... | collective-permute-start | bytes 393224 | tf_op jit(solution)/shard_map/scatter_z/ppermute | solution.py:36
  126.6 4.5 %collective-permute-start.11 = (bf16[16,4096]{1,0:T(8,128)(2,1)S(1)}, bf16[16,4096]{1,0:T(8,128)(2,1)S(1)}, u32[]{:S(2)}, u32[]{:S(2)}) collective-permute-start(bf16[16,4096]{1,0:T(8,128)(2,1)S(1)} %get-tuple-element.50), channel_id=1, source_target_pairs={{0,384},{16,400},{32,416},{48,432},{64,448},{80,464},{96,480},{112... | collective-permute-start | bytes 393224 | tf_op jit(solution)/shard_map/scatter_z/ppermute | solution.py:36
  131.2 8.2 %query_grad.1 = bf16[1,256,4096]{2,1,0:T(8,128)(2,1)} custom-call(bf16[256,256]{1,0:T(8,128)(2,1)S(1)} %get-tuple-element.25.refs_0_, bf16[256,256]{1,0:T(8,128)(2,1)S(1)} %get-tuple-element.26.refs_1_, bf16[256,32]{1,0:T(8,128)(2,1)S(1)} %bitcast_convert_fusion.refs_2_, bf16[256,256]{1,0:T(8,128)(2,1)S(1)} %copy-done.3, bf16[256,256]{1,0:T(8,128)(2,1)S(1)} %copy-done.2, ...), custom_call_target="tpu_custom_call" | custom-call | flops 2281701376 | bytes 6553600 | tf_op jit(solution)/shard_map/d_query/query_grad/pallas_call | solution.py:155
  139.4 0.0 collective-permute-done.13
  139.4 0.0 collective-permute-done.12
  139.4 0.0 collective-permute-done.11
  139.4 0.7 fusion.19
  140.1 0.0 all-to-all-done.2
  140.1 1.0 reshape.326
  141.2 0.8 fusion.1
  (21 shorter events, 0.1 us)
Async XLA Ops:
  4.2 15.4 %collective-permute-start.2 = (bf16[16,4096]{1,0:T(8,128)(2,1)}, bf16[16,4096]{1,0:T(8,128)(2,1)S(1)}, u32[]{:S(2)}, u32[]{:S(2)}) collective-permute-start(bf16[16,4096]{1,0:T(8,128)(2,1)} %bitcast.84), channel_id=1, source_target_pairs={{0,384},{16,400},{32,416},{48,432},{64,448},{80,464},{96,480},{112... | collective-permute-start | bytes 393224 | tf_op jit(solution)/shard_map/gather_z/ppermute | solution.py:36
  11.3 8.3 %collective-permute-start.1 = (bf16[16,4096]{1,0:T(8,128)(2,1)}, bf16[16,4096]{1,0:T(8,128)(2,1)S(1)}, u32[]{:S(2)}, u32[]{:S(2)}) collective-permute-start(bf16[16,4096]{1,0:T(8,128)(2,1)} %bitcast.85), channel_id=1, source_target_pairs={{0,256},{16,272},{32,288},{48,304},{64,320},{80,336},{96,352},{112... | collective-permute-start | bytes 393224 | tf_op jit(solution)/shard_map/gather_z/ppermute | solution.py:36
  13.2 8.5 %collective-permute-start = (bf16[16,4096]{1,0:T(8,128)(2,1)}, bf16[16,4096]{1,0:T(8,128)(2,1)S(1)}, u32[]{:S(2)}, u32[]{:S(2)}) collective-permute-start(bf16[16,4096]{1,0:T(8,128)(2,1)} %bitcast.86), channel_id=1, source_target_pairs={{0,128},{16,144},{32,160},{48,176},{64,192},{80,208},{96,224},{112... | collective-permute-start | bytes 393224 | tf_op jit(solution)/shard_map/gather_z/ppermute | solution.py:36
  15.4 9.8 %all-to-all-start.1 = ((bf16[4,8,4224]{2,1,0:T(8,128)(2,1)}), bf16[4,8,4224]{2,1,0:T(8,128)(2,1)S(1)}, u32[]{:S(2)}, u32[]{:S(2)}) async-start(bf16[4,8,4224]{2,1,0:T(8,128)(2,1)} %bitcast.82), calls=%async_computation.1 | async-start | bytes 540672 | tf_op jit(solution)/shard_map/hard_y/all_to_all | solution.py:67
  26.8 41.5 %copy-start.7 = (s32[1,256]{1,0:T(1,128)S(1)}, s32[1,256]{1,0:T(1,128)}, u32[]{:S(2)}) copy-start(s32[1,256]{1,0:T(1,128)} %param.7) | copy-start | bytes 3076
  26.8 41.7 %copy-start = (bf16[1,256,4096]{2,1,0:T(8,128)(2,1)S(1)}, bf16[1,256,4096]{2,1,0:T(8,128)(2,1)}, u32[]{:S(2)}) copy-start(bf16[1,256,4096]{2,1,0:T(8,128)(2,1)} %param.5) | copy-start | bytes 6291460
  26.8 32.3 %all-to-all-start = ((bf16[4,64,4096]{2,1,0:T(8,128)(2,1)}), bf16[4,64,4096]{2,1,0:T(8,128)(2,1)}, u32[]{:S(2)}, u32[]{:S(2)}) async-start(bf16[4,64,4096]{2,1,0:T(8,128)(2,1)} %broadcast_in_dim.23), calls=%async_computation | async-start | bytes 4194304 | tf_op jit(solution)/shard_map/gather_x/all_to_all | solution.py:67
  31.7 22.9 %collective-permute-start.3 = (bf16[8,4224]{1,0:T(8,128)(2,1)S(1)}, bf16[8,4224]{1,0:T(8,128)(2,1)S(1)}, u32[]{:S(2)}, u32[]{:S(2)}) collective-permute-start(bf16[8,4224]{1,0:T(8,128)(2,1)S(1)} %pad_maximum_fusion.1), channel_id=1, source_target_pairs={{0,1},{1,2},{2,3},{3,0},{4,5},{5,6},{6,7},{7,4},{8,9},{9,10},{10,1... | collective-permute-start | bytes 202760 | tf_op jit(solution)/shard_map/hard_h/ppermute | solution.py:36
  40.6 15.7 %collective-permute-start.4 = (bf16[8,4224]{1,0:T(8,128)(2,1)S(1)}, bf16[8,4224]{1,0:T(8,128)(2,1)S(1)}, u32[]{:S(2)}, u32[]{:S(2)}) collective-permute-start(bf16[8,4224]{1,0:T(8,128)(2,1)S(1)} %pad_maximum_fusion.2), channel_id=1, source_target_pairs={{0,2},{1,3},{2,0},{3,1},{4,6},{5,7},{6,4},{7,5},{8,10},{9,11},{10,... | collective-permute-start | bytes 202760 | tf_op jit(solution)/shard_map/hard_h/ppermute | solution.py:36
  49.3 9.6 %collective-permute-start.5 = (bf16[8,4224]{1,0:T(8,128)(2,1)S(1)}, bf16[8,4224]{1,0:T(8,128)(2,1)S(1)}, u32[]{:S(2)}, u32[]{:S(2)}) collective-permute-start(bf16[8,4224]{1,0:T(8,128)(2,1)S(1)} %pad_maximum_fusion.3), channel_id=1, source_target_pairs={{0,3},{1,0},{2,1},{3,2},{4,7},{5,4},{6,5},{7,6},{8,11},{9,8},{10,9... | collective-permute-start | bytes 202760 | tf_op jit(solution)/shard_map/hard_h/ppermute | solution.py:36
  59.1 13.3 %collective-permute-start.6 = (bf16[256,4096]{1,0:T(8,128)(2,1)}, bf16[256,4096]{1,0:T(8,128)(2,1)}, u32[]{:S(2)}, u32[]{:S(2)}) collective-permute-start(bf16[256,4096]{1,0:T(8,128)(2,1)} %bitcast.4.refs_6_), channel_id=1, source_target_pairs={{0,16},{16,0},{32,48},{48,32},{64,80},{80,64},{96,112},{112,96},{1... | collective-permute-start | bytes 6291464 | tf_op jit(solution)/shard_map/gather_core/ppermute | solution.py:201
  69.2 5.5 %copy-start.4 = (f32[32,256]{0,1:T(8,128)}, f32[32,256]{0,1:T(8,128)S(1)}, u32[]{:S(2)}) copy-start(f32[32,256]{0,1:T(8,128)S(1)} %get-tuple-element.72) | copy-start | bytes 98308
  79.0 6.3 %collective-permute-start.7 = (bf16[256,4096]{1,0:T(8,128)(2,1)}, bf16[256,4096]{1,0:T(8,128)(2,1)S(1)}, u32[]{:S(2)}, u32[]{:S(2)}) collective-permute-start(bf16[256,4096]{1,0:T(8,128)(2,1)} %convolution_convert_fusion), channel_id=1, source_target_pairs={{0,16},{16,0},{32,48},{48,32},{64,80},{80,64},{96,112},{112,96},{1... | collective-permute-start | bytes 6291464 | tf_op jit(solution)/shard_map/scatter_core/ppermute | solution.py:243
  85.3 15.6 %copy-start.5 = (f32[32,256]{0,1:T(8,128)S(1)}, f32[32,256]{0,1:T(8,128)}, u32[]{:S(2)}) copy-start(f32[32,256]{0,1:T(8,128)} %copy-done.4) | copy-start | bytes 98308
  89.5 23.1 %collective-permute-start.10 = (bf16[64,4096]{1,0:T(8,128)(2,1)}, bf16[64,4096]{1,0:T(8,128)(2,1)}, u32[]{:S(2)}, u32[]{:S(2)}) collective-permute-start(bf16[64,4096]{1,0:T(8,128)(2,1)} %get-tuple-element.34), channel_id=1, source_target_pairs={{0,32},{16,48},{32,64},{48,80},{64,96},{80,112},{96,0},{112,16},{1... | collective-permute-start | bytes 1572872 | tf_op jit(solution)/shard_map/scatter_x/ppermute | solution.py:36
  93.4 25.6 %collective-permute-start.9 = (bf16[64,4096]{1,0:T(8,128)(2,1)}, bf16[64,4096]{1,0:T(8,128)(2,1)}, u32[]{:S(2)}, u32[]{:S(2)}) collective-permute-start(bf16[64,4096]{1,0:T(8,128)(2,1)} %get-tuple-element.33), channel_id=1, source_target_pairs={{0,64},{16,80},{32,96},{48,112},{64,0},{80,16},{96,32},{112,48},{1... | collective-permute-start | bytes 1572872 | tf_op jit(solution)/shard_map/scatter_x/ppermute | solution.py:36
  97.8 22.7 %collective-permute-start.8 = (bf16[64,4096]{1,0:T(8,128)(2,1)}, bf16[64,4096]{1,0:T(8,128)(2,1)}, u32[]{:S(2)}, u32[]{:S(2)}) collective-permute-start(bf16[64,4096]{1,0:T(8,128)(2,1)} %get-tuple-element.32), channel_id=1, source_target_pairs={{0,96},{16,112},{32,0},{48,16},{64,32},{80,48},{96,64},{112,80},{1... | collective-permute-start | bytes 1572872 | tf_op jit(solution)/shard_map/scatter_x/ppermute | solution.py:36
  104.3 35.8 %all-to-all-start.2 = ((bf16[16,2,4096]{2,1,0:T(2,128)(2,1)}), bf16[16,2,4096]{2,1,0:T(2,128)(2,1)}, u32[]{:S(2)}, u32[]{:S(2)}) async-start(bf16[16,2,4096]{2,1,0:T(2,128)(2,1)} %reshape.325), calls=%async_computation.2 | async-start | bytes 524288 | tf_op jit(solution)/shard_map/hard_back/all_to_all | solution.py:258
  120.4 10.7 %copy-start.1 = (bf16[32,4096]{1,0:T(8,128)(2,1)S(1)}, bf16[32,4096]{1,0:T(8,128)(2,1)}, u32[]{:S(2)}) copy-start(bf16[32,4096]{1,0:T(8,128)(2,1)} %slice.106.refs_8_) | copy-start | bytes 786436
  120.4 10.7 %copy-start.2 = (bf16[256,256]{1,0:T(8,128)(2,1)S(1)}, bf16[256,256]{1,0:T(8,128)(2,1)}, u32[]{:S(2)}) copy-start(bf16[256,256]{1,0:T(8,128)(2,1)} %get-tuple-element.29.refs_4_) | copy-start | bytes 393220
  120.4 10.7 %copy-start.3 = (bf16[256,256]{1,0:T(8,128)(2,1)S(1)}, bf16[256,256]{1,0:T(8,128)(2,1)}, u32[]{:S(2)}) copy-start(bf16[256,256]{1,0:T(8,128)(2,1)} %get-tuple-element.28.refs_3_) | copy-start | bytes 393220
  122.1 17.3 %collective-permute-start.13 = (bf16[16,4096]{1,0:T(8,128)(2,1)S(1)}, bf16[16,4096]{1,0:T(8,128)(2,1)S(1)}, u32[]{:S(2)}, u32[]{:S(2)}) collective-permute-start(bf16[16,4096]{1,0:T(8,128)(2,1)S(1)} %get-tuple-element.51), channel_id=1, source_target_pairs={{0,128},{16,144},{32,160},{48,176},{64,192},{80,208},{96,224},{112... | collective-permute-start | bytes 393224 | tf_op jit(solution)/shard_map/scatter_z/ppermute | solution.py:36
  124.0 15.3 %collective-permute-start.12 = (bf16[16,4096]{1,0:T(8,128)(2,1)S(1)}, bf16[16,4096]{1,0:T(8,128)(2,1)S(1)}, u32[]{:S(2)}, u32[]{:S(2)}) collective-permute-start(bf16[16,4096]{1,0:T(8,128)(2,1)S(1)} %get-tuple-element.52), channel_id=1, source_target_pairs={{0,256},{16,272},{32,288},{48,304},{64,320},{80,336},{96,352},{112... | collective-permute-start | bytes 393224 | tf_op jit(solution)/shard_map/scatter_z/ppermute | solution.py:36
  126.6 14.6 %copy-start.6 = (bf16[16,32]{1,0:T(8,128)(2,1)S(1)}, bf16[16,32]{1,0:T(8,128)(2,1)}, u32[]{:S(2)}) copy-start(bf16[16,32]{1,0:T(8,128)(2,1)} %get-tuple-element.35) | copy-start | bytes 3076
  126.6 12.8 %collective-permute-start.11 = (bf16[16,4096]{1,0:T(8,128)(2,1)S(1)}, bf16[16,4096]{1,0:T(8,128)(2,1)S(1)}, u32[]{:S(2)}, u32[]{:S(2)}) collective-permute-start(bf16[16,4096]{1,0:T(8,128)(2,1)S(1)} %get-tuple-element.50), channel_id=1, source_target_pairs={{0,384},{16,400},{32,416},{48,432},{64,448},{80,464},{96,480},{112... | collective-permute-start | bytes 393224 | tf_op jit(solution)/shard_map/scatter_z/ppermute | solution.py:36

commit v4 on v2

v4 whole, which is shorter than its diff:
```python
import functools

import jax
import jax.numpy as jnp
from jax import lax
from jax.experimental import pallas as pl
from jax.experimental.pallas import tpu as pltpu
from jax.sharding import PartitionSpec as P

NZ, NX, NC = 4, 4, 2
CORE_SWAP = [(i, i ^ 1) for i in range(NZ * NX * NC)]
FLAG = 128
BF16, F32 = jnp.bfloat16, jnp.float32


def z_shift(d):
    step = NX * NC
    return [(i, (i // step + d) % NZ * step + i % step) for i in range(NZ * step)]


def x_shift(d):
    step = NX * NC
    return [(i, i // step * step + (i + d * NC) % step) for i in range(NZ * step)]


def exchange(parts, axis, perm, sign=1):
    return parts[:1] + [lax.ppermute(p, axis, perm(sign * d)) for d, p in enumerate(parts) if d]


def pieces(x, n):
    k = x.shape[0] // n
    return [x[i * k : (i + 1) * k] for i in range(n)]


def dot_t(a, b):
    return lax.dot_general(a, b, (((1,), (1,)), ((), ())), preferred_element_type=F32)


def t_dot(a, b):
    return lax.dot_general(a, b, (((0,), (0,)), ((), ())), preferred_element_type=F32)


def dot(a, b):
    return jnp.dot(a, b, preferred_element_type=F32)


def split(a):
    hi = a.astype(BF16)
    return hi, (a - hi.astype(F32)).astype(BF16)


def iota(dims, dim):
    return lax.broadcasted_iota(jnp.int32, dims, dim)


def shape(dims, dtype=BF16):
    return jax.ShapeDtypeStruct(dims, dtype)


def call(kernel, outs, args, name, flops, grant, scalars=1):
    size = sum(a.size * a.dtype.itemsize for a in (*args, *outs))
    return pl.pallas_call(
        kernel,
        in_specs=[pl.BlockSpec(memory_space=pltpu.SMEM)] * scalars
        + [pl.BlockSpec(memory_space=pltpu.VMEM)] * (len(args) - scalars),
        out_specs=[pl.BlockSpec(memory_space=pltpu.VMEM)] * len(outs),
        out_shape=outs,
        cost_estimate=pl.CostEstimate(flops=flops, bytes_accessed=size, transcendentals=0),
        compiler_params=pltpu.CompilerParams(vmem_limit_bytes=grant << 20),
        name=name,
    )(*args)


def over_columns(width, step, block=512):
    @pl.loop(0, width // block)
    def _(i):
        step(pl.ds(pl.multiple_of(i * block, block), block))


def joined(refs, cols=slice(None)):
    return jnp.concatenate([r[:, cols] for r in refs], axis=0)


def flip(x):
    n = x.shape[1]
    return dot_t((iota((n, n), 0) == iota((n, n), 1)).astype(BF16), x).astype(BF16)


def pack_kernel(groups, slots, dest_ref, rows_ref, packed_ref, placing_ref):
    dest = dest_ref[...]
    count, width = rows_ref.shape
    hot = (dest == iota((groups, count), 0)).astype(F32)
    ahead = (iota((count, count), 0) < iota((count, count), 1)).astype(F32)
    rank = jnp.sum(dot(hot, ahead) * hot, axis=0, keepdims=True).astype(jnp.int32)
    placing = (dest * slots + rank == iota((groups * slots, count), 0)).astype(BF16)
    packed_ref[:, :width] = dot(placing, rows_ref[...]).astype(BF16)
    packed_ref[:, width:] = dot(placing, jnp.ones((count, FLAG), BF16)).astype(BF16)
    placing_ref[...] = placing


def near_kernel(scale, q_ref, *refs):
    refs[-1][...] = scale * dot_t(q_ref[...], joined(refs[:-1]))


def coef_kernel(
    scale, q_ref, far0, far1, far2, far3, got_ref, s0_ref, column_ref,
    away_ref, mine_ref, hard_ref, hi0_ref, lo0_ref, hi1_ref, lo1_ref, hih_ref, loh_ref, loss_ref,
):
    count, width = q_ref.shape
    q, s0 = q_ref[...], s0_ref[...]
    half = s0.shape[1]
    s1 = scale * dot_t(q, joined((far0, far1, far2, far3)))
    flags = dot_t(jnp.ones((count, FLAG), BF16), got_ref[:, width:])
    sh = jnp.where(flags > 0.5 * FLAG, scale * dot_t(q, got_ref[:, :width]), -jnp.inf)
    top = jnp.maximum(
        jnp.max(jnp.maximum(s0, s1), axis=1, keepdims=True), jnp.max(sh, axis=1, keepdims=True)
    )
    total = jnp.sum(jnp.exp(s0 - top) + jnp.exp(s1 - top), axis=1, keepdims=True)
    total = total + jnp.sum(jnp.exp(sh - top), axis=1, keepdims=True)
    log_total = top + jnp.log(total)
    column = column_ref[...]
    hot0 = column == iota((count, half), 1)
    hot1 = column == iota((count, half), 1) + half
    at_target = jnp.sum(jnp.where(hot0, s0, 0.0) + jnp.where(hot1, s1, 0.0), axis=1, keepdims=True)
    loss_ref[...] = log_total - at_target
    hi1, lo1 = split(jnp.exp(s1 - log_total) - hot1.astype(F32))
    away = flip(hi1)

    def send(cols):
        away_ref[:, cols] = dot(away, q_ref[:, cols]).astype(BF16)

    over_columns(width, send)
    hi1_ref[...], lo1_ref[...] = hi1, lo1
    hi0, lo0 = split(jnp.exp(s0 - log_total) - hot0.astype(F32))
    hi0_ref[...], lo0_ref[...] = hi0, lo0
    mine_ref[...] = flip(hi0)
    hih, loh = split(jnp.exp(sh - log_total))
    hih_ref[...], loh_ref[...] = hih, loh
    hard_ref[...] = flip(hih)


def core_sum_kernel(coef_ref, q_ref, away_ref, own_ref, *sent_refs):
    n = own_ref.shape[0]

    def add(cols):
        total = dot(coef_ref[...], q_ref[:, cols]) + away_ref[:, cols].astype(F32)
        own_ref[:, cols] = total[:n]
        for d, ref in enumerate(sent_refs):
            ref[:, cols] = total[(d + 1) * n : (d + 2) * n].astype(BF16)

    over_columns(q_ref.shape[1], add)


def query_grad_kernel(scale, *refs):
    coefs, near, far, got, out = refs[:6], refs[6:10], refs[10:14], refs[14], refs[15]

    def grad(cols):
        rows = (joined(near, cols), joined(far, cols), got[:, cols])
        total = dot(coefs[0][...], rows[0])
        for i in range(1, 6):
            total = total + dot(coefs[i][...], rows[i % 3])
        out[0, :, cols] = (scale * total).astype(out.dtype)

    over_columns(out.shape[2], grad)


def body(queries, passages, positives, hard_rows, hard_dest):
    q = queries[0]
    own = passages[0]
    targets = positives[0]
    owned_hard = hard_rows[0]
    count, width = q.shape
    rows = own.shape[0]
    groups = lax.axis_size("group")
    slots = max(2, 2 * owned_hard.shape[0] // groups)
    half, places = NZ * NX * rows, groups * slots
    scale = width ** (-0.5)
    blk = lax.axis_index("blk")
    my_z, my_x, my_c = blk // (NX * NC), blk // NC % NX, blk % NC

    with jax.named_scope("gather_z"):
        z_rows = jnp.concatenate(exchange([own] * NZ, "blk", z_shift), axis=0)
    with jax.named_scope("hard_out"):
        packed, placing = call(
            functools.partial(pack_kernel, groups, slots),
            [shape((places, width + FLAG)), shape((places, owned_hard.shape[0]))],
            (hard_dest.reshape(1, -1), owned_hard),
            "pack", 2 * places * owned_hard.size, 2, 0,
        )
        received = lax.all_to_all(
            packed.reshape(groups, slots, -1), "group", split_axis=0, concat_axis=0, tiled=True
        ).reshape(places, -1)
    with jax.named_scope("gather_x"):
        near = exchange([z_rows] * NX, "blk", x_shift)
        near[-1], received = lax.optimization_barrier((near[-1], received))
    with jax.named_scope("gather_core"):
        far = [lax.ppermute(x, "blk", CORE_SWAP) for x in near]

    owner = targets // rows
    o_z, o_x, o_c = owner // (NX * NC), owner // NC % NX, owner % NC
    column = (
        (o_c != my_c).astype(jnp.int32) * half
        + ((my_x - o_x) % NX * NZ + (my_z - o_z) % NZ) * rows
        + targets % rows
    )
    with jax.named_scope("scores"):
        [s0] = call(
            functools.partial(near_kernel, scale),
            [shape((count, half), F32)],
            (q, *near),
            "near", 2 * count * half * width, 8, 0,
        )
        square, thin = shape((count, half)), shape((count, places))
        away, mine_rows, hard_cols, hi0, lo0, hi1, lo1, hih, loh, loss_rows = call(
            functools.partial(coef_kernel, scale),
            [
                shape((half, width)), shape((half, count)), shape((places, count)),
                square, square, square, square, thin, thin, shape((count, 1), F32),
            ],
            (q, *far, received, s0, column.reshape(-1, 1)),
            "coef", 4 * count * half * width, 12, 0,
        )
    with jax.named_scope("scatter_core"):
        away = lax.ppermute(away, "blk", CORE_SWAP)
    with jax.named_scope("scatter_x"):
        n = half // NX
        mine = call(
            core_sum_kernel,
            [shape((n, width), F32)] + [shape((n, width))] * (NX - 1),
            (mine_rows, q, away),
            "core_sum", 2 * count * half * width, 8, 0,
        )
        chunks = [c.astype(F32) for c in exchange(list(mine), "blk", x_shift, -1)]
        mine_x = pieces(functools.reduce(jnp.add, chunks), NZ)

    hard_cols, hi0, _ = lax.optimization_barrier((hard_cols, hi0, away))
    with jax.named_scope("hard_back"):
        g = (scale * dot(hard_cols, q)).astype(BF16)
        returned = lax.all_to_all(
            g.reshape(groups, slots, width), "group", split_axis=0, concat_axis=0, tiled=True
        ).reshape(places, width)
        d_owned = t_dot(placing, returned).astype(BF16)
    with jax.named_scope("d_query"):
        [d_query] = call(
            functools.partial(query_grad_kernel, scale),
            [shape((1, count, width))],
            (hi0, hi1, hih, lo0, lo1, loh, *near, *far, received),
            "query_grad", 4 * count * (2 * half + places) * width, 8, 0,
        )
    with jax.named_scope("scatter_z"):
        sent = [mine_x[0]] + [m.astype(BF16) for m in mine_x[1:]]
        chunks = [c.astype(F32) for c in exchange(sent, "blk", z_shift, -1)]
        d_passage = (scale * functools.reduce(jnp.add, chunks)).astype(BF16)
    return (loss_rows.reshape(1, -1), d_query, d_passage[None], d_owned[None])


def solution(mesh):
    return jax.shard_map(
        body,
        mesh=mesh,
        in_specs=(
            P("group", "blk", None),
            P("group", "blk", None),
            P("group", "blk"),
            P("group", "blk", None),
            P("group", "blk", None),
        ),
        out_specs=(
            P("group", "blk"),
            P("group", "blk", None),
            P("group", "blk", None),
            P("group", "blk", None),
        ),
        check_vma=False,
    )
```

time: 155 us -> 142 us (0.916)
  matrix products: 30.7 us -> 2.79 us
  Pallas kernels: 0 us -> 18.5 us
  waiting for transfers between devices: 32 us -> 19.2 us
  starting transfers between devices: 76.5 us -> 87.3 us
  other arithmetic: 6.44 us -> 4.77 us
    pallas_call x0 -> x5, Pallas kernels: none -> 18.5 us  [call(): pl.pallas_call(kernel, in_specs=[pl.BlockSpec(memory_space=pltpu.SMEM)] *...]
    dot_general x8 -> x1, matrix products: 20.3 us -> 1.92 us  [dot(): return jnp.dot(a, b, preferred_element_type=F32)]
    ppermute x14 -> x17, starting transfers between devices: 47.1 us -> 57.8 us  [the longest x12 40.3 us: exchange(): lax.ppermute(p, axis, perm(sign * d))]
    ppermute x14 -> x17, waiting for transfers between devices: 27.4 us -> 19.1 us  [the longest x12 15.4 us: exchange(): lax.ppermute(p, axis, perm(sign * d))]
    dot_general x3 -> x0, matrix products: 5.45 us -> none  [dot_t(): lax.dot_general(a, b, (((1,), (1,)), ((), ())), preferred_element_type=F32)]
    all_to_all x2 -> x1, waiting for transfers between devices: 4.61 us -> 0.01 us  [body(): lax.all_to_all(packed.reshape(groups, slots, -1), 'group', split_axis=0,...]
    dot_general x4 -> x1, matrix products: 4.95 us -> 0.87 us  [t_dot(): lax.dot_general(a, b, (((0,), (0,)), ((), ())), preferred_element_type=F32)]
    concatenate x1 -> x0, local copies, waits for them, and re-layouts: 1.88 us -> none  [body(): half0 = jnp.concatenate(parts, axis=0)]
  transfers between devices with their start and end apart: 17 -> 19, of which waited for: 7 -> 4; matrix products, arithmetic and copies ran while one was open for 19% -> 8% of each run, Pallas kernels for 0% -> 7%
where the time goes in v4:
time: 142 us; the launch traced here: 141 us
  starting transfers between devices  87.3 us (61%)
  waiting for transfers between devices  19.2 us (14%)
  Pallas kernels  18.5 us (13%)
  local copies, waits for them, and re-layouts  7.21 us (5%)
  other arithmetic  4.77 us (3%)
  matrix products  2.79 us (2%)
    ppermute x12, starting transfers between devices, exchange(): lax.ppermute(p, axis, perm(sign * d))  40.3 us
    pallas_call x5, Pallas kernels, call(): pl.pallas_call(kernel, in_specs=[pl.BlockSpec(memory_space=pltpu.SMEM)] *...  18.5 us
    all_to_all x1, starting transfers between devices, body(): lax.all_to_all(packed.reshape(groups, slots, -1), 'group', split_axis=0,...  15.6 us
    ppermute x12, waiting for transfers between devices, exchange(): lax.ppermute(p, axis, perm(sign * d))  15.4 us
    ppermute x4, starting transfers between devices, body(): far = [lax.ppermute(x, 'blk', CORE_SWAP) for x in near]  15.1 us
    all_to_all x1, starting transfers between devices, body(): lax.all_to_all(g.reshape(groups, slots, width), 'group', split_axis=0, co...  13.8 us
    ppermute x1, waiting for transfers between devices, body(): away = lax.ppermute(away, 'blk', CORE_SWAP)  3.76 us
  transfers between devices with their start and end apart: 19, of which 4 were waited for; matrix products, arithmetic and copies ran while one was open for 8% of the time, Pallas kernels for 7%

profile of v4, /device:TPU:1, one launch (start us, length us, event | category | flops | bytes accessed | tf_op | source)
XLA Modules:
  0.0 140.9 jit_solution(16836311229458279874)
XLA Ops:
  0.6 7.2 %collective-permute-start.2 = (bf16[16,4096]{1,0:T(8,128)(2,1)}, bf16[16,4096]{1,0:T(8,128)(2,1)S(1)}, u32[]{:S(2)}, u32[]{:S(2)}) collective-permute-start(bf16[16,4096]{1,0:T(8,128)(2,1)} %bitcast.20), channel_id=1, source_target_pairs={{0,384},{16,400},{32,416},{48,432},{64,448},{80,464},{96,480},{112... | collective-permute-start | bytes 393224 | tf_op jit(solution)/shard_map/gather_z/ppermute | solution.py:27
  7.9 1.9 %collective-permute-start.1 = (bf16[16,4096]{1,0:T(8,128)(2,1)}, bf16[16,4096]{1,0:T(8,128)(2,1)S(1)}, u32[]{:S(2)}, u32[]{:S(2)}) collective-permute-start(bf16[16,4096]{1,0:T(8,128)(2,1)} %bitcast.21), channel_id=1, source_target_pairs={{0,256},{16,272},{32,288},{48,304},{64,320},{80,336},{96,352},{112... | collective-permute-start | bytes 393224 | tf_op jit(solution)/shard_map/gather_z/ppermute | solution.py:27
  9.8 2.2 %collective-permute-start = (bf16[16,4096]{1,0:T(8,128)(2,1)}, bf16[16,4096]{1,0:T(8,128)(2,1)S(1)}, u32[]{:S(2)}, u32[]{:S(2)}) collective-permute-start(bf16[16,4096]{1,0:T(8,128)(2,1)} %bitcast.22), channel_id=1, source_target_pairs={{0,128},{16,144},{32,160},{48,176},{64,192},{80,208},{96,224},{112... | collective-permute-start | bytes 393224 | tf_op jit(solution)/shard_map/gather_z/ppermute | solution.py:27
  12.0 0.9 copy-done.2
  12.9 0.7 copy-done.4
  13.6 0.3 pack.1
  13.9 0.8 reshape.343
  14.7 15.6 %all-to-all-start = ((bf16[16,2,4224]{2,1,0:T(2,128)(2,1)}), bf16[16,2,4224]{2,1,0:T(2,128)(2,1)}, u32[]{:S(2)}, u32[]{:S(2)}) async-start(bf16[16,2,4224]{2,1,0:T(2,128)(2,1)} %reshape.343), calls=%async_computation | async-start | bytes 540672 | tf_op jit(solution)/shard_map/hard_out/all_to_all | solution.py:190
  30.3 0.0 collective-permute-done.2
  30.3 0.0 collective-permute-done.1
  30.3 0.0 collective-permute-done
  30.4 0.9 pad_maximum_fusion.refs_0_.refs_6_
  31.3 4.6 %collective-permute-start.6 = (bf16[64,4096]{1,0:T(8,128)(2,1)S(1)}, bf16[64,4096]{1,0:T(8,128)(2,1)S(1)}, u32[]{:S(2)}, u32[]{:S(2)}) collective-permute-start(bf16[64,4096]{1,0:T(8,128)(2,1)S(1)} %pad_maximum_fusion.refs_0_.refs_6_), channel_id=1, source_target_pairs={{0,64},{16,80},{32,96},{48,112},{64,0},{80,16},{96,32},{112,48},{1... | collective-permute-start | bytes 1572872 | tf_op jit(solution)/shard_map/gather_x/ppermute | solution.py:27
  36.0 2.2 %collective-permute-start.4 = (bf16[64,4096]{1,0:T(8,128)(2,1)S(1)}, bf16[64,4096]{1,0:T(8,128)(2,1)}, u32[]{:S(2)}, u32[]{:S(2)}) collective-permute-start(bf16[64,4096]{1,0:T(8,128)(2,1)S(1)} %pad_maximum_fusion.refs_0_.refs_6_), channel_id=1, source_target_pairs={{0,32},{16,48},{32,64},{48,80},{64,96},{80,112},{96,0},{112,16},{1... | collective-permute-start | bytes 1572872 | tf_op jit(solution)/shard_map/gather_x/ppermute | solution.py:27
  38.2 4.3 %collective-permute-start.8 = (bf16[64,4096]{1,0:T(8,128)(2,1)S(1)}, bf16[64,4096]{1,0:T(8,128)(2,1)}, u32[]{:S(2)}, u32[]{:S(2)}) collective-permute-start(bf16[64,4096]{1,0:T(8,128)(2,1)S(1)} %pad_maximum_fusion.refs_0_.refs_6_), channel_id=1, source_target_pairs={{0,96},{16,112},{32,0},{48,16},{64,32},{80,48},{96,64},{112,80},{1... | collective-permute-start | bytes 1572872 | tf_op jit(solution)/shard_map/gather_x/ppermute | solution.py:27
  42.5 4.5 %collective-permute-start.3 = (bf16[64,4096]{1,0:T(8,128)(2,1)S(1)}, bf16[64,4096]{1,0:T(8,128)(2,1)}, u32[]{:S(2)}, u32[]{:S(2)}) collective-permute-start(bf16[64,4096]{1,0:T(8,128)(2,1)S(1)} %pad_maximum_fusion.refs_0_.refs_6_), channel_id=1, source_target_pairs={{0,16},{16,0},{32,48},{48,32},{64,80},{80,64},{96,112},{112,96},{1... | collective-permute-start | bytes 1572872 | tf_op jit(solution)/shard_map/gather_core/ppermute | solution.py:197
  47.0 0.0 collective-permute-done.6.refs_2_.refs_8_
  47.0 6.3 %collective-permute-start.7 = (bf16[64,4096]{1,0:T(8,128)(2,1)S(1)}, bf16[64,4096]{1,0:T(8,128)(2,1)}, u32[]{:S(2)}, u32[]{:S(2)}) collective-permute-start(bf16[64,4096]{1,0:T(8,128)(2,1)S(1)} %collective-permute-done.6.refs_2_.refs_8_), channel_id=1, source_target_pairs={{0,16},{16,0},{32,48},{48,32},{64,80},{80,64},{96,112},{112,96},{1... | collective-permute-start | bytes 1572872 | tf_op jit(solution)/shard_map/gather_core/ppermute | solution.py:197
  53.3 6.6 %collective-permute-done.4.refs_1_.refs_7_ = bf16[64,4096]{1,0:T(8,128)(2,1)} collective-permute-done((bf16[64,4096]{1,0:T(8,128)(2,1)S(1)}, bf16[64,4096]{1,0:T(8,128)(2,1)}, u32[]{:S(2)}, u32[]{:S(2)}) %collective-permute-start.4) | collective-permute-done | bytes 524320 | tf_op jit(solution)/shard_map/gather_x/ppermute | solution.py:27
  59.9 2.4 %collective-permute-start.5 = (bf16[64,4096]{1,0:T(8,128)(2,1)}, bf16[64,4096]{1,0:T(8,128)(2,1)}, u32[]{:S(2)}, u32[]{:S(2)}) collective-permute-start(bf16[64,4096]{1,0:T(8,128)(2,1)} %collective-permute-done.4.refs_1_.refs_7_), channel_id=1, source_target_pairs={{0,16},{16,0},{32,48},{48,32},{64,80},{80,64},{96,112},{112,96},{1... | collective-permute-start | bytes 1572872 | tf_op jit(solution)/shard_map/gather_core/ppermute | solution.py:197
  62.3 0.0 all-to-all-done
  62.3 1.1 reshape.344.got_ref.refs_14_
  63.4 0.0 collective-permute-done.8.refs_3_.refs_9_
  63.4 1.9 %collective-permute-start.9 = (bf16[64,4096]{1,0:T(8,128)(2,1)}, bf16[64,4096]{1,0:T(8,128)(2,1)}, u32[]{:S(2)}, u32[]{:S(2)}) collective-permute-start(bf16[64,4096]{1,0:T(8,128)(2,1)} %collective-permute-done.8.refs_3_.refs_9_), channel_id=1, source_target_pairs={{0,16},{16,0},{32,48},{48,32},{64,80},{80,64},{96,112},{112,96},{1... | collective-permute-start | bytes 1572872 | tf_op jit(solution)/shard_map/gather_core/ppermute | solution.py:197
  65.3 0.8 copy.9
  66.2 0.5 fusion.14.column_ref
  66.7 1.9 %near.1.s0_ref = f32[256,256]{1,0:T(8,128)S(1)} custom-call(bf16[256,4096]{1,0:T(8,128)(2,1)S(1)} %bitcast.15, bf16[64,4096]{1,0:T(8,128)(2,1)S(1)} %pad_maximum_fusion.refs_0_.refs_6_, bf16[64,4096]{1,0:T(8,128)(2,1)} %collective-permute-done.4.refs_1_.refs_7_, bf16[64,4096]{1,0:T(8,128)(2,1)S(1)} %collective-permute-done.6.refs_2_.refs_8_, ...), custom_call_target="tpu_custom_call" | custom-call | flops 536870912 | bytes 4456448 | tf_op jit(solution)/shard_map/scores/near/pallas_call | solution.py:62
  68.6 0.0 collective-permute-done.3.far0.refs_10_
  68.6 0.0 collective-permute-done.7.far2.refs_12_
  68.6 0.0 collective-permute-done.5.far1.refs_11_
  68.6 0.0 collective-permute-done.9.far3.refs_13_
  68.6 5.5 %coef.1 = (bf16[256,4096]{1,0:T(8,128)(2,1)S(1)}, bf16[256,256]{1,0:T(8,128)(2,1)S(1)}, bf16[32,256]{1,0:T(8,128)(2,1)S(1)}, bf16[256,256]{1,0:T(8,128)(2,1)S(1)...) custom-call(bf16[256,4096]{1,0:T(8,128)(2,1)S(1)} %bitcast.16, ...), custom_call_target="tpu_custom_call" | custom-call | flops 1073741824 | bytes 7530496 | tf_op jit(solution)/shard_map/scores/coef/pallas_call | solution.py:62
  74.1 0.0 copy-start.5
  74.1 0.0 copy-start.9
  74.1 0.0 copy-start.11
  74.2 0.0 copy-start.13
  74.2 0.0 copy-start.15
  74.2 2.4 %collective-permute-start.10 = (bf16[256,4096]{1,0:T(8,128)(2,1)S(1)}, bf16[256,4096]{1,0:T(8,128)(2,1)S(1)}, u32[]{:S(2)}, u32[]{:S(2)}) collective-permute-start(bf16[256,4096]{1,0:T(8,128)(2,1)S(1)} %get-tuple-element.30), channel_id=1, source_target_pairs={{0,16},{16,0},{32,48},{48,32},{64,80},{80,64},{96,112},{112,96},{1... | collective-permute-start | bytes 6291464 | tf_op jit(solution)/shard_map/scatter_core/ppermute | solution.py:224
  76.6 3.8 %collective-permute-done.10.away_ref = bf16[256,4096]{1,0:T(8,128)(2,1)S(1)} collective-permute-done((bf16[256,4096]{1,0:T(8,128)(2,1)S(1)}, bf16[256,4096]{1,0:T(8,128)(2,1)S(1)}, u32[]{:S(2)}, u32[]{:S(2)}) %collective-permute-start.10) | collective-permute-done | bytes 2097184 | tf_op jit(solution)/shard_map/scatter_core/ppermute | solution.py:224
  80.3 3.0 %core_sum.1 = (f32[64,4096]{1,0:T(8,128)S(1)}, bf16[64,4096]{1,0:T(8,128)(2,1)}, bf16[64,4096]{1,0:T(8,128)(2,1)}, bf16[64,4096]{1,0:T(8,128)(2,1)}) custom-call(bf16[256,256]{1,0:T(8,128)(2,1)S(1)} %get-tuple-element.37.coef_ref, bf16[256,4096]{1,0:T(8,128)(2,1)S(1)} %bitcast.17, bf16[256,4096]{1,0:T(8,128)(2,1)S(1)} %collective-permute-done.10.away_ref), custom_call_target="tpu_custom_call" | custom-call | flops 536870912 | bytes 6946816 | tf_op jit(solution)/shard_map/scatter_x/core_sum/pallas_call | solution.py:62
  83.4 0.0 copy-start.1
  83.4 1.0 copy-done.1
  84.3 2.2 %collective-permute-start.11 = (bf16[64,4096]{1,0:T(8,128)(2,1)}, bf16[64,4096]{1,0:T(8,128)(2,1)}, u32[]{:S(2)}, u32[]{:S(2)}) collective-permute-start(bf16[64,4096]{1,0:T(8,128)(2,1)} %get-tuple-element.39), channel_id=1, source_target_pairs={{0,96},{16,112},{32,0},{48,16},{64,32},{80,48},{96,64},{112,80},{1... | collective-permute-start | bytes 1572872 | tf_op jit(solution)/shard_map/scatter_x/ppermute | solution.py:27
  86.6 4.6 %collective-permute-start.12 = (bf16[64,4096]{1,0:T(8,128)(2,1)}, bf16[64,4096]{1,0:T(8,128)(2,1)}, u32[]{:S(2)}, u32[]{:S(2)}) collective-permute-start(bf16[64,4096]{1,0:T(8,128)(2,1)} %get-tuple-element.40), channel_id=1, source_target_pairs={{0,64},{16,80},{32,96},{48,112},{64,0},{80,16},{96,32},{112,48},{1... | collective-permute-start | bytes 1572872 | tf_op jit(solution)/shard_map/scatter_x/ppermute | solution.py:27
  91.2 2.4 %collective-permute-start.13 = (bf16[64,4096]{1,0:T(8,128)(2,1)}, bf16[64,4096]{1,0:T(8,128)(2,1)}, u32[]{:S(2)}, u32[]{:S(2)}) collective-permute-start(bf16[64,4096]{1,0:T(8,128)(2,1)} %get-tuple-element.41), channel_id=1, source_target_pairs={{0,32},{16,48},{32,64},{48,80},{64,96},{80,112},{96,0},{112,16},{1... | collective-permute-start | bytes 1572872 | tf_op jit(solution)/shard_map/scatter_x/ppermute | solution.py:27
  93.7 0.7 reduce
  94.3 1.9 %fusion = bf16[32,4096]{1,0:T(8,128)(2,1)} fusion(bf16[32,256]{1,0:T(8,128)(2,1)} %copy-done.3, bf16[1,256,4096]{2,1,0:T(8,128)(2,1)S(1)} %copy-done), kind=kOutput, calls=%fused_computation.1 | convolution fusion | flops 67371008 | bytes 2375680 | tf_op jit(solution)/shard_map/hard_back/dot_general | solution.py:44
  96.3 1.8 %reshape.346 = bf16[16,2,4096]{2,1,0:T(2,128)(2,1)} reshape(bf16[32,4096]{1,0:T(8,128)(2,1)} %fusion) | data formatting | bytes 524288 | tf_op jit(solution)/shard_map/hard_back/reshape | solution.py:240
  98.1 13.8 %all-to-all-start.1 = ((bf16[16,2,4096]{2,1,0:T(2,128)(2,1)}), bf16[16,2,4096]{2,1,0:T(2,128)(2,1)S(1)}, u32[]{:S(2)}, u32[]{:S(2)}) async-start(bf16[16,2,4096]{2,1,0:T(2,128)(2,1)} %reshape.346), calls=%async_computation.1 | async-start | bytes 524288 | tf_op jit(solution)/shard_map/hard_back/all_to_all | solution.py:239
  111.9 0.0 collective-permute-done.11
  111.9 0.0 collective-permute-done.12
  112.0 3.4 %collective-permute-done.13 = bf16[64,4096]{1,0:T(8,128)(2,1)} collective-permute-done((bf16[64,4096]{1,0:T(8,128)(2,1)}, bf16[64,4096]{1,0:T(8,128)(2,1)}, u32[]{:S(2)}, u32[]{:S(2)}) %collective-permute-start.13) | collective-permute-done | bytes 524320 | tf_op jit(solution)/shard_map/scatter_x/ppermute | solution.py:27
  115.4 2.0 %fusion.23 = (bf16[64,4096]{1,0:T(8,128)(2,1)S(1)}, f32[64,4096]{1,0:T(8,128)S(1)}) fusion(bf16[64,4096]{1,0:T(8,128)(2,1)} %collective-permute-done.13, bf16[64,4096]{1,0:T(8,128)(2,1)} %collective-permute-done.12, f32[64,4096]{1,0:T(8,128)} %copy-done.1, bf16[64,4096]{1,0:T(8,128)(2,1)} %collective-permute-done.11), kind=kLoop, calls=%fused_computation.52 | loop fusion | flops 1835008 | bytes 4194304 | tf_op jit(solution)/shard_map/convert.2
  117.4 4.4 %collective-permute-start.14 = (bf16[16,4096]{1,0:T(8,128)(2,1)S(1)}, bf16[16,4096]{1,0:T(8,128)(2,1)S(1)}, u32[]{:S(2)}, u32[]{:S(2)}) collective-permute-start(bf16[16,4096]{1,0:T(8,128)(2,1)S(1)} %get-tuple-element.46), channel_id=1, source_target_pairs={{0,384},{16,400},{32,416},{48,432},{64,448},{80,464},{96,480},{112... | collective-permute-start | bytes 393224 | tf_op jit(solution)/shard_map/scatter_z/ppermute | solution.py:27
  121.9 1.9 %collective-permute-start.16 = (bf16[16,4096]{1,0:T(8,128)(2,1)S(1)}, bf16[16,4096]{1,0:T(8,128)(2,1)S(1)}, u32[]{:S(2)}, u32[]{:S(2)}) collective-permute-start(bf16[16,4096]{1,0:T(8,128)(2,1)S(1)} %get-tuple-element.47), channel_id=1, source_target_pairs={{0,128},{16,144},{32,160},{48,176},{64,192},{80,208},{96,224},{112... | collective-permute-start | bytes 393224 | tf_op jit(solution)/shard_map/scatter_z/ppermute | solution.py:27
  123.8 2.2 %collective-permute-start.15 = (bf16[16,4096]{1,0:T(8,128)(2,1)S(1)}, bf16[16,4096]{1,0:T(8,128)(2,1)S(1)}, u32[]{:S(2)}, u32[]{:S(2)}) collective-permute-start(bf16[16,4096]{1,0:T(8,128)(2,1)S(1)} %get-tuple-element.48), channel_id=1, source_target_pairs={{0,256},{16,272},{32,288},{48,304},{64,320},{80,336},{96,352},{112... | collective-permute-start | bytes 393224 | tf_op jit(solution)/shard_map/scatter_z/ppermute | solution.py:27
  126.1 7.8 %query_grad.1 = bf16[1,256,4096]{2,1,0:T(8,128)(2,1)} custom-call(bf16[256,256]{1,0:T(8,128)(2,1)S(1)} %copy-done.6, bf16[256,256]{1,0:T(8,128)(2,1)S(1)} %copy-done.10, bf16[256,32]{1,0:T(8,128)(2,1)S(1)} %copy-done.14, bf16[256,256]{1,0:T(8,128)(2,1)S(1)} %copy-done.8, bf16[256,256]{1,0:T(8,128)(2,1)S(1)} %copy-done.12, bf16[256,32]{1,0:T(8,128)(2,1)S(1)} %copy-done.16, ...), custom_call_target="tpu_custom_call" | custom-call | flops 2281701376 | bytes 7118848 | tf_op jit(solution)/shard_map/d_query/query_grad/pallas_call | solution.py:62
  133.8 0.0 collective-permute-done.14
  133.9 0.0 collective-permute-done.16
  133.9 5.3 %collective-permute-done.15 = bf16[16,4096]{1,0:T(8,128)(2,1)S(1)} collective-permute-done((bf16[16,4096]{1,0:T(8,128)(2,1)S(1)}, bf16[16,4096]{1,0:T(8,128)(2,1)S(1)}, u32[]{:S(2)}, u32[]{:S(2)}) %collective-permute-start.15) | collective-permute-done | bytes 131104 | tf_op jit(solution)/shard_map/scatter_z/ppermute | solution.py:27
  139.2 0.7 fusion.18
  139.9 0.0 all-to-all-done.1
  139.9 0.1 reshape.347
  140.0 0.9 fusion.1
  (26 shorter events, 0.1 us)
Async XLA Ops:
  0.6 66.0 %copy-start = (bf16[1,256,4096]{2,1,0:T(8,128)(2,1)S(1)}, bf16[1,256,4096]{2,1,0:T(8,128)(2,1)}, u32[]{:S(2)}) copy-start(bf16[1,256,4096]{2,1,0:T(8,128)(2,1)} %param.5) | copy-start | bytes 6291460
  0.6 29.7 %collective-permute-start.2 = (bf16[16,4096]{1,0:T(8,128)(2,1)}, bf16[16,4096]{1,0:T(8,128)(2,1)S(1)}, u32[]{:S(2)}, u32[]{:S(2)}) collective-permute-start(bf16[16,4096]{1,0:T(8,128)(2,1)} %bitcast.20), channel_id=1, source_target_pairs={{0,384},{16,400},{32,416},{48,432},{64,448},{80,464},{96,480},{112... | collective-permute-start | bytes 393224 | tf_op jit(solution)/shard_map/gather_z/ppermute | solution.py:27
  7.9 22.5 %collective-permute-start.1 = (bf16[16,4096]{1,0:T(8,128)(2,1)}, bf16[16,4096]{1,0:T(8,128)(2,1)S(1)}, u32[]{:S(2)}, u32[]{:S(2)}) collective-permute-start(bf16[16,4096]{1,0:T(8,128)(2,1)} %bitcast.21), channel_id=1, source_target_pairs={{0,256},{16,272},{32,288},{48,304},{64,320},{80,336},{96,352},{112... | collective-permute-start | bytes 393224 | tf_op jit(solution)/shard_map/gather_z/ppermute | solution.py:27
  9.8 20.6 %collective-permute-start = (bf16[16,4096]{1,0:T(8,128)(2,1)}, bf16[16,4096]{1,0:T(8,128)(2,1)S(1)}, u32[]{:S(2)}, u32[]{:S(2)}) collective-permute-start(bf16[16,4096]{1,0:T(8,128)(2,1)} %bitcast.22), channel_id=1, source_target_pairs={{0,128},{16,144},{32,160},{48,176},{64,192},{80,208},{96,224},{112... | collective-permute-start | bytes 393224 | tf_op jit(solution)/shard_map/gather_z/ppermute | solution.py:27
  12.0 0.9 copy-start.2
  12.9 0.7 copy-start.4
  14.7 47.6 %all-to-all-start = ((bf16[16,2,4224]{2,1,0:T(2,128)(2,1)}), bf16[16,2,4224]{2,1,0:T(2,128)(2,1)}, u32[]{:S(2)}, u32[]{:S(2)}) async-start(bf16[16,2,4224]{2,1,0:T(2,128)(2,1)} %reshape.343), calls=%async_computation | async-start | bytes 540672 | tf_op jit(solution)/shard_map/hard_out/all_to_all | solution.py:190
  31.3 15.7 %collective-permute-start.6 = (bf16[64,4096]{1,0:T(8,128)(2,1)S(1)}, bf16[64,4096]{1,0:T(8,128)(2,1)S(1)}, u32[]{:S(2)}, u32[]{:S(2)}) collective-permute-start(bf16[64,4096]{1,0:T(8,128)(2,1)S(1)} %pad_maximum_fusion.refs_0_.refs_6_), channel_id=1, source_target_pairs={{0,64},{16,80},{32,96},{48,112},{64,0},{80,16},{96,32},{112,48},{1... | collective-permute-start | bytes 1572872 | tf_op jit(solution)/shard_map/gather_x/ppermute | solution.py:27
  36.0 23.9 %collective-permute-start.4 = (bf16[64,4096]{1,0:T(8,128)(2,1)S(1)}, bf16[64,4096]{1,0:T(8,128)(2,1)}, u32[]{:S(2)}, u32[]{:S(2)}) collective-permute-start(bf16[64,4096]{1,0:T(8,128)(2,1)S(1)} %pad_maximum_fusion.refs_0_.refs_6_), channel_id=1, source_target_pairs={{0,32},{16,48},{32,64},{48,80},{64,96},{80,112},{96,0},{112,16},{1... | collective-permute-start | bytes 1572872 | tf_op jit(solution)/shard_map/gather_x/ppermute | solution.py:27
  38.2 25.2 %collective-permute-start.8 = (bf16[64,4096]{1,0:T(8,128)(2,1)S(1)}, bf16[64,4096]{1,0:T(8,128)(2,1)}, u32[]{:S(2)}, u32[]{:S(2)}) collective-permute-start(bf16[64,4096]{1,0:T(8,128)(2,1)S(1)} %pad_maximum_fusion.refs_0_.refs_6_), channel_id=1, source_target_pairs={{0,96},{16,112},{32,0},{48,16},{64,32},{80,48},{96,64},{112,80},{1... | collective-permute-start | bytes 1572872 | tf_op jit(solution)/shard_map/gather_x/ppermute | solution.py:27
  42.5 26.1 %collective-permute-start.3 = (bf16[64,4096]{1,0:T(8,128)(2,1)S(1)}, bf16[64,4096]{1,0:T(8,128)(2,1)}, u32[]{:S(2)}, u32[]{:S(2)}) collective-permute-start(bf16[64,4096]{1,0:T(8,128)(2,1)S(1)} %pad_maximum_fusion.refs_0_.refs_6_), channel_id=1, source_target_pairs={{0,16},{16,0},{32,48},{48,32},{64,80},{80,64},{96,112},{112,96},{1... | collective-permute-start | bytes 1572872 | tf_op jit(solution)/shard_map/gather_core/ppermute | solution.py:197
  47.0 21.6 %collective-permute-start.7 = (bf16[64,4096]{1,0:T(8,128)(2,1)S(1)}, bf16[64,4096]{1,0:T(8,128)(2,1)}, u32[]{:S(2)}, u32[]{:S(2)}) collective-permute-start(bf16[64,4096]{1,0:T(8,128)(2,1)S(1)} %collective-permute-done.6.refs_2_.refs_8_), channel_id=1, source_target_pairs={{0,16},{16,0},{32,48},{48,32},{64,80},{80,64},{96,112},{112,96},{1... | collective-permute-start | bytes 1572872 | tf_op jit(solution)/shard_map/gather_core/ppermute | solution.py:197
  59.9 8.7 %collective-permute-start.5 = (bf16[64,4096]{1,0:T(8,128)(2,1)}, bf16[64,4096]{1,0:T(8,128)(2,1)}, u32[]{:S(2)}, u32[]{:S(2)}) collective-permute-start(bf16[64,4096]{1,0:T(8,128)(2,1)} %collective-permute-done.4.refs_1_.refs_7_), channel_id=1, source_target_pairs={{0,16},{16,0},{32,48},{48,32},{64,80},{80,64},{96,112},{112,96},{1... | collective-permute-start | bytes 1572872 | tf_op jit(solution)/shard_map/gather_core/ppermute | solution.py:197
  63.4 5.3 %collective-permute-start.9 = (bf16[64,4096]{1,0:T(8,128)(2,1)}, bf16[64,4096]{1,0:T(8,128)(2,1)}, u32[]{:S(2)}, u32[]{:S(2)}) collective-permute-start(bf16[64,4096]{1,0:T(8,128)(2,1)} %collective-permute-done.8.refs_3_.refs_9_), channel_id=1, source_target_pairs={{0,16},{16,0},{32,48},{48,32},{64,80},{80,64},{96,112},{112,96},{1... | collective-permute-start | bytes 1572872 | tf_op jit(solution)/shard_map/gather_core/ppermute | solution.py:197
  74.1 9.2 %copy-start.3 = (bf16[32,256]{1,0:T(8,128)(2,1)}, bf16[32,256]{1,0:T(8,128)(2,1)S(1)}, u32[]{:S(2)}) copy-start(bf16[32,256]{1,0:T(8,128)(2,1)S(1)} %get-tuple-element.43) | copy-start | bytes 49156
  74.1 9.2 %copy-start.5 = (bf16[256,256]{1,0:T(8,128)(2,1)}, bf16[256,256]{1,0:T(8,128)(2,1)S(1)}, u32[]{:S(2)}) copy-start(bf16[256,256]{1,0:T(8,128)(2,1)S(1)} %get-tuple-element.31.refs_0_) | copy-start | bytes 393220
  74.1 9.2 %copy-start.7 = (bf16[256,256]{1,0:T(8,128)(2,1)}, bf16[256,256]{1,0:T(8,128)(2,1)S(1)}, u32[]{:S(2)}) copy-start(bf16[256,256]{1,0:T(8,128)(2,1)S(1)} %get-tuple-element.34.refs_3_) | copy-start | bytes 393220
  74.1 9.2 %copy-start.9 = (bf16[256,256]{1,0:T(8,128)(2,1)}, bf16[256,256]{1,0:T(8,128)(2,1)S(1)}, u32[]{:S(2)}) copy-start(bf16[256,256]{1,0:T(8,128)(2,1)S(1)} %get-tuple-element.32.refs_1_) | copy-start | bytes 393220
  74.1 9.2 %copy-start.11 = (bf16[256,256]{1,0:T(8,128)(2,1)}, bf16[256,256]{1,0:T(8,128)(2,1)S(1)}, u32[]{:S(2)}) copy-start(bf16[256,256]{1,0:T(8,128)(2,1)S(1)} %get-tuple-element.35.refs_4_) | copy-start | bytes 393220
  74.2 9.2 %copy-start.13 = (bf16[256,32]{1,0:T(8,128)(2,1)}, bf16[256,32]{1,0:T(8,128)(2,1)S(1)}, u32[]{:S(2)}) copy-start(bf16[256,32]{1,0:T(8,128)(2,1)S(1)} %get-tuple-element.33.refs_2_) | copy-start | bytes 49156
  74.2 9.2 %copy-start.15 = (bf16[256,32]{1,0:T(8,128)(2,1)}, bf16[256,32]{1,0:T(8,128)(2,1)S(1)}, u32[]{:S(2)}) copy-start(bf16[256,32]{1,0:T(8,128)(2,1)S(1)} %get-tuple-element.36.refs_5_) | copy-start | bytes 49156
  74.2 6.2 %collective-permute-start.10 = (bf16[256,4096]{1,0:T(8,128)(2,1)S(1)}, bf16[256,4096]{1,0:T(8,128)(2,1)S(1)}, u32[]{:S(2)}, u32[]{:S(2)}) collective-permute-start(bf16[256,4096]{1,0:T(8,128)(2,1)S(1)} %get-tuple-element.30), channel_id=1, source_target_pairs={{0,16},{16,0},{32,48},{48,32},{64,80},{80,64},{96,112},{112,96},{1... | collective-permute-start | bytes 6291464 | tf_op jit(solution)/shard_map/scatter_core/ppermute | solution.py:224
  83.4 1.0 copy-start.1
  84.3 27.6 %collective-permute-start.11 = (bf16[64,4096]{1,0:T(8,128)(2,1)}, bf16[64,4096]{1,0:T(8,128)(2,1)}, u32[]{:S(2)}, u32[]{:S(2)}) collective-permute-start(bf16[64,4096]{1,0:T(8,128)(2,1)} %get-tuple-element.39), channel_id=1, source_target_pairs={{0,96},{16,112},{32,0},{48,16},{64,32},{80,48},{96,64},{112,80},{1... | collective-permute-start | bytes 1572872 | tf_op jit(solution)/shard_map/scatter_x/ppermute | solution.py:27
  86.6 25.4 %collective-permute-start.12 = (bf16[64,4096]{1,0:T(8,128)(2,1)}, bf16[64,4096]{1,0:T(8,128)(2,1)}, u32[]{:S(2)}, u32[]{:S(2)}) collective-permute-start(bf16[64,4096]{1,0:T(8,128)(2,1)} %get-tuple-element.40), channel_id=1, source_target_pairs={{0,64},{16,80},{32,96},{48,112},{64,0},{80,16},{96,32},{112,48},{1... | collective-permute-start | bytes 1572872 | tf_op jit(solution)/shard_map/scatter_x/ppermute | solution.py:27
  91.2 24.1 %collective-permute-start.13 = (bf16[64,4096]{1,0:T(8,128)(2,1)}, bf16[64,4096]{1,0:T(8,128)(2,1)}, u32[]{:S(2)}, u32[]{:S(2)}) collective-permute-start(bf16[64,4096]{1,0:T(8,128)(2,1)} %get-tuple-element.41), channel_id=1, source_target_pairs={{0,32},{16,48},{32,64},{48,80},{64,96},{80,112},{96,0},{112,16},{1... | collective-permute-start | bytes 1572872 | tf_op jit(solution)/shard_map/scatter_x/ppermute | solution.py:27
  98.1 41.8 %all-to-all-start.1 = ((bf16[16,2,4096]{2,1,0:T(2,128)(2,1)}), bf16[16,2,4096]{2,1,0:T(2,128)(2,1)S(1)}, u32[]{:S(2)}, u32[]{:S(2)}) async-start(bf16[16,2,4096]{2,1,0:T(2,128)(2,1)} %reshape.346), calls=%async_computation.1 | async-start | bytes 524288 | tf_op jit(solution)/shard_map/hard_back/all_to_all | solution.py:239
  115.4 10.6 %copy-start.6 = (bf16[256,256]{1,0:T(8,128)(2,1)S(1)}, bf16[256,256]{1,0:T(8,128)(2,1)}, u32[]{:S(2)}) copy-start(bf16[256,256]{1,0:T(8,128)(2,1)} %copy-done.5) | copy-start | bytes 393220
  115.4 10.6 %copy-start.8 = (bf16[256,256]{1,0:T(8,128)(2,1)S(1)}, bf16[256,256]{1,0:T(8,128)(2,1)}, u32[]{:S(2)}) copy-start(bf16[256,256]{1,0:T(8,128)(2,1)} %copy-done.7) | copy-start | bytes 393220
  115.4 10.6 %copy-start.10 = (bf16[256,256]{1,0:T(8,128)(2,1)S(1)}, bf16[256,256]{1,0:T(8,128)(2,1)}, u32[]{:S(2)}) copy-start(bf16[256,256]{1,0:T(8,128)(2,1)} %copy-done.9) | copy-start | bytes 393220
  115.4 10.6 %copy-start.12 = (bf16[256,256]{1,0:T(8,128)(2,1)S(1)}, bf16[256,256]{1,0:T(8,128)(2,1)}, u32[]{:S(2)}) copy-start(bf16[256,256]{1,0:T(8,128)(2,1)} %copy-done.11) | copy-start | bytes 393220
  115.4 10.6 %copy-start.14 = (bf16[256,32]{1,0:T(8,128)(2,1)S(1)}, bf16[256,32]{1,0:T(8,128)(2,1)}, u32[]{:S(2)}) copy-start(bf16[256,32]{1,0:T(8,128)(2,1)} %copy-done.13) | copy-start | bytes 49156
  115.4 10.6 %copy-start.16 = (bf16[256,32]{1,0:T(8,128)(2,1)S(1)}, bf16[256,32]{1,0:T(8,128)(2,1)}, u32[]{:S(2)}) copy-start(bf16[256,32]{1,0:T(8,128)(2,1)} %copy-done.15) | copy-start | bytes 49156
  117.4 16.4 %collective-permute-start.14 = (bf16[16,4096]{1,0:T(8,128)(2,1)S(1)}, bf16[16,4096]{1,0:T(8,128)(2,1)S(1)}, u32[]{:S(2)}, u32[]{:S(2)}) collective-permute-start(bf16[16,4096]{1,0:T(8,128)(2,1)S(1)} %get-tuple-element.46), channel_id=1, source_target_pairs={{0,384},{16,400},{32,416},{48,432},{64,448},{80,464},{96,480},{112... | collective-permute-start | bytes 393224 | tf_op jit(solution)/shard_map/scatter_z/ppermute | solution.py:27
  121.9 12.0 %collective-permute-start.16 = (bf16[16,4096]{1,0:T(8,128)(2,1)S(1)}, bf16[16,4096]{1,0:T(8,128)(2,1)S(1)}, u32[]{:S(2)}, u32[]{:S(2)}) collective-permute-start(bf16[16,4096]{1,0:T(8,128)(2,1)S(1)} %get-tuple-element.47), channel_id=1, source_target_pairs={{0,128},{16,144},{32,160},{48,176},{64,192},{80,208},{96,224},{112... | collective-permute-start | bytes 393224 | tf_op jit(solution)/shard_map/scatter_z/ppermute | solution.py:27
  123.8 15.4 %collective-permute-start.15 = (bf16[16,4096]{1,0:T(8,128)(2,1)S(1)}, bf16[16,4096]{1,0:T(8,128)(2,1)S(1)}, u32[]{:S(2)}, u32[]{:S(2)}) collective-permute-start(bf16[16,4096]{1,0:T(8,128)(2,1)S(1)} %get-tuple-element.48), channel_id=1, source_target_pairs={{0,256},{16,272},{32,288},{48,304},{64,320},{80,336},{96,352},{112... | collective-permute-start | bytes 393224 | tf_op jit(solution)/shard_map/scatter_z/ppermute | solution.py:27

commit v5 on v4

--- a/solution.py
+++ b/solution.py
@@ -8,6 +8,9 @@
 from jax.sharding import PartitionSpec as P
 
 NZ, NX, NC = 4, 4, 2
+NY, NH = 4, 4
+Y_GROUPS = [[y * NH + h for y in range(NY)] for h in range(NH)]
+H_GROUPS = [[y * NH + h for h in range(NH)] for y in range(NY)]
 CORE_SWAP = [(i, i ^ 1) for i in range(NZ * NX * NC)]
 FLAG = 128
 BF16, F32 = jnp.bfloat16, jnp.float32
@@ -47,6 +50,19 @@
 def split(a):
     hi = a.astype(BF16)
     return hi, (a - hi.astype(F32)).astype(BF16)
+
+
+def swap(x, members):
+    return lax.all_to_all(
+        x, "group", split_axis=0, concat_axis=0, axis_index_groups=members, tiled=True
+    )
+
+
+def turn(x, outer, inner):
+    cut = pieces(x, outer * inner)
+    return jnp.concatenate(
+        [cut[o * inner + i] for i in range(inner) for o in range(outer)], axis=0
+    )
 
 
 def iota(dims, dim):
@@ -104,7 +120,7 @@
 
 def coef_kernel(
     scale, q_ref, far0, far1, far2, far3, got_ref, s0_ref, column_ref,
-    away_ref, mine_ref, hard_ref, hi0_ref, lo0_ref, hi1_ref, lo1_ref, hih_ref, loh_ref, loss_ref,
+    away_ref, mine_ref, hard_ref, both0_ref, both1_ref, bothh_ref, loss_ref,
 ):
     count, width = q_ref.shape
     q, s0 = q_ref[...], s0_ref[...]
@@ -130,12 +146,12 @@
         away_ref[:, cols] = dot(away, q_ref[:, cols]).astype(BF16)
 
     over_columns(width, send)
-    hi1_ref[...], lo1_ref[...] = hi1, lo1
+    both1_ref[:count], both1_ref[count:] = hi1, lo1
     hi0, lo0 = split(jnp.exp(s0 - log_total) - hot0.astype(F32))
-    hi0_ref[...], lo0_ref[...] = hi0, lo0
+    both0_ref[:count], both0_ref[count:] = hi0, lo0
     mine_ref[...] = flip(hi0)
     hih, loh = split(jnp.exp(sh - log_total))
-    hih_ref[...], loh_ref[...] = hih, loh
+    bothh_ref[:count], bothh_ref[count:] = hih, loh
     hard_ref[...] = flip(hih)
 
 
@@ -151,15 +167,14 @@
     over_columns(q_ref.shape[1], add)
 
 
-def query_grad_kernel(scale, *refs):
-    coefs, near, far, got, out = refs[:6], refs[6:10], refs[10:14], refs[14], refs[15]
+def query_grad_kernel(scale, c0, c1, ch, *refs):
+    near, far, got, out = refs[:4], refs[4:8], refs[8], refs[9]
+    count = out.shape[1]
 
     def grad(cols):
-        rows = (joined(near, cols), joined(far, cols), got[:, cols])
-        total = dot(coefs[0][...], rows[0])
-        for i in range(1, 6):
-            total = total + dot(coefs[i][...], rows[i % 3])
-        out[0, :, cols] = (scale * total).astype(out.dtype)
+        both = dot(c0[...], joined(near, cols)) + dot(c1[...], joined(far, cols))
+        both = both + dot(ch[...], got[:, cols])
+        out[0, :, cols] = (scale * (both[:count] + both[count:])).astype(out.dtype)
 
     over_columns(out.shape[2], grad)
 
@@ -171,7 +186,7 @@
     owned_hard = hard_rows[0]
     count, width = q.shape
     rows = own.shape[0]
-    groups = lax.axis_size("group")
+    groups = NY * NH
     slots = max(2, 2 * owned_hard.shape[0] // groups)
     half, places = NZ * NX * rows, groups * slots
     scale = width ** (-0.5)
@@ -187,12 +202,11 @@
             (hard_dest.reshape(1, -1), owned_hard),
             "pack", 2 * places * owned_hard.size, 2, 0,
         )
-        received = lax.all_to_all(
-            packed.reshape(groups, slots, -1), "group", split_axis=0, concat_axis=0, tiled=True
-        ).reshape(places, -1)
+        from_y = swap(packed, Y_GROUPS)
+        received = swap(turn(from_y, NY, NH), H_GROUPS)
     with jax.named_scope("gather_x"):
-        near = exchange([z_rows] * NX, "blk", x_shift)
-        near[-1], received = lax.optimization_barrier((near[-1], received))
+        last, _ = lax.optimization_barrier((z_rows, from_y))
+        near = exchange([z_rows] * (NX - 1) + [last], "blk", x_shift)
     with jax.named_scope("gather_core"):
         far = [lax.ppermute(x, "blk", CORE_SWAP) for x in near]
 
@@ -210,12 +224,12 @@
             (q, *near),
             "near", 2 * count * half * width, 8, 0,
         )
-        square, thin = shape((count, half)), shape((count, places))
-        away, mine_rows, hard_cols, hi0, lo0, hi1, lo1, hih, loh, loss_rows = call(
+        away, mine_rows, hard_cols, both0, both1, both_hard, loss_rows = call(
             functools.partial(coef_kernel, scale),
             [
                 shape((half, width)), shape((half, count)), shape((places, count)),
-                square, square, square, square, thin, thin, shape((count, 1), F32),
+                shape((2 * count, half)), shape((2 * count, half)), shape((2 * count, places)),
+                shape((count, 1), F32),
             ],
             (q, *far, received, s0, column.reshape(-1, 1)),
             "coef", 4 * count * half * width, 12, 0,
@@ -233,18 +247,16 @@
         chunks = [c.astype(F32) for c in exchange(list(mine), "blk", x_shift, -1)]
         mine_x = pieces(functools.reduce(jnp.add, chunks), NZ)
 
-    hard_cols, hi0, _ = lax.optimization_barrier((hard_cols, hi0, away))
+    hard_cols, both0, _ = lax.optimization_barrier((hard_cols, both0, away))
     with jax.named_scope("hard_back"):
         g = (scale * dot(hard_cols, q)).astype(BF16)
-        returned = lax.all_to_all(
-            g.reshape(groups, slots, width), "group", split_axis=0, concat_axis=0, tiled=True
-        ).reshape(places, width)
+        returned = swap(turn(swap(g, H_GROUPS), NH, NY), Y_GROUPS)
         d_owned = t_dot(placing, returned).astype(BF16)
     with jax.named_scope("d_query"):
         [d_query] = call(
             functools.partial(query_grad_kernel, scale),
             [shape((1, count, width))],
-            (hi0, hi1, hih, lo0, lo1, loh, *near, *far, received),
+            (both0, both1, both_hard, *near, *far, received),
             "query_grad", 4 * count * (2 * half + places) * width, 8, 0,
         )
     with jax.named_scope("scatter_z"):

time: 142 us -> 143 us (level)
  starting transfers between devices: 87.3 us -> 83.4 us
  local copies, waits for them, and re-layouts: 7.21 us -> 10.6 us
    all_to_all x2 -> x4, waiting for transfers between devices: 0.01 us -> 6.97 us  [swap(): lax.all_to_all(x, 'group', split_axis=0, concat_axis=0, axis_index_groups...]
    ppermute x12, waiting for transfers between devices: 15.4 us -> 8.79 us  [exchange(): lax.ppermute(p, axis, perm(sign * d))]
    concatenate x0 -> x2, local copies, waits for them, and re-layouts: none -> 5.82 us  [turn(): jnp.concatenate([cut[o * inner + i] for i in range(inner) for o in range(...]
    ppermute x4, starting transfers between devices: 15.1 us -> 9.76 us  [body(): far = [lax.ppermute(x, 'blk', CORE_SWAP) for x in near]]
    reshape x4 -> x0, local copies, waits for them, and re-layouts: 3.8 us -> none  [the longest x1 1.84 us: body(): g.reshape(groups, slots, width)]
    ppermute x1, starting transfers between devices: 2.39 us -> 5.48 us  [body(): away = lax.ppermute(away, 'blk', CORE_SWAP)]
    all_to_all x2 -> x4, starting transfers between devices: 29.4 us -> 26.6 us  [swap(): lax.all_to_all(x, 'group', split_axis=0, concat_axis=0, axis_index_groups...]
    unnamed x34 -> x24, local copies, waits for them, and re-layouts: 2.58 us -> 4.16 us
  transfers between devices with their start and end apart: 19 -> 21, of which waited for: 4 -> 5; matrix products, arithmetic and copies ran while one was open for 8% -> 9% of each run, Pallas kernels for 7% -> 8%
where the time goes in v5:
time: 143 us; the launch traced here: 141 us
  starting transfers between devices  83.4 us (58%)
  Pallas kernels  19.6 us (14%)
  waiting for transfers between devices  19.5 us (14%)
  local copies, waits for them, and re-layouts  10.6 us (7%)
  other arithmetic  4.41 us (3%)
  matrix products  2.08 us (1%)
    ppermute x12, starting transfers between devices, exchange(): lax.ppermute(p, axis, perm(sign * d))  41.6 us
    all_to_all x4, starting transfers between devices, swap(): lax.all_to_all(x, 'group', split_axis=0, concat_axis=0, axis_index_groups...  26.6 us
    pallas_call x5, Pallas kernels, call(): pl.pallas_call(kernel, in_specs=[pl.BlockSpec(memory_space=pltpu.SMEM)] *...  19.6 us
    ppermute x4, starting transfers between devices, body(): far = [lax.ppermute(x, 'blk', CORE_SWAP) for x in near]  9.76 us
    ppermute x12, waiting for transfers between devices, exchange(): lax.ppermute(p, axis, perm(sign * d))  8.79 us
    all_to_all x4, waiting for transfers between devices, swap(): lax.all_to_all(x, 'group', split_axis=0, concat_axis=0, axis_index_groups...  6.97 us
    concatenate x2, local copies, waits for them, and re-layouts, turn(): jnp.concatenate([cut[o * inner + i] for i in range(inner) for o in range(...  5.82 us
    ppermute x1, starting transfers between devices, body(): away = lax.ppermute(away, 'blk', CORE_SWAP)  5.48 us
  transfers between devices with their start and end apart: 21, of which 5 were waited for; matrix products, arithmetic and copies ran while one was open for 9% of the time, Pallas kernels for 8%

profile of v5, /device:TPU:1, one launch (start us, length us, event | category | flops | bytes accessed | tf_op | source)
XLA Modules:
  0.0 140.8 jit_solution(7391422969589364334)
XLA Ops:
  0.6 7.2 %collective-permute-start.2 = (bf16[16,4096]{1,0:T(8,128)(2,1)}, bf16[16,4096]{1,0:T(8,128)(2,1)S(1)}, u32[]{:S(2)}, u32[]{:S(2)}) collective-permute-start(bf16[16,4096]{1,0:T(8,128)(2,1)} %bitcast.34), channel_id=1, source_target_pairs={{0,384},{16,400},{32,416},{48,432},{64,448},{80,464},{96,480},{112... | collective-permute-start | bytes 393224 | tf_op jit(solution)/shard_map/gather_z/ppermute | solution.py:30
  7.9 1.9 %collective-permute-start.1 = (bf16[16,4096]{1,0:T(8,128)(2,1)}, bf16[16,4096]{1,0:T(8,128)(2,1)S(1)}, u32[]{:S(2)}, u32[]{:S(2)}) collective-permute-start(bf16[16,4096]{1,0:T(8,128)(2,1)} %bitcast.35), channel_id=1, source_target_pairs={{0,256},{16,272},{32,288},{48,304},{64,320},{80,336},{96,352},{112... | collective-permute-start | bytes 393224 | tf_op jit(solution)/shard_map/gather_z/ppermute | solution.py:30
  9.8 2.2 %collective-permute-start = (bf16[16,4096]{1,0:T(8,128)(2,1)}, bf16[16,4096]{1,0:T(8,128)(2,1)S(1)}, u32[]{:S(2)}, u32[]{:S(2)}) collective-permute-start(bf16[16,4096]{1,0:T(8,128)(2,1)} %bitcast.36), channel_id=1, source_target_pairs={{0,128},{16,144},{32,160},{48,176},{64,192},{80,208},{96,224},{112... | collective-permute-start | bytes 393224 | tf_op jit(solution)/shard_map/gather_z/ppermute | solution.py:30
  12.0 0.9 copy-done.3
  12.9 0.7 copy-done.4
  13.6 1.0 pack.1
  14.6 4.2 %all-to-all-start = ((bf16[4,8,4224]{2,1,0:T(8,128)(2,1)}), bf16[4,8,4224]{2,1,0:T(8,128)(2,1)S(1)}, u32[]{:S(2)}, u32[]{:S(2)}) async-start(bf16[4,8,4224]{2,1,0:T(8,128)(2,1)} %bitcast.4), calls=%async_computation | async-start | bytes 540672 | tf_op jit(solution)/shard_map/hard_out/all_to_all | solution.py:56
  18.8 0.0 collective-permute-done.2
  18.8 0.0 collective-permute-done.1
  18.8 0.0 collective-permute-done
  18.8 0.9 pad_maximum_fusion.refs_0_
  19.7 6.3 %collective-permute-start.6 = (bf16[64,4096]{1,0:T(8,128)(2,1)S(1)}, bf16[64,4096]{1,0:T(8,128)(2,1)}, u32[]{:S(2)}, u32[]{:S(2)}) collective-permute-start(bf16[64,4096]{1,0:T(8,128)(2,1)S(1)} %pad_maximum_fusion.refs_0_), channel_id=1, source_target_pairs={{0,64},{16,80},{32,96},{48,112},{64,0},{80,16},{96,32},{112,48},{1... | collective-permute-start | bytes 1572872 | tf_op jit(solution)/shard_map/gather_x/ppermute | solution.py:30
  26.1 2.2 %collective-permute-start.4 = (bf16[64,4096]{1,0:T(8,128)(2,1)S(1)}, bf16[64,4096]{1,0:T(8,128)(2,1)}, u32[]{:S(2)}, u32[]{:S(2)}) collective-permute-start(bf16[64,4096]{1,0:T(8,128)(2,1)S(1)} %pad_maximum_fusion.refs_0_), channel_id=1, source_target_pairs={{0,32},{16,48},{32,64},{48,80},{64,96},{80,112},{96,0},{112,16},{1... | collective-permute-start | bytes 1572872 | tf_op jit(solution)/shard_map/gather_x/ppermute | solution.py:30
  28.3 0.0 all-to-all-done
  28.3 4.3 %collective-permute-start.8 = (bf16[64,4096]{1,0:T(8,128)(2,1)S(1)}, bf16[64,4096]{1,0:T(8,128)(2,1)}, u32[]{:S(2)}, u32[]{:S(2)}) collective-permute-start(bf16[64,4096]{1,0:T(8,128)(2,1)S(1)} %pad_maximum_fusion.refs_0_), channel_id=1, source_target_pairs={{0,96},{16,112},{32,0},{48,16},{64,32},{80,48},{96,64},{112,80},{1... | collective-permute-start | bytes 1572872 | tf_op jit(solution)/shard_map/gather_x/ppermute | solution.py:30
  32.6 0.2 fusion.27
  32.8 3.0 %concatenate.10 = bf16[32,4224]{1,0:T(8,128)(2,1)} concatenate(bf16[2,4224]{1,0:T(2,128)(2,1)S(1)} %get-tuple-element.56, bf16[2,4224]{1,0:T(2,128)(2,1)S(1)} %get-tuple-element.55, bf16[2,4224]{1,0:T(2,128)(2,1)S(1)} %get-tuple-element.54, bf16[2,4224]{1,0:T(2,128)(2,1)S(1)} %get-tuple-element.53, bf16[2,4224]{1,0:T(2,128)(2,1)S(1)} %get-tuple-element.52, ...), dimensions={0} | concatenate | bytes 540672 | tf_op jit(solution)/shard_map/hard_out/concatenate | solution.py:63
  35.7 13.1 %all-to-all-start.1 = ((bf16[4,8,4224]{2,1,0:T(8,128)(2,1)}), bf16[4,8,4224]{2,1,0:T(8,128)(2,1)S(1)}, u32[]{:S(2)}, u32[]{:S(2)}) async-start(bf16[4,8,4224]{2,1,0:T(8,128)(2,1)} %bitcast.6), calls=%async_computation.1 | async-start | bytes 540672 | tf_op jit(solution)/shard_map/hard_out/all_to_all | solution.py:56
  48.8 3.5 %collective-permute-start.3 = (bf16[64,4096]{1,0:T(8,128)(2,1)S(1)}, bf16[64,4096]{1,0:T(8,128)(2,1)}, u32[]{:S(2)}, u32[]{:S(2)}) collective-permute-start(bf16[64,4096]{1,0:T(8,128)(2,1)S(1)} %pad_maximum_fusion.refs_0_), channel_id=1, source_target_pairs={{0,16},{16,0},{32,48},{48,32},{64,80},{80,64},{96,112},{112,96},{1... | collective-permute-start | bytes 1572872 | tf_op jit(solution)/shard_map/gather_core/ppermute | solution.py:211
  52.4 0.0 collective-permute-done.6.refs_2_
  52.4 1.9 %collective-permute-start.7 = (bf16[64,4096]{1,0:T(8,128)(2,1)}, bf16[64,4096]{1,0:T(8,128)(2,1)}, u32[]{:S(2)}, u32[]{:S(2)}) collective-permute-start(bf16[64,4096]{1,0:T(8,128)(2,1)} %collective-permute-done.6.refs_2_), channel_id=1, source_target_pairs={{0,16},{16,0},{32,48},{48,32},{64,80},{80,64},{96,112},{112,96},{1... | collective-permute-start | bytes 1572872 | tf_op jit(solution)/shard_map/gather_core/ppermute | solution.py:211
  54.3 0.0 collective-permute-done.4.refs_1_
  54.3 2.4 %collective-permute-start.5 = (bf16[64,4096]{1,0:T(8,128)(2,1)}, bf16[64,4096]{1,0:T(8,128)(2,1)}, u32[]{:S(2)}, u32[]{:S(2)}) collective-permute-start(bf16[64,4096]{1,0:T(8,128)(2,1)} %collective-permute-done.4.refs_1_), channel_id=1, source_target_pairs={{0,16},{16,0},{32,48},{48,32},{64,80},{80,64},{96,112},{112,96},{1... | collective-permute-start | bytes 1572872 | tf_op jit(solution)/shard_map/gather_core/ppermute | solution.py:211
  56.7 0.0 collective-permute-done.8.refs_3_
  56.7 1.9 %collective-permute-start.9 = (bf16[64,4096]{1,0:T(8,128)(2,1)}, bf16[64,4096]{1,0:T(8,128)(2,1)}, u32[]{:S(2)}, u32[]{:S(2)}) collective-permute-start(bf16[64,4096]{1,0:T(8,128)(2,1)} %collective-permute-done.8.refs_3_), channel_id=1, source_target_pairs={{0,16},{16,0},{32,48},{48,32},{64,80},{80,64},{96,112},{112,96},{1... | collective-permute-start | bytes 1572872 | tf_op jit(solution)/shard_map/gather_core/ppermute | solution.py:211
  58.7 0.1 copy.9
  58.9 0.5 fusion.16.column_ref
  59.4 2.1 %near.1.s0_ref = f32[256,256]{1,0:T(8,128)S(1)} custom-call(bf16[256,4096]{1,0:T(8,128)(2,1)S(1)} %bitcast.25, bf16[64,4096]{1,0:T(8,128)(2,1)S(1)} %pad_maximum_fusion.refs_0_, bf16[64,4096]{1,0:T(8,128)(2,1)} %collective-permute-done.4.refs_1_, bf16[64,4096]{1,0:T(8,128)(2,1)} %collective-permute-done.6.refs_2_, ...), custom_call_target="tpu_custom_call" | custom-call | flops 536870912 | bytes 4456448 | tf_op jit(solution)/shard_map/scores/near/pallas_call | solution.py:78
  61.5 0.0 collective-permute-done.3.far0.refs_4_
  61.5 3.5 %all-to-all-done.1 = bf16[4,8,4224]{2,1,0:T(8,128)(2,1)S(1)} async-done(((bf16[4,8,4224]{2,1,0:T(8,128)(2,1)}), bf16[4,8,4224]{2,1,0:T(8,128)(2,1)S(1)}, u32[]{:S(2)}, u32[]{:S(2)}) %all-to-all-start.1) | async-done | bytes 270368 | tf_op jit(solution)/shard_map/hard_out/all_to_all | solution.py:56
  65.0 0.0 collective-permute-done.7.far2.refs_6_
  65.0 0.0 collective-permute-done.5.far1.refs_5_
  65.0 0.0 collective-permute-done.9.far3.refs_7_
  65.0 5.4 %coef.1 = (bf16[256,4096]{1,0:T(8,128)(2,1)S(1)}, bf16[256,256]{1,0:T(8,128)(2,1)S(1)}, bf16[32,256]{1,0:T(8,128)(2,1)S(1)}, bf16[512,256]{1,0:T(8,128)(2,1)S(1)...) custom-call(bf16[256,4096]{1,0:T(8,128)(2,1)S(1)} %bitcast.26, ...), custom_call_target="tpu_custom_call" | custom-call | flops 1073741824 | bytes 7530496 | tf_op jit(solution)/shard_map/scores/coef/pallas_call | solution.py:78
  70.4 0.0 copy-start.5
  70.4 0.7 copy-done.5
  71.1 5.5 %collective-permute-start.10 = (bf16[256,4096]{1,0:T(8,128)(2,1)S(1)}, bf16[256,4096]{1,0:T(8,128)(2,1)S(1)}, u32[]{:S(2)}, u32[]{:S(2)}) collective-permute-start(bf16[256,4096]{1,0:T(8,128)(2,1)S(1)} %get-tuple-element.25), channel_id=1, source_target_pairs={{0,16},{16,0},{32,48},{48,32},{64,80},{80,64},{96,112},{112,96},{1... | collective-permute-start | bytes 6291464 | tf_op jit(solution)/shard_map/scatter_core/ppermute | solution.py:238
  76.6 3.8 %collective-permute-done.10.away_ref = bf16[256,4096]{1,0:T(8,128)(2,1)S(1)} collective-permute-done((bf16[256,4096]{1,0:T(8,128)(2,1)S(1)}, bf16[256,4096]{1,0:T(8,128)(2,1)S(1)}, u32[]{:S(2)}, u32[]{:S(2)}) %collective-permute-start.10) | collective-permute-done | bytes 2097184 | tf_op jit(solution)/shard_map/scatter_core/ppermute | solution.py:238
  80.4 3.1 %core_sum.1 = (f32[64,4096]{1,0:T(8,128)S(1)}, bf16[64,4096]{1,0:T(8,128)(2,1)}, bf16[64,4096]{1,0:T(8,128)(2,1)}, bf16[64,4096]{1,0:T(8,128)(2,1)}) custom-call(bf16[256,256]{1,0:T(8,128)(2,1)S(1)} %get-tuple-element.29.coef_ref, bf16[256,4096]{1,0:T(8,128)(2,1)S(1)} %bitcast.27, bf16[256,4096]{1,0:T(8,128)(2,1)S(1)} %collective-permute-done.10.away_ref), custom_call_target="tpu_custom_call" | custom-call | flops 536870912 | bytes 6946816 | tf_op jit(solution)/shard_map/scatter_x/core_sum/pallas_call | solution.py:78
  83.4 1.0 copy-done.1
  84.4 2.0 %collective-permute-start.11 = (bf16[64,4096]{1,0:T(8,128)(2,1)}, bf16[64,4096]{1,0:T(8,128)(2,1)}, u32[]{:S(2)}, u32[]{:S(2)}) collective-permute-start(bf16[64,4096]{1,0:T(8,128)(2,1)} %get-tuple-element.31), channel_id=1, source_target_pairs={{0,96},{16,112},{32,0},{48,16},{64,32},{80,48},{96,64},{112,80},{1... | collective-permute-start | bytes 1572872 | tf_op jit(solution)/shard_map/scatter_x/ppermute | solution.py:30
  86.5 2.8 %collective-permute-start.12 = (bf16[64,4096]{1,0:T(8,128)(2,1)}, bf16[64,4096]{1,0:T(8,128)(2,1)}, u32[]{:S(2)}, u32[]{:S(2)}) collective-permute-start(bf16[64,4096]{1,0:T(8,128)(2,1)} %get-tuple-element.32), channel_id=1, source_target_pairs={{0,64},{16,80},{32,96},{48,112},{64,0},{80,16},{96,32},{112,48},{1... | collective-permute-start | bytes 1572872 | tf_op jit(solution)/shard_map/scatter_x/ppermute | solution.py:30
  89.3 2.5 %collective-permute-start.13 = (bf16[64,4096]{1,0:T(8,128)(2,1)}, bf16[64,4096]{1,0:T(8,128)(2,1)}, u32[]{:S(2)}, u32[]{:S(2)}) collective-permute-start(bf16[64,4096]{1,0:T(8,128)(2,1)} %get-tuple-element.33), channel_id=1, source_target_pairs={{0,32},{16,48},{32,64},{48,80},{64,96},{80,112},{96,0},{112,16},{1... | collective-permute-start | bytes 1572872 | tf_op jit(solution)/shard_map/scatter_x/ppermute | solution.py:30
  91.8 0.7 reduce
  92.5 1.2 fusion.1
  93.7 5.2 %all-to-all-start.2 = ((bf16[4,8,4096]{2,1,0:T(8,128)(2,1)}), bf16[4,8,4096]{2,1,0:T(8,128)(2,1)S(1)}, u32[]{:S(2)}, u32[]{:S(2)}) async-start(bf16[4,8,4096]{2,1,0:T(8,128)(2,1)} %fusion.1), calls=%async_computation.2 | async-start | bytes 524288 | tf_op jit(solution)/shard_map/hard_back/all_to_all | solution.py:56
  98.9 0.9 copy-done.10
  99.8 8.0 %query_grad.1 = bf16[1,256,4096]{2,1,0:T(8,128)(2,1)} custom-call(bf16[512,256]{1,0:T(8,128)(2,1)S(1)} %copy-done.6, bf16[512,256]{1,0:T(8,128)(2,1)S(1)} %copy-done.8, bf16[512,32]{1,0:T(8,128)(2,1)S(1)} %copy-done.10, bf16[64,4096]{1,0:T(8,128)(2,1)S(1)} %pad_maximum_fusion.refs_0_, bf16[64,4096]{1,0:T(8,128)(2,1)} %collective-permute-done.4.refs_1_, ...), custom_call_target="tpu_custom_call" | custom-call | flops 2281701376 | bytes 7118848 | tf_op jit(solution)/shard_map/d_query/query_grad/pallas_call | solution.py:78
  107.8 0.0 collective-permute-done.11
  107.8 0.0 collective-permute-done.12
  107.8 7.4 %collective-permute-done.13 = bf16[64,4096]{1,0:T(8,128)(2,1)} collective-permute-done((bf16[64,4096]{1,0:T(8,128)(2,1)}, bf16[64,4096]{1,0:T(8,128)(2,1)}, u32[]{:S(2)}, u32[]{:S(2)}) %collective-permute-start.13) | collective-permute-done | bytes 524320 | tf_op jit(solution)/shard_map/scatter_x/ppermute | solution.py:30
  115.3 1.6 %fusion.25 = (bf16[64,4096]{1,0:T(8,128)(2,1)S(1)}, f32[64,4096]{1,0:T(8,128)S(1)}) fusion(bf16[64,4096]{1,0:T(8,128)(2,1)} %collective-permute-done.13, bf16[64,4096]{1,0:T(8,128)(2,1)} %collective-permute-done.12, f32[64,4096]{1,0:T(8,128)S(1)} %copy-done.2, bf16[64,4096]{1,0:T(8,128)(2,1)} %collective-permute-done.11), kind=kLoop, calls=%fused_computation.54 | loop fusion | flops 1835008 | bytes 4194304 | tf_op jit(solution)/shard_map/convert.2
  116.9 4.0 %collective-permute-start.14 = (bf16[16,4096]{1,0:T(8,128)(2,1)S(1)}, bf16[16,4096]{1,0:T(8,128)(2,1)S(1)}, u32[]{:S(2)}, u32[]{:S(2)}) collective-permute-start(bf16[16,4096]{1,0:T(8,128)(2,1)S(1)} %get-tuple-element.38), channel_id=1, source_target_pairs={{0,384},{16,400},{32,416},{48,432},{64,448},{80,464},{96,480},{112... | collective-permute-start | bytes 393224 | tf_op jit(solution)/shard_map/scatter_z/ppermute | solution.py:30
  121.0 1.9 %collective-permute-start.16 = (bf16[16,4096]{1,0:T(8,128)(2,1)S(1)}, bf16[16,4096]{1,0:T(8,128)(2,1)S(1)}, u32[]{:S(2)}, u32[]{:S(2)}) collective-permute-start(bf16[16,4096]{1,0:T(8,128)(2,1)S(1)} %get-tuple-element.39), channel_id=1, source_target_pairs={{0,128},{16,144},{32,160},{48,176},{64,192},{80,208},{96,224},{112... | collective-permute-start | bytes 393224 | tf_op jit(solution)/shard_map/scatter_z/ppermute | solution.py:30
  122.9 4.2 %collective-permute-start.15 = (bf16[16,4096]{1,0:T(8,128)(2,1)S(1)}, bf16[16,4096]{1,0:T(8,128)(2,1)S(1)}, u32[]{:S(2)}, u32[]{:S(2)}) collective-permute-start(bf16[16,4096]{1,0:T(8,128)(2,1)S(1)} %get-tuple-element.40), channel_id=1, source_target_pairs={{0,256},{16,272},{32,288},{48,304},{64,320},{80,336},{96,352},{112... | collective-permute-start | bytes 393224 | tf_op jit(solution)/shard_map/scatter_z/ppermute | solution.py:30
  127.1 0.0 all-to-all-done.2
  127.1 0.3 fusion.28
  127.4 2.9 %concatenate.11 = bf16[32,4096]{1,0:T(8,128)(2,1)} concatenate(bf16[2,4096]{1,0:T(2,128)(2,1)S(1)} %get-tuple-element.72, bf16[2,4096]{1,0:T(2,128)(2,1)S(1)} %get-tuple-element.71, bf16[2,4096]{1,0:T(2,128)(2,1)S(1)} %get-tuple-element.70, bf16[2,4096]{1,0:T(2,128)(2,1)S(1)} %get-tuple-element.69, bf16[2,4096]{1,0:T(2,128)(2,1)S(1)} %get-tuple-element.68, ...), dimensions={0} | concatenate | bytes 524288 | tf_op jit(solution)/shard_map/hard_back/concatenate | solution.py:63
  130.2 4.1 %all-to-all-start.3 = ((bf16[4,8,4096]{2,1,0:T(8,128)(2,1)}), bf16[4,8,4096]{2,1,0:T(8,128)(2,1)S(1)}, u32[]{:S(2)}, u32[]{:S(2)}) async-start(bf16[4,8,4096]{2,1,0:T(8,128)(2,1)} %bitcast.12), calls=%async_computation.3 | async-start | bytes 524288 | tf_op jit(solution)/shard_map/hard_back/all_to_all | solution.py:56
  134.4 0.0 collective-permute-done.14
  134.4 1.3 collective-permute-done.15
  135.7 0.7 fusion.20
  136.4 3.5 %all-to-all-done.3 = bf16[4,8,4096]{2,1,0:T(8,128)(2,1)S(1)} async-done(((bf16[4,8,4096]{2,1,0:T(8,128)(2,1)}), bf16[4,8,4096]{2,1,0:T(8,128)(2,1)S(1)}, u32[]{:S(2)}, u32[]{:S(2)}) %all-to-all-start.3) | async-done | bytes 262176 | tf_op jit(solution)/shard_map/hard_back/all_to_all | solution.py:56
  139.9 0.9 fusion.2
  (20 shorter events, 0.1 us)
Async XLA Ops:
  0.6 58.7 %copy-start = (bf16[1,256,4096]{2,1,0:T(8,128)(2,1)S(1)}, bf16[1,256,4096]{2,1,0:T(8,128)(2,1)}, u32[]{:S(2)}) copy-start(bf16[1,256,4096]{2,1,0:T(8,128)(2,1)} %param.5) | copy-start | bytes 6291460
  0.6 18.1 %collective-permute-start.2 = (bf16[16,4096]{1,0:T(8,128)(2,1)}, bf16[16,4096]{1,0:T(8,128)(2,1)S(1)}, u32[]{:S(2)}, u32[]{:S(2)}) collective-permute-start(bf16[16,4096]{1,0:T(8,128)(2,1)} %bitcast.34), channel_id=1, source_target_pairs={{0,384},{16,400},{32,416},{48,432},{64,448},{80,464},{96,480},{112... | collective-permute-start | bytes 393224 | tf_op jit(solution)/shard_map/gather_z/ppermute | solution.py:30
  7.9 10.9 %collective-permute-start.1 = (bf16[16,4096]{1,0:T(8,128)(2,1)}, bf16[16,4096]{1,0:T(8,128)(2,1)S(1)}, u32[]{:S(2)}, u32[]{:S(2)}) collective-permute-start(bf16[16,4096]{1,0:T(8,128)(2,1)} %bitcast.35), channel_id=1, source_target_pairs={{0,256},{16,272},{32,288},{48,304},{64,320},{80,336},{96,352},{112... | collective-permute-start | bytes 393224 | tf_op jit(solution)/shard_map/gather_z/ppermute | solution.py:30
  9.8 9.0 %collective-permute-start = (bf16[16,4096]{1,0:T(8,128)(2,1)}, bf16[16,4096]{1,0:T(8,128)(2,1)S(1)}, u32[]{:S(2)}, u32[]{:S(2)}) collective-permute-start(bf16[16,4096]{1,0:T(8,128)(2,1)} %bitcast.36), channel_id=1, source_target_pairs={{0,128},{16,144},{32,160},{48,176},{64,192},{80,208},{96,224},{112... | collective-permute-start | bytes 393224 | tf_op jit(solution)/shard_map/gather_z/ppermute | solution.py:30
  12.0 0.9 copy-start.3
  12.9 0.7 copy-start.4
  13.6 45.2 %copy-start.11 = (s32[1,256]{1,0:T(1,128)S(1)}, s32[1,256]{1,0:T(1,128)}, u32[]{:S(2)}) copy-start(s32[1,256]{1,0:T(1,128)} %param.7) | copy-start | bytes 3076
  14.6 13.7 %all-to-all-start = ((bf16[4,8,4224]{2,1,0:T(8,128)(2,1)}), bf16[4,8,4224]{2,1,0:T(8,128)(2,1)S(1)}, u32[]{:S(2)}, u32[]{:S(2)}) async-start(bf16[4,8,4224]{2,1,0:T(8,128)(2,1)} %bitcast.4), calls=%async_computation | async-start | bytes 540672 | tf_op jit(solution)/shard_map/hard_out/all_to_all | solution.py:56
  19.7 32.6 %collective-permute-start.6 = (bf16[64,4096]{1,0:T(8,128)(2,1)S(1)}, bf16[64,4096]{1,0:T(8,128)(2,1)}, u32[]{:S(2)}, u32[]{:S(2)}) collective-permute-start(bf16[64,4096]{1,0:T(8,128)(2,1)S(1)} %pad_maximum_fusion.refs_0_), channel_id=1, source_target_pairs={{0,64},{16,80},{32,96},{48,112},{64,0},{80,16},{96,32},{112,48},{1... | collective-permute-start | bytes 1572872 | tf_op jit(solution)/shard_map/gather_x/ppermute | solution.py:30
  26.1 28.3 %collective-permute-start.4 = (bf16[64,4096]{1,0:T(8,128)(2,1)S(1)}, bf16[64,4096]{1,0:T(8,128)(2,1)}, u32[]{:S(2)}, u32[]{:S(2)}) collective-permute-start(bf16[64,4096]{1,0:T(8,128)(2,1)S(1)} %pad_maximum_fusion.refs_0_), channel_id=1, source_target_pairs={{0,32},{16,48},{32,64},{48,80},{64,96},{80,112},{96,0},{112,16},{1... | collective-permute-start | bytes 1572872 | tf_op jit(solution)/shard_map/gather_x/ppermute | solution.py:30
  28.3 28.4 %collective-permute-start.8 = (bf16[64,4096]{1,0:T(8,128)(2,1)S(1)}, bf16[64,4096]{1,0:T(8,128)(2,1)}, u32[]{:S(2)}, u32[]{:S(2)}) collective-permute-start(bf16[64,4096]{1,0:T(8,128)(2,1)S(1)} %pad_maximum_fusion.refs_0_), channel_id=1, source_target_pairs={{0,96},{16,112},{32,0},{48,16},{64,32},{80,48},{96,64},{112,80},{1... | collective-permute-start | bytes 1572872 | tf_op jit(solution)/shard_map/gather_x/ppermute | solution.py:30
  35.7 29.2 %all-to-all-start.1 = ((bf16[4,8,4224]{2,1,0:T(8,128)(2,1)}), bf16[4,8,4224]{2,1,0:T(8,128)(2,1)S(1)}, u32[]{:S(2)}, u32[]{:S(2)}) async-start(bf16[4,8,4224]{2,1,0:T(8,128)(2,1)} %bitcast.6), calls=%async_computation.1 | async-start | bytes 540672 | tf_op jit(solution)/shard_map/hard_out/all_to_all | solution.py:56
  48.8 12.6 %collective-permute-start.3 = (bf16[64,4096]{1,0:T(8,128)(2,1)S(1)}, bf16[64,4096]{1,0:T(8,128)(2,1)}, u32[]{:S(2)}, u32[]{:S(2)}) collective-permute-start(bf16[64,4096]{1,0:T(8,128)(2,1)S(1)} %pad_maximum_fusion.refs_0_), channel_id=1, source_target_pairs={{0,16},{16,0},{32,48},{48,32},{64,80},{80,64},{96,112},{112,96},{1... | collective-permute-start | bytes 1572872 | tf_op jit(solution)/shard_map/gather_core/ppermute | solution.py:211
  52.4 12.6 %collective-permute-start.7 = (bf16[64,4096]{1,0:T(8,128)(2,1)}, bf16[64,4096]{1,0:T(8,128)(2,1)}, u32[]{:S(2)}, u32[]{:S(2)}) collective-permute-start(bf16[64,4096]{1,0:T(8,128)(2,1)} %collective-permute-done.6.refs_2_), channel_id=1, source_target_pairs={{0,16},{16,0},{32,48},{48,32},{64,80},{80,64},{96,112},{112,96},{1... | collective-permute-start | bytes 1572872 | tf_op jit(solution)/shard_map/gather_core/ppermute | solution.py:211
  54.3 10.6 %collective-permute-start.5 = (bf16[64,4096]{1,0:T(8,128)(2,1)}, bf16[64,4096]{1,0:T(8,128)(2,1)}, u32[]{:S(2)}, u32[]{:S(2)}) collective-permute-start(bf16[64,4096]{1,0:T(8,128)(2,1)} %collective-permute-done.4.refs_1_), channel_id=1, source_target_pairs={{0,16},{16,0},{32,48},{48,32},{64,80},{80,64},{96,112},{112,96},{1... | collective-permute-start | bytes 1572872 | tf_op jit(solution)/shard_map/gather_core/ppermute | solution.py:211
  56.7 8.2 %collective-permute-start.9 = (bf16[64,4096]{1,0:T(8,128)(2,1)}, bf16[64,4096]{1,0:T(8,128)(2,1)}, u32[]{:S(2)}, u32[]{:S(2)}) collective-permute-start(bf16[64,4096]{1,0:T(8,128)(2,1)} %collective-permute-done.8.refs_3_), channel_id=1, source_target_pairs={{0,16},{16,0},{32,48},{48,32},{64,80},{80,64},{96,112},{112,96},{1... | collective-permute-start | bytes 1572872 | tf_op jit(solution)/shard_map/gather_core/ppermute | solution.py:211
  70.4 0.7 copy-start.5
  71.1 12.3 %copy-start.7 = (bf16[512,256]{1,0:T(8,128)(2,1)}, bf16[512,256]{1,0:T(8,128)(2,1)S(1)}, u32[]{:S(2)}) copy-start(bf16[512,256]{1,0:T(8,128)(2,1)S(1)} %get-tuple-element.27.c1) | copy-start | bytes 786436
  71.1 12.3 %copy-start.9 = (bf16[512,32]{1,0:T(8,128)(2,1)}, bf16[512,32]{1,0:T(8,128)(2,1)S(1)}, u32[]{:S(2)}) copy-start(bf16[512,32]{1,0:T(8,128)(2,1)S(1)} %get-tuple-element.28.ch) | copy-start | bytes 98308
  71.1 9.2 %collective-permute-start.10 = (bf16[256,4096]{1,0:T(8,128)(2,1)S(1)}, bf16[256,4096]{1,0:T(8,128)(2,1)S(1)}, u32[]{:S(2)}, u32[]{:S(2)}) collective-permute-start(bf16[256,4096]{1,0:T(8,128)(2,1)S(1)} %get-tuple-element.25), channel_id=1, source_target_pairs={{0,16},{16,0},{32,48},{48,32},{64,80},{80,64},{96,112},{112,96},{1... | collective-permute-start | bytes 6291464 | tf_op jit(solution)/shard_map/scatter_core/ppermute | solution.py:238
  83.4 1.0 copy-start.1
  84.4 14.5 %copy-start.6 = (bf16[512,256]{1,0:T(8,128)(2,1)S(1)}, bf16[512,256]{1,0:T(8,128)(2,1)}, u32[]{:S(2)}) copy-start(bf16[512,256]{1,0:T(8,128)(2,1)} %copy-done.5) | copy-start | bytes 786436
  84.4 23.4 %collective-permute-start.11 = (bf16[64,4096]{1,0:T(8,128)(2,1)}, bf16[64,4096]{1,0:T(8,128)(2,1)}, u32[]{:S(2)}, u32[]{:S(2)}) collective-permute-start(bf16[64,4096]{1,0:T(8,128)(2,1)} %get-tuple-element.31), channel_id=1, source_target_pairs={{0,96},{16,112},{32,0},{48,16},{64,32},{80,48},{96,64},{112,80},{1... | collective-permute-start | bytes 1572872 | tf_op jit(solution)/shard_map/scatter_x/ppermute | solution.py:30
  86.5 21.3 %collective-permute-start.12 = (bf16[64,4096]{1,0:T(8,128)(2,1)}, bf16[64,4096]{1,0:T(8,128)(2,1)}, u32[]{:S(2)}, u32[]{:S(2)}) collective-permute-start(bf16[64,4096]{1,0:T(8,128)(2,1)} %get-tuple-element.32), channel_id=1, source_target_pairs={{0,64},{16,80},{32,96},{48,112},{64,0},{80,16},{96,32},{112,48},{1... | collective-permute-start | bytes 1572872 | tf_op jit(solution)/shard_map/scatter_x/ppermute | solution.py:30
  89.3 26.0 %collective-permute-start.13 = (bf16[64,4096]{1,0:T(8,128)(2,1)}, bf16[64,4096]{1,0:T(8,128)(2,1)}, u32[]{:S(2)}, u32[]{:S(2)}) collective-permute-start(bf16[64,4096]{1,0:T(8,128)(2,1)} %get-tuple-element.33), channel_id=1, source_target_pairs={{0,32},{16,48},{32,64},{48,80},{64,96},{80,112},{96,0},{112,16},{1... | collective-permute-start | bytes 1572872 | tf_op jit(solution)/shard_map/scatter_x/ppermute | solution.py:30
  92.4 6.4 %copy-start.8 = (bf16[512,256]{1,0:T(8,128)(2,1)S(1)}, bf16[512,256]{1,0:T(8,128)(2,1)}, u32[]{:S(2)}) copy-start(bf16[512,256]{1,0:T(8,128)(2,1)} %copy-done.7) | copy-start | bytes 786436
  93.7 33.4 %all-to-all-start.2 = ((bf16[4,8,4096]{2,1,0:T(8,128)(2,1)}), bf16[4,8,4096]{2,1,0:T(8,128)(2,1)S(1)}, u32[]{:S(2)}, u32[]{:S(2)}) async-start(bf16[4,8,4096]{2,1,0:T(8,128)(2,1)} %fusion.1), calls=%async_computation.2 | async-start | bytes 524288 | tf_op jit(solution)/shard_map/hard_back/all_to_all | solution.py:56
  98.9 0.9 copy-start.10
  99.8 15.5 %copy-start.2 = (f32[64,4096]{1,0:T(8,128)S(1)}, f32[64,4096]{1,0:T(8,128)}, u32[]{:S(2)}) copy-start(f32[64,4096]{1,0:T(8,128)} %copy-done.1) | copy-start | bytes 3145732
  116.9 17.4 %collective-permute-start.14 = (bf16[16,4096]{1,0:T(8,128)(2,1)S(1)}, bf16[16,4096]{1,0:T(8,128)(2,1)S(1)}, u32[]{:S(2)}, u32[]{:S(2)}) collective-permute-start(bf16[16,4096]{1,0:T(8,128)(2,1)S(1)} %get-tuple-element.38), channel_id=1, source_target_pairs={{0,384},{16,400},{32,416},{48,432},{64,448},{80,464},{96,480},{112... | collective-permute-start | bytes 393224 | tf_op jit(solution)/shard_map/scatter_z/ppermute | solution.py:30
  121.0 13.4 %collective-permute-start.16 = (bf16[16,4096]{1,0:T(8,128)(2,1)S(1)}, bf16[16,4096]{1,0:T(8,128)(2,1)S(1)}, u32[]{:S(2)}, u32[]{:S(2)}) collective-permute-start(bf16[16,4096]{1,0:T(8,128)(2,1)S(1)} %get-tuple-element.39), channel_id=1, source_target_pairs={{0,128},{16,144},{32,160},{48,176},{64,192},{80,208},{96,224},{112... | collective-permute-start | bytes 393224 | tf_op jit(solution)/shard_map/scatter_z/ppermute | solution.py:30
  122.9 12.8 %collective-permute-start.15 = (bf16[16,4096]{1,0:T(8,128)(2,1)S(1)}, bf16[16,4096]{1,0:T(8,128)(2,1)S(1)}, u32[]{:S(2)}, u32[]{:S(2)}) collective-permute-start(bf16[16,4096]{1,0:T(8,128)(2,1)S(1)} %get-tuple-element.40), channel_id=1, source_target_pairs={{0,256},{16,272},{32,288},{48,304},{64,320},{80,336},{96,352},{112... | collective-permute-start | bytes 393224 | tf_op jit(solution)/shard_map/scatter_z/ppermute | solution.py:30
  130.2 9.7 %all-to-all-start.3 = ((bf16[4,8,4096]{2,1,0:T(8,128)(2,1)}), bf16[4,8,4096]{2,1,0:T(8,128)(2,1)S(1)}, u32[]{:S(2)}, u32[]{:S(2)}) async-start(bf16[4,8,4096]{2,1,0:T(8,128)(2,1)} %bitcast.12), calls=%async_computation.3 | async-start | bytes 524288 | tf_op jit(solution)/shard_map/hard_back/all_to_all | solution.py:56

commit v6 on v5

--- a/solution.py
+++ b/solution.py
@@ -55,13 +55,6 @@
 def swap(x, members):
     return lax.all_to_all(
         x, "group", split_axis=0, concat_axis=0, axis_index_groups=members, tiled=True
-    )
-
-
-def turn(x, outer, inner):
-    cut = pieces(x, outer * inner)
-    return jnp.concatenate(
-        [cut[o * inner + i] for i in range(inner) for o in range(outer)], axis=0
     )
 
 
@@ -97,72 +90,110 @@
     return jnp.concatenate([r[:, cols] for r in refs], axis=0)
 
 
-def flip(x):
+def flip(x, pick=None):
     n = x.shape[1]
-    return dot_t((iota((n, n), 0) == iota((n, n), 1)).astype(BF16), x).astype(BF16)
-
-
-def pack_kernel(groups, slots, dest_ref, rows_ref, packed_ref, placing_ref):
+    pick = iota((n, n), 0) == iota((n, n), 1) if pick is None else pick
+    return dot_t(pick.astype(BF16), x).astype(BF16)
+
+
+def swapped(n, slots):
+    row, col = iota((n, n), 0), iota((n, n), 1)
+    place = row // slots
+    return (place % NH * NY + place // NH) * slots + row % slots == col
+
+
+def turn_kernel(slots, in_ref, out_ref):
+    pick = swapped(in_ref.shape[0], slots).astype(BF16)
+    out_ref[...] = dot(pick, in_ref[...]).astype(BF16)
+
+
+def turn(x, slots):
+    [out] = call(
+        functools.partial(turn_kernel, slots), [shape(x.shape)], (x,),
+        "turn", 2 * x.shape[0] * x.size, 2, 0,
+    )
+    return out
+
+
+def pack_kernel(slots, dest_ref, rows_ref, packed_ref, placing_ref):
     dest = dest_ref[...]
     count, width = rows_ref.shape
+    groups = NY * NH
     hot = (dest == iota((groups, count), 0)).astype(F32)
     ahead = (iota((count, count), 0) < iota((count, count), 1)).astype(F32)
     rank = jnp.sum(dot(hot, ahead) * hot, axis=0, keepdims=True).astype(jnp.int32)
-    placing = (dest * slots + rank == iota((groups * slots, count), 0)).astype(BF16)
-    packed_ref[:, :width] = dot(placing, rows_ref[...]).astype(BF16)
-    packed_ref[:, width:] = dot(placing, jnp.ones((count, FLAG), BF16)).astype(BF16)
-    placing_ref[...] = placing
+    at = iota((groups * slots, count), 0)
+    send = (dest * slots + rank == at).astype(BF16)
+    packed_ref[:, :width] = dot(send, rows_ref[...]).astype(BF16)
+    packed_ref[:, width:] = dot(send, jnp.ones((count, FLAG), BF16)).astype(BF16)
+    placing_ref[...] = ((dest % NH * NY + dest // NH) * slots + rank == at).astype(BF16)
 
 
 def near_kernel(scale, q_ref, *refs):
     refs[-1][...] = scale * dot_t(q_ref[...], joined(refs[:-1]))
 
 
-def coef_kernel(
+def hot(column_ref, dims, start):
+    return column_ref[...] == iota(dims, 1) + start
+
+
+def away_kernel(
     scale, q_ref, far0, far1, far2, far3, got_ref, s0_ref, column_ref,
-    away_ref, mine_ref, hard_ref, both0_ref, both1_ref, bothh_ref, loss_ref,
+    first_ref, second_ref, s1_ref, sh_ref, log_ref,
 ):
     count, width = q_ref.shape
     q, s0 = q_ref[...], s0_ref[...]
     half = s0.shape[1]
-    s1 = scale * dot_t(q, joined((far0, far1, far2, far3)))
     flags = dot_t(jnp.ones((count, FLAG), BF16), got_ref[:, width:])
     sh = jnp.where(flags > 0.5 * FLAG, scale * dot_t(q, got_ref[:, :width]), -jnp.inf)
+    s1 = scale * dot_t(q, joined((far0, far1, far2, far3)))
     top = jnp.maximum(
         jnp.max(jnp.maximum(s0, s1), axis=1, keepdims=True), jnp.max(sh, axis=1, keepdims=True)
     )
     total = jnp.sum(jnp.exp(s0 - top) + jnp.exp(s1 - top), axis=1, keepdims=True)
     total = total + jnp.sum(jnp.exp(sh - top), axis=1, keepdims=True)
     log_total = top + jnp.log(total)
-    column = column_ref[...]
-    hot0 = column == iota((count, half), 1)
-    hot1 = column == iota((count, half), 1) + half
+    c1 = jnp.exp(s1 - log_total) - hot(column_ref, (count, half), half).astype(F32)
+    away = flip(c1.astype(BF16))
+    n = half // NX
+
+    def send(cols):
+        rows = dot(away, q_ref[:, cols]).astype(BF16)
+        first_ref[:, cols] = rows[n : 3 * n]
+        second_ref[:n, cols], second_ref[n:, cols] = rows[:n], rows[3 * n :]
+
+    over_columns(width, send)
+    s1_ref[...], sh_ref[...], log_ref[...] = s1, sh, log_total
+
+
+def coef_kernel(
+    slots, s0_ref, s1_ref, sh_ref, log_ref, column_ref,
+    mine_ref, hard_ref, both0_ref, both1_ref, bothh_ref, loss_ref,
+):
+    s0, s1, log_total = s0_ref[...], s1_ref[...], log_ref[...]
+    count, half = s0.shape
+    hot0, hot1 = hot(column_ref, s0.shape, 0), hot(column_ref, s0.shape, half)
+    hi0, lo0 = split(jnp.exp(s0 - log_total) - hot0.astype(F32))
+    mine_ref[...] = flip(hi0)
+    both0_ref[:count], both0_ref[count:] = hi0, lo0
+    hih, loh = split(jnp.exp(sh_ref[...] - log_total))
+    hard_ref[...] = flip(hih, swapped(hih.shape[1], slots))
+    bothh_ref[:count], bothh_ref[count:] = hih, loh
+    hi1, lo1 = split(jnp.exp(s1 - log_total) - hot1.astype(F32))
+    both1_ref[:count], both1_ref[count:] = hi1, lo1
     at_target = jnp.sum(jnp.where(hot0, s0, 0.0) + jnp.where(hot1, s1, 0.0), axis=1, keepdims=True)
     loss_ref[...] = log_total - at_target
-    hi1, lo1 = split(jnp.exp(s1 - log_total) - hot1.astype(F32))
-    away = flip(hi1)
-
-    def send(cols):
-        away_ref[:, cols] = dot(away, q_ref[:, cols]).astype(BF16)
-
-    over_columns(width, send)
-    both1_ref[:count], both1_ref[count:] = hi1, lo1
-    hi0, lo0 = split(jnp.exp(s0 - log_total) - hot0.astype(F32))
-    both0_ref[:count], both0_ref[count:] = hi0, lo0
-    mine_ref[...] = flip(hi0)
-    hih, loh = split(jnp.exp(sh - log_total))
-    bothh_ref[:count], bothh_ref[count:] = hih, loh
-    hard_ref[...] = flip(hih)
-
-
-def core_sum_kernel(coef_ref, q_ref, away_ref, own_ref, *sent_refs):
-    n = own_ref.shape[0]
+
+
+def core_sum_kernel(first, coef_ref, q_ref, away_ref, *out_refs):
+    n = out_refs[0].shape[0]
+    coef = coef_ref[...]
+    coef = coef[n : 3 * n] if first else jnp.concatenate([coef[:n], coef[3 * n :]], axis=0)
 
     def add(cols):
-        total = dot(coef_ref[...], q_ref[:, cols]) + away_ref[:, cols].astype(F32)
-        own_ref[:, cols] = total[:n]
-        for d, ref in enumerate(sent_refs):
-            ref[:, cols] = total[(d + 1) * n : (d + 2) * n].astype(BF16)
+        total = dot(coef, q_ref[:, cols]) + away_ref[:, cols].astype(F32)
+        for i, ref in enumerate(out_refs):
+            ref[:, cols] = total[i * n : (i + 1) * n].astype(ref.dtype)
 
     over_columns(q_ref.shape[1], add)
 
@@ -197,13 +228,13 @@
         z_rows = jnp.concatenate(exchange([own] * NZ, "blk", z_shift), axis=0)
     with jax.named_scope("hard_out"):
         packed, placing = call(
-            functools.partial(pack_kernel, groups, slots),
+            functools.partial(pack_kernel, slots),
             [shape((places, width + FLAG)), shape((places, owned_hard.shape[0]))],
             (hard_dest.reshape(1, -1), owned_hard),
             "pack", 2 * places * owned_hard.size, 2, 0,
         )
         from_y = swap(packed, Y_GROUPS)
-        received = swap(turn(from_y, NY, NH), H_GROUPS)
+        received = swap(turn(from_y, slots), H_GROUPS)
     with jax.named_scope("gather_x"):
         last, _ = lax.optimization_barrier((z_rows, from_y))
         near = exchange([z_rows] * (NX - 1) + [last], "blk", x_shift)
@@ -224,34 +255,48 @@
             (q, *near),
             "near", 2 * count * half * width, 8, 0,
         )
-        away, mine_rows, hard_cols, both0, both1, both_hard, loss_rows = call(
-            functools.partial(coef_kernel, scale),
+        first, second, s1, sh, log_total = call(
+            functools.partial(away_kernel, scale),
             [
-                shape((half, width)), shape((half, count)), shape((places, count)),
-                shape((2 * count, half)), shape((2 * count, half)), shape((2 * count, places)),
-                shape((count, 1), F32),
+                shape((half // 2, width)), shape((half // 2, width)), shape((count, half), F32),
+                shape((count, places), F32), shape((count, 1), F32),
             ],
             (q, *far, received, s0, column.reshape(-1, 1)),
-            "coef", 4 * count * half * width, 12, 0,
+            "away", 4 * count * half * width, 12, 0,
+        )
+        mine_rows, hard_cols, both0, both1, both_hard, loss_rows = call(
+            functools.partial(coef_kernel, slots),
+            [
+                shape((half, count)), shape((places, count)), shape((2 * count, half)),
+                shape((2 * count, half)), shape((2 * count, places)), shape((count, 1), F32),
+            ],
+            (s0, s1, sh, log_total, column.reshape(-1, 1)),
+            "coef", count * half * half, 8, 0,
         )
     with jax.named_scope("scatter_core"):
-        away = lax.ppermute(away, "blk", CORE_SWAP)
+        first = lax.ppermute(first, "blk", CORE_SWAP)
+        second = lax.ppermute(second, "blk", CORE_SWAP)
     with jax.named_scope("scatter_x"):
         n = half // NX
-        mine = call(
-            core_sum_kernel,
-            [shape((n, width), F32)] + [shape((n, width))] * (NX - 1),
-            (mine_rows, q, away),
-            "core_sum", 2 * count * half * width, 8, 0,
-        )
-        chunks = [c.astype(F32) for c in exchange(list(mine), "blk", x_shift, -1)]
+        flops = count * half * width
+        one, two = call(
+            functools.partial(core_sum_kernel, True), [shape((n, width))] * 2,
+            (mine_rows, q, first), "core_sum_first", flops, 8, 0,
+        )
+        zero, three = call(
+            functools.partial(core_sum_kernel, False), [shape((n, width), F32), shape((n, width))],
+            (mine_rows, q, second), "core_sum_second", flops, 8, 0,
+        )
+        chunks = [c.astype(F32) for c in exchange([zero, one, two, three], "blk", x_shift, -1)]
         mine_x = pieces(functools.reduce(jnp.add, chunks), NZ)
 
-    hard_cols, both0, _ = lax.optimization_barrier((hard_cols, both0, away))
+    hard_cols, _ = lax.optimization_barrier((hard_cols, second))
     with jax.named_scope("hard_back"):
         g = (scale * dot(hard_cols, q)).astype(BF16)
-        returned = swap(turn(swap(g, H_GROUPS), NH, NY), Y_GROUPS)
+        back = turn(swap(g, Y_GROUPS), slots)
+        returned = swap(back, H_GROUPS)
         d_owned = t_dot(placing, returned).astype(BF16)
+    both0, _ = lax.optimization_barrier((both0, back))
     with jax.named_scope("d_query"):
         [d_query] = call(
             functools.partial(query_grad_kernel, scale),

time: 143 us -> 136 us (0.951)
  local copies, waits for them, and re-layouts: 10.6 us -> 2.43 us
  waiting for transfers between devices: 19.5 us -> 15.3 us
  Pallas kernels: 19.6 us -> 23.4 us
  starting transfers between devices: 83.4 us -> 85.9 us
    concatenate x2 -> x0, local copies, waits for them, and re-layouts: 5.82 us -> none  [turn(): jnp.concatenate([cut[o * inner + i] for i in range(inner) for o in range(...]
    ppermute x1 -> x2, waiting for transfers between devices: 3.76 us -> 0.01 us  [the longest x1 0.01 us: body(): second = lax.ppermute(second, 'blk', CORE_SWAP)]
    pallas_call x5 -> x9, Pallas kernels: 19.6 us -> 23.4 us  [call(): pl.pallas_call(kernel, in_specs=[pl.BlockSpec(memory_space=pltpu.SMEM)] *...]
    ppermute x12, waiting for transfers between devices: 8.79 us -> 6.54 us  [exchange(): lax.ppermute(p, axis, perm(sign * d))]
    ppermute x1 -> x2, starting transfers between devices: 5.48 us -> 7.39 us  [the longest x1 5.47 us: body(): second = lax.ppermute(second, 'blk', CORE_SWAP)]
    unnamed x24 -> x20, local copies, waits for them, and re-layouts: 4.16 us -> 2.27 us
    all_to_all x4, waiting for transfers between devices: 6.97 us -> 8.73 us  [swap(): lax.all_to_all(x, 'group', split_axis=0, concat_axis=0, axis_index_groups...]
  transfers between devices with their start and end apart: 21 -> 22, of which waited for: 5 -> 4; matrix products, arithmetic and copies ran while one was open for 9% -> 4% of each run, Pallas kernels for 8% -> 14%
where the time goes in v6:
time: 136 us; the launch traced here: 135 us
  starting transfers between devices  85.9 us (63%)
  Pallas kernels  23.4 us (17%)
  waiting for transfers between devices  15.3 us (11%)
  other arithmetic  4.45 us (3%)
  local copies, waits for them, and re-layouts  2.43 us (2%)
  matrix products  2.04 us (2%)
    ppermute x12, starting transfers between devices, exchange(): lax.ppermute(p, axis, perm(sign * d))  41.1 us
    all_to_all x4, starting transfers between devices, swap(): lax.all_to_all(x, 'group', split_axis=0, concat_axis=0, axis_index_groups...  27.6 us
    pallas_call x9, Pallas kernels, call(): pl.pallas_call(kernel, in_specs=[pl.BlockSpec(memory_space=pltpu.SMEM)] *...  23.4 us
    ppermute x4, starting transfers between devices, body(): far = [lax.ppermute(x, 'blk', CORE_SWAP) for x in near]  9.77 us
    all_to_all x4, waiting for transfers between devices, swap(): lax.all_to_all(x, 'group', split_axis=0, concat_axis=0, axis_index_groups...  8.73 us
    ppermute x12, waiting for transfers between devices, exchange(): lax.ppermute(p, axis, perm(sign * d))  6.54 us
    ppermute x1, starting transfers between devices, body(): second = lax.ppermute(second, 'blk', CORE_SWAP)  5.47 us
  transfers between devices with their start and end apart: 22, of which 4 were waited for; matrix products, arithmetic and copies ran while one was open for 4% of the time, Pallas kernels for 14%

profile of v6, /device:TPU:1, one launch (start us, length us, event | category | flops | bytes accessed | tf_op | source)
XLA Modules:
  0.0 134.5 jit_solution(18309069593809139826)
XLA Ops:
  0.6 7.2 %collective-permute-start.2 = (bf16[16,4096]{1,0:T(8,128)(2,1)}, bf16[16,4096]{1,0:T(8,128)(2,1)S(1)}, u32[]{:S(2)}, u32[]{:S(2)}) collective-permute-start(bf16[16,4096]{1,0:T(8,128)(2,1)} %bitcast.35), channel_id=1, source_target_pairs={{0,384},{16,400},{32,416},{48,432},{64,448},{80,464},{96,480},{112... | collective-permute-start | bytes 393224 | tf_op jit(solution)/shard_map/gather_z/ppermute | solution.py:30
  7.9 1.9 %collective-permute-start.1 = (bf16[16,4096]{1,0:T(8,128)(2,1)}, bf16[16,4096]{1,0:T(8,128)(2,1)S(1)}, u32[]{:S(2)}, u32[]{:S(2)}) collective-permute-start(bf16[16,4096]{1,0:T(8,128)(2,1)} %bitcast.36), channel_id=1, source_target_pairs={{0,256},{16,272},{32,288},{48,304},{64,320},{80,336},{96,352},{112... | collective-permute-start | bytes 393224 | tf_op jit(solution)/shard_map/gather_z/ppermute | solution.py:30
  9.8 2.2 %collective-permute-start = (bf16[16,4096]{1,0:T(8,128)(2,1)}, bf16[16,4096]{1,0:T(8,128)(2,1)S(1)}, u32[]{:S(2)}, u32[]{:S(2)}) collective-permute-start(bf16[16,4096]{1,0:T(8,128)(2,1)} %bitcast.37), channel_id=1, source_target_pairs={{0,128},{16,144},{32,160},{48,176},{64,192},{80,208},{96,224},{112... | collective-permute-start | bytes 393224 | tf_op jit(solution)/shard_map/gather_z/ppermute | solution.py:30
  12.0 0.9 copy-done.3
  12.9 0.7 copy-done.4
  13.6 1.0 pack.1
  14.6 4.2 %all-to-all-start = ((bf16[4,8,4224]{2,1,0:T(8,128)(2,1)}), bf16[4,8,4224]{2,1,0:T(8,128)(2,1)S(1)}, u32[]{:S(2)}, u32[]{:S(2)}) async-start(bf16[4,8,4224]{2,1,0:T(8,128)(2,1)} %bitcast.4), calls=%async_computation | async-start | bytes 540672 | tf_op jit(solution)/shard_map/hard_out/all_to_all | solution.py:56
  18.8 0.0 collective-permute-done.2
  18.8 0.0 collective-permute-done.1
  18.8 0.0 collective-permute-done
  18.8 0.9 pad_maximum_fusion.refs_0_
  19.7 6.3 %collective-permute-start.4 = (bf16[64,4096]{1,0:T(8,128)(2,1)S(1)}, bf16[64,4096]{1,0:T(8,128)(2,1)}, u32[]{:S(2)}, u32[]{:S(2)}) collective-permute-start(bf16[64,4096]{1,0:T(8,128)(2,1)S(1)} %pad_maximum_fusion.refs_0_), channel_id=1, source_target_pairs={{0,64},{16,80},{32,96},{48,112},{64,0},{80,16},{96,32},{112,48},{1... | collective-permute-start | bytes 1572872 | tf_op jit(solution)/shard_map/gather_x/ppermute | solution.py:30
  26.1 2.2 %collective-permute-start.3 = (bf16[64,4096]{1,0:T(8,128)(2,1)S(1)}, bf16[64,4096]{1,0:T(8,128)(2,1)}, u32[]{:S(2)}, u32[]{:S(2)}) collective-permute-start(bf16[64,4096]{1,0:T(8,128)(2,1)S(1)} %pad_maximum_fusion.refs_0_), channel_id=1, source_target_pairs={{0,32},{16,48},{32,64},{48,80},{64,96},{80,112},{96,0},{112,16},{1... | collective-permute-start | bytes 1572872 | tf_op jit(solution)/shard_map/gather_x/ppermute | solution.py:30
  28.3 0.0 all-to-all-done
  28.3 4.3 %collective-permute-start.5 = (bf16[64,4096]{1,0:T(8,128)(2,1)S(1)}, bf16[64,4096]{1,0:T(8,128)(2,1)}, u32[]{:S(2)}, u32[]{:S(2)}) collective-permute-start(bf16[64,4096]{1,0:T(8,128)(2,1)S(1)} %pad_maximum_fusion.refs_0_), channel_id=1, source_target_pairs={{0,96},{16,112},{32,0},{48,16},{64,32},{80,48},{96,64},{112,80},{1... | collective-permute-start | bytes 1572872 | tf_op jit(solution)/shard_map/gather_x/ppermute | solution.py:30
  32.6 0.9 turn.2
  33.5 13.1 %all-to-all-start.1 = ((bf16[4,8,4224]{2,1,0:T(8,128)(2,1)}), bf16[4,8,4224]{2,1,0:T(8,128)(2,1)S(1)}, u32[]{:S(2)}, u32[]{:S(2)}) async-start(bf16[4,8,4224]{2,1,0:T(8,128)(2,1)} %bitcast.6), calls=%async_computation.1 | async-start | bytes 540672 | tf_op jit(solution)/shard_map/hard_out/all_to_all | solution.py:56
  46.6 3.5 %collective-permute-start.6 = (bf16[64,4096]{1,0:T(8,128)(2,1)S(1)}, bf16[64,4096]{1,0:T(8,128)(2,1)}, u32[]{:S(2)}, u32[]{:S(2)}) collective-permute-start(bf16[64,4096]{1,0:T(8,128)(2,1)S(1)} %pad_maximum_fusion.refs_0_), channel_id=1, source_target_pairs={{0,16},{16,0},{32,48},{48,32},{64,80},{80,64},{96,112},{112,96},{1... | collective-permute-start | bytes 1572872 | tf_op jit(solution)/shard_map/gather_core/ppermute | solution.py:242
  50.1 0.0 collective-permute-done.4.refs_2_
  50.1 1.9 %collective-permute-start.8 = (bf16[64,4096]{1,0:T(8,128)(2,1)}, bf16[64,4096]{1,0:T(8,128)(2,1)}, u32[]{:S(2)}, u32[]{:S(2)}) collective-permute-start(bf16[64,4096]{1,0:T(8,128)(2,1)} %collective-permute-done.4.refs_2_), channel_id=1, source_target_pairs={{0,16},{16,0},{32,48},{48,32},{64,80},{80,64},{96,112},{112,96},{1... | collective-permute-start | bytes 1572872 | tf_op jit(solution)/shard_map/gather_core/ppermute | solution.py:242
  52.1 0.0 collective-permute-done.3.refs_1_
  52.1 2.4 %collective-permute-start.7 = (bf16[64,4096]{1,0:T(8,128)(2,1)}, bf16[64,4096]{1,0:T(8,128)(2,1)}, u32[]{:S(2)}, u32[]{:S(2)}) collective-permute-start(bf16[64,4096]{1,0:T(8,128)(2,1)} %collective-permute-done.3.refs_1_), channel_id=1, source_target_pairs={{0,16},{16,0},{32,48},{48,32},{64,80},{80,64},{96,112},{112,96},{1... | collective-permute-start | bytes 1572872 | tf_op jit(solution)/shard_map/gather_core/ppermute | solution.py:242
  54.5 0.0 collective-permute-done.5.refs_3_
  54.5 1.9 %collective-permute-start.9 = (bf16[64,4096]{1,0:T(8,128)(2,1)}, bf16[64,4096]{1,0:T(8,128)(2,1)}, u32[]{:S(2)}, u32[]{:S(2)}) collective-permute-start(bf16[64,4096]{1,0:T(8,128)(2,1)} %collective-permute-done.5.refs_3_), channel_id=1, source_target_pairs={{0,16},{16,0},{32,48},{48,32},{64,80},{80,64},{96,112},{112,96},{1... | collective-permute-start | bytes 1572872 | tf_op jit(solution)/shard_map/gather_core/ppermute | solution.py:242
  56.5 0.1 copy.9
  56.6 0.5 fusion.16.column_ref
  57.1 2.1 %near.1.s0_ref = f32[256,256]{1,0:T(8,128)S(1)} custom-call(bf16[256,4096]{1,0:T(8,128)(2,1)S(1)} %bitcast.25, bf16[64,4096]{1,0:T(8,128)(2,1)S(1)} %pad_maximum_fusion.refs_0_, bf16[64,4096]{1,0:T(8,128)(2,1)} %collective-permute-done.3.refs_1_, bf16[64,4096]{1,0:T(8,128)(2,1)} %collective-permute-done.4.refs_2_, ...), custom_call_target="tpu_custom_call" | custom-call | flops 536870912 | bytes 4456448 | tf_op jit(solution)/shard_map/scores/near/pallas_call | solution.py:71
  59.2 0.0 collective-permute-done.6.far0.refs_4_
  59.2 3.5 %all-to-all-done.1 = bf16[4,8,4224]{2,1,0:T(8,128)(2,1)S(1)} async-done(((bf16[4,8,4224]{2,1,0:T(8,128)(2,1)}), bf16[4,8,4224]{2,1,0:T(8,128)(2,1)S(1)}, u32[]{:S(2)}, u32[]{:S(2)}) %all-to-all-start.1) | async-done | bytes 270368 | tf_op jit(solution)/shard_map/hard_out/all_to_all | solution.py:56
  62.7 0.0 collective-permute-done.8.far2.refs_6_
  62.7 0.0 collective-permute-done.7.far1.refs_5_
  62.7 0.0 collective-permute-done.9.far3.refs_7_
  62.7 5.1 %away.1 = (bf16[128,4096]{1,0:T(8,128)(2,1)S(1)}, bf16[128,4096]{1,0:T(8,128)(2,1)S(1)}, f32[256,256]{1,0:T(8,128)S(1)}, f32[256,32]{1,0:T(8,128)S(1)}, f32[256,1]{1,0:T(8,128)S(1)}) custom-call(bf16[256,4096]{1,0:T(8,128)(2,1)S(1)} %bitcast.26, bf16[64,4096]{1,0:T(8,128)(2,1)} %collective-permute-done.6.far0.refs_4_, ...), custom_call_target="tpu_custom_call" | custom-call | flops 1073741824 | bytes 7120896 | tf_op jit(solution)/shard_map/scores/away/pallas_call | solution.py:71
  67.9 5.5 %collective-permute-start.10 = (bf16[128,4096]{1,0:T(8,128)(2,1)S(1)}, bf16[128,4096]{1,0:T(8,128)(2,1)S(1)}, u32[]{:S(2)}, u32[]{:S(2)}) collective-permute-start(bf16[128,4096]{1,0:T(8,128)(2,1)S(1)} %get-tuple-element.32), channel_id=1, source_target_pairs={{0,16},{16,0},{32,48},{48,32},{64,80},{80,64},{96,112},{112,96},{1... | collective-permute-start | bytes 3145736 | tf_op jit(solution)/shard_map/scatter_core/ppermute | solution.py:278
  73.3 1.9 %collective-permute-start.11 = (bf16[128,4096]{1,0:T(8,128)(2,1)S(1)}, bf16[128,4096]{1,0:T(8,128)(2,1)S(1)}, u32[]{:S(2)}, u32[]{:S(2)}) collective-permute-start(bf16[128,4096]{1,0:T(8,128)(2,1)S(1)} %get-tuple-element.39), channel_id=1, source_target_pairs={{0,16},{16,0},{32,48},{48,32},{64,80},{80,64},{96,112},{112,96},{1... | collective-permute-start | bytes 3145736 | tf_op jit(solution)/shard_map/scatter_core/ppermute | solution.py:277
  75.3 0.5 coef.1
  75.8 0.7 copy-done.7
  76.5 0.0 collective-permute-done.10.away_ref
  76.5 2.3 %core_sum_second.1 = (f32[64,4096]{1,0:T(8,128)S(1)}, bf16[64,4096]{1,0:T(8,128)(2,1)}) custom-call(bf16[256,256]{1,0:T(8,128)(2,1)S(1)} %get-tuple-element.37.coef_ref, bf16[256,4096]{1,0:T(8,128)(2,1)S(1)} %bitcast.27, bf16[128,4096]{1,0:T(8,128)(2,1)S(1)} %collective-permute-done.10.away_ref), custom_call_target="tpu_custom_call" | custom-call | flops 268435456 | bytes 4849664 | tf_op jit(solution)/shard_map/scatter_x/core_sum_second/pallas_call | solution.py:71
  78.8 1.9 %collective-permute-start.14 = (bf16[64,4096]{1,0:T(8,128)(2,1)}, bf16[64,4096]{1,0:T(8,128)(2,1)}, u32[]{:S(2)}, u32[]{:S(2)}) collective-permute-start(bf16[64,4096]{1,0:T(8,128)(2,1)} %get-tuple-element.42), channel_id=1, source_target_pairs={{0,32},{16,48},{32,64},{48,80},{64,96},{80,112},{96,0},{112,16},{1... | collective-permute-start | bytes 1572872 | tf_op jit(solution)/shard_map/scatter_x/ppermute | solution.py:30
  80.7 0.0 collective-permute-done.11.away_ref
  80.7 2.5 %core_sum_first.1 = (bf16[64,4096]{1,0:T(8,128)(2,1)}, bf16[64,4096]{1,0:T(8,128)(2,1)}) custom-call(bf16[256,256]{1,0:T(8,128)(2,1)S(1)} %get-tuple-element.37.coef_ref, bf16[256,4096]{1,0:T(8,128)(2,1)S(1)} %bitcast.28, bf16[128,4096]{1,0:T(8,128)(2,1)S(1)} %collective-permute-done.11.away_ref), custom_call_target="tpu_custom_call" | custom-call | flops 268435456 | bytes 4325376 | tf_op jit(solution)/shard_map/scatter_x/core_sum_first/pallas_call | solution.py:71
  83.3 4.6 %collective-permute-start.12 = (bf16[64,4096]{1,0:T(8,128)(2,1)}, bf16[64,4096]{1,0:T(8,128)(2,1)}, u32[]{:S(2)}, u32[]{:S(2)}) collective-permute-start(bf16[64,4096]{1,0:T(8,128)(2,1)} %get-tuple-element.40), channel_id=1, source_target_pairs={{0,96},{16,112},{32,0},{48,16},{64,32},{80,48},{96,64},{112,80},{1... | collective-permute-start | bytes 1572872 | tf_op jit(solution)/shard_map/scatter_x/ppermute | solution.py:30
  87.8 1.9 %collective-permute-start.13 = (bf16[64,4096]{1,0:T(8,128)(2,1)}, bf16[64,4096]{1,0:T(8,128)(2,1)}, u32[]{:S(2)}, u32[]{:S(2)}) collective-permute-start(bf16[64,4096]{1,0:T(8,128)(2,1)} %get-tuple-element.41), channel_id=1, source_target_pairs={{0,64},{16,80},{32,96},{48,112},{64,0},{80,16},{96,32},{112,48},{1... | collective-permute-start | bytes 1572872 | tf_op jit(solution)/shard_map/scatter_x/ppermute | solution.py:30
  89.8 1.2 fusion.1
  90.9 4.4 %all-to-all-start.2 = ((bf16[4,8,4096]{2,1,0:T(8,128)(2,1)}), bf16[4,8,4096]{2,1,0:T(8,128)(2,1)S(1)}, u32[]{:S(2)}, u32[]{:S(2)}) async-start(bf16[4,8,4096]{2,1,0:T(8,128)(2,1)} %fusion.1), calls=%async_computation.2 | async-start | bytes 524288 | tf_op jit(solution)/shard_map/hard_back/all_to_all | solution.py:56
  95.4 0.7 reduce
  96.1 5.3 %all-to-all-done.2 = bf16[4,8,4096]{2,1,0:T(8,128)(2,1)S(1)} async-done(((bf16[4,8,4096]{2,1,0:T(8,128)(2,1)}), bf16[4,8,4096]{2,1,0:T(8,128)(2,1)S(1)}, u32[]{:S(2)}, u32[]{:S(2)}) %all-to-all-start.2) | async-done | bytes 262176 | tf_op jit(solution)/shard_map/hard_back/all_to_all | solution.py:56
  101.3 0.9 turn.3
  102.2 5.9 %all-to-all-start.3 = ((bf16[4,8,4096]{2,1,0:T(8,128)(2,1)}), bf16[4,8,4096]{2,1,0:T(8,128)(2,1)S(1)}, u32[]{:S(2)}, u32[]{:S(2)}) async-start(bf16[4,8,4096]{2,1,0:T(8,128)(2,1)} %bitcast.12), calls=%async_computation.3 | async-start | bytes 524288 | tf_op jit(solution)/shard_map/hard_back/all_to_all | solution.py:56
  108.1 0.0 collective-permute-done.14
  108.1 0.0 collective-permute-done.12
  108.1 0.0 collective-permute-done.13
  108.2 1.6 %fusion.25 = (bf16[64,4096]{1,0:T(8,128)(2,1)S(1)}, f32[64,4096]{1,0:T(8,128)S(1)}) fusion(bf16[64,4096]{1,0:T(8,128)(2,1)} %collective-permute-done.14, bf16[64,4096]{1,0:T(8,128)(2,1)} %collective-permute-done.13, f32[64,4096]{1,0:T(8,128)S(1)} %copy-done.2, bf16[64,4096]{1,0:T(8,128)(2,1)} %collective-permute-done.12), kind=kLoop, calls=%fused_computation.54 | loop fusion | flops 1835008 | bytes 4194304 | tf_op jit(solution)/shard_map/convert.2
  109.8 3.3 %collective-permute-start.15 = (bf16[16,4096]{1,0:T(8,128)(2,1)S(1)}, bf16[16,4096]{1,0:T(8,128)(2,1)S(1)}, u32[]{:S(2)}, u32[]{:S(2)}) collective-permute-start(bf16[16,4096]{1,0:T(8,128)(2,1)S(1)} %get-tuple-element.46), channel_id=1, source_target_pairs={{0,384},{16,400},{32,416},{48,432},{64,448},{80,464},{96,480},{112... | collective-permute-start | bytes 393224 | tf_op jit(solution)/shard_map/scatter_z/ppermute | solution.py:30
  113.2 1.9 %collective-permute-start.17 = (bf16[16,4096]{1,0:T(8,128)(2,1)S(1)}, bf16[16,4096]{1,0:T(8,128)(2,1)S(1)}, u32[]{:S(2)}, u32[]{:S(2)}) collective-permute-start(bf16[16,4096]{1,0:T(8,128)(2,1)S(1)} %get-tuple-element.47), channel_id=1, source_target_pairs={{0,128},{16,144},{32,160},{48,176},{64,192},{80,208},{96,224},{112... | collective-permute-start | bytes 393224 | tf_op jit(solution)/shard_map/scatter_z/ppermute | solution.py:30
  115.1 3.3 %collective-permute-start.16 = (bf16[16,4096]{1,0:T(8,128)(2,1)S(1)}, bf16[16,4096]{1,0:T(8,128)(2,1)S(1)}, u32[]{:S(2)}, u32[]{:S(2)}) collective-permute-start(bf16[16,4096]{1,0:T(8,128)(2,1)S(1)} %get-tuple-element.48), channel_id=1, source_target_pairs={{0,256},{16,272},{32,288},{48,304},{64,320},{80,336},{96,352},{112... | collective-permute-start | bytes 393224 | tf_op jit(solution)/shard_map/scatter_z/ppermute | solution.py:30
  118.5 7.9 %query_grad.1 = bf16[1,256,4096]{2,1,0:T(8,128)(2,1)} custom-call(bf16[512,256]{1,0:T(8,128)(2,1)S(1)} %copy-done.6, bf16[512,256]{1,0:T(8,128)(2,1)S(1)} %copy-done.8, bf16[512,32]{1,0:T(8,128)(2,1)S(1)} %get-tuple-element.36.ch, bf16[64,4096]{1,0:T(8,128)(2,1)S(1)} %pad_maximum_fusion.refs_0_, bf16[64,4096]{1,0:T(8,128)(2,1)} %collective-permute-done.3.refs_1_, ...), custom_call_target="tpu_custom_call" | custom-call | flops 2281701376 | bytes 7118848 | tf_op jit(solution)/shard_map/d_query/query_grad/pallas_call | solution.py:71
  126.4 0.0 collective-permute-done.15
  126.4 0.4 collective-permute-done.17
  126.9 6.1 %collective-permute-done.16 = bf16[16,4096]{1,0:T(8,128)(2,1)S(1)} collective-permute-done((bf16[16,4096]{1,0:T(8,128)(2,1)S(1)}, bf16[16,4096]{1,0:T(8,128)(2,1)S(1)}, u32[]{:S(2)}, u32[]{:S(2)}) %collective-permute-start.16) | collective-permute-done | bytes 131104 | tf_op jit(solution)/shard_map/scatter_z/ppermute | solution.py:30
  132.9 0.7 fusion.20
  133.7 0.0 all-to-all-done.3
  133.7 0.9 fusion.2
  (18 shorter events, 0.1 us)
Async XLA Ops:
  0.6 56.5 %copy-start = (bf16[1,256,4096]{2,1,0:T(8,128)(2,1)S(1)}, bf16[1,256,4096]{2,1,0:T(8,128)(2,1)}, u32[]{:S(2)}) copy-start(bf16[1,256,4096]{2,1,0:T(8,128)(2,1)} %param.5) | copy-start | bytes 6291460
  0.6 18.1 %collective-permute-start.2 = (bf16[16,4096]{1,0:T(8,128)(2,1)}, bf16[16,4096]{1,0:T(8,128)(2,1)S(1)}, u32[]{:S(2)}, u32[]{:S(2)}) collective-permute-start(bf16[16,4096]{1,0:T(8,128)(2,1)} %bitcast.35), channel_id=1, source_target_pairs={{0,384},{16,400},{32,416},{48,432},{64,448},{80,464},{96,480},{112... | collective-permute-start | bytes 393224 | tf_op jit(solution)/shard_map/gather_z/ppermute | solution.py:30
  7.9 10.9 %collective-permute-start.1 = (bf16[16,4096]{1,0:T(8,128)(2,1)}, bf16[16,4096]{1,0:T(8,128)(2,1)S(1)}, u32[]{:S(2)}, u32[]{:S(2)}) collective-permute-start(bf16[16,4096]{1,0:T(8,128)(2,1)} %bitcast.36), channel_id=1, source_target_pairs={{0,256},{16,272},{32,288},{48,304},{64,320},{80,336},{96,352},{112... | collective-permute-start | bytes 393224 | tf_op jit(solution)/shard_map/gather_z/ppermute | solution.py:30
  9.8 9.0 %collective-permute-start = (bf16[16,4096]{1,0:T(8,128)(2,1)}, bf16[16,4096]{1,0:T(8,128)(2,1)S(1)}, u32[]{:S(2)}, u32[]{:S(2)}) collective-permute-start(bf16[16,4096]{1,0:T(8,128)(2,1)} %bitcast.37), channel_id=1, source_target_pairs={{0,128},{16,144},{32,160},{48,176},{64,192},{80,208},{96,224},{112... | collective-permute-start | bytes 393224 | tf_op jit(solution)/shard_map/gather_z/ppermute | solution.py:30
  12.0 0.9 copy-start.3
  12.9 0.7 copy-start.4
  13.6 42.9 %copy-start.9 = (s32[1,256]{1,0:T(1,128)S(1)}, s32[1,256]{1,0:T(1,128)}, u32[]{:S(2)}) copy-start(s32[1,256]{1,0:T(1,128)} %param.7) | copy-start | bytes 3076
  14.6 13.7 %all-to-all-start = ((bf16[4,8,4224]{2,1,0:T(8,128)(2,1)}), bf16[4,8,4224]{2,1,0:T(8,128)(2,1)S(1)}, u32[]{:S(2)}, u32[]{:S(2)}) async-start(bf16[4,8,4224]{2,1,0:T(8,128)(2,1)} %bitcast.4), calls=%async_computation | async-start | bytes 540672 | tf_op jit(solution)/shard_map/hard_out/all_to_all | solution.py:56
  19.7 30.4 %collective-permute-start.4 = (bf16[64,4096]{1,0:T(8,128)(2,1)S(1)}, bf16[64,4096]{1,0:T(8,128)(2,1)}, u32[]{:S(2)}, u32[]{:S(2)}) collective-permute-start(bf16[64,4096]{1,0:T(8,128)(2,1)S(1)} %pad_maximum_fusion.refs_0_), channel_id=1, source_target_pairs={{0,64},{16,80},{32,96},{48,112},{64,0},{80,16},{96,32},{112,48},{1... | collective-permute-start | bytes 1572872 | tf_op jit(solution)/shard_map/gather_x/ppermute | solution.py:30
  26.1 26.0 %collective-permute-start.3 = (bf16[64,4096]{1,0:T(8,128)(2,1)S(1)}, bf16[64,4096]{1,0:T(8,128)(2,1)}, u32[]{:S(2)}, u32[]{:S(2)}) collective-permute-start(bf16[64,4096]{1,0:T(8,128)(2,1)S(1)} %pad_maximum_fusion.refs_0_), channel_id=1, source_target_pairs={{0,32},{16,48},{32,64},{48,80},{64,96},{80,112},{96,0},{112,16},{1... | collective-permute-start | bytes 1572872 | tf_op jit(solution)/shard_map/gather_x/ppermute | solution.py:30
  28.3 26.2 %collective-permute-start.5 = (bf16[64,4096]{1,0:T(8,128)(2,1)S(1)}, bf16[64,4096]{1,0:T(8,128)(2,1)}, u32[]{:S(2)}, u32[]{:S(2)}) collective-permute-start(bf16[64,4096]{1,0:T(8,128)(2,1)S(1)} %pad_maximum_fusion.refs_0_), channel_id=1, source_target_pairs={{0,96},{16,112},{32,0},{48,16},{64,32},{80,48},{96,64},{112,80},{1... | collective-permute-start | bytes 1572872 | tf_op jit(solution)/shard_map/gather_x/ppermute | solution.py:30
  33.5 29.2 %all-to-all-start.1 = ((bf16[4,8,4224]{2,1,0:T(8,128)(2,1)}), bf16[4,8,4224]{2,1,0:T(8,128)(2,1)S(1)}, u32[]{:S(2)}, u32[]{:S(2)}) async-start(bf16[4,8,4224]{2,1,0:T(8,128)(2,1)} %bitcast.6), calls=%async_computation.1 | async-start | bytes 540672 | tf_op jit(solution)/shard_map/hard_out/all_to_all | solution.py:56
  46.6 12.6 %collective-permute-start.6 = (bf16[64,4096]{1,0:T(8,128)(2,1)S(1)}, bf16[64,4096]{1,0:T(8,128)(2,1)}, u32[]{:S(2)}, u32[]{:S(2)}) collective-permute-start(bf16[64,4096]{1,0:T(8,128)(2,1)S(1)} %pad_maximum_fusion.refs_0_), channel_id=1, source_target_pairs={{0,16},{16,0},{32,48},{48,32},{64,80},{80,64},{96,112},{112,96},{1... | collective-permute-start | bytes 1572872 | tf_op jit(solution)/shard_map/gather_core/ppermute | solution.py:242
  50.1 12.6 %collective-permute-start.8 = (bf16[64,4096]{1,0:T(8,128)(2,1)}, bf16[64,4096]{1,0:T(8,128)(2,1)}, u32[]{:S(2)}, u32[]{:S(2)}) collective-permute-start(bf16[64,4096]{1,0:T(8,128)(2,1)} %collective-permute-done.4.refs_2_), channel_id=1, source_target_pairs={{0,16},{16,0},{32,48},{48,32},{64,80},{80,64},{96,112},{112,96},{1... | collective-permute-start | bytes 1572872 | tf_op jit(solution)/shard_map/gather_core/ppermute | solution.py:242
  52.1 10.6 %collective-permute-start.7 = (bf16[64,4096]{1,0:T(8,128)(2,1)}, bf16[64,4096]{1,0:T(8,128)(2,1)}, u32[]{:S(2)}, u32[]{:S(2)}) collective-permute-start(bf16[64,4096]{1,0:T(8,128)(2,1)} %collective-permute-done.3.refs_1_), channel_id=1, source_target_pairs={{0,16},{16,0},{32,48},{48,32},{64,80},{80,64},{96,112},{112,96},{1... | collective-permute-start | bytes 1572872 | tf_op jit(solution)/shard_map/gather_core/ppermute | solution.py:242
  54.5 8.2 %collective-permute-start.9 = (bf16[64,4096]{1,0:T(8,128)(2,1)}, bf16[64,4096]{1,0:T(8,128)(2,1)}, u32[]{:S(2)}, u32[]{:S(2)}) collective-permute-start(bf16[64,4096]{1,0:T(8,128)(2,1)} %collective-permute-done.5.refs_3_), channel_id=1, source_target_pairs={{0,16},{16,0},{32,48},{48,32},{64,80},{80,64},{96,112},{112,96},{1... | collective-permute-start | bytes 1572872 | tf_op jit(solution)/shard_map/gather_core/ppermute | solution.py:242
  67.9 8.6 %collective-permute-start.10 = (bf16[128,4096]{1,0:T(8,128)(2,1)S(1)}, bf16[128,4096]{1,0:T(8,128)(2,1)S(1)}, u32[]{:S(2)}, u32[]{:S(2)}) collective-permute-start(bf16[128,4096]{1,0:T(8,128)(2,1)S(1)} %get-tuple-element.32), channel_id=1, source_target_pairs={{0,16},{16,0},{32,48},{48,32},{64,80},{80,64},{96,112},{112,96},{1... | collective-permute-start | bytes 3145736 | tf_op jit(solution)/shard_map/scatter_core/ppermute | solution.py:278
  73.3 7.4 %collective-permute-start.11 = (bf16[128,4096]{1,0:T(8,128)(2,1)S(1)}, bf16[128,4096]{1,0:T(8,128)(2,1)S(1)}, u32[]{:S(2)}, u32[]{:S(2)}) collective-permute-start(bf16[128,4096]{1,0:T(8,128)(2,1)S(1)} %get-tuple-element.39), channel_id=1, source_target_pairs={{0,16},{16,0},{32,48},{48,32},{64,80},{80,64},{96,112},{112,96},{1... | collective-permute-start | bytes 3145736 | tf_op jit(solution)/shard_map/scatter_core/ppermute | solution.py:277
  75.8 0.7 copy-start.7
  76.4 6.8 %copy-start.5 = (bf16[512,256]{1,0:T(8,128)(2,1)}, bf16[512,256]{1,0:T(8,128)(2,1)S(1)}, u32[]{:S(2)}) copy-start(bf16[512,256]{1,0:T(8,128)(2,1)S(1)} %get-tuple-element.34.c0) | copy-start | bytes 786436
  78.8 4.5 %copy-start.1 = (f32[64,4096]{1,0:T(8,128)}, f32[64,4096]{1,0:T(8,128)S(1)}, u32[]{:S(2)}) copy-start(f32[64,4096]{1,0:T(8,128)S(1)} %get-tuple-element.38) | copy-start | bytes 3145732
  78.8 29.3 %collective-permute-start.14 = (bf16[64,4096]{1,0:T(8,128)(2,1)}, bf16[64,4096]{1,0:T(8,128)(2,1)}, u32[]{:S(2)}, u32[]{:S(2)}) collective-permute-start(bf16[64,4096]{1,0:T(8,128)(2,1)} %get-tuple-element.42), channel_id=1, source_target_pairs={{0,32},{16,48},{32,64},{48,80},{64,96},{80,112},{96,0},{112,16},{1... | collective-permute-start | bytes 1572872 | tf_op jit(solution)/shard_map/scatter_x/ppermute | solution.py:30
  83.3 24.8 %collective-permute-start.12 = (bf16[64,4096]{1,0:T(8,128)(2,1)}, bf16[64,4096]{1,0:T(8,128)(2,1)}, u32[]{:S(2)}, u32[]{:S(2)}) collective-permute-start(bf16[64,4096]{1,0:T(8,128)(2,1)} %get-tuple-element.40), channel_id=1, source_target_pairs={{0,96},{16,112},{32,0},{48,16},{64,32},{80,48},{96,64},{112,80},{1... | collective-permute-start | bytes 1572872 | tf_op jit(solution)/shard_map/scatter_x/ppermute | solution.py:30
  87.8 20.3 %collective-permute-start.13 = (bf16[64,4096]{1,0:T(8,128)(2,1)}, bf16[64,4096]{1,0:T(8,128)(2,1)}, u32[]{:S(2)}, u32[]{:S(2)}) collective-permute-start(bf16[64,4096]{1,0:T(8,128)(2,1)} %get-tuple-element.41), channel_id=1, source_target_pairs={{0,64},{16,80},{32,96},{48,112},{64,0},{80,16},{96,32},{112,48},{1... | collective-permute-start | bytes 1572872 | tf_op jit(solution)/shard_map/scatter_x/ppermute | solution.py:30
  90.9 17.2 %copy-start.2 = (f32[64,4096]{1,0:T(8,128)S(1)}, f32[64,4096]{1,0:T(8,128)}, u32[]{:S(2)}) copy-start(f32[64,4096]{1,0:T(8,128)} %copy-done.1) | copy-start | bytes 3145732
  90.9 10.4 %all-to-all-start.2 = ((bf16[4,8,4096]{2,1,0:T(8,128)(2,1)}), bf16[4,8,4096]{2,1,0:T(8,128)(2,1)S(1)}, u32[]{:S(2)}, u32[]{:S(2)}) async-start(bf16[4,8,4096]{2,1,0:T(8,128)(2,1)} %fusion.1), calls=%async_computation.2 | async-start | bytes 524288 | tf_op jit(solution)/shard_map/hard_back/all_to_all | solution.py:56
  102.2 31.4 %all-to-all-start.3 = ((bf16[4,8,4096]{2,1,0:T(8,128)(2,1)}), bf16[4,8,4096]{2,1,0:T(8,128)(2,1)S(1)}, u32[]{:S(2)}, u32[]{:S(2)}) async-start(bf16[4,8,4096]{2,1,0:T(8,128)(2,1)} %bitcast.12), calls=%async_computation.3 | async-start | bytes 524288 | tf_op jit(solution)/shard_map/hard_back/all_to_all | solution.py:56
  108.1 10.3 %copy-start.6 = (bf16[512,256]{1,0:T(8,128)(2,1)S(1)}, bf16[512,256]{1,0:T(8,128)(2,1)}, u32[]{:S(2)}) copy-start(bf16[512,256]{1,0:T(8,128)(2,1)} %copy-done.5) | copy-start | bytes 786436
  108.2 10.3 %copy-start.8 = (bf16[512,256]{1,0:T(8,128)(2,1)S(1)}, bf16[512,256]{1,0:T(8,128)(2,1)}, u32[]{:S(2)}) copy-start(bf16[512,256]{1,0:T(8,128)(2,1)} %copy-done.7) | copy-start | bytes 786436
  109.8 16.6 %collective-permute-start.15 = (bf16[16,4096]{1,0:T(8,128)(2,1)S(1)}, bf16[16,4096]{1,0:T(8,128)(2,1)S(1)}, u32[]{:S(2)}, u32[]{:S(2)}) collective-permute-start(bf16[16,4096]{1,0:T(8,128)(2,1)S(1)} %get-tuple-element.46), channel_id=1, source_target_pairs={{0,384},{16,400},{32,416},{48,432},{64,448},{80,464},{96,480},{112... | collective-permute-start | bytes 393224 | tf_op jit(solution)/shard_map/scatter_z/ppermute | solution.py:30
  113.2 13.7 %collective-permute-start.17 = (bf16[16,4096]{1,0:T(8,128)(2,1)S(1)}, bf16[16,4096]{1,0:T(8,128)(2,1)S(1)}, u32[]{:S(2)}, u32[]{:S(2)}) collective-permute-start(bf16[16,4096]{1,0:T(8,128)(2,1)S(1)} %get-tuple-element.47), channel_id=1, source_target_pairs={{0,128},{16,144},{32,160},{48,176},{64,192},{80,208},{96,224},{112... | collective-permute-start | bytes 393224 | tf_op jit(solution)/shard_map/scatter_z/ppermute | solution.py:30
  115.1 17.8 %collective-permute-start.16 = (bf16[16,4096]{1,0:T(8,128)(2,1)S(1)}, bf16[16,4096]{1,0:T(8,128)(2,1)S(1)}, u32[]{:S(2)}, u32[]{:S(2)}) collective-permute-start(bf16[16,4096]{1,0:T(8,128)(2,1)S(1)} %get-tuple-element.48), channel_id=1, source_target_pairs={{0,256},{16,272},{32,288},{48,304},{64,320},{80,336},{96,352},{112... | collective-permute-start | bytes 393224 | tf_op jit(solution)/shard_map/scatter_z/ppermute | solution.py:30

commit v7 on v6

--- a/solution.py
+++ b/solution.py
@@ -126,7 +126,7 @@
     send = (dest * slots + rank == at).astype(BF16)
     packed_ref[:, :width] = dot(send, rows_ref[...]).astype(BF16)
     packed_ref[:, width:] = dot(send, jnp.ones((count, FLAG), BF16)).astype(BF16)
-    placing_ref[...] = ((dest % NH * NY + dest // NH) * slots + rank == at).astype(BF16)
+    placing_ref[...] = send
 
 
 def near_kernel(scale, q_ref, *refs):
@@ -178,7 +178,7 @@
     both0_ref[:count], both0_ref[count:] = hi0, lo0
     hih, loh = split(jnp.exp(sh_ref[...] - log_total))
     hard_ref[...] = flip(hih, swapped(hih.shape[1], slots))
-    bothh_ref[:count], bothh_ref[count:] = hih, loh
+    bothh_ref[...] = jnp.concatenate([hih, loh], axis=1)
     hi1, lo1 = split(jnp.exp(s1 - log_total) - hot1.astype(F32))
     both1_ref[:count], both1_ref[count:] = hi1, lo1
     at_target = jnp.sum(jnp.where(hot0, s0, 0.0) + jnp.where(hot1, s1, 0.0), axis=1, keepdims=True)
@@ -198,14 +198,26 @@
     over_columns(q_ref.shape[1], add)
 
 
+def hard_grad_kernel(scale, coef_ref, q_ref, out_ref):
+    places, slots, width = out_ref.shape
+
+    def grad(cols):
+        rows = scale * dot(coef_ref[...], q_ref[:, cols])
+        for i in range(places):
+            out_ref[i, :, cols] = rows[i * slots : (i + 1) * slots].astype(out_ref.dtype)
+
+    over_columns(width, grad)
+
+
 def query_grad_kernel(scale, c0, c1, ch, *refs):
     near, far, got, out = refs[:4], refs[4:8], refs[8], refs[9]
     count = out.shape[1]
 
     def grad(cols):
         both = dot(c0[...], joined(near, cols)) + dot(c1[...], joined(far, cols))
-        both = both + dot(ch[...], got[:, cols])
-        out[0, :, cols] = (scale * (both[:count] + both[count:])).astype(out.dtype)
+        hard = got[:, cols]
+        thin = dot(ch[...], jnp.concatenate([hard, hard], axis=0))
+        out[0, :, cols] = (scale * (both[:count] + both[count:] + thin)).astype(out.dtype)
 
     over_columns(out.shape[2], grad)
 
@@ -268,7 +280,7 @@
             functools.partial(coef_kernel, slots),
             [
                 shape((half, count)), shape((places, count)), shape((2 * count, half)),
-                shape((2 * count, half)), shape((2 * count, places)), shape((count, 1), F32),
+                shape((2 * count, half)), shape((count, 2 * places)), shape((count, 1), F32),
             ],
             (s0, s1, sh, log_total, column.reshape(-1, 1)),
             "coef", count * half * half, 8, 0,
@@ -292,11 +304,13 @@
 
     hard_cols, _ = lax.optimization_barrier((hard_cols, second))
     with jax.named_scope("hard_back"):
-        g = (scale * dot(hard_cols, q)).astype(BF16)
-        back = turn(swap(g, Y_GROUPS), slots)
-        returned = swap(back, H_GROUPS)
-        d_owned = t_dot(placing, returned).astype(BF16)
-    both0, _ = lax.optimization_barrier((both0, back))
+        [g] = call(
+            functools.partial(hard_grad_kernel, scale), [shape((groups, slots, width))],
+            (hard_cols, q), "hard_grad", 2 * places * count * width, 4, 0,
+        )
+        returned = lax.all_to_all(g, "group", split_axis=0, concat_axis=0, tiled=True)
+        d_owned = t_dot(placing, returned.reshape(places, width)).astype(BF16)
+    both0, _ = lax.optimization_barrier((both0, g))
     with jax.named_scope("d_query"):
         [d_query] = call(
             functools.partial(query_grad_kernel, scale),

time: 136 us -> 135 us (level)
  the two profiles are of different devices: /device:TPU:1 before, /device:TPU:14 now
where the time goes in v7:
time: 135 us; the launch traced here: 134 us
  starting transfers between devices  82.2 us (61%)
  Pallas kernels  24 us (18%)
  waiting for transfers between devices  17.9 us (13%)
  other arithmetic  4.77 us (4%)
  local copies, waits for them, and re-layouts  3.49 us (3%)
    ppermute x12, starting transfers between devices, exchange(): lax.ppermute(p, axis, perm(sign * d))  41.8 us
    pallas_call x9, Pallas kernels, call(): pl.pallas_call(kernel, in_specs=[pl.BlockSpec(memory_space=pltpu.SMEM)] *...  24 us
    all_to_all x2, starting transfers between devices, swap(): lax.all_to_all(x, 'group', split_axis=0, concat_axis=0, axis_index_groups...  18.3 us
    ppermute x12, waiting for transfers between devices, exchange(): lax.ppermute(p, axis, perm(sign * d))  11.1 us
    all_to_all x1, starting transfers between devices, body(): lax.all_to_all(g, 'group', split_axis=0, concat_axis=0, tiled=True)  9.24 us
    ppermute x4, starting transfers between devices, body(): far = [lax.ppermute(x, 'blk', CORE_SWAP) for x in near]  8.65 us
    all_to_all x2, waiting for transfers between devices, swap(): lax.all_to_all(x, 'group', split_axis=0, concat_axis=0, axis_index_groups...  6.81 us
    unnamed x18, local copies, waits for them, and re-layouts  3.23 us
  transfers between devices with their start and end apart: 21, of which 4 were waited for; matrix products, arithmetic and copies ran while one was open for 4% of the time, Pallas kernels for 14%

profile of v7, /device:TPU:14, one launch (start us, length us, event | category | flops | bytes accessed | tf_op | source)
XLA Modules:
  0.0 134.3 jit_solution(6943754354533253312)
XLA Ops:
  0.6 6.7 %collective-permute-start.2 = (bf16[16,4096]{1,0:T(8,128)(2,1)}, bf16[16,4096]{1,0:T(8,128)(2,1)S(1)}, u32[]{:S(2)}, u32[]{:S(2)}) collective-permute-start(bf16[16,4096]{1,0:T(8,128)(2,1)} %bitcast.26), channel_id=1, source_target_pairs={{0,384},{16,400},{32,416},{48,432},{64,448},{80,464},{96,480},{112... | collective-permute-start | bytes 393224 | tf_op jit(solution)/shard_map/gather_z/ppermute | solution.py:30
  7.3 1.9 %collective-permute-start.1 = (bf16[16,4096]{1,0:T(8,128)(2,1)}, bf16[16,4096]{1,0:T(8,128)(2,1)S(1)}, u32[]{:S(2)}, u32[]{:S(2)}) collective-permute-start(bf16[16,4096]{1,0:T(8,128)(2,1)} %bitcast.27), channel_id=1, source_target_pairs={{0,256},{16,272},{32,288},{48,304},{64,320},{80,336},{96,352},{112... | collective-permute-start | bytes 393224 | tf_op jit(solution)/shard_map/gather_z/ppermute | solution.py:30
  9.2 2.6 %collective-permute-start = (bf16[16,4096]{1,0:T(8,128)(2,1)}, bf16[16,4096]{1,0:T(8,128)(2,1)S(1)}, u32[]{:S(2)}, u32[]{:S(2)}) collective-permute-start(bf16[16,4096]{1,0:T(8,128)(2,1)} %bitcast.28), channel_id=1, source_target_pairs={{0,128},{16,144},{32,160},{48,176},{64,192},{80,208},{96,224},{112... | collective-permute-start | bytes 393224 | tf_op jit(solution)/shard_map/gather_z/ppermute | solution.py:30
  11.8 0.0 copy-start.2
  11.8 0.9 copy-done.2
  12.7 0.7 copy-done.3
  13.4 1.0 pack.1
  14.4 4.9 %all-to-all-start = ((bf16[4,8,4224]{2,1,0:T(8,128)(2,1)}), bf16[4,8,4224]{2,1,0:T(8,128)(2,1)S(1)}, u32[]{:S(2)}, u32[]{:S(2)}) async-start(bf16[4,8,4224]{2,1,0:T(8,128)(2,1)} %bitcast.4), calls=%async_computation | async-start | bytes 540672 | tf_op jit(solution)/shard_map/hard_out/all_to_all | solution.py:56
  19.3 0.0 collective-permute-done.2
  19.3 0.1 collective-permute-done.1
  19.4 0.0 collective-permute-done
  19.4 0.9 pad_maximum_fusion.refs_0_
  20.4 3.3 %collective-permute-start.4 = (bf16[64,4096]{1,0:T(8,128)(2,1)S(1)}, bf16[64,4096]{1,0:T(8,128)(2,1)}, u32[]{:S(2)}, u32[]{:S(2)}) collective-permute-start(bf16[64,4096]{1,0:T(8,128)(2,1)S(1)} %pad_maximum_fusion.refs_0_), channel_id=1, source_target_pairs={{0,64},{16,80},{32,96},{48,112},{64,0},{80,16},{96,32},{112,48},{1... | collective-permute-start | bytes 1572872 | tf_op jit(solution)/shard_map/gather_x/ppermute | solution.py:30
  23.7 4.0 %collective-permute-start.3 = (bf16[64,4096]{1,0:T(8,128)(2,1)S(1)}, bf16[64,4096]{1,0:T(8,128)(2,1)}, u32[]{:S(2)}, u32[]{:S(2)}) collective-permute-start(bf16[64,4096]{1,0:T(8,128)(2,1)S(1)} %pad_maximum_fusion.refs_0_), channel_id=1, source_target_pairs={{0,32},{16,48},{32,64},{48,80},{64,96},{80,112},{96,0},{112,16},{1... | collective-permute-start | bytes 1572872 | tf_op jit(solution)/shard_map/gather_x/ppermute | solution.py:30
  27.7 0.0 all-to-all-done
  27.7 1.9 %collective-permute-start.5 = (bf16[64,4096]{1,0:T(8,128)(2,1)S(1)}, bf16[64,4096]{1,0:T(8,128)(2,1)}, u32[]{:S(2)}, u32[]{:S(2)}) collective-permute-start(bf16[64,4096]{1,0:T(8,128)(2,1)S(1)} %pad_maximum_fusion.refs_0_), channel_id=1, source_target_pairs={{0,96},{16,112},{32,0},{48,16},{64,32},{80,48},{96,64},{112,80},{1... | collective-permute-start | bytes 1572872 | tf_op jit(solution)/shard_map/gather_x/ppermute | solution.py:30
  29.7 0.9 turn.1
  30.6 13.4 %all-to-all-start.1 = ((bf16[4,8,4224]{2,1,0:T(8,128)(2,1)}), bf16[4,8,4224]{2,1,0:T(8,128)(2,1)S(1)}, u32[]{:S(2)}, u32[]{:S(2)}) async-start(bf16[4,8,4224]{2,1,0:T(8,128)(2,1)} %bitcast.6), calls=%async_computation.1 | async-start | bytes 540672 | tf_op jit(solution)/shard_map/hard_out/all_to_all | solution.py:56
  44.0 1.9 %collective-permute-start.6 = (bf16[64,4096]{1,0:T(8,128)(2,1)S(1)}, bf16[64,4096]{1,0:T(8,128)(2,1)}, u32[]{:S(2)}, u32[]{:S(2)}) collective-permute-start(bf16[64,4096]{1,0:T(8,128)(2,1)S(1)} %pad_maximum_fusion.refs_0_), channel_id=1, source_target_pairs={{0,16},{16,0},{32,48},{48,32},{64,80},{80,64},{96,112},{112,96},{1... | collective-permute-start | bytes 1572872 | tf_op jit(solution)/shard_map/gather_core/ppermute | solution.py:254
  45.9 0.0 collective-permute-done.4.refs_2_
  45.9 2.4 %collective-permute-start.8 = (bf16[64,4096]{1,0:T(8,128)(2,1)}, bf16[64,4096]{1,0:T(8,128)(2,1)}, u32[]{:S(2)}, u32[]{:S(2)}) collective-permute-start(bf16[64,4096]{1,0:T(8,128)(2,1)} %collective-permute-done.4.refs_2_), channel_id=1, source_target_pairs={{0,16},{16,0},{32,48},{48,32},{64,80},{80,64},{96,112},{112,96},{1... | collective-permute-start | bytes 1572872 | tf_op jit(solution)/shard_map/gather_core/ppermute | solution.py:254
  48.3 0.0 collective-permute-done.3.refs_1_
  48.3 1.9 %collective-permute-start.7 = (bf16[64,4096]{1,0:T(8,128)(2,1)}, bf16[64,4096]{1,0:T(8,128)(2,1)}, u32[]{:S(2)}, u32[]{:S(2)}) collective-permute-start(bf16[64,4096]{1,0:T(8,128)(2,1)} %collective-permute-done.3.refs_1_), channel_id=1, source_target_pairs={{0,16},{16,0},{32,48},{48,32},{64,80},{80,64},{96,112},{112,96},{1... | collective-permute-start | bytes 1572872 | tf_op jit(solution)/shard_map/gather_core/ppermute | solution.py:254
  50.3 0.0 collective-permute-done.5.refs_3_
  50.3 2.4 %collective-permute-start.9 = (bf16[64,4096]{1,0:T(8,128)(2,1)}, bf16[64,4096]{1,0:T(8,128)(2,1)}, u32[]{:S(2)}, u32[]{:S(2)}) collective-permute-start(bf16[64,4096]{1,0:T(8,128)(2,1)} %collective-permute-done.5.refs_3_), channel_id=1, source_target_pairs={{0,16},{16,0},{32,48},{48,32},{64,80},{80,64},{96,112},{112,96},{1... | collective-permute-start | bytes 1572872 | tf_op jit(solution)/shard_map/gather_core/ppermute | solution.py:254
  52.7 0.1 copy.9
  52.9 0.5 fusion.13.column_ref
  53.4 2.1 %near.1.s0_ref = f32[256,256]{1,0:T(8,128)S(1)} custom-call(bf16[256,4096]{1,0:T(8,128)(2,1)S(1)} %bitcast.16, bf16[64,4096]{1,0:T(8,128)(2,1)S(1)} %pad_maximum_fusion.refs_0_, bf16[64,4096]{1,0:T(8,128)(2,1)} %collective-permute-done.3.refs_1_, bf16[64,4096]{1,0:T(8,128)(2,1)} %collective-permute-done.4.refs_2_, ...), custom_call_target="tpu_custom_call" | custom-call | flops 536870912 | bytes 4456448 | tf_op jit(solution)/shard_map/scores/near/pallas_call | solution.py:71
  55.5 0.0 collective-permute-done.6.far0.refs_4_
  55.5 6.8 %all-to-all-done.1 = bf16[4,8,4224]{2,1,0:T(8,128)(2,1)S(1)} async-done(((bf16[4,8,4224]{2,1,0:T(8,128)(2,1)}), bf16[4,8,4224]{2,1,0:T(8,128)(2,1)S(1)}, u32[]{:S(2)}, u32[]{:S(2)}) %all-to-all-start.1) | async-done | bytes 270368 | tf_op jit(solution)/shard_map/hard_out/all_to_all | solution.py:56
  62.3 0.0 collective-permute-done.8.far2.refs_6_
  62.3 0.0 collective-permute-done.7.far1.refs_5_
  62.3 0.0 collective-permute-done.9.far3.refs_7_
  62.3 5.1 %away.1 = (bf16[128,4096]{1,0:T(8,128)(2,1)S(1)}, bf16[128,4096]{1,0:T(8,128)(2,1)S(1)}, f32[256,256]{1,0:T(8,128)S(1)}, f32[256,32]{1,0:T(8,128)S(1)}, f32[256,1]{1,0:T(8,128)S(1)}) custom-call(bf16[256,4096]{1,0:T(8,128)(2,1)S(1)} %bitcast.17, bf16[64,4096]{1,0:T(8,128)(2,1)} %collective-permute-done.6.far0.refs_4_, ...), custom_call_target="tpu_custom_call" | custom-call | flops 1073741824 | bytes 7120896 | tf_op jit(solution)/shard_map/scores/away/pallas_call | solution.py:71
  67.4 1.9 %collective-permute-start.10 = (bf16[128,4096]{1,0:T(8,128)(2,1)S(1)}, bf16[128,4096]{1,0:T(8,128)(2,1)S(1)}, u32[]{:S(2)}, u32[]{:S(2)}) collective-permute-start(bf16[128,4096]{1,0:T(8,128)(2,1)S(1)} %get-tuple-element.32), channel_id=1, source_target_pairs={{0,16},{16,0},{32,48},{48,32},{64,80},{80,64},{96,112},{112,96},{1... | collective-permute-start | bytes 3145736 | tf_op jit(solution)/shard_map/scatter_core/ppermute | solution.py:290
  69.4 2.4 %collective-permute-start.11 = (bf16[128,4096]{1,0:T(8,128)(2,1)S(1)}, bf16[128,4096]{1,0:T(8,128)(2,1)S(1)}, u32[]{:S(2)}, u32[]{:S(2)}) collective-permute-start(bf16[128,4096]{1,0:T(8,128)(2,1)S(1)} %get-tuple-element.39), channel_id=1, source_target_pairs={{0,16},{16,0},{32,48},{48,32},{64,80},{80,64},{96,112},{112,96},{1... | collective-permute-start | bytes 3145736 | tf_op jit(solution)/shard_map/scatter_core/ppermute | solution.py:289
  71.8 0.5 coef.1
  72.3 0.7 copy-done.6
  73.0 0.0 collective-permute-done.10.away_ref
  73.0 2.4 %core_sum_second.1 = (f32[64,4096]{1,0:T(8,128)S(1)}, bf16[64,4096]{1,0:T(8,128)(2,1)}) custom-call(bf16[256,256]{1,0:T(8,128)(2,1)S(1)} %get-tuple-element.37.coef_ref, bf16[256,4096]{1,0:T(8,128)(2,1)S(1)} %bitcast.18, bf16[128,4096]{1,0:T(8,128)(2,1)S(1)} %collective-permute-done.10.away_ref), custom_call_target="tpu_custom_call" | custom-call | flops 268435456 | bytes 4849664 | tf_op jit(solution)/shard_map/scatter_x/core_sum_second/pallas_call | solution.py:71
  75.3 1.0 copy-done.1
  76.3 5.0 %collective-permute-start.14 = (bf16[64,4096]{1,0:T(8,128)(2,1)}, bf16[64,4096]{1,0:T(8,128)(2,1)}, u32[]{:S(2)}, u32[]{:S(2)}) collective-permute-start(bf16[64,4096]{1,0:T(8,128)(2,1)} %get-tuple-element.42), channel_id=1, source_target_pairs={{0,32},{16,48},{32,64},{48,80},{64,96},{80,112},{96,0},{112,16},{1... | collective-permute-start | bytes 1572872 | tf_op jit(solution)/shard_map/scatter_x/ppermute | solution.py:30
  81.3 0.0 collective-permute-done.11.away_ref
  81.3 2.5 %core_sum_first.1 = (bf16[64,4096]{1,0:T(8,128)(2,1)}, bf16[64,4096]{1,0:T(8,128)(2,1)}) custom-call(bf16[256,256]{1,0:T(8,128)(2,1)S(1)} %get-tuple-element.37.coef_ref, bf16[256,4096]{1,0:T(8,128)(2,1)S(1)} %bitcast.19, bf16[128,4096]{1,0:T(8,128)(2,1)S(1)} %collective-permute-done.11.away_ref), custom_call_target="tpu_custom_call" | custom-call | flops 268435456 | bytes 4325376 | tf_op jit(solution)/shard_map/scatter_x/core_sum_first/pallas_call | solution.py:71
  83.9 1.9 %collective-permute-start.12 = (bf16[64,4096]{1,0:T(8,128)(2,1)}, bf16[64,4096]{1,0:T(8,128)(2,1)}, u32[]{:S(2)}, u32[]{:S(2)}) collective-permute-start(bf16[64,4096]{1,0:T(8,128)(2,1)} %get-tuple-element.40), channel_id=1, source_target_pairs={{0,96},{16,112},{32,0},{48,16},{64,32},{80,48},{96,64},{112,80},{1... | collective-permute-start | bytes 1572872 | tf_op jit(solution)/shard_map/scatter_x/ppermute | solution.py:30
  85.8 3.4 %collective-permute-start.13 = (bf16[64,4096]{1,0:T(8,128)(2,1)}, bf16[64,4096]{1,0:T(8,128)(2,1)}, u32[]{:S(2)}, u32[]{:S(2)}) collective-permute-start(bf16[64,4096]{1,0:T(8,128)(2,1)} %get-tuple-element.41), channel_id=1, source_target_pairs={{0,64},{16,80},{32,96},{48,112},{64,0},{80,16},{96,32},{112,48},{1... | collective-permute-start | bytes 1572872 | tf_op jit(solution)/shard_map/scatter_x/ppermute | solution.py:30
  89.2 0.7 reduce
  89.8 2.0 %hard_grad.1 = bf16[16,2,4096]{2,1,0:T(2,128)(2,1)} custom-call(bf16[32,256]{1,0:T(8,128)(2,1)S(1)} %get-tuple-element.33.coef_ref, bf16[256,4096]{1,0:T(8,128)(2,1)S(1)} %bitcast.20), custom_call_target="tpu_custom_call" | custom-call | flops 67108864 | bytes 2375680 | tf_op jit(solution)/shard_map/hard_back/hard_grad/pallas_call | solution.py:71
  91.8 9.2 %all-to-all-start.2 = ((bf16[16,2,4096]{2,1,0:T(2,128)(2,1)}), bf16[16,2,4096]{2,1,0:T(2,128)(2,1)S(1)}, u32[]{:S(2)}, u32[]{:S(2)}) async-start(bf16[16,2,4096]{2,1,0:T(2,128)(2,1)} %hard_grad.1), calls=%async_computation.2 | async-start | bytes 524288 | tf_op jit(solution)/shard_map/hard_back/all_to_all | solution.py:311
  101.1 3.1 %collective-permute-done.14 = bf16[64,4096]{1,0:T(8,128)(2,1)} collective-permute-done((bf16[64,4096]{1,0:T(8,128)(2,1)}, bf16[64,4096]{1,0:T(8,128)(2,1)}, u32[]{:S(2)}, u32[]{:S(2)}) %collective-permute-start.14) | collective-permute-done | bytes 524320 | tf_op jit(solution)/shard_map/scatter_x/ppermute | solution.py:30
  104.2 7.9 %collective-permute-done.12 = bf16[64,4096]{1,0:T(8,128)(2,1)} collective-permute-done((bf16[64,4096]{1,0:T(8,128)(2,1)}, bf16[64,4096]{1,0:T(8,128)(2,1)}, u32[]{:S(2)}, u32[]{:S(2)}) %collective-permute-start.12) | collective-permute-done | bytes 524320 | tf_op jit(solution)/shard_map/scatter_x/ppermute | solution.py:30
  112.1 0.0 collective-permute-done.13
  112.1 2.0 %fusion.21 = (bf16[64,4096]{1,0:T(8,128)(2,1)S(1)}, f32[64,4096]{1,0:T(8,128)S(1)}) fusion(bf16[64,4096]{1,0:T(8,128)(2,1)} %collective-permute-done.14, bf16[64,4096]{1,0:T(8,128)(2,1)} %collective-permute-done.13, f32[64,4096]{1,0:T(8,128)} %copy-done.1, bf16[64,4096]{1,0:T(8,128)(2,1)} %collective-permute-done.12), kind=kLoop, calls=%fused_computation.49 | loop fusion | flops 1835008 | bytes 4194304 | tf_op jit(solution)/shard_map/convert.2
  114.1 4.3 %collective-permute-start.15 = (bf16[16,4096]{1,0:T(8,128)(2,1)S(1)}, bf16[16,4096]{1,0:T(8,128)(2,1)S(1)}, u32[]{:S(2)}, u32[]{:S(2)}) collective-permute-start(bf16[16,4096]{1,0:T(8,128)(2,1)S(1)} %get-tuple-element.46), channel_id=1, source_target_pairs={{0,384},{16,400},{32,416},{48,432},{64,448},{80,464},{96,480},{112... | collective-permute-start | bytes 393224 | tf_op jit(solution)/shard_map/scatter_z/ppermute | solution.py:30
  118.4 1.9 %collective-permute-start.17 = (bf16[16,4096]{1,0:T(8,128)(2,1)S(1)}, bf16[16,4096]{1,0:T(8,128)(2,1)S(1)}, u32[]{:S(2)}, u32[]{:S(2)}) collective-permute-start(bf16[16,4096]{1,0:T(8,128)(2,1)S(1)} %get-tuple-element.47), channel_id=1, source_target_pairs={{0,128},{16,144},{32,160},{48,176},{64,192},{80,208},{96,224},{112... | collective-permute-start | bytes 393224 | tf_op jit(solution)/shard_map/scatter_z/ppermute | solution.py:30
  120.3 4.8 %collective-permute-start.16 = (bf16[16,4096]{1,0:T(8,128)(2,1)S(1)}, bf16[16,4096]{1,0:T(8,128)(2,1)S(1)}, u32[]{:S(2)}, u32[]{:S(2)}) collective-permute-start(bf16[16,4096]{1,0:T(8,128)(2,1)S(1)} %get-tuple-element.48), channel_id=1, source_target_pairs={{0,256},{16,272},{32,288},{48,304},{64,320},{80,336},{96,352},{112... | collective-permute-start | bytes 393224 | tf_op jit(solution)/shard_map/scatter_z/ppermute | solution.py:30
  125.2 7.4 %query_grad.1 = bf16[1,256,4096]{2,1,0:T(8,128)(2,1)} custom-call(bf16[512,256]{1,0:T(8,128)(2,1)S(1)} %copy-done.5, bf16[512,256]{1,0:T(8,128)(2,1)S(1)} %copy-done.7, bf16[256,64]{1,0:T(8,128)(2,1)S(1)} %get-tuple-element.36.ch, bf16[64,4096]{1,0:T(8,128)(2,1)S(1)} %pad_maximum_fusion.refs_0_, bf16[64,4096]{1,0:T(8,128)(2,1)} %collective-permute-done.3.refs_1_, ...), custom_call_target="tpu_custom_call" | custom-call | flops 2281701376 | bytes 7118848 | tf_op jit(solution)/shard_map/d_query/query_grad/pallas_call | solution.py:71
  132.6 0.0 collective-permute-done.15
  132.6 0.0 collective-permute-done.17
  132.6 0.0 collective-permute-done.16
  132.6 0.7 fusion.17
  133.3 0.0 all-to-all-done.2
  133.3 0.1 reshape.340
  133.4 0.9 fusion
  (14 shorter events, 0.1 us)
Async XLA Ops:
  0.6 52.7 %copy-start = (bf16[1,256,4096]{2,1,0:T(8,128)(2,1)S(1)}, bf16[1,256,4096]{2,1,0:T(8,128)(2,1)}, u32[]{:S(2)}) copy-start(bf16[1,256,4096]{2,1,0:T(8,128)(2,1)} %param.5) | copy-start | bytes 6291460
  0.6 18.7 %collective-permute-start.2 = (bf16[16,4096]{1,0:T(8,128)(2,1)}, bf16[16,4096]{1,0:T(8,128)(2,1)S(1)}, u32[]{:S(2)}, u32[]{:S(2)}) collective-permute-start(bf16[16,4096]{1,0:T(8,128)(2,1)} %bitcast.26), channel_id=1, source_target_pairs={{0,384},{16,400},{32,416},{48,432},{64,448},{80,464},{96,480},{112... | collective-permute-start | bytes 393224 | tf_op jit(solution)/shard_map/gather_z/ppermute | solution.py:30
  7.3 12.1 %collective-permute-start.1 = (bf16[16,4096]{1,0:T(8,128)(2,1)}, bf16[16,4096]{1,0:T(8,128)(2,1)S(1)}, u32[]{:S(2)}, u32[]{:S(2)}) collective-permute-start(bf16[16,4096]{1,0:T(8,128)(2,1)} %bitcast.27), channel_id=1, source_target_pairs={{0,256},{16,272},{32,288},{48,304},{64,320},{80,336},{96,352},{112... | collective-permute-start | bytes 393224 | tf_op jit(solution)/shard_map/gather_z/ppermute | solution.py:30
  9.2 10.2 %collective-permute-start = (bf16[16,4096]{1,0:T(8,128)(2,1)}, bf16[16,4096]{1,0:T(8,128)(2,1)S(1)}, u32[]{:S(2)}, u32[]{:S(2)}) collective-permute-start(bf16[16,4096]{1,0:T(8,128)(2,1)} %bitcast.28), channel_id=1, source_target_pairs={{0,128},{16,144},{32,160},{48,176},{64,192},{80,208},{96,224},{112... | collective-permute-start | bytes 393224 | tf_op jit(solution)/shard_map/gather_z/ppermute | solution.py:30
  11.8 0.9 copy-start.2
  12.7 0.7 copy-start.3
  13.4 39.3 %copy-start.8 = (s32[1,256]{1,0:T(1,128)S(1)}, s32[1,256]{1,0:T(1,128)}, u32[]{:S(2)}) copy-start(s32[1,256]{1,0:T(1,128)} %param.7) | copy-start | bytes 3076
  14.4 13.3 %all-to-all-start = ((bf16[4,8,4224]{2,1,0:T(8,128)(2,1)}), bf16[4,8,4224]{2,1,0:T(8,128)(2,1)S(1)}, u32[]{:S(2)}, u32[]{:S(2)}) async-start(bf16[4,8,4224]{2,1,0:T(8,128)(2,1)} %bitcast.4), calls=%async_computation | async-start | bytes 540672 | tf_op jit(solution)/shard_map/hard_out/all_to_all | solution.py:56
  20.4 25.5 %collective-permute-start.4 = (bf16[64,4096]{1,0:T(8,128)(2,1)S(1)}, bf16[64,4096]{1,0:T(8,128)(2,1)}, u32[]{:S(2)}, u32[]{:S(2)}) collective-permute-start(bf16[64,4096]{1,0:T(8,128)(2,1)S(1)} %pad_maximum_fusion.refs_0_), channel_id=1, source_target_pairs={{0,64},{16,80},{32,96},{48,112},{64,0},{80,16},{96,32},{112,48},{1... | collective-permute-start | bytes 1572872 | tf_op jit(solution)/shard_map/gather_x/ppermute | solution.py:30
  23.7 24.6 %collective-permute-start.3 = (bf16[64,4096]{1,0:T(8,128)(2,1)S(1)}, bf16[64,4096]{1,0:T(8,128)(2,1)}, u32[]{:S(2)}, u32[]{:S(2)}) collective-permute-start(bf16[64,4096]{1,0:T(8,128)(2,1)S(1)} %pad_maximum_fusion.refs_0_), channel_id=1, source_target_pairs={{0,32},{16,48},{32,64},{48,80},{64,96},{80,112},{96,0},{112,16},{1... | collective-permute-start | bytes 1572872 | tf_op jit(solution)/shard_map/gather_x/ppermute | solution.py:30
  27.7 22.5 %collective-permute-start.5 = (bf16[64,4096]{1,0:T(8,128)(2,1)S(1)}, bf16[64,4096]{1,0:T(8,128)(2,1)}, u32[]{:S(2)}, u32[]{:S(2)}) collective-permute-start(bf16[64,4096]{1,0:T(8,128)(2,1)S(1)} %pad_maximum_fusion.refs_0_), channel_id=1, source_target_pairs={{0,96},{16,112},{32,0},{48,16},{64,32},{80,48},{96,64},{112,80},{1... | collective-permute-start | bytes 1572872 | tf_op jit(solution)/shard_map/gather_x/ppermute | solution.py:30
  30.6 31.7 %all-to-all-start.1 = ((bf16[4,8,4224]{2,1,0:T(8,128)(2,1)}), bf16[4,8,4224]{2,1,0:T(8,128)(2,1)S(1)}, u32[]{:S(2)}, u32[]{:S(2)}) async-start(bf16[4,8,4224]{2,1,0:T(8,128)(2,1)} %bitcast.6), calls=%async_computation.1 | async-start | bytes 540672 | tf_op jit(solution)/shard_map/hard_out/all_to_all | solution.py:56
  44.0 11.5 %collective-permute-start.6 = (bf16[64,4096]{1,0:T(8,128)(2,1)S(1)}, bf16[64,4096]{1,0:T(8,128)(2,1)}, u32[]{:S(2)}, u32[]{:S(2)}) collective-permute-start(bf16[64,4096]{1,0:T(8,128)(2,1)S(1)} %pad_maximum_fusion.refs_0_), channel_id=1, source_target_pairs={{0,16},{16,0},{32,48},{48,32},{64,80},{80,64},{96,112},{112,96},{1... | collective-permute-start | bytes 1572872 | tf_op jit(solution)/shard_map/gather_core/ppermute | solution.py:254
  45.9 16.4 %collective-permute-start.8 = (bf16[64,4096]{1,0:T(8,128)(2,1)}, bf16[64,4096]{1,0:T(8,128)(2,1)}, u32[]{:S(2)}, u32[]{:S(2)}) collective-permute-start(bf16[64,4096]{1,0:T(8,128)(2,1)} %collective-permute-done.4.refs_2_), channel_id=1, source_target_pairs={{0,16},{16,0},{32,48},{48,32},{64,80},{80,64},{96,112},{112,96},{1... | collective-permute-start | bytes 1572872 | tf_op jit(solution)/shard_map/gather_core/ppermute | solution.py:254
  48.3 14.0 %collective-permute-start.7 = (bf16[64,4096]{1,0:T(8,128)(2,1)}, bf16[64,4096]{1,0:T(8,128)(2,1)}, u32[]{:S(2)}, u32[]{:S(2)}) collective-permute-start(bf16[64,4096]{1,0:T(8,128)(2,1)} %collective-permute-done.3.refs_1_), channel_id=1, source_target_pairs={{0,16},{16,0},{32,48},{48,32},{64,80},{80,64},{96,112},{112,96},{1... | collective-permute-start | bytes 1572872 | tf_op jit(solution)/shard_map/gather_core/ppermute | solution.py:254
  50.3 12.0 %collective-permute-start.9 = (bf16[64,4096]{1,0:T(8,128)(2,1)}, bf16[64,4096]{1,0:T(8,128)(2,1)}, u32[]{:S(2)}, u32[]{:S(2)}) collective-permute-start(bf16[64,4096]{1,0:T(8,128)(2,1)} %collective-permute-done.5.refs_3_), channel_id=1, source_target_pairs={{0,16},{16,0},{32,48},{48,32},{64,80},{80,64},{96,112},{112,96},{1... | collective-permute-start | bytes 1572872 | tf_op jit(solution)/shard_map/gather_core/ppermute | solution.py:254
  67.4 5.5 %collective-permute-start.10 = (bf16[128,4096]{1,0:T(8,128)(2,1)S(1)}, bf16[128,4096]{1,0:T(8,128)(2,1)S(1)}, u32[]{:S(2)}, u32[]{:S(2)}) collective-permute-start(bf16[128,4096]{1,0:T(8,128)(2,1)S(1)} %get-tuple-element.32), channel_id=1, source_target_pairs={{0,16},{16,0},{32,48},{48,32},{64,80},{80,64},{96,112},{112,96},{1... | collective-permute-start | bytes 3145736 | tf_op jit(solution)/shard_map/scatter_core/ppermute | solution.py:290
  69.4 12.0 %collective-permute-start.11 = (bf16[128,4096]{1,0:T(8,128)(2,1)S(1)}, bf16[128,4096]{1,0:T(8,128)(2,1)S(1)}, u32[]{:S(2)}, u32[]{:S(2)}) collective-permute-start(bf16[128,4096]{1,0:T(8,128)(2,1)S(1)} %get-tuple-element.39), channel_id=1, source_target_pairs={{0,16},{16,0},{32,48},{48,32},{64,80},{80,64},{96,112},{112,96},{1... | collective-permute-start | bytes 3145736 | tf_op jit(solution)/shard_map/scatter_core/ppermute | solution.py:289
  72.2 0.7 copy-start.6
  73.0 10.9 %copy-start.4 = (bf16[512,256]{1,0:T(8,128)(2,1)}, bf16[512,256]{1,0:T(8,128)(2,1)S(1)}, u32[]{:S(2)}) copy-start(bf16[512,256]{1,0:T(8,128)(2,1)S(1)} %get-tuple-element.34.c0) | copy-start | bytes 786436
  75.3 1.0 copy-start.1
  76.3 27.9 %collective-permute-start.14 = (bf16[64,4096]{1,0:T(8,128)(2,1)}, bf16[64,4096]{1,0:T(8,128)(2,1)}, u32[]{:S(2)}, u32[]{:S(2)}) collective-permute-start(bf16[64,4096]{1,0:T(8,128)(2,1)} %get-tuple-element.42), channel_id=1, source_target_pairs={{0,32},{16,48},{32,64},{48,80},{64,96},{80,112},{96,0},{112,16},{1... | collective-permute-start | bytes 1572872 | tf_op jit(solution)/shard_map/scatter_x/ppermute | solution.py:30
  83.9 28.2 %collective-permute-start.12 = (bf16[64,4096]{1,0:T(8,128)(2,1)}, bf16[64,4096]{1,0:T(8,128)(2,1)}, u32[]{:S(2)}, u32[]{:S(2)}) collective-permute-start(bf16[64,4096]{1,0:T(8,128)(2,1)} %get-tuple-element.40), channel_id=1, source_target_pairs={{0,96},{16,112},{32,0},{48,16},{64,32},{80,48},{96,64},{112,80},{1... | collective-permute-start | bytes 1572872 | tf_op jit(solution)/shard_map/scatter_x/ppermute | solution.py:30
  85.8 26.3 %collective-permute-start.13 = (bf16[64,4096]{1,0:T(8,128)(2,1)}, bf16[64,4096]{1,0:T(8,128)(2,1)}, u32[]{:S(2)}, u32[]{:S(2)}) collective-permute-start(bf16[64,4096]{1,0:T(8,128)(2,1)} %get-tuple-element.41), channel_id=1, source_target_pairs={{0,64},{16,80},{32,96},{48,112},{64,0},{80,16},{96,32},{112,48},{1... | collective-permute-start | bytes 1572872 | tf_op jit(solution)/shard_map/scatter_x/ppermute | solution.py:30
  91.8 41.5 %all-to-all-start.2 = ((bf16[16,2,4096]{2,1,0:T(2,128)(2,1)}), bf16[16,2,4096]{2,1,0:T(2,128)(2,1)S(1)}, u32[]{:S(2)}, u32[]{:S(2)}) async-start(bf16[16,2,4096]{2,1,0:T(2,128)(2,1)} %hard_grad.1), calls=%async_computation.2 | async-start | bytes 524288 | tf_op jit(solution)/shard_map/hard_back/all_to_all | solution.py:311
  112.1 13.1 %copy-start.5 = (bf16[512,256]{1,0:T(8,128)(2,1)S(1)}, bf16[512,256]{1,0:T(8,128)(2,1)}, u32[]{:S(2)}) copy-start(bf16[512,256]{1,0:T(8,128)(2,1)} %copy-done.4) | copy-start | bytes 786436
  112.1 13.1 %copy-start.7 = (bf16[512,256]{1,0:T(8,128)(2,1)S(1)}, bf16[512,256]{1,0:T(8,128)(2,1)}, u32[]{:S(2)}) copy-start(bf16[512,256]{1,0:T(8,128)(2,1)} %copy-done.6) | copy-start | bytes 786436
  114.1 18.5 %collective-permute-start.15 = (bf16[16,4096]{1,0:T(8,128)(2,1)S(1)}, bf16[16,4096]{1,0:T(8,128)(2,1)S(1)}, u32[]{:S(2)}, u32[]{:S(2)}) collective-permute-start(bf16[16,4096]{1,0:T(8,128)(2,1)S(1)} %get-tuple-element.46), channel_id=1, source_target_pairs={{0,384},{16,400},{32,416},{48,432},{64,448},{80,464},{96,480},{112... | collective-permute-start | bytes 393224 | tf_op jit(solution)/shard_map/scatter_z/ppermute | solution.py:30
  118.4 14.2 %collective-permute-start.17 = (bf16[16,4096]{1,0:T(8,128)(2,1)S(1)}, bf16[16,4096]{1,0:T(8,128)(2,1)S(1)}, u32[]{:S(2)}, u32[]{:S(2)}) collective-permute-start(bf16[16,4096]{1,0:T(8,128)(2,1)S(1)} %get-tuple-element.47), channel_id=1, source_target_pairs={{0,128},{16,144},{32,160},{48,176},{64,192},{80,208},{96,224},{112... | collective-permute-start | bytes 393224 | tf_op jit(solution)/shard_map/scatter_z/ppermute | solution.py:30
  120.3 12.3 %collective-permute-start.16 = (bf16[16,4096]{1,0:T(8,128)(2,1)S(1)}, bf16[16,4096]{1,0:T(8,128)(2,1)S(1)}, u32[]{:S(2)}, u32[]{:S(2)}) collective-permute-start(bf16[16,4096]{1,0:T(8,128)(2,1)S(1)} %get-tuple-element.48), channel_id=1, source_target_pairs={{0,256},{16,272},{32,288},{48,304},{64,320},{80,336},{96,352},{112... | collective-permute-start | bytes 393224 | tf_op jit(solution)/shard_map/scatter_z/ppermute | solution.py:30

commit v8 on v7

--- a/solution.py
+++ b/solution.py
@@ -66,24 +66,23 @@
     return jax.ShapeDtypeStruct(dims, dtype)
 
 
-def call(kernel, outs, args, name, flops, grant, scalars=1):
+def call(kernel, outs, args, name, flops, grant, place=pltpu.VMEM, scratch=()):
     size = sum(a.size * a.dtype.itemsize for a in (*args, *outs))
     return pl.pallas_call(
         kernel,
-        in_specs=[pl.BlockSpec(memory_space=pltpu.SMEM)] * scalars
-        + [pl.BlockSpec(memory_space=pltpu.VMEM)] * (len(args) - scalars),
-        out_specs=[pl.BlockSpec(memory_space=pltpu.VMEM)] * len(outs),
+        in_specs=[pl.BlockSpec(memory_space=pltpu.VMEM)] * len(args),
+        out_specs=[pl.BlockSpec(memory_space=place)] * len(outs),
         out_shape=outs,
+        scratch_shapes=scratch,
         cost_estimate=pl.CostEstimate(flops=flops, bytes_accessed=size, transcendentals=0),
         compiler_params=pltpu.CompilerParams(vmem_limit_bytes=grant << 20),
         name=name,
     )(*args)
 
 
-def over_columns(width, step, block=512):
-    @pl.loop(0, width // block)
-    def _(i):
-        step(pl.ds(pl.multiple_of(i * block, block), block))
+def over_columns(width, step, block=1024):
+    for i in range(0, width, block):
+        step(slice(i, i + block))
 
 
 def joined(refs, cols=slice(None)):
@@ -110,7 +109,7 @@
 def turn(x, slots):
     [out] = call(
         functools.partial(turn_kernel, slots), [shape(x.shape)], (x,),
-        "turn", 2 * x.shape[0] * x.size, 2, 0,
+        "turn", 2 * x.shape[0] * x.size, 2,
     )
     return out
 
@@ -210,16 +209,25 @@
 
 
 def query_grad_kernel(scale, c0, c1, ch, *refs):
-    near, far, got, out = refs[:4], refs[4:8], refs[8], refs[9]
-    count = out.shape[1]
+    near, far, got = refs[:4], refs[4:8], refs[8]
+    out, made, sems = refs[9:]
+    count, width = made.shape
+    copies = []
 
     def grad(cols):
         both = dot(c0[...], joined(near, cols)) + dot(c1[...], joined(far, cols))
         hard = got[:, cols]
         thin = dot(ch[...], jnp.concatenate([hard, hard], axis=0))
-        out[0, :, cols] = (scale * (both[:count] + both[count:] + thin)).astype(out.dtype)
-
-    over_columns(out.shape[2], grad)
+        made[:, cols] = (scale * (both[:count] + both[count:] + thin)).astype(made.dtype)
+        copy = pltpu.make_async_copy(
+            made.at[:, cols], out.at[0, :, cols], sems.at[len(copies)]
+        )
+        copy.start()
+        copies.append(copy)
+
+    over_columns(width, grad)
+    for copy in copies:
+        copy.wait()
 
 
 def body(queries, passages, positives, hard_rows, hard_dest):
@@ -243,7 +251,7 @@
             functools.partial(pack_kernel, slots),
             [shape((places, width + FLAG)), shape((places, owned_hard.shape[0]))],
             (hard_dest.reshape(1, -1), owned_hard),
-            "pack", 2 * places * owned_hard.size, 2, 0,
+            "pack", 2 * places * owned_hard.size, 2,
         )
         from_y = swap(packed, Y_GROUPS)
         received = swap(turn(from_y, slots), H_GROUPS)
@@ -265,7 +273,7 @@
             functools.partial(near_kernel, scale),
             [shape((count, half), F32)],
             (q, *near),
-            "near", 2 * count * half * width, 8, 0,
+            "near", 2 * count * half * width, 8,
         )
         first, second, s1, sh, log_total = call(
             functools.partial(away_kernel, scale),
@@ -274,7 +282,7 @@
                 shape((count, places), F32), shape((count, 1), F32),
             ],
             (q, *far, received, s0, column.reshape(-1, 1)),
-            "away", 4 * count * half * width, 12, 0,
+            "away", 4 * count * half * width, 10,
         )
         mine_rows, hard_cols, both0, both1, both_hard, loss_rows = call(
             functools.partial(coef_kernel, slots),
@@ -283,7 +291,7 @@
                 shape((2 * count, half)), shape((count, 2 * places)), shape((count, 1), F32),
             ],
             (s0, s1, sh, log_total, column.reshape(-1, 1)),
-            "coef", count * half * half, 8, 0,
+            "coef", count * half * half, 8,
         )
     with jax.named_scope("scatter_core"):
         first = lax.ppermute(first, "blk", CORE_SWAP)
@@ -293,11 +301,11 @@
         flops = count * half * width
         one, two = call(
             functools.partial(core_sum_kernel, True), [shape((n, width))] * 2,
-            (mine_rows, q, first), "core_sum_first", flops, 8, 0,
+            (mine_rows, q, first), "core_sum_first", flops, 8,
         )
         zero, three = call(
             functools.partial(core_sum_kernel, False), [shape((n, width), F32), shape((n, width))],
-            (mine_rows, q, second), "core_sum_second", flops, 8, 0,
+            (mine_rows, q, second), "core_sum_second", flops, 8,
         )
         chunks = [c.astype(F32) for c in exchange([zero, one, two, three], "blk", x_shift, -1)]
         mine_x = pieces(functools.reduce(jnp.add, chunks), NZ)
@@ -306,7 +314,7 @@
     with jax.named_scope("hard_back"):
         [g] = call(
             functools.partial(hard_grad_kernel, scale), [shape((groups, slots, width))],
-            (hard_cols, q), "hard_grad", 2 * places * count * width, 4, 0,
+            (hard_cols, q), "hard_grad", 2 * places * count * width, 4,
         )
         returned = lax.all_to_all(g, "group", split_axis=0, concat_axis=0, tiled=True)
         d_owned = t_dot(placing, returned.reshape(places, width)).astype(BF16)
@@ -316,7 +324,8 @@
             functools.partial(query_grad_kernel, scale),
             [shape((1, count, width))],
             (both0, both1, both_hard, *near, *far, received),
-            "query_grad", 4 * count * (2 * half + places) * width, 8, 0,
+            "query_grad", 4 * count * (2 * half + places) * width, 12, pl.ANY,
+            [pltpu.VMEM((count, width), BF16), pltpu.SemaphoreType.DMA((width // 1024,))],
         )
     with jax.named_scope("scatter_z"):
         sent = [mine_x[0]] + [m.astype(BF16) for m in mine_x[1:]]

time: 135 us -> 132 us (0.978)
  the two profiles are of different devices: /device:TPU:14 before, /device:TPU:15 now
where the time goes in v8:
time: 132 us; the launch traced here: 131 us
  starting transfers between devices  81.9 us (62%)
  waiting for transfers between devices  20.5 us (16%)
  Pallas kernels  18 us (14%)
  other arithmetic  4.77 us (4%)
  local copies, waits for them, and re-layouts  4.18 us (3%)
    ppermute x12, starting transfers between devices, exchange(): lax.ppermute(p, axis, perm(sign * d))  39.2 us
    pallas_call x9, Pallas kernels, call(): pl.pallas_call(kernel, in_specs=[pl.BlockSpec(memory_space=pltpu.VMEM)] *...  18 us
    all_to_all x2, starting transfers between devices, swap(): lax.all_to_all(x, 'group', split_axis=0, concat_axis=0, axis_index_groups...  17.4 us
    ppermute x12, waiting for transfers between devices, exchange(): lax.ppermute(p, axis, perm(sign * d))  16.7 us
    ppermute x4, starting transfers between devices, body(): far = [lax.ppermute(x, 'blk', CORE_SWAP) for x in near]  9.48 us
    all_to_all x1, starting transfers between devices, body(): lax.all_to_all(g, 'group', split_axis=0, concat_axis=0, tiled=True)  8.39 us
    ppermute x1, starting transfers between devices, body(): second = lax.ppermute(second, 'blk', CORE_SWAP)  5.47 us
    unnamed x18, local copies, waits for them, and re-layouts  3.92 us
  transfers between devices with their start and end apart: 21, of which 5 were waited for; matrix products, arithmetic and copies ran while one was open for 4% of the time, Pallas kernels for 11%

profile of v8, /device:TPU:15, one launch (start us, length us, event | category | flops | bytes accessed | tf_op | source)
XLA Modules:
  0.0 131.2 jit_solution(13349633980976978998)
XLA Ops:
  0.6 6.4 %collective-permute-start.2 = (bf16[16,4096]{1,0:T(8,128)(2,1)}, bf16[16,4096]{1,0:T(8,128)(2,1)S(1)}, u32[]{:S(2)}, u32[]{:S(2)}) collective-permute-start(bf16[16,4096]{1,0:T(8,128)(2,1)} %bitcast.26), channel_id=1, source_target_pairs={{0,384},{16,400},{32,416},{48,432},{64,448},{80,464},{96,480},{112... | collective-permute-start | bytes 393224 | tf_op jit(solution)/shard_map/gather_z/ppermute | solution.py:30
  7.0 1.9 %collective-permute-start.1 = (bf16[16,4096]{1,0:T(8,128)(2,1)}, bf16[16,4096]{1,0:T(8,128)(2,1)S(1)}, u32[]{:S(2)}, u32[]{:S(2)}) collective-permute-start(bf16[16,4096]{1,0:T(8,128)(2,1)} %bitcast.27), channel_id=1, source_target_pairs={{0,256},{16,272},{32,288},{48,304},{64,320},{80,336},{96,352},{112... | collective-permute-start | bytes 393224 | tf_op jit(solution)/shard_map/gather_z/ppermute | solution.py:30
  9.0 2.2 %collective-permute-start = (bf16[16,4096]{1,0:T(8,128)(2,1)}, bf16[16,4096]{1,0:T(8,128)(2,1)S(1)}, u32[]{:S(2)}, u32[]{:S(2)}) collective-permute-start(bf16[16,4096]{1,0:T(8,128)(2,1)} %bitcast.28), channel_id=1, source_target_pairs={{0,128},{16,144},{32,160},{48,176},{64,192},{80,208},{96,224},{112... | collective-permute-start | bytes 393224 | tf_op jit(solution)/shard_map/gather_z/ppermute | solution.py:30
  11.2 0.9 copy-done.2
  12.1 0.7 copy-done.3
  12.7 1.0 pack.1
  13.8 4.3 %all-to-all-start = ((bf16[4,8,4224]{2,1,0:T(8,128)(2,1)}), bf16[4,8,4224]{2,1,0:T(8,128)(2,1)S(1)}, u32[]{:S(2)}, u32[]{:S(2)}) async-start(bf16[4,8,4224]{2,1,0:T(8,128)(2,1)} %bitcast.4), calls=%async_computation | async-start | bytes 540672 | tf_op jit(solution)/shard_map/hard_out/all_to_all | solution.py:56
  18.1 0.0 collective-permute-done.2
  18.1 1.5 %collective-permute-done.1 = bf16[16,4096]{1,0:T(8,128)(2,1)S(1)} collective-permute-done((bf16[16,4096]{1,0:T(8,128)(2,1)}, bf16[16,4096]{1,0:T(8,128)(2,1)S(1)}, u32[]{:S(2)}, u32[]{:S(2)}) %collective-permute-start.1) | collective-permute-done | bytes 131104 | tf_op jit(solution)/shard_map/gather_z/ppermute | solution.py:30
  19.6 0.0 collective-permute-done
  19.6 0.9 pad_maximum_fusion.refs_0_
  20.6 3.0 %collective-permute-start.4 = (bf16[64,4096]{1,0:T(8,128)(2,1)S(1)}, bf16[64,4096]{1,0:T(8,128)(2,1)}, u32[]{:S(2)}, u32[]{:S(2)}) collective-permute-start(bf16[64,4096]{1,0:T(8,128)(2,1)S(1)} %pad_maximum_fusion.refs_0_), channel_id=1, source_target_pairs={{0,64},{16,80},{32,96},{48,112},{64,0},{80,16},{96,32},{112,48},{1... | collective-permute-start | bytes 1572872 | tf_op jit(solution)/shard_map/gather_x/ppermute | solution.py:30
  23.6 3.7 %collective-permute-start.3 = (bf16[64,4096]{1,0:T(8,128)(2,1)S(1)}, bf16[64,4096]{1,0:T(8,128)(2,1)}, u32[]{:S(2)}, u32[]{:S(2)}) collective-permute-start(bf16[64,4096]{1,0:T(8,128)(2,1)S(1)} %pad_maximum_fusion.refs_0_), channel_id=1, source_target_pairs={{0,32},{16,48},{32,64},{48,80},{64,96},{80,112},{96,0},{112,16},{1... | collective-permute-start | bytes 1572872 | tf_op jit(solution)/shard_map/gather_x/ppermute | solution.py:30
  27.3 0.0 all-to-all-done
  27.4 1.9 %collective-permute-start.5 = (bf16[64,4096]{1,0:T(8,128)(2,1)S(1)}, bf16[64,4096]{1,0:T(8,128)(2,1)}, u32[]{:S(2)}, u32[]{:S(2)}) collective-permute-start(bf16[64,4096]{1,0:T(8,128)(2,1)S(1)} %pad_maximum_fusion.refs_0_), channel_id=1, source_target_pairs={{0,96},{16,112},{32,0},{48,16},{64,32},{80,48},{96,64},{112,80},{1... | collective-permute-start | bytes 1572872 | tf_op jit(solution)/shard_map/gather_x/ppermute | solution.py:30
  29.3 0.9 turn.1
  30.2 13.1 %all-to-all-start.1 = ((bf16[4,8,4224]{2,1,0:T(8,128)(2,1)}), bf16[4,8,4224]{2,1,0:T(8,128)(2,1)S(1)}, u32[]{:S(2)}, u32[]{:S(2)}) async-start(bf16[4,8,4224]{2,1,0:T(8,128)(2,1)} %bitcast.6), calls=%async_computation.1 | async-start | bytes 540672 | tf_op jit(solution)/shard_map/hard_out/all_to_all | solution.py:56
  43.3 3.2 %collective-permute-start.6 = (bf16[64,4096]{1,0:T(8,128)(2,1)S(1)}, bf16[64,4096]{1,0:T(8,128)(2,1)}, u32[]{:S(2)}, u32[]{:S(2)}) collective-permute-start(bf16[64,4096]{1,0:T(8,128)(2,1)S(1)} %pad_maximum_fusion.refs_0_), channel_id=1, source_target_pairs={{0,16},{16,0},{32,48},{48,32},{64,80},{80,64},{96,112},{112,96},{1... | collective-permute-start | bytes 1572872 | tf_op jit(solution)/shard_map/gather_core/ppermute | solution.py:262
  46.6 0.0 collective-permute-done.4.refs_2_
  46.6 1.9 %collective-permute-start.8 = (bf16[64,4096]{1,0:T(8,128)(2,1)}, bf16[64,4096]{1,0:T(8,128)(2,1)}, u32[]{:S(2)}, u32[]{:S(2)}) collective-permute-start(bf16[64,4096]{1,0:T(8,128)(2,1)} %collective-permute-done.4.refs_2_), channel_id=1, source_target_pairs={{0,16},{16,0},{32,48},{48,32},{64,80},{80,64},{96,112},{112,96},{1... | collective-permute-start | bytes 1572872 | tf_op jit(solution)/shard_map/gather_core/ppermute | solution.py:262
  48.5 0.0 collective-permute-done.3.refs_1_
  48.5 2.4 %collective-permute-start.7 = (bf16[64,4096]{1,0:T(8,128)(2,1)}, bf16[64,4096]{1,0:T(8,128)(2,1)}, u32[]{:S(2)}, u32[]{:S(2)}) collective-permute-start(bf16[64,4096]{1,0:T(8,128)(2,1)} %collective-permute-done.3.refs_1_), channel_id=1, source_target_pairs={{0,16},{16,0},{32,48},{48,32},{64,80},{80,64},{96,112},{112,96},{1... | collective-permute-start | bytes 1572872 | tf_op jit(solution)/shard_map/gather_core/ppermute | solution.py:262
  50.9 0.0 collective-permute-done.5.refs_3_
  50.9 1.9 %collective-permute-start.9 = (bf16[64,4096]{1,0:T(8,128)(2,1)}, bf16[64,4096]{1,0:T(8,128)(2,1)}, u32[]{:S(2)}, u32[]{:S(2)}) collective-permute-start(bf16[64,4096]{1,0:T(8,128)(2,1)} %collective-permute-done.5.refs_3_), channel_id=1, source_target_pairs={{0,16},{16,0},{32,48},{48,32},{64,80},{80,64},{96,112},{112,96},{1... | collective-permute-start | bytes 1572872 | tf_op jit(solution)/shard_map/gather_core/ppermute | solution.py:262
  52.9 0.1 copy.9
  53.1 0.5 fusion.13.column_ref
  53.5 2.1 %near.1.s0_ref = f32[256,256]{1,0:T(8,128)S(1)} custom-call(bf16[256,4096]{1,0:T(8,128)(2,1)S(1)} %bitcast.16, bf16[64,4096]{1,0:T(8,128)(2,1)S(1)} %pad_maximum_fusion.refs_0_, bf16[64,4096]{1,0:T(8,128)(2,1)} %collective-permute-done.3.refs_1_, bf16[64,4096]{1,0:T(8,128)(2,1)} %collective-permute-done.4.refs_2_, ...), custom_call_target="tpu_custom_call" | custom-call | flops 536870912 | bytes 4456448 | tf_op jit(solution)/shard_map/scores/near/pallas_call | solution.py:71
  55.6 0.0 collective-permute-done.6.far0.refs_4_
  55.7 3.7 %all-to-all-done.1 = bf16[4,8,4224]{2,1,0:T(8,128)(2,1)S(1)} async-done(((bf16[4,8,4224]{2,1,0:T(8,128)(2,1)}), bf16[4,8,4224]{2,1,0:T(8,128)(2,1)S(1)}, u32[]{:S(2)}, u32[]{:S(2)}) %all-to-all-start.1) | async-done | bytes 270368 | tf_op jit(solution)/shard_map/hard_out/all_to_all | solution.py:56
  59.4 0.0 collective-permute-done.8.far2.refs_6_
  59.4 0.0 collective-permute-done.7.far1.refs_5_
  59.4 0.0 collective-permute-done.9.far3.refs_7_
  59.4 3.8 %away.1 = (bf16[128,4096]{1,0:T(8,128)(2,1)S(1)}, bf16[128,4096]{1,0:T(8,128)(2,1)S(1)}, f32[256,256]{1,0:T(8,128)S(1)}, f32[256,32]{1,0:T(8,128)S(1)}, f32[256,1]{1,0:T(8,128)S(1)}) custom-call(bf16[256,4096]{1,0:T(8,128)(2,1)S(1)} %bitcast.17, bf16[64,4096]{1,0:T(8,128)(2,1)} %collective-permute-done.6.far0.refs_4_, ...), custom_call_target="tpu_custom_call" | custom-call | flops 1073741824 | bytes 7120896 | tf_op jit(solution)/shard_map/scores/away/pallas_call | solution.py:71
  63.3 5.5 %collective-permute-start.10 = (bf16[128,4096]{1,0:T(8,128)(2,1)S(1)}, bf16[128,4096]{1,0:T(8,128)(2,1)S(1)}, u32[]{:S(2)}, u32[]{:S(2)}) collective-permute-start(bf16[128,4096]{1,0:T(8,128)(2,1)S(1)} %get-tuple-element.32), channel_id=1, source_target_pairs={{0,16},{16,0},{32,48},{48,32},{64,80},{80,64},{96,112},{112,96},{1... | collective-permute-start | bytes 3145736 | tf_op jit(solution)/shard_map/scatter_core/ppermute | solution.py:298
  68.7 1.9 %collective-permute-start.11 = (bf16[128,4096]{1,0:T(8,128)(2,1)S(1)}, bf16[128,4096]{1,0:T(8,128)(2,1)S(1)}, u32[]{:S(2)}, u32[]{:S(2)}) collective-permute-start(bf16[128,4096]{1,0:T(8,128)(2,1)S(1)} %get-tuple-element.39), channel_id=1, source_target_pairs={{0,16},{16,0},{32,48},{48,32},{64,80},{80,64},{96,112},{112,96},{1... | collective-permute-start | bytes 3145736 | tf_op jit(solution)/shard_map/scatter_core/ppermute | solution.py:297
  70.7 0.5 coef.1
  71.2 0.7 copy-done.4
  71.8 0.7 copy-done.6
  72.5 0.0 collective-permute-done.10.away_ref
  72.5 1.3 core_sum_second.1
  73.8 1.0 copy-done.1
  74.8 4.8 %collective-permute-start.14 = (bf16[64,4096]{1,0:T(8,128)(2,1)}, bf16[64,4096]{1,0:T(8,128)(2,1)}, u32[]{:S(2)}, u32[]{:S(2)}) collective-permute-start(bf16[64,4096]{1,0:T(8,128)(2,1)} %get-tuple-element.42), channel_id=1, source_target_pairs={{0,32},{16,48},{32,64},{48,80},{64,96},{80,112},{96,0},{112,16},{1... | collective-permute-start | bytes 1572872 | tf_op jit(solution)/shard_map/scatter_x/ppermute | solution.py:30
  79.5 0.0 collective-permute-done.11.away_ref
  79.6 1.4 %core_sum_first.1 = (bf16[64,4096]{1,0:T(8,128)(2,1)}, bf16[64,4096]{1,0:T(8,128)(2,1)}) custom-call(bf16[256,256]{1,0:T(8,128)(2,1)S(1)} %get-tuple-element.37.coef_ref, bf16[256,4096]{1,0:T(8,128)(2,1)S(1)} %bitcast.19, bf16[128,4096]{1,0:T(8,128)(2,1)S(1)} %collective-permute-done.11.away_ref), custom_call_target="tpu_custom_call" | custom-call | flops 268435456 | bytes 4325376 | tf_op jit(solution)/shard_map/scatter_x/core_sum_first/pallas_call | solution.py:71
  81.0 1.9 %collective-permute-start.12 = (bf16[64,4096]{1,0:T(8,128)(2,1)}, bf16[64,4096]{1,0:T(8,128)(2,1)}, u32[]{:S(2)}, u32[]{:S(2)}) collective-permute-start(bf16[64,4096]{1,0:T(8,128)(2,1)} %get-tuple-element.40), channel_id=1, source_target_pairs={{0,96},{16,112},{32,0},{48,16},{64,32},{80,48},{96,64},{112,80},{1... | collective-permute-start | bytes 1572872 | tf_op jit(solution)/shard_map/scatter_x/ppermute | solution.py:30
  82.9 3.1 %collective-permute-start.13 = (bf16[64,4096]{1,0:T(8,128)(2,1)}, bf16[64,4096]{1,0:T(8,128)(2,1)}, u32[]{:S(2)}, u32[]{:S(2)}) collective-permute-start(bf16[64,4096]{1,0:T(8,128)(2,1)} %get-tuple-element.41), channel_id=1, source_target_pairs={{0,64},{16,80},{32,96},{48,112},{64,0},{80,16},{96,32},{112,48},{1... | collective-permute-start | bytes 1572872 | tf_op jit(solution)/shard_map/scatter_x/ppermute | solution.py:30
  86.0 0.7 reduce
  86.7 1.2 hard_grad.1
  87.9 8.4 %all-to-all-start.2 = ((bf16[16,2,4096]{2,1,0:T(2,128)(2,1)}), bf16[16,2,4096]{2,1,0:T(2,128)(2,1)S(1)}, u32[]{:S(2)}, u32[]{:S(2)}) async-start(bf16[16,2,4096]{2,1,0:T(2,128)(2,1)} %hard_grad.1), calls=%async_computation.2 | async-start | bytes 524288 | tf_op jit(solution)/shard_map/hard_back/all_to_all | solution.py:319
  96.3 5.5 %collective-permute-done.14 = bf16[64,4096]{1,0:T(8,128)(2,1)} collective-permute-done((bf16[64,4096]{1,0:T(8,128)(2,1)}, bf16[64,4096]{1,0:T(8,128)(2,1)}, u32[]{:S(2)}, u32[]{:S(2)}) %collective-permute-start.14) | collective-permute-done | bytes 524320 | tf_op jit(solution)/shard_map/scatter_x/ppermute | solution.py:30
  101.7 6.6 %collective-permute-done.12 = bf16[64,4096]{1,0:T(8,128)(2,1)} collective-permute-done((bf16[64,4096]{1,0:T(8,128)(2,1)}, bf16[64,4096]{1,0:T(8,128)(2,1)}, u32[]{:S(2)}, u32[]{:S(2)}) %collective-permute-start.12) | collective-permute-done | bytes 524320 | tf_op jit(solution)/shard_map/scatter_x/ppermute | solution.py:30
  108.3 0.0 collective-permute-done.13
  108.3 2.0 %fusion.21 = (bf16[64,4096]{1,0:T(8,128)(2,1)S(1)}, f32[64,4096]{1,0:T(8,128)S(1)}) fusion(bf16[64,4096]{1,0:T(8,128)(2,1)} %collective-permute-done.14, bf16[64,4096]{1,0:T(8,128)(2,1)} %collective-permute-done.13, f32[64,4096]{1,0:T(8,128)} %copy-done.1, bf16[64,4096]{1,0:T(8,128)(2,1)} %collective-permute-done.12), kind=kLoop, calls=%fused_computation.49 | loop fusion | flops 1835008 | bytes 4194304 | tf_op jit(solution)/shard_map/convert.2
  110.3 4.0 %collective-permute-start.15 = (bf16[16,4096]{1,0:T(8,128)(2,1)S(1)}, bf16[16,4096]{1,0:T(8,128)(2,1)S(1)}, u32[]{:S(2)}, u32[]{:S(2)}) collective-permute-start(bf16[16,4096]{1,0:T(8,128)(2,1)S(1)} %get-tuple-element.46), channel_id=1, source_target_pairs={{0,384},{16,400},{32,416},{48,432},{64,448},{80,464},{96,480},{112... | collective-permute-start | bytes 393224 | tf_op jit(solution)/shard_map/scatter_z/ppermute | solution.py:30
  114.4 1.9 %collective-permute-start.17 = (bf16[16,4096]{1,0:T(8,128)(2,1)S(1)}, bf16[16,4096]{1,0:T(8,128)(2,1)S(1)}, u32[]{:S(2)}, u32[]{:S(2)}) collective-permute-start(bf16[16,4096]{1,0:T(8,128)(2,1)S(1)} %get-tuple-element.47), channel_id=1, source_target_pairs={{0,128},{16,144},{32,160},{48,176},{64,192},{80,208},{96,224},{112... | collective-permute-start | bytes 393224 | tf_op jit(solution)/shard_map/scatter_z/ppermute | solution.py:30
  116.3 4.2 %collective-permute-start.16 = (bf16[16,4096]{1,0:T(8,128)(2,1)S(1)}, bf16[16,4096]{1,0:T(8,128)(2,1)S(1)}, u32[]{:S(2)}, u32[]{:S(2)}) collective-permute-start(bf16[16,4096]{1,0:T(8,128)(2,1)S(1)} %get-tuple-element.48), channel_id=1, source_target_pairs={{0,256},{16,272},{32,288},{48,304},{64,320},{80,336},{96,352},{112... | collective-permute-start | bytes 393224 | tf_op jit(solution)/shard_map/scatter_z/ppermute | solution.py:30
  120.6 5.7 %query_grad.1 = bf16[1,256,4096]{2,1,0:T(8,128)(2,1)} custom-call(bf16[512,256]{1,0:T(8,128)(2,1)S(1)} %copy-done.5, bf16[512,256]{1,0:T(8,128)(2,1)S(1)} %copy-done.7, bf16[256,64]{1,0:T(8,128)(2,1)S(1)} %get-tuple-element.36.ch, bf16[64,4096]{1,0:T(8,128)(2,1)S(1)} %pad_maximum_fusion.refs_0_, bf16[64,4096]{1,0:T(8,128)(2,1)} %collective-permute-done.3.refs_1_, ...), custom_call_target="tpu_custom_call" | custom-call | flops 2281701376 | bytes 7118848 | tf_op jit(solution)/shard_map/d_query/query_grad/pallas_call | solution.py:71
  126.3 0.0 collective-permute-done.15
  126.3 0.0 collective-permute-done.17
  126.3 3.2 %collective-permute-done.16 = bf16[16,4096]{1,0:T(8,128)(2,1)S(1)} collective-permute-done((bf16[16,4096]{1,0:T(8,128)(2,1)S(1)}, bf16[16,4096]{1,0:T(8,128)(2,1)S(1)}, u32[]{:S(2)}, u32[]{:S(2)}) %collective-permute-start.16) | collective-permute-done | bytes 131104 | tf_op jit(solution)/shard_map/scatter_z/ppermute | solution.py:30
  129.5 0.7 fusion.17
  130.2 0.0 all-to-all-done.2
  130.2 0.1 reshape.340
  130.3 0.9 fusion
  (14 shorter events, 0.1 us)
Async XLA Ops:
  0.6 52.9 %copy-start = (bf16[1,256,4096]{2,1,0:T(8,128)(2,1)S(1)}, bf16[1,256,4096]{2,1,0:T(8,128)(2,1)}, u32[]{:S(2)}) copy-start(bf16[1,256,4096]{2,1,0:T(8,128)(2,1)} %param.5) | copy-start | bytes 6291460
  0.6 17.5 %collective-permute-start.2 = (bf16[16,4096]{1,0:T(8,128)(2,1)}, bf16[16,4096]{1,0:T(8,128)(2,1)S(1)}, u32[]{:S(2)}, u32[]{:S(2)}) collective-permute-start(bf16[16,4096]{1,0:T(8,128)(2,1)} %bitcast.26), channel_id=1, source_target_pairs={{0,384},{16,400},{32,416},{48,432},{64,448},{80,464},{96,480},{112... | collective-permute-start | bytes 393224 | tf_op jit(solution)/shard_map/gather_z/ppermute | solution.py:30
  7.0 12.6 %collective-permute-start.1 = (bf16[16,4096]{1,0:T(8,128)(2,1)}, bf16[16,4096]{1,0:T(8,128)(2,1)S(1)}, u32[]{:S(2)}, u32[]{:S(2)}) collective-permute-start(bf16[16,4096]{1,0:T(8,128)(2,1)} %bitcast.27), channel_id=1, source_target_pairs={{0,256},{16,272},{32,288},{48,304},{64,320},{80,336},{96,352},{112... | collective-permute-start | bytes 393224 | tf_op jit(solution)/shard_map/gather_z/ppermute | solution.py:30
  9.0 10.7 %collective-permute-start = (bf16[16,4096]{1,0:T(8,128)(2,1)}, bf16[16,4096]{1,0:T(8,128)(2,1)S(1)}, u32[]{:S(2)}, u32[]{:S(2)}) collective-permute-start(bf16[16,4096]{1,0:T(8,128)(2,1)} %bitcast.28), channel_id=1, source_target_pairs={{0,128},{16,144},{32,160},{48,176},{64,192},{80,208},{96,224},{112... | collective-permute-start | bytes 393224 | tf_op jit(solution)/shard_map/gather_z/ppermute | solution.py:30
  11.2 0.9 copy-start.2
  12.1 0.7 copy-start.3
  12.7 40.2 %copy-start.8 = (s32[1,256]{1,0:T(1,128)S(1)}, s32[1,256]{1,0:T(1,128)}, u32[]{:S(2)}) copy-start(s32[1,256]{1,0:T(1,128)} %param.7) | copy-start | bytes 3076
  13.8 13.6 %all-to-all-start = ((bf16[4,8,4224]{2,1,0:T(8,128)(2,1)}), bf16[4,8,4224]{2,1,0:T(8,128)(2,1)S(1)}, u32[]{:S(2)}, u32[]{:S(2)}) async-start(bf16[4,8,4224]{2,1,0:T(8,128)(2,1)} %bitcast.4), calls=%async_computation | async-start | bytes 540672 | tf_op jit(solution)/shard_map/hard_out/all_to_all | solution.py:56
  20.6 26.0 %collective-permute-start.4 = (bf16[64,4096]{1,0:T(8,128)(2,1)S(1)}, bf16[64,4096]{1,0:T(8,128)(2,1)}, u32[]{:S(2)}, u32[]{:S(2)}) collective-permute-start(bf16[64,4096]{1,0:T(8,128)(2,1)S(1)} %pad_maximum_fusion.refs_0_), channel_id=1, source_target_pairs={{0,64},{16,80},{32,96},{48,112},{64,0},{80,16},{96,32},{112,48},{1... | collective-permute-start | bytes 1572872 | tf_op jit(solution)/shard_map/gather_x/ppermute | solution.py:30
  23.6 24.9 %collective-permute-start.3 = (bf16[64,4096]{1,0:T(8,128)(2,1)S(1)}, bf16[64,4096]{1,0:T(8,128)(2,1)}, u32[]{:S(2)}, u32[]{:S(2)}) collective-permute-start(bf16[64,4096]{1,0:T(8,128)(2,1)S(1)} %pad_maximum_fusion.refs_0_), channel_id=1, source_target_pairs={{0,32},{16,48},{32,64},{48,80},{64,96},{80,112},{96,0},{112,16},{1... | collective-permute-start | bytes 1572872 | tf_op jit(solution)/shard_map/gather_x/ppermute | solution.py:30
  27.4 23.6 %collective-permute-start.5 = (bf16[64,4096]{1,0:T(8,128)(2,1)S(1)}, bf16[64,4096]{1,0:T(8,128)(2,1)}, u32[]{:S(2)}, u32[]{:S(2)}) collective-permute-start(bf16[64,4096]{1,0:T(8,128)(2,1)S(1)} %pad_maximum_fusion.refs_0_), channel_id=1, source_target_pairs={{0,96},{16,112},{32,0},{48,16},{64,32},{80,48},{96,64},{112,80},{1... | collective-permute-start | bytes 1572872 | tf_op jit(solution)/shard_map/gather_x/ppermute | solution.py:30
  30.2 29.2 %all-to-all-start.1 = ((bf16[4,8,4224]{2,1,0:T(8,128)(2,1)}), bf16[4,8,4224]{2,1,0:T(8,128)(2,1)S(1)}, u32[]{:S(2)}, u32[]{:S(2)}) async-start(bf16[4,8,4224]{2,1,0:T(8,128)(2,1)} %bitcast.6), calls=%async_computation.1 | async-start | bytes 540672 | tf_op jit(solution)/shard_map/hard_out/all_to_all | solution.py:56
  43.3 12.3 %collective-permute-start.6 = (bf16[64,4096]{1,0:T(8,128)(2,1)S(1)}, bf16[64,4096]{1,0:T(8,128)(2,1)}, u32[]{:S(2)}, u32[]{:S(2)}) collective-permute-start(bf16[64,4096]{1,0:T(8,128)(2,1)S(1)} %pad_maximum_fusion.refs_0_), channel_id=1, source_target_pairs={{0,16},{16,0},{32,48},{48,32},{64,80},{80,64},{96,112},{112,96},{1... | collective-permute-start | bytes 1572872 | tf_op jit(solution)/shard_map/gather_core/ppermute | solution.py:262
  46.6 12.8 %collective-permute-start.8 = (bf16[64,4096]{1,0:T(8,128)(2,1)}, bf16[64,4096]{1,0:T(8,128)(2,1)}, u32[]{:S(2)}, u32[]{:S(2)}) collective-permute-start(bf16[64,4096]{1,0:T(8,128)(2,1)} %collective-permute-done.4.refs_2_), channel_id=1, source_target_pairs={{0,16},{16,0},{32,48},{48,32},{64,80},{80,64},{96,112},{112,96},{1... | collective-permute-start | bytes 1572872 | tf_op jit(solution)/shard_map/gather_core/ppermute | solution.py:262
  48.5 10.9 %collective-permute-start.7 = (bf16[64,4096]{1,0:T(8,128)(2,1)}, bf16[64,4096]{1,0:T(8,128)(2,1)}, u32[]{:S(2)}, u32[]{:S(2)}) collective-permute-start(bf16[64,4096]{1,0:T(8,128)(2,1)} %collective-permute-done.3.refs_1_), channel_id=1, source_target_pairs={{0,16},{16,0},{32,48},{48,32},{64,80},{80,64},{96,112},{112,96},{1... | collective-permute-start | bytes 1572872 | tf_op jit(solution)/shard_map/gather_core/ppermute | solution.py:262
  50.9 8.5 %collective-permute-start.9 = (bf16[64,4096]{1,0:T(8,128)(2,1)}, bf16[64,4096]{1,0:T(8,128)(2,1)}, u32[]{:S(2)}, u32[]{:S(2)}) collective-permute-start(bf16[64,4096]{1,0:T(8,128)(2,1)} %collective-permute-done.5.refs_3_), channel_id=1, source_target_pairs={{0,16},{16,0},{32,48},{48,32},{64,80},{80,64},{96,112},{112,96},{1... | collective-permute-start | bytes 1572872 | tf_op jit(solution)/shard_map/gather_core/ppermute | solution.py:262
  63.3 9.3 %collective-permute-start.10 = (bf16[128,4096]{1,0:T(8,128)(2,1)S(1)}, bf16[128,4096]{1,0:T(8,128)(2,1)S(1)}, u32[]{:S(2)}, u32[]{:S(2)}) collective-permute-start(bf16[128,4096]{1,0:T(8,128)(2,1)S(1)} %get-tuple-element.32), channel_id=1, source_target_pairs={{0,16},{16,0},{32,48},{48,32},{64,80},{80,64},{96,112},{112,96},{1... | collective-permute-start | bytes 3145736 | tf_op jit(solution)/shard_map/scatter_core/ppermute | solution.py:298
  68.7 10.8 %collective-permute-start.11 = (bf16[128,4096]{1,0:T(8,128)(2,1)S(1)}, bf16[128,4096]{1,0:T(8,128)(2,1)S(1)}, u32[]{:S(2)}, u32[]{:S(2)}) collective-permute-start(bf16[128,4096]{1,0:T(8,128)(2,1)S(1)} %get-tuple-element.39), channel_id=1, source_target_pairs={{0,16},{16,0},{32,48},{48,32},{64,80},{80,64},{96,112},{112,96},{1... | collective-permute-start | bytes 3145736 | tf_op jit(solution)/shard_map/scatter_core/ppermute | solution.py:297
  71.1 0.7 copy-start.4
  71.8 0.7 copy-start.6
  73.8 1.0 copy-start.1
  74.8 26.9 %collective-permute-start.14 = (bf16[64,4096]{1,0:T(8,128)(2,1)}, bf16[64,4096]{1,0:T(8,128)(2,1)}, u32[]{:S(2)}, u32[]{:S(2)}) collective-permute-start(bf16[64,4096]{1,0:T(8,128)(2,1)} %get-tuple-element.42), channel_id=1, source_target_pairs={{0,32},{16,48},{32,64},{48,80},{64,96},{80,112},{96,0},{112,16},{1... | collective-permute-start | bytes 1572872 | tf_op jit(solution)/shard_map/scatter_x/ppermute | solution.py:30
  81.0 27.3 %collective-permute-start.12 = (bf16[64,4096]{1,0:T(8,128)(2,1)}, bf16[64,4096]{1,0:T(8,128)(2,1)}, u32[]{:S(2)}, u32[]{:S(2)}) collective-permute-start(bf16[64,4096]{1,0:T(8,128)(2,1)} %get-tuple-element.40), channel_id=1, source_target_pairs={{0,96},{16,112},{32,0},{48,16},{64,32},{80,48},{96,64},{112,80},{1... | collective-permute-start | bytes 1572872 | tf_op jit(solution)/shard_map/scatter_x/ppermute | solution.py:30
  82.9 25.4 %collective-permute-start.13 = (bf16[64,4096]{1,0:T(8,128)(2,1)}, bf16[64,4096]{1,0:T(8,128)(2,1)}, u32[]{:S(2)}, u32[]{:S(2)}) collective-permute-start(bf16[64,4096]{1,0:T(8,128)(2,1)} %get-tuple-element.41), channel_id=1, source_target_pairs={{0,64},{16,80},{32,96},{48,112},{64,0},{80,16},{96,32},{112,48},{1... | collective-permute-start | bytes 1572872 | tf_op jit(solution)/shard_map/scatter_x/ppermute | solution.py:30
  87.9 42.3 %all-to-all-start.2 = ((bf16[16,2,4096]{2,1,0:T(2,128)(2,1)}), bf16[16,2,4096]{2,1,0:T(2,128)(2,1)S(1)}, u32[]{:S(2)}, u32[]{:S(2)}) async-start(bf16[16,2,4096]{2,1,0:T(2,128)(2,1)} %hard_grad.1), calls=%async_computation.2 | async-start | bytes 524288 | tf_op jit(solution)/shard_map/hard_back/all_to_all | solution.py:319
  108.3 12.2 %copy-start.5 = (bf16[512,256]{1,0:T(8,128)(2,1)S(1)}, bf16[512,256]{1,0:T(8,128)(2,1)}, u32[]{:S(2)}) copy-start(bf16[512,256]{1,0:T(8,128)(2,1)} %copy-done.4) | copy-start | bytes 786436
  108.3 12.3 %copy-start.7 = (bf16[512,256]{1,0:T(8,128)(2,1)S(1)}, bf16[512,256]{1,0:T(8,128)(2,1)}, u32[]{:S(2)}) copy-start(bf16[512,256]{1,0:T(8,128)(2,1)} %copy-done.6) | copy-start | bytes 786436
  110.3 16.0 %collective-permute-start.15 = (bf16[16,4096]{1,0:T(8,128)(2,1)S(1)}, bf16[16,4096]{1,0:T(8,128)(2,1)S(1)}, u32[]{:S(2)}, u32[]{:S(2)}) collective-permute-start(bf16[16,4096]{1,0:T(8,128)(2,1)S(1)} %get-tuple-element.46), channel_id=1, source_target_pairs={{0,384},{16,400},{32,416},{48,432},{64,448},{80,464},{96,480},{112... | collective-permute-start | bytes 393224 | tf_op jit(solution)/shard_map/scatter_z/ppermute | solution.py:30
  114.4 11.9 %collective-permute-start.17 = (bf16[16,4096]{1,0:T(8,128)(2,1)S(1)}, bf16[16,4096]{1,0:T(8,128)(2,1)S(1)}, u32[]{:S(2)}, u32[]{:S(2)}) collective-permute-start(bf16[16,4096]{1,0:T(8,128)(2,1)S(1)} %get-tuple-element.47), channel_id=1, source_target_pairs={{0,128},{16,144},{32,160},{48,176},{64,192},{80,208},{96,224},{112... | collective-permute-start | bytes 393224 | tf_op jit(solution)/shard_map/scatter_z/ppermute | solution.py:30
  116.3 13.2 %collective-permute-start.16 = (bf16[16,4096]{1,0:T(8,128)(2,1)S(1)}, bf16[16,4096]{1,0:T(8,128)(2,1)S(1)}, u32[]{:S(2)}, u32[]{:S(2)}) collective-permute-start(bf16[16,4096]{1,0:T(8,128)(2,1)S(1)} %get-tuple-element.48), channel_id=1, source_target_pairs={{0,256},{16,272},{32,288},{48,304},{64,320},{80,336},{96,352},{112... | collective-permute-start | bytes 393224 | tf_op jit(solution)/shard_map/scatter_z/ppermute | solution.py:30

commit v9 on v8

--- a/solution.py
+++ b/solution.py
@@ -66,12 +66,13 @@
     return jax.ShapeDtypeStruct(dims, dtype)
 
 
-def call(kernel, outs, args, name, flops, grant, place=pltpu.VMEM, scratch=()):
+def call(kernel, outs, args, name, flops, grant, hbm=0, scratch=()):
     size = sum(a.size * a.dtype.itemsize for a in (*args, *outs))
     return pl.pallas_call(
         kernel,
         in_specs=[pl.BlockSpec(memory_space=pltpu.VMEM)] * len(args),
-        out_specs=[pl.BlockSpec(memory_space=place)] * len(outs),
+        out_specs=[pl.BlockSpec(memory_space=pltpu.VMEM)] * (len(outs) - hbm)
+        + [pl.BlockSpec(memory_space=pltpu.HBM)] * hbm,
         out_shape=outs,
         scratch_shapes=scratch,
         cost_estimate=pl.CostEstimate(flops=flops, bytes_accessed=size, transcendentals=0),
@@ -165,47 +166,58 @@
     s1_ref[...], sh_ref[...], log_ref[...] = s1, sh, log_total
 
 
-def coef_kernel(
-    slots, s0_ref, s1_ref, sh_ref, log_ref, column_ref,
-    mine_ref, hard_ref, both0_ref, both1_ref, bothh_ref, loss_ref,
+def mine_kernel(s_ref, log_ref, column_ref, out_ref):
+    coef = jnp.exp(s_ref[...] - log_ref[...]) - hot(column_ref, s_ref.shape, 0).astype(F32)
+    out_ref[...] = flip(coef.astype(BF16))
+
+
+def core_sum_kernel(start, skip, coef_ref, q_ref, away_ref, *out_refs):
+    n = out_refs[0].shape[0]
+    rows = n * len(out_refs)
+
+    def add(cols):
+        total = dot(coef_ref[start : start + rows], q_ref[:, cols])
+        total = total + away_ref[skip : skip + rows, cols].astype(F32)
+        for i, ref in enumerate(out_refs):
+            ref[:, cols] = total[i * n : (i + 1) * n].astype(ref.dtype)
+
+    over_columns(q_ref.shape[1], add)
+
+
+def rest_kernel(
+    scale, slots, s0_ref, s1_ref, sh_ref, log_ref, column_ref, mine_ref, q_ref, away_ref,
+    hard_ref, bothh_ref, loss_ref, both0_ref, both1_ref, own_ref,
+    made0, made1, made_own, sems,
 ):
     s0, s1, log_total = s0_ref[...], s1_ref[...], log_ref[...]
     count, half = s0.shape
+    copies = [
+        pltpu.make_async_copy(made, out, sems.at[i])
+        for i, (made, out) in enumerate(
+            ((made_own, own_ref), (made0, both0_ref), (made1, both1_ref))
+        )
+    ]
+    core_sum_kernel(0, 0, mine_ref, q_ref, away_ref, made_own)
+    copies[0].start()
     hot0, hot1 = hot(column_ref, s0.shape, 0), hot(column_ref, s0.shape, half)
-    hi0, lo0 = split(jnp.exp(s0 - log_total) - hot0.astype(F32))
-    mine_ref[...] = flip(hi0)
-    both0_ref[:count], both0_ref[count:] = hi0, lo0
+    made0[:count], made0[count:] = split(jnp.exp(s0 - log_total) - hot0.astype(F32))
+    copies[1].start()
+    made1[:count], made1[count:] = split(jnp.exp(s1 - log_total) - hot1.astype(F32))
+    copies[2].start()
     hih, loh = split(jnp.exp(sh_ref[...] - log_total))
-    hard_ref[...] = flip(hih, swapped(hih.shape[1], slots))
     bothh_ref[...] = jnp.concatenate([hih, loh], axis=1)
-    hi1, lo1 = split(jnp.exp(s1 - log_total) - hot1.astype(F32))
-    both1_ref[:count], both1_ref[count:] = hi1, lo1
+    coef = flip(hih, swapped(hih.shape[1], slots))
+
+    def grad(cols):
+        rows = scale * dot(coef, q_ref[:, cols])
+        for i in range(hard_ref.shape[0]):
+            hard_ref[i, :, cols] = rows[i * slots : (i + 1) * slots].astype(BF16)
+
+    over_columns(q_ref.shape[1], grad)
     at_target = jnp.sum(jnp.where(hot0, s0, 0.0) + jnp.where(hot1, s1, 0.0), axis=1, keepdims=True)
     loss_ref[...] = log_total - at_target
-
-
-def core_sum_kernel(first, coef_ref, q_ref, away_ref, *out_refs):
-    n = out_refs[0].shape[0]
-    coef = coef_ref[...]
-    coef = coef[n : 3 * n] if first else jnp.concatenate([coef[:n], coef[3 * n :]], axis=0)
-
-    def add(cols):
-        total = dot(coef, q_ref[:, cols]) + away_ref[:, cols].astype(F32)
-        for i, ref in enumerate(out_refs):
-            ref[:, cols] = total[i * n : (i + 1) * n].astype(ref.dtype)
-
-    over_columns(q_ref.shape[1], add)
-
-
-def hard_grad_kernel(scale, coef_ref, q_ref, out_ref):
-    places, slots, width = out_ref.shape
-
-    def grad(cols):
-        rows = scale * dot(coef_ref[...], q_ref[:, cols])
-        for i in range(places):
-            out_ref[i, :, cols] = rows[i * slots : (i + 1) * slots].astype(out_ref.dtype)
-
-    over_columns(width, grad)
+    for copy in copies:
+        copy.wait()
 
 
 def query_grad_kernel(scale, c0, c1, ch, *refs):
@@ -284,14 +296,9 @@
             (q, *far, received, s0, column.reshape(-1, 1)),
             "away", 4 * count * half * width, 10,
         )
-        mine_rows, hard_cols, both0, both1, both_hard, loss_rows = call(
-            functools.partial(coef_kernel, slots),
-            [
-                shape((half, count)), shape((places, count)), shape((2 * count, half)),
-                shape((2 * count, half)), shape((count, 2 * places)), shape((count, 1), F32),
-            ],
-            (s0, s1, sh, log_total, column.reshape(-1, 1)),
-            "coef", count * half * half, 8,
+        [mine_rows] = call(
+            mine_kernel, [shape((half, count))], (s0, log_total, column.reshape(-1, 1)),
+            "mine", 2 * count * half * half, 4,
         )
     with jax.named_scope("scatter_core"):
         first = lax.ppermute(first, "blk", CORE_SWAP)
@@ -299,32 +306,41 @@
     with jax.named_scope("scatter_x"):
         n = half // NX
         flops = count * half * width
+        [three] = call(
+            functools.partial(core_sum_kernel, 3 * n, n), [shape((n, width))],
+            (mine_rows, q, second), "core_sum_second", flops // 2, 8,
+        )
         one, two = call(
-            functools.partial(core_sum_kernel, True), [shape((n, width))] * 2,
+            functools.partial(core_sum_kernel, n, 0), [shape((n, width))] * 2,
             (mine_rows, q, first), "core_sum_first", flops, 8,
         )
-        zero, three = call(
-            functools.partial(core_sum_kernel, False), [shape((n, width), F32), shape((n, width))],
-            (mine_rows, q, second), "core_sum_second", flops, 8,
-        )
+    with jax.named_scope("rest"):
+        parts = shape((2 * count, half))
+        g, both_hard, loss_rows, both0, both1, zero = call(
+            functools.partial(rest_kernel, scale, slots),
+            [
+                shape((groups, slots, width)), shape((count, 2 * places)), shape((count, 1), F32),
+                parts, parts, shape((n, width), F32),
+            ],
+            (s0, s1, sh, log_total, column.reshape(-1, 1), mine_rows, q, second),
+            "rest", flops, 12, 3,
+            [
+                pltpu.VMEM(parts.shape, BF16), pltpu.VMEM(parts.shape, BF16),
+                pltpu.VMEM((n, width), F32), pltpu.SemaphoreType.DMA((3,)),
+            ],
+        )
+    with jax.named_scope("scatter_x"):
         chunks = [c.astype(F32) for c in exchange([zero, one, two, three], "blk", x_shift, -1)]
         mine_x = pieces(functools.reduce(jnp.add, chunks), NZ)
-
-    hard_cols, _ = lax.optimization_barrier((hard_cols, second))
     with jax.named_scope("hard_back"):
-        [g] = call(
-            functools.partial(hard_grad_kernel, scale), [shape((groups, slots, width))],
-            (hard_cols, q), "hard_grad", 2 * places * count * width, 4,
-        )
         returned = lax.all_to_all(g, "group", split_axis=0, concat_axis=0, tiled=True)
         d_owned = t_dot(placing, returned.reshape(places, width)).astype(BF16)
-    both0, _ = lax.optimization_barrier((both0, g))
     with jax.named_scope("d_query"):
         [d_query] = call(
             functools.partial(query_grad_kernel, scale),
             [shape((1, count, width))],
             (both0, both1, both_hard, *near, *far, received),
-            "query_grad", 4 * count * (2 * half + places) * width, 12, pl.ANY,
+            "query_grad", 4 * count * (2 * half + places) * width, 12, 1,
             [pltpu.VMEM((count, width), BF16), pltpu.SemaphoreType.DMA((width // 1024,))],
         )
     with jax.named_scope("scatter_z"):

time: 132 us -> 130 us (0.985)
  the two profiles are of different devices: /device:TPU:15 before, /device:TPU:1 now
where the time goes in v9:
time: 130 us; the launch traced here: 129 us
  starting transfers between devices  87.2 us (67%)
  Pallas kernels  19 us (15%)
  waiting for transfers between devices  11.8 us (9%)
  other arithmetic  4.76 us (4%)
  local copies, waits for them, and re-layouts  4.19 us (3%)
    ppermute x12, starting transfers between devices, exchange(): lax.ppermute(p, axis, perm(sign * d))  39.8 us
    pallas_call x9, Pallas kernels, call(): pl.pallas_call(kernel, in_specs=[pl.BlockSpec(memory_space=pltpu.VMEM)] *...  19 us
    all_to_all x2, starting transfers between devices, swap(): lax.all_to_all(x, 'group', split_axis=0, concat_axis=0, axis_index_groups...  16.9 us
    ppermute x12, waiting for transfers between devices, exchange(): lax.ppermute(p, axis, perm(sign * d))  11.7 us
    ppermute x4, starting transfers between devices, body(): far = [lax.ppermute(x, 'blk', CORE_SWAP) for x in near]  11.1 us
    ppermute x1, starting transfers between devices, body(): first = lax.ppermute(first, 'blk', CORE_SWAP)  9.13 us
    all_to_all x1, starting transfers between devices, body(): lax.all_to_all(g, 'group', split_axis=0, concat_axis=0, tiled=True)  8.44 us
    unnamed x18, local copies, waits for them, and re-layouts  3.93 us
  transfers between devices with their start and end apart: 21, of which 2 were waited for; matrix products, arithmetic and copies ran while one was open for 4% of the time, Pallas kernels for 12%

profile of v9, /device:TPU:1, one launch (start us, length us, event | category | flops | bytes accessed | tf_op | source)
XLA Modules:
  0.0 128.9 jit_solution(8040292058467495419)
XLA Ops:
  0.6 4.5 %collective-permute-start = (bf16[16,4096]{1,0:T(8,128)(2,1)}, bf16[16,4096]{1,0:T(8,128)(2,1)S(1)}, u32[]{:S(2)}, u32[]{:S(2)}) collective-permute-start(bf16[16,4096]{1,0:T(8,128)(2,1)} %bitcast.26), channel_id=1, source_target_pairs={{0,128},{16,144},{32,160},{48,176},{64,192},{80,208},{96,224},{112... | collective-permute-start | bytes 393224 | tf_op jit(solution)/shard_map/gather_z/ppermute | solution.py:30
  5.2 4.9 %collective-permute-start.1 = (bf16[16,4096]{1,0:T(8,128)(2,1)}, bf16[16,4096]{1,0:T(8,128)(2,1)S(1)}, u32[]{:S(2)}, u32[]{:S(2)}) collective-permute-start(bf16[16,4096]{1,0:T(8,128)(2,1)} %bitcast.27), channel_id=1, source_target_pairs={{0,256},{16,272},{32,288},{48,304},{64,320},{80,336},{96,352},{112... | collective-permute-start | bytes 393224 | tf_op jit(solution)/shard_map/gather_z/ppermute | solution.py:30
  10.1 2.6 %collective-permute-start.2 = (bf16[16,4096]{1,0:T(8,128)(2,1)}, bf16[16,4096]{1,0:T(8,128)(2,1)S(1)}, u32[]{:S(2)}, u32[]{:S(2)}) collective-permute-start(bf16[16,4096]{1,0:T(8,128)(2,1)} %bitcast.28), channel_id=1, source_target_pairs={{0,384},{16,400},{32,416},{48,432},{64,448},{80,464},{96,480},{112... | collective-permute-start | bytes 393224 | tf_op jit(solution)/shard_map/gather_z/ppermute | solution.py:30
  12.7 0.9 copy-done.2
  13.6 0.7 copy-done.3
  14.3 1.0 pack.1
  15.3 4.2 %all-to-all-start = ((bf16[4,8,4224]{2,1,0:T(8,128)(2,1)}), bf16[4,8,4224]{2,1,0:T(8,128)(2,1)S(1)}, u32[]{:S(2)}, u32[]{:S(2)}) async-start(bf16[4,8,4224]{2,1,0:T(8,128)(2,1)} %bitcast.4), calls=%async_computation | async-start | bytes 540672 | tf_op jit(solution)/shard_map/hard_out/all_to_all | solution.py:56
  19.5 0.0 collective-permute-done
  19.5 0.0 collective-permute-done.1
  19.5 0.0 collective-permute-done.2
  19.5 0.9 pad_maximum_fusion.refs_0_
  20.5 3.4 %collective-permute-start.3 = (bf16[64,4096]{1,0:T(8,128)(2,1)S(1)}, bf16[64,4096]{1,0:T(8,128)(2,1)}, u32[]{:S(2)}, u32[]{:S(2)}) collective-permute-start(bf16[64,4096]{1,0:T(8,128)(2,1)S(1)} %pad_maximum_fusion.refs_0_), channel_id=1, source_target_pairs={{0,32},{16,48},{32,64},{48,80},{64,96},{80,112},{96,0},{112,16},{1... | collective-permute-start | bytes 1572872 | tf_op jit(solution)/shard_map/gather_x/ppermute | solution.py:30
  23.8 4.4 %collective-permute-start.4 = (bf16[64,4096]{1,0:T(8,128)(2,1)S(1)}, bf16[64,4096]{1,0:T(8,128)(2,1)}, u32[]{:S(2)}, u32[]{:S(2)}) collective-permute-start(bf16[64,4096]{1,0:T(8,128)(2,1)S(1)} %pad_maximum_fusion.refs_0_), channel_id=1, source_target_pairs={{0,64},{16,80},{32,96},{48,112},{64,0},{80,16},{96,32},{112,48},{1... | collective-permute-start | bytes 1572872 | tf_op jit(solution)/shard_map/gather_x/ppermute | solution.py:30
  28.2 0.0 all-to-all-done
  28.2 3.1 %collective-permute-start.5 = (bf16[64,4096]{1,0:T(8,128)(2,1)S(1)}, bf16[64,4096]{1,0:T(8,128)(2,1)}, u32[]{:S(2)}, u32[]{:S(2)}) collective-permute-start(bf16[64,4096]{1,0:T(8,128)(2,1)S(1)} %pad_maximum_fusion.refs_0_), channel_id=1, source_target_pairs={{0,96},{16,112},{32,0},{48,16},{64,32},{80,48},{96,64},{112,80},{1... | collective-permute-start | bytes 1572872 | tf_op jit(solution)/shard_map/gather_x/ppermute | solution.py:30
  31.3 0.9 turn.1
  32.2 12.7 %all-to-all-start.1 = ((bf16[4,8,4224]{2,1,0:T(8,128)(2,1)}), bf16[4,8,4224]{2,1,0:T(8,128)(2,1)S(1)}, u32[]{:S(2)}, u32[]{:S(2)}) async-start(bf16[4,8,4224]{2,1,0:T(8,128)(2,1)} %bitcast.6), calls=%async_computation.1 | async-start | bytes 540672 | tf_op jit(solution)/shard_map/hard_out/all_to_all | solution.py:56
  45.0 4.8 %collective-permute-start.6 = (bf16[64,4096]{1,0:T(8,128)(2,1)S(1)}, bf16[64,4096]{1,0:T(8,128)(2,1)}, u32[]{:S(2)}, u32[]{:S(2)}) collective-permute-start(bf16[64,4096]{1,0:T(8,128)(2,1)S(1)} %pad_maximum_fusion.refs_0_), channel_id=1, source_target_pairs={{0,16},{16,0},{32,48},{48,32},{64,80},{80,64},{96,112},{112,96},{1... | collective-permute-start | bytes 1572872 | tf_op jit(solution)/shard_map/gather_core/ppermute | solution.py:274
  49.8 0.0 collective-permute-done.3.refs_1_
  49.8 1.9 %collective-permute-start.7 = (bf16[64,4096]{1,0:T(8,128)(2,1)}, bf16[64,4096]{1,0:T(8,128)(2,1)}, u32[]{:S(2)}, u32[]{:S(2)}) collective-permute-start(bf16[64,4096]{1,0:T(8,128)(2,1)} %collective-permute-done.3.refs_1_), channel_id=1, source_target_pairs={{0,16},{16,0},{32,48},{48,32},{64,80},{80,64},{96,112},{112,96},{1... | collective-permute-start | bytes 1572872 | tf_op jit(solution)/shard_map/gather_core/ppermute | solution.py:274
  51.7 0.0 collective-permute-done.4.refs_2_
  51.7 2.4 %collective-permute-start.8 = (bf16[64,4096]{1,0:T(8,128)(2,1)}, bf16[64,4096]{1,0:T(8,128)(2,1)}, u32[]{:S(2)}, u32[]{:S(2)}) collective-permute-start(bf16[64,4096]{1,0:T(8,128)(2,1)} %collective-permute-done.4.refs_2_), channel_id=1, source_target_pairs={{0,16},{16,0},{32,48},{48,32},{64,80},{80,64},{96,112},{112,96},{1... | collective-permute-start | bytes 1572872 | tf_op jit(solution)/shard_map/gather_core/ppermute | solution.py:274
  54.2 0.0 collective-permute-done.5.refs_3_
  54.2 1.9 %collective-permute-start.9 = (bf16[64,4096]{1,0:T(8,128)(2,1)}, bf16[64,4096]{1,0:T(8,128)(2,1)}, u32[]{:S(2)}, u32[]{:S(2)}) collective-permute-start(bf16[64,4096]{1,0:T(8,128)(2,1)} %collective-permute-done.5.refs_3_), channel_id=1, source_target_pairs={{0,16},{16,0},{32,48},{48,32},{64,80},{80,64},{96,112},{112,96},{1... | collective-permute-start | bytes 1572872 | tf_op jit(solution)/shard_map/gather_core/ppermute | solution.py:274
  56.1 0.1 copy.9
  56.3 0.5 fusion.13.column_ref
  56.8 2.1 %near.1.s0_ref.s_ref = f32[256,256]{1,0:T(8,128)S(1)} custom-call(bf16[256,4096]{1,0:T(8,128)(2,1)S(1)} %bitcast.16, bf16[64,4096]{1,0:T(8,128)(2,1)S(1)} %pad_maximum_fusion.refs_0_, bf16[64,4096]{1,0:T(8,128)(2,1)} %collective-permute-done.3.refs_1_, bf16[64,4096]{1,0:T(8,128)(2,1)} %collective-permute-done.4.refs_2_, ...), custom_call_target="tpu_custom_call" | custom-call | flops 536870912 | bytes 4456448 | tf_op jit(solution)/shard_map/scores/near/pallas_call | solution.py:71
  58.9 0.0 collective-permute-done.6.far0.refs_4_
  58.9 0.0 all-to-all-done.1
  58.9 0.0 collective-permute-done.7.far1.refs_5_
  58.9 0.0 collective-permute-done.8.far2.refs_6_
  58.9 0.0 collective-permute-done.9.far3.refs_7_
  58.9 3.8 %away.1 = (bf16[128,4096]{1,0:T(8,128)(2,1)S(1)}, bf16[128,4096]{1,0:T(8,128)(2,1)S(1)}, f32[256,256]{1,0:T(8,128)S(1)}, f32[256,32]{1,0:T(8,128)S(1)}, f32[256,1]{1,0:T(8,128)S(1)}) custom-call(bf16[256,4096]{1,0:T(8,128)(2,1)S(1)} %bitcast.17, bf16[64,4096]{1,0:T(8,128)(2,1)} %collective-permute-done.6.far0.refs_4_, ...), custom_call_target="tpu_custom_call" | custom-call | flops 1073741824 | bytes 7120896 | tf_op jit(solution)/shard_map/scores/away/pallas_call | solution.py:71
  62.8 9.1 %collective-permute-start.11 = (bf16[128,4096]{1,0:T(8,128)(2,1)S(1)}, bf16[128,4096]{1,0:T(8,128)(2,1)S(1)}, u32[]{:S(2)}, u32[]{:S(2)}) collective-permute-start(bf16[128,4096]{1,0:T(8,128)(2,1)S(1)} %get-tuple-element.31), channel_id=1, source_target_pairs={{0,16},{16,0},{32,48},{48,32},{64,80},{80,64},{96,112},{112,96},{1... | collective-permute-start | bytes 3145736 | tf_op jit(solution)/shard_map/scatter_core/ppermute | solution.py:304
  71.9 1.9 %collective-permute-start.10 = (bf16[128,4096]{1,0:T(8,128)(2,1)S(1)}, bf16[128,4096]{1,0:T(8,128)(2,1)S(1)}, u32[]{:S(2)}, u32[]{:S(2)}) collective-permute-start(bf16[128,4096]{1,0:T(8,128)(2,1)S(1)} %get-tuple-element.25), channel_id=1, source_target_pairs={{0,16},{16,0},{32,48},{48,32},{64,80},{80,64},{96,112},{112,96},{1... | collective-permute-start | bytes 3145736 | tf_op jit(solution)/shard_map/scatter_core/ppermute | solution.py:305
  73.8 0.3 mine.1.mine_ref.coef_ref
  74.2 0.0 collective-permute-done.11.away_ref
  74.2 1.4 %core_sum_first.1 = (bf16[64,4096]{1,0:T(8,128)(2,1)}, bf16[64,4096]{1,0:T(8,128)(2,1)}) custom-call(bf16[256,256]{1,0:T(8,128)(2,1)S(1)} %mine.1.mine_ref.coef_ref, bf16[256,4096]{1,0:T(8,128)(2,1)S(1)} %bitcast.18, bf16[128,4096]{1,0:T(8,128)(2,1)S(1)} %collective-permute-done.11.away_ref), custom_call_target="tpu_custom_call" | custom-call | flops 268435456 | bytes 4325376 | tf_op jit(solution)/shard_map/scatter_x/core_sum_first/pallas_call | solution.py:71
  75.6 1.9 %collective-permute-start.12 = (bf16[64,4096]{1,0:T(8,128)(2,1)}, bf16[64,4096]{1,0:T(8,128)(2,1)}, u32[]{:S(2)}, u32[]{:S(2)}) collective-permute-start(bf16[64,4096]{1,0:T(8,128)(2,1)} %get-tuple-element.32), channel_id=1, source_target_pairs={{0,96},{16,112},{32,0},{48,16},{64,32},{80,48},{96,64},{112,80},{1... | collective-permute-start | bytes 1572872 | tf_op jit(solution)/shard_map/scatter_x/ppermute | solution.py:30
  77.5 4.0 %collective-permute-start.13 = (bf16[64,4096]{1,0:T(8,128)(2,1)}, bf16[64,4096]{1,0:T(8,128)(2,1)}, u32[]{:S(2)}, u32[]{:S(2)}) collective-permute-start(bf16[64,4096]{1,0:T(8,128)(2,1)} %get-tuple-element.33), channel_id=1, source_target_pairs={{0,64},{16,80},{32,96},{48,112},{64,0},{80,16},{96,32},{112,48},{1... | collective-permute-start | bytes 1572872 | tf_op jit(solution)/shard_map/scatter_x/ppermute | solution.py:30
  81.5 0.0 collective-permute-done.10.away_ref
  81.5 1.3 %core_sum_second.1 = bf16[64,4096]{1,0:T(8,128)(2,1)} custom-call(bf16[256,256]{1,0:T(8,128)(2,1)S(1)} %mine.1.mine_ref.coef_ref, bf16[256,4096]{1,0:T(8,128)(2,1)S(1)} %bitcast.19, bf16[128,4096]{1,0:T(8,128)(2,1)S(1)} %collective-permute-done.10.away_ref), custom_call_target="tpu_custom_call" | custom-call | flops 134217728 | bytes 3801088 | tf_op jit(solution)/shard_map/scatter_x/core_sum_second/pallas_call | solution.py:71
  82.8 1.9 %collective-permute-start.14 = (bf16[64,4096]{1,0:T(8,128)(2,1)}, bf16[64,4096]{1,0:T(8,128)(2,1)}, u32[]{:S(2)}, u32[]{:S(2)}) collective-permute-start(bf16[64,4096]{1,0:T(8,128)(2,1)} %core_sum_second.1), channel_id=1, source_target_pairs={{0,32},{16,48},{32,64},{48,80},{64,96},{80,112},{96,0},{112,16},{1... | collective-permute-start | bytes 1572872 | tf_op jit(solution)/shard_map/scatter_x/ppermute | solution.py:30
  84.8 2.3 %rest.1 = (bf16[16,2,4096]{2,1,0:T(2,128)(2,1)}, bf16[256,64]{1,0:T(8,128)(2,1)S(1)}, f32[256,1]{1,0:T(8,128)S(1)}, bf16[512,256]{1,0:T(8,128)(2,1)S(1)}, bf16[5...) custom-call(f32[256,256]{1,0:T(8,128)S(1)} %near.1.s0_ref.s_ref, f32[256,256]{1,0:T(8,128)S(1)} %get-tuple-element.22.s1_ref, ...), custom_call_target="tpu_custom_call" | custom-call | flops 268435456 | bytes 5704704 | tf_op jit(solution)/shard_map/rest/rest/pallas_call | solution.py:71
  87.1 0.0 copy-start.1
  87.1 1.0 copy-done.1
  88.0 0.7 copy-done.4
  88.7 0.7 copy-done.6
  89.4 8.4 %all-to-all-start.2 = ((bf16[16,2,4096]{2,1,0:T(2,128)(2,1)}), bf16[16,2,4096]{2,1,0:T(2,128)(2,1)S(1)}, u32[]{:S(2)}, u32[]{:S(2)}) async-start(bf16[16,2,4096]{2,1,0:T(2,128)(2,1)} %get-tuple-element.35), calls=%async_computation.2 | async-start | bytes 524288 | tf_op jit(solution)/shard_map/hard_back/all_to_all | solution.py:336
  97.9 0.0 collective-permute-done.12
  97.9 0.0 collective-permute-done.13
  97.9 8.4 %collective-permute-done.14 = bf16[64,4096]{1,0:T(8,128)(2,1)} collective-permute-done((bf16[64,4096]{1,0:T(8,128)(2,1)}, bf16[64,4096]{1,0:T(8,128)(2,1)}, u32[]{:S(2)}, u32[]{:S(2)}) %collective-permute-start.14) | collective-permute-done | bytes 524320 | tf_op jit(solution)/shard_map/scatter_x/ppermute | solution.py:30
  106.3 2.0 %fusion.21 = (bf16[64,4096]{1,0:T(8,128)(2,1)S(1)}, f32[64,4096]{1,0:T(8,128)S(1)}) fusion(bf16[64,4096]{1,0:T(8,128)(2,1)} %collective-permute-done.14, bf16[64,4096]{1,0:T(8,128)(2,1)} %collective-permute-done.13, f32[64,4096]{1,0:T(8,128)} %copy-done.1, bf16[64,4096]{1,0:T(8,128)(2,1)} %collective-permute-done.12), kind=kLoop, calls=%fused_computation.49 | loop fusion | flops 1835008 | bytes 4194304 | tf_op jit(solution)/shard_map/convert.2
  108.3 5.0 %collective-permute-start.15 = (bf16[16,4096]{1,0:T(8,128)(2,1)S(1)}, bf16[16,4096]{1,0:T(8,128)(2,1)S(1)}, u32[]{:S(2)}, u32[]{:S(2)}) collective-permute-start(bf16[16,4096]{1,0:T(8,128)(2,1)S(1)} %get-tuple-element.38), channel_id=1, source_target_pairs={{0,384},{16,400},{32,416},{48,432},{64,448},{80,464},{96,480},{112... | collective-permute-start | bytes 393224 | tf_op jit(solution)/shard_map/scatter_z/ppermute | solution.py:30
  113.4 2.0 %collective-permute-start.16 = (bf16[16,4096]{1,0:T(8,128)(2,1)S(1)}, bf16[16,4096]{1,0:T(8,128)(2,1)S(1)}, u32[]{:S(2)}, u32[]{:S(2)}) collective-permute-start(bf16[16,4096]{1,0:T(8,128)(2,1)S(1)} %get-tuple-element.40), channel_id=1, source_target_pairs={{0,256},{16,272},{32,288},{48,304},{64,320},{80,336},{96,352},{112... | collective-permute-start | bytes 393224 | tf_op jit(solution)/shard_map/scatter_z/ppermute | solution.py:30
  115.3 2.1 %collective-permute-start.17 = (bf16[16,4096]{1,0:T(8,128)(2,1)S(1)}, bf16[16,4096]{1,0:T(8,128)(2,1)S(1)}, u32[]{:S(2)}, u32[]{:S(2)}) collective-permute-start(bf16[16,4096]{1,0:T(8,128)(2,1)S(1)} %get-tuple-element.39), channel_id=1, source_target_pairs={{0,128},{16,144},{32,160},{48,176},{64,192},{80,208},{96,224},{112... | collective-permute-start | bytes 393224 | tf_op jit(solution)/shard_map/scatter_z/ppermute | solution.py:30
  117.5 5.7 %query_grad.1 = bf16[1,256,4096]{2,1,0:T(8,128)(2,1)} custom-call(bf16[512,256]{1,0:T(8,128)(2,1)S(1)} %copy-done.5, bf16[512,256]{1,0:T(8,128)(2,1)S(1)} %copy-done.7, bf16[256,64]{1,0:T(8,128)(2,1)S(1)} %get-tuple-element.29.ch, bf16[64,4096]{1,0:T(8,128)(2,1)S(1)} %pad_maximum_fusion.refs_0_, bf16[64,4096]{1,0:T(8,128)(2,1)} %collective-permute-done.3.refs_1_, ...), custom_call_target="tpu_custom_call" | custom-call | flops 2281701376 | bytes 7118848 | tf_op jit(solution)/shard_map/d_query/query_grad/pallas_call | solution.py:71
  123.2 0.7 reduce
  123.9 0.0 collective-permute-done.15
  123.9 3.3 %collective-permute-done.16 = bf16[16,4096]{1,0:T(8,128)(2,1)S(1)} collective-permute-done((bf16[16,4096]{1,0:T(8,128)(2,1)S(1)}, bf16[16,4096]{1,0:T(8,128)(2,1)S(1)}, u32[]{:S(2)}, u32[]{:S(2)}) %collective-permute-start.16) | collective-permute-done | bytes 131104 | tf_op jit(solution)/shard_map/scatter_z/ppermute | solution.py:30
  127.2 0.0 collective-permute-done.17
  127.2 0.7 fusion.17
  127.9 0.1 reshape.341
  128.0 0.9 fusion
  (14 shorter events, 0.1 us)
Async XLA Ops:
  0.6 56.1 %copy-start = (bf16[1,256,4096]{2,1,0:T(8,128)(2,1)S(1)}, bf16[1,256,4096]{2,1,0:T(8,128)(2,1)}, u32[]{:S(2)}) copy-start(bf16[1,256,4096]{2,1,0:T(8,128)(2,1)} %param.5) | copy-start | bytes 6291460
  0.6 18.9 %collective-permute-start = (bf16[16,4096]{1,0:T(8,128)(2,1)}, bf16[16,4096]{1,0:T(8,128)(2,1)S(1)}, u32[]{:S(2)}, u32[]{:S(2)}) collective-permute-start(bf16[16,4096]{1,0:T(8,128)(2,1)} %bitcast.26), channel_id=1, source_target_pairs={{0,128},{16,144},{32,160},{48,176},{64,192},{80,208},{96,224},{112... | collective-permute-start | bytes 393224 | tf_op jit(solution)/shard_map/gather_z/ppermute | solution.py:30
  5.2 14.3 %collective-permute-start.1 = (bf16[16,4096]{1,0:T(8,128)(2,1)}, bf16[16,4096]{1,0:T(8,128)(2,1)S(1)}, u32[]{:S(2)}, u32[]{:S(2)}) collective-permute-start(bf16[16,4096]{1,0:T(8,128)(2,1)} %bitcast.27), channel_id=1, source_target_pairs={{0,256},{16,272},{32,288},{48,304},{64,320},{80,336},{96,352},{112... | collective-permute-start | bytes 393224 | tf_op jit(solution)/shard_map/gather_z/ppermute | solution.py:30
  10.1 9.4 %collective-permute-start.2 = (bf16[16,4096]{1,0:T(8,128)(2,1)}, bf16[16,4096]{1,0:T(8,128)(2,1)S(1)}, u32[]{:S(2)}, u32[]{:S(2)}) collective-permute-start(bf16[16,4096]{1,0:T(8,128)(2,1)} %bitcast.28), channel_id=1, source_target_pairs={{0,384},{16,400},{32,416},{48,432},{64,448},{80,464},{96,480},{112... | collective-permute-start | bytes 393224 | tf_op jit(solution)/shard_map/gather_z/ppermute | solution.py:30
  12.7 0.9 copy-start.2
  13.6 0.7 copy-start.3
  14.3 41.9 %copy-start.8 = (s32[1,256]{1,0:T(1,128)S(1)}, s32[1,256]{1,0:T(1,128)}, u32[]{:S(2)}) copy-start(s32[1,256]{1,0:T(1,128)} %param.7) | copy-start | bytes 3076
  15.3 12.9 %all-to-all-start = ((bf16[4,8,4224]{2,1,0:T(8,128)(2,1)}), bf16[4,8,4224]{2,1,0:T(8,128)(2,1)S(1)}, u32[]{:S(2)}, u32[]{:S(2)}) async-start(bf16[4,8,4224]{2,1,0:T(8,128)(2,1)} %bitcast.4), calls=%async_computation | async-start | bytes 540672 | tf_op jit(solution)/shard_map/hard_out/all_to_all | solution.py:56
  20.5 29.3 %collective-permute-start.3 = (bf16[64,4096]{1,0:T(8,128)(2,1)S(1)}, bf16[64,4096]{1,0:T(8,128)(2,1)}, u32[]{:S(2)}, u32[]{:S(2)}) collective-permute-start(bf16[64,4096]{1,0:T(8,128)(2,1)S(1)} %pad_maximum_fusion.refs_0_), channel_id=1, source_target_pairs={{0,32},{16,48},{32,64},{48,80},{64,96},{80,112},{96,0},{112,16},{1... | collective-permute-start | bytes 1572872 | tf_op jit(solution)/shard_map/gather_x/ppermute | solution.py:30
  23.8 27.9 %collective-permute-start.4 = (bf16[64,4096]{1,0:T(8,128)(2,1)S(1)}, bf16[64,4096]{1,0:T(8,128)(2,1)}, u32[]{:S(2)}, u32[]{:S(2)}) collective-permute-start(bf16[64,4096]{1,0:T(8,128)(2,1)S(1)} %pad_maximum_fusion.refs_0_), channel_id=1, source_target_pairs={{0,64},{16,80},{32,96},{48,112},{64,0},{80,16},{96,32},{112,48},{1... | collective-permute-start | bytes 1572872 | tf_op jit(solution)/shard_map/gather_x/ppermute | solution.py:30
  28.2 25.9 %collective-permute-start.5 = (bf16[64,4096]{1,0:T(8,128)(2,1)S(1)}, bf16[64,4096]{1,0:T(8,128)(2,1)}, u32[]{:S(2)}, u32[]{:S(2)}) collective-permute-start(bf16[64,4096]{1,0:T(8,128)(2,1)S(1)} %pad_maximum_fusion.refs_0_), channel_id=1, source_target_pairs={{0,96},{16,112},{32,0},{48,16},{64,32},{80,48},{96,64},{112,80},{1... | collective-permute-start | bytes 1572872 | tf_op jit(solution)/shard_map/gather_x/ppermute | solution.py:30
  32.2 26.7 %all-to-all-start.1 = ((bf16[4,8,4224]{2,1,0:T(8,128)(2,1)}), bf16[4,8,4224]{2,1,0:T(8,128)(2,1)S(1)}, u32[]{:S(2)}, u32[]{:S(2)}) async-start(bf16[4,8,4224]{2,1,0:T(8,128)(2,1)} %bitcast.6), calls=%async_computation.1 | async-start | bytes 540672 | tf_op jit(solution)/shard_map/hard_out/all_to_all | solution.py:56
  45.0 13.9 %collective-permute-start.6 = (bf16[64,4096]{1,0:T(8,128)(2,1)S(1)}, bf16[64,4096]{1,0:T(8,128)(2,1)}, u32[]{:S(2)}, u32[]{:S(2)}) collective-permute-start(bf16[64,4096]{1,0:T(8,128)(2,1)S(1)} %pad_maximum_fusion.refs_0_), channel_id=1, source_target_pairs={{0,16},{16,0},{32,48},{48,32},{64,80},{80,64},{96,112},{112,96},{1... | collective-permute-start | bytes 1572872 | tf_op jit(solution)/shard_map/gather_core/ppermute | solution.py:274
  49.8 9.1 %collective-permute-start.7 = (bf16[64,4096]{1,0:T(8,128)(2,1)}, bf16[64,4096]{1,0:T(8,128)(2,1)}, u32[]{:S(2)}, u32[]{:S(2)}) collective-permute-start(bf16[64,4096]{1,0:T(8,128)(2,1)} %collective-permute-done.3.refs_1_), channel_id=1, source_target_pairs={{0,16},{16,0},{32,48},{48,32},{64,80},{80,64},{96,112},{112,96},{1... | collective-permute-start | bytes 1572872 | tf_op jit(solution)/shard_map/gather_core/ppermute | solution.py:274
  51.7 7.2 %collective-permute-start.8 = (bf16[64,4096]{1,0:T(8,128)(2,1)}, bf16[64,4096]{1,0:T(8,128)(2,1)}, u32[]{:S(2)}, u32[]{:S(2)}) collective-permute-start(bf16[64,4096]{1,0:T(8,128)(2,1)} %collective-permute-done.4.refs_2_), channel_id=1, source_target_pairs={{0,16},{16,0},{32,48},{48,32},{64,80},{80,64},{96,112},{112,96},{1... | collective-permute-start | bytes 1572872 | tf_op jit(solution)/shard_map/gather_core/ppermute | solution.py:274
  54.2 4.8 %collective-permute-start.9 = (bf16[64,4096]{1,0:T(8,128)(2,1)}, bf16[64,4096]{1,0:T(8,128)(2,1)}, u32[]{:S(2)}, u32[]{:S(2)}) collective-permute-start(bf16[64,4096]{1,0:T(8,128)(2,1)} %collective-permute-done.5.refs_3_), channel_id=1, source_target_pairs={{0,16},{16,0},{32,48},{48,32},{64,80},{80,64},{96,112},{112,96},{1... | collective-permute-start | bytes 1572872 | tf_op jit(solution)/shard_map/gather_core/ppermute | solution.py:274
  62.8 11.4 %collective-permute-start.11 = (bf16[128,4096]{1,0:T(8,128)(2,1)S(1)}, bf16[128,4096]{1,0:T(8,128)(2,1)S(1)}, u32[]{:S(2)}, u32[]{:S(2)}) collective-permute-start(bf16[128,4096]{1,0:T(8,128)(2,1)S(1)} %get-tuple-element.31), channel_id=1, source_target_pairs={{0,16},{16,0},{32,48},{48,32},{64,80},{80,64},{96,112},{112,96},{1... | collective-permute-start | bytes 3145736 | tf_op jit(solution)/shard_map/scatter_core/ppermute | solution.py:304
  71.9 9.6 %collective-permute-start.10 = (bf16[128,4096]{1,0:T(8,128)(2,1)S(1)}, bf16[128,4096]{1,0:T(8,128)(2,1)S(1)}, u32[]{:S(2)}, u32[]{:S(2)}) collective-permute-start(bf16[128,4096]{1,0:T(8,128)(2,1)S(1)} %get-tuple-element.25), channel_id=1, source_target_pairs={{0,16},{16,0},{32,48},{48,32},{64,80},{80,64},{96,112},{112,96},{1... | collective-permute-start | bytes 3145736 | tf_op jit(solution)/shard_map/scatter_core/ppermute | solution.py:305
  75.6 22.3 %collective-permute-start.12 = (bf16[64,4096]{1,0:T(8,128)(2,1)}, bf16[64,4096]{1,0:T(8,128)(2,1)}, u32[]{:S(2)}, u32[]{:S(2)}) collective-permute-start(bf16[64,4096]{1,0:T(8,128)(2,1)} %get-tuple-element.32), channel_id=1, source_target_pairs={{0,96},{16,112},{32,0},{48,16},{64,32},{80,48},{96,64},{112,80},{1... | collective-permute-start | bytes 1572872 | tf_op jit(solution)/shard_map/scatter_x/ppermute | solution.py:30
  77.5 20.4 %collective-permute-start.13 = (bf16[64,4096]{1,0:T(8,128)(2,1)}, bf16[64,4096]{1,0:T(8,128)(2,1)}, u32[]{:S(2)}, u32[]{:S(2)}) collective-permute-start(bf16[64,4096]{1,0:T(8,128)(2,1)} %get-tuple-element.33), channel_id=1, source_target_pairs={{0,64},{16,80},{32,96},{48,112},{64,0},{80,16},{96,32},{112,48},{1... | collective-permute-start | bytes 1572872 | tf_op jit(solution)/shard_map/scatter_x/ppermute | solution.py:30
  82.8 23.5 %collective-permute-start.14 = (bf16[64,4096]{1,0:T(8,128)(2,1)}, bf16[64,4096]{1,0:T(8,128)(2,1)}, u32[]{:S(2)}, u32[]{:S(2)}) collective-permute-start(bf16[64,4096]{1,0:T(8,128)(2,1)} %core_sum_second.1), channel_id=1, source_target_pairs={{0,32},{16,48},{32,64},{48,80},{64,96},{80,112},{96,0},{112,16},{1... | collective-permute-start | bytes 1572872 | tf_op jit(solution)/shard_map/scatter_x/ppermute | solution.py:30
  87.1 1.0 copy-start.1
  88.0 0.7 copy-start.4
  88.7 0.7 copy-start.6
  89.4 38.5 %all-to-all-start.2 = ((bf16[16,2,4096]{2,1,0:T(2,128)(2,1)}), bf16[16,2,4096]{2,1,0:T(2,128)(2,1)S(1)}, u32[]{:S(2)}, u32[]{:S(2)}) async-start(bf16[16,2,4096]{2,1,0:T(2,128)(2,1)} %get-tuple-element.35), calls=%async_computation.2 | async-start | bytes 524288 | tf_op jit(solution)/shard_map/hard_back/all_to_all | solution.py:336
  106.3 11.2 %copy-start.5 = (bf16[512,256]{1,0:T(8,128)(2,1)S(1)}, bf16[512,256]{1,0:T(8,128)(2,1)}, u32[]{:S(2)}) copy-start(bf16[512,256]{1,0:T(8,128)(2,1)} %copy-done.4) | copy-start | bytes 786436
  106.3 11.2 %copy-start.7 = (bf16[512,256]{1,0:T(8,128)(2,1)S(1)}, bf16[512,256]{1,0:T(8,128)(2,1)}, u32[]{:S(2)}) copy-start(bf16[512,256]{1,0:T(8,128)(2,1)} %copy-done.6) | copy-start | bytes 786436
  108.3 15.6 %collective-permute-start.15 = (bf16[16,4096]{1,0:T(8,128)(2,1)S(1)}, bf16[16,4096]{1,0:T(8,128)(2,1)S(1)}, u32[]{:S(2)}, u32[]{:S(2)}) collective-permute-start(bf16[16,4096]{1,0:T(8,128)(2,1)S(1)} %get-tuple-element.38), channel_id=1, source_target_pairs={{0,384},{16,400},{32,416},{48,432},{64,448},{80,464},{96,480},{112... | collective-permute-start | bytes 393224 | tf_op jit(solution)/shard_map/scatter_z/ppermute | solution.py:30
  113.4 13.8 %collective-permute-start.16 = (bf16[16,4096]{1,0:T(8,128)(2,1)S(1)}, bf16[16,4096]{1,0:T(8,128)(2,1)S(1)}, u32[]{:S(2)}, u32[]{:S(2)}) collective-permute-start(bf16[16,4096]{1,0:T(8,128)(2,1)S(1)} %get-tuple-element.40), channel_id=1, source_target_pairs={{0,256},{16,272},{32,288},{48,304},{64,320},{80,336},{96,352},{112... | collective-permute-start | bytes 393224 | tf_op jit(solution)/shard_map/scatter_z/ppermute | solution.py:30
  115.3 11.8 %collective-permute-start.17 = (bf16[16,4096]{1,0:T(8,128)(2,1)S(1)}, bf16[16,4096]{1,0:T(8,128)(2,1)S(1)}, u32[]{:S(2)}, u32[]{:S(2)}) collective-permute-start(bf16[16,4096]{1,0:T(8,128)(2,1)S(1)} %get-tuple-element.39), channel_id=1, source_target_pairs={{0,128},{16,144},{32,160},{48,176},{64,192},{80,208},{96,224},{112... | collective-permute-start | bytes 393224 | tf_op jit(solution)/shard_map/scatter_z/ppermute | solution.py:30

commit v10 on v9

--- a/solution.py
+++ b/solution.py
@@ -218,6 +218,21 @@
     loss_ref[...] = log_total - at_target
     for copy in copies:
         copy.wait()
+
+
+def x_sum_kernel(*refs):
+    chunks, outs, held, sems = refs[:NX], refs[NX : NX + NZ], refs[NX + NZ : -1], refs[-1]
+    copies = [
+        pltpu.make_async_copy(c, h, sems.at[i]) for i, (c, h) in enumerate(zip(chunks, held))
+    ]
+    for copy in copies:
+        copy.start()
+    for copy in copies:
+        copy.wait()
+    total = functools.reduce(jnp.add, [h[...].astype(F32) for h in held])
+    n = outs[0].shape[0]
+    for d, ref in enumerate(outs):
+        ref[...] = total[d * n : (d + 1) * n].astype(ref.dtype)
 
 
 def query_grad_kernel(scale, c0, c1, ch, *refs):
@@ -330,8 +345,22 @@
             ],
         )
     with jax.named_scope("scatter_x"):
-        chunks = [c.astype(F32) for c in exchange([zero, one, two, three], "blk", x_shift, -1)]
-        mine_x = pieces(functools.reduce(jnp.add, chunks), NZ)
+        chunks = exchange([zero, one, two, three], "blk", x_shift, -1)
+        loss_rows = loss_rows.reshape(1, -1)
+        chunks[1], loss_rows = lax.optimization_barrier((chunks[1], loss_rows))
+        mine_x = pl.pallas_call(
+            x_sum_kernel,
+            in_specs=[pl.BlockSpec(memory_space=pltpu.HBM)] * NX,
+            out_specs=[pl.BlockSpec(memory_space=pltpu.VMEM)] * NZ,
+            out_shape=[shape((rows, width), F32)] + [shape((rows, width))] * (NZ - 1),
+            scratch_shapes=[pltpu.VMEM(c.shape, c.dtype) for c in chunks]
+            + [pltpu.SemaphoreType.DMA((NX,))],
+            cost_estimate=pl.CostEstimate(
+                flops=4 * n * width, bytes_accessed=12 * n * width, transcendentals=0
+            ),
+            compiler_params=pltpu.CompilerParams(vmem_limit_bytes=8 << 20),
+            name="x_sum",
+        )(*chunks)
     with jax.named_scope("hard_back"):
         returned = lax.all_to_all(g, "group", split_axis=0, concat_axis=0, tiled=True)
         d_owned = t_dot(placing, returned.reshape(places, width)).astype(BF16)
@@ -344,10 +373,9 @@
             [pltpu.VMEM((count, width), BF16), pltpu.SemaphoreType.DMA((width // 1024,))],
         )
     with jax.named_scope("scatter_z"):
-        sent = [mine_x[0]] + [m.astype(BF16) for m in mine_x[1:]]
-        chunks = [c.astype(F32) for c in exchange(sent, "blk", z_shift, -1)]
+        chunks = [c.astype(F32) for c in exchange(list(mine_x), "blk", z_shift, -1)]
         d_passage = (scale * functools.reduce(jnp.add, chunks)).astype(BF16)
-    return (loss_rows.reshape(1, -1), d_query, d_passage[None], d_owned[None])
+    return (loss_rows, d_query, d_passage[None], d_owned[None])
 
 
 def solution(mesh):

time: 130 us -> 130 us (level)
  other arithmetic: 4.76 us -> 2.8 us
  starting transfers between devices: 87.2 us -> 85.4 us
  Pallas kernels: 19 us -> 20.6 us
    ppermute x1, starting transfers between devices: 9.13 us -> 5.47 us  [body(): first = lax.ppermute(first, 'blk', CORE_SWAP)]
    all_to_all x2, waiting for transfers between devices: 0.01 us -> 3.48 us  [swap(): lax.all_to_all(x, 'group', split_axis=0, concat_axis=0, axis_index_groups...]
    ppermute x12, waiting for transfers between devices: 11.7 us -> 9.02 us  [exchange(): lax.ppermute(p, axis, perm(sign * d))]
    another operation x1 -> x0, other arithmetic: 1.96 us -> none
    pallas_call x0 -> x1, Pallas kernels: none -> 1.68 us  [body(): pl.pallas_call(x_sum_kernel, in_specs=[pl.BlockSpec(memory_space=pltpu.HB...]
    ppermute x12, starting transfers between devices: 39.8 us -> 41.5 us  [exchange(): lax.ppermute(p, axis, perm(sign * d))]
    unnamed x18 -> x20, local copies, waits for them, and re-layouts: 3.93 us -> 5.16 us
  transfers between devices with their start and end apart: 21 -> 21, of which waited for: 2 -> 3; matrix products, arithmetic and copies ran while one was open for 4% -> 2% of each run, Pallas kernels for 12% -> 13%
where the time goes in v10:
time: 130 us; the launch traced here: 129 us
  starting transfers between devices  85.4 us (66%)
  Pallas kernels  20.6 us (16%)
  waiting for transfers between devices  12.5 us (10%)
  local copies, waits for them, and re-layouts  5.39 us (4%)
  other arithmetic  2.8 us (2%)
    ppermute x12, starting transfers between devices, exchange(): lax.ppermute(p, axis, perm(sign * d))  41.5 us
    pallas_call x9, Pallas kernels, call(): pl.pallas_call(kernel, in_specs=[pl.BlockSpec(memory_space=pltpu.VMEM)] *...  19 us
    all_to_all x2, starting transfers between devices, swap(): lax.all_to_all(x, 'group', split_axis=0, concat_axis=0, axis_index_groups...  17.3 us
    ppermute x4, starting transfers between devices, body(): far = [lax.ppermute(x, 'blk', CORE_SWAP) for x in near]  9.77 us
    all_to_all x1, starting transfers between devices, body(): lax.all_to_all(g, 'group', split_axis=0, concat_axis=0, tiled=True)  9.47 us
    ppermute x12, waiting for transfers between devices, exchange(): lax.ppermute(p, axis, perm(sign * d))  9.02 us
    ppermute x1, starting transfers between devices, body(): first = lax.ppermute(first, 'blk', CORE_SWAP)  5.47 us
    unnamed x20, local copies, waits for them, and re-layouts  5.16 us
  transfers between devices with their start and end apart: 21, of which 3 were waited for; matrix products, arithmetic and copies ran while one was open for 2% of the time, Pallas kernels for 13%

profile of v10, /device:TPU:1, one launch (start us, length us, event | category | flops | bytes accessed | tf_op | source)
XLA Modules:
  0.0 128.7 jit_solution(16683839380939120229)
XLA Ops:
  0.6 7.2 %collective-permute-start.2 = (bf16[16,4096]{1,0:T(8,128)(2,1)}, bf16[16,4096]{1,0:T(8,128)(2,1)S(1)}, u32[]{:S(2)}, u32[]{:S(2)}) collective-permute-start(bf16[16,4096]{1,0:T(8,128)(2,1)} %bitcast.26), channel_id=1, source_target_pairs={{0,384},{16,400},{32,416},{48,432},{64,448},{80,464},{96,480},{112... | collective-permute-start | bytes 393224 | tf_op jit(solution)/shard_map/gather_z/ppermute | solution.py:30
  7.9 1.9 %collective-permute-start.1 = (bf16[16,4096]{1,0:T(8,128)(2,1)}, bf16[16,4096]{1,0:T(8,128)(2,1)S(1)}, u32[]{:S(2)}, u32[]{:S(2)}) collective-permute-start(bf16[16,4096]{1,0:T(8,128)(2,1)} %bitcast.27), channel_id=1, source_target_pairs={{0,256},{16,272},{32,288},{48,304},{64,320},{80,336},{96,352},{112... | collective-permute-start | bytes 393224 | tf_op jit(solution)/shard_map/gather_z/ppermute | solution.py:30
  9.8 2.2 %collective-permute-start = (bf16[16,4096]{1,0:T(8,128)(2,1)}, bf16[16,4096]{1,0:T(8,128)(2,1)S(1)}, u32[]{:S(2)}, u32[]{:S(2)}) collective-permute-start(bf16[16,4096]{1,0:T(8,128)(2,1)} %bitcast.28), channel_id=1, source_target_pairs={{0,128},{16,144},{32,160},{48,176},{64,192},{80,208},{96,224},{112... | collective-permute-start | bytes 393224 | tf_op jit(solution)/shard_map/gather_z/ppermute | solution.py:30
  12.0 0.9 copy-done.3
  12.9 0.7 copy-done.4
  13.6 1.0 pack.1
  14.6 4.2 %all-to-all-start = ((bf16[4,8,4224]{2,1,0:T(8,128)(2,1)}), bf16[4,8,4224]{2,1,0:T(8,128)(2,1)S(1)}, u32[]{:S(2)}, u32[]{:S(2)}) async-start(bf16[4,8,4224]{2,1,0:T(8,128)(2,1)} %bitcast.4), calls=%async_computation | async-start | bytes 540672 | tf_op jit(solution)/shard_map/hard_out/all_to_all | solution.py:56
  18.8 0.0 collective-permute-done.2
  18.8 0.0 collective-permute-done.1
  18.8 0.0 collective-permute-done
  18.8 0.9 pad_maximum_fusion.refs_0_
  19.7 6.3 %collective-permute-start.4 = (bf16[64,4096]{1,0:T(8,128)(2,1)S(1)}, bf16[64,4096]{1,0:T(8,128)(2,1)}, u32[]{:S(2)}, u32[]{:S(2)}) collective-permute-start(bf16[64,4096]{1,0:T(8,128)(2,1)S(1)} %pad_maximum_fusion.refs_0_), channel_id=1, source_target_pairs={{0,64},{16,80},{32,96},{48,112},{64,0},{80,16},{96,32},{112,48},{1... | collective-permute-start | bytes 1572872 | tf_op jit(solution)/shard_map/gather_x/ppermute | solution.py:30
  26.1 2.2 %collective-permute-start.3 = (bf16[64,4096]{1,0:T(8,128)(2,1)S(1)}, bf16[64,4096]{1,0:T(8,128)(2,1)}, u32[]{:S(2)}, u32[]{:S(2)}) collective-permute-start(bf16[64,4096]{1,0:T(8,128)(2,1)S(1)} %pad_maximum_fusion.refs_0_), channel_id=1, source_target_pairs={{0,32},{16,48},{32,64},{48,80},{64,96},{80,112},{96,0},{112,16},{1... | collective-permute-start | bytes 1572872 | tf_op jit(solution)/shard_map/gather_x/ppermute | solution.py:30
  28.3 0.0 all-to-all-done
  28.3 4.3 %collective-permute-start.5 = (bf16[64,4096]{1,0:T(8,128)(2,1)S(1)}, bf16[64,4096]{1,0:T(8,128)(2,1)}, u32[]{:S(2)}, u32[]{:S(2)}) collective-permute-start(bf16[64,4096]{1,0:T(8,128)(2,1)S(1)} %pad_maximum_fusion.refs_0_), channel_id=1, source_target_pairs={{0,96},{16,112},{32,0},{48,16},{64,32},{80,48},{96,64},{112,80},{1... | collective-permute-start | bytes 1572872 | tf_op jit(solution)/shard_map/gather_x/ppermute | solution.py:30
  32.6 0.9 turn.1
  33.5 13.1 %all-to-all-start.1 = ((bf16[4,8,4224]{2,1,0:T(8,128)(2,1)}), bf16[4,8,4224]{2,1,0:T(8,128)(2,1)S(1)}, u32[]{:S(2)}, u32[]{:S(2)}) async-start(bf16[4,8,4224]{2,1,0:T(8,128)(2,1)} %bitcast.6), calls=%async_computation.1 | async-start | bytes 540672 | tf_op jit(solution)/shard_map/hard_out/all_to_all | solution.py:56
  46.6 3.5 %collective-permute-start.6 = (bf16[64,4096]{1,0:T(8,128)(2,1)S(1)}, bf16[64,4096]{1,0:T(8,128)(2,1)}, u32[]{:S(2)}, u32[]{:S(2)}) collective-permute-start(bf16[64,4096]{1,0:T(8,128)(2,1)S(1)} %pad_maximum_fusion.refs_0_), channel_id=1, source_target_pairs={{0,16},{16,0},{32,48},{48,32},{64,80},{80,64},{96,112},{112,96},{1... | collective-permute-start | bytes 1572872 | tf_op jit(solution)/shard_map/gather_core/ppermute | solution.py:289
  50.1 0.0 collective-permute-done.4.refs_2_
  50.1 1.9 %collective-permute-start.8 = (bf16[64,4096]{1,0:T(8,128)(2,1)}, bf16[64,4096]{1,0:T(8,128)(2,1)}, u32[]{:S(2)}, u32[]{:S(2)}) collective-permute-start(bf16[64,4096]{1,0:T(8,128)(2,1)} %collective-permute-done.4.refs_2_), channel_id=1, source_target_pairs={{0,16},{16,0},{32,48},{48,32},{64,80},{80,64},{96,112},{112,96},{1... | collective-permute-start | bytes 1572872 | tf_op jit(solution)/shard_map/gather_core/ppermute | solution.py:289
  52.1 0.0 collective-permute-done.3.refs_1_
  52.1 2.4 %collective-permute-start.7 = (bf16[64,4096]{1,0:T(8,128)(2,1)}, bf16[64,4096]{1,0:T(8,128)(2,1)}, u32[]{:S(2)}, u32[]{:S(2)}) collective-permute-start(bf16[64,4096]{1,0:T(8,128)(2,1)} %collective-permute-done.3.refs_1_), channel_id=1, source_target_pairs={{0,16},{16,0},{32,48},{48,32},{64,80},{80,64},{96,112},{112,96},{1... | collective-permute-start | bytes 1572872 | tf_op jit(solution)/shard_map/gather_core/ppermute | solution.py:289
  54.5 0.0 collective-permute-done.5.refs_3_
  54.5 1.9 %collective-permute-start.9 = (bf16[64,4096]{1,0:T(8,128)(2,1)}, bf16[64,4096]{1,0:T(8,128)(2,1)}, u32[]{:S(2)}, u32[]{:S(2)}) collective-permute-start(bf16[64,4096]{1,0:T(8,128)(2,1)} %collective-permute-done.5.refs_3_), channel_id=1, source_target_pairs={{0,16},{16,0},{32,48},{48,32},{64,80},{80,64},{96,112},{112,96},{1... | collective-permute-start | bytes 1572872 | tf_op jit(solution)/shard_map/gather_core/ppermute | solution.py:289
  56.5 0.1 copy.9
  56.6 0.5 fusion.9.column_ref
  57.1 2.1 %near.1.s0_ref.s_ref = f32[256,256]{1,0:T(8,128)S(1)} custom-call(bf16[256,4096]{1,0:T(8,128)(2,1)S(1)} %bitcast.16, bf16[64,4096]{1,0:T(8,128)(2,1)S(1)} %pad_maximum_fusion.refs_0_, bf16[64,4096]{1,0:T(8,128)(2,1)} %collective-permute-done.3.refs_1_, bf16[64,4096]{1,0:T(8,128)(2,1)} %collective-permute-done.4.refs_2_, ...), custom_call_target="tpu_custom_call" | custom-call | flops 536870912 | bytes 4456448 | tf_op jit(solution)/shard_map/scores/near/pallas_call | solution.py:71
  59.2 0.0 collective-permute-done.6.far0.refs_4_
  59.2 3.5 %all-to-all-done.1 = bf16[4,8,4224]{2,1,0:T(8,128)(2,1)S(1)} async-done(((bf16[4,8,4224]{2,1,0:T(8,128)(2,1)}), bf16[4,8,4224]{2,1,0:T(8,128)(2,1)S(1)}, u32[]{:S(2)}, u32[]{:S(2)}) %all-to-all-start.1) | async-done | bytes 270368 | tf_op jit(solution)/shard_map/hard_out/all_to_all | solution.py:56
  62.7 0.0 collective-permute-done.9.far3.refs_7_
  62.7 3.8 %away.1 = (bf16[128,4096]{1,0:T(8,128)(2,1)S(1)}, bf16[128,4096]{1,0:T(8,128)(2,1)S(1)}, f32[256,256]{1,0:T(8,128)S(1)}, f32[256,32]{1,0:T(8,128)S(1)}, f32[256,1]{1,0:T(8,128)S(1)}) custom-call(bf16[256,4096]{1,0:T(8,128)(2,1)S(1)} %bitcast.17, bf16[64,4096]{1,0:T(8,128)(2,1)} %collective-permute-done.6.far0.refs_4_, ...), custom_call_target="tpu_custom_call" | custom-call | flops 1073741824 | bytes 7120896 | tf_op jit(solution)/shard_map/scores/away/pallas_call | solution.py:71
  66.6 5.5 %collective-permute-start.10 = (bf16[128,4096]{1,0:T(8,128)(2,1)S(1)}, bf16[128,4096]{1,0:T(8,128)(2,1)S(1)}, u32[]{:S(2)}, u32[]{:S(2)}) collective-permute-start(bf16[128,4096]{1,0:T(8,128)(2,1)S(1)} %get-tuple-element.29), channel_id=1, source_target_pairs={{0,16},{16,0},{32,48},{48,32},{64,80},{80,64},{96,112},{112,96},{1... | collective-permute-start | bytes 3145736 | tf_op jit(solution)/shard_map/scatter_core/ppermute | solution.py:319
  72.0 1.9 %collective-permute-start.12 = (bf16[128,4096]{1,0:T(8,128)(2,1)S(1)}, bf16[128,4096]{1,0:T(8,128)(2,1)S(1)}, u32[]{:S(2)}, u32[]{:S(2)}) collective-permute-start(bf16[128,4096]{1,0:T(8,128)(2,1)S(1)} %get-tuple-element.33), channel_id=1, source_target_pairs={{0,16},{16,0},{32,48},{48,32},{64,80},{80,64},{96,112},{112,96},{1... | collective-permute-start | bytes 3145736 | tf_op jit(solution)/shard_map/scatter_core/ppermute | solution.py:320
  74.0 0.3 mine.1.coef_ref.mine_ref
  74.3 0.0 collective-permute-done.10.away_ref
  74.3 1.4 %core_sum_first.1 = (bf16[64,4096]{1,0:T(8,128)(2,1)}, bf16[64,4096]{1,0:T(8,128)(2,1)}) custom-call(bf16[256,256]{1,0:T(8,128)(2,1)S(1)} %mine.1.coef_ref.mine_ref, bf16[256,4096]{1,0:T(8,128)(2,1)S(1)} %bitcast.18, bf16[128,4096]{1,0:T(8,128)(2,1)S(1)} %collective-permute-done.10.away_ref), custom_call_target="tpu_custom_call" | custom-call | flops 268435456 | bytes 4325376 | tf_op jit(solution)/shard_map/scatter_x/core_sum_first/pallas_call | solution.py:71
  75.8 1.9 %collective-permute-start.11 = (bf16[64,4096]{1,0:T(8,128)(2,1)}, bf16[64,4096]{1,0:T(8,128)(2,1)}, u32[]{:S(2)}, u32[]{:S(2)}) collective-permute-start(bf16[64,4096]{1,0:T(8,128)(2,1)} %get-tuple-element.30), channel_id=1, source_target_pairs={{0,96},{16,112},{32,0},{48,16},{64,32},{80,48},{96,64},{112,80},{1... | collective-permute-start | bytes 1572872 | tf_op jit(solution)/shard_map/scatter_x/ppermute | solution.py:30
  77.7 2.8 %collective-permute-start.13 = (bf16[64,4096]{1,0:T(8,128)(2,1)}, bf16[64,4096]{1,0:T(8,128)(2,1)}, u32[]{:S(2)}, u32[]{:S(2)}) collective-permute-start(bf16[64,4096]{1,0:T(8,128)(2,1)} %get-tuple-element.41), channel_id=1, source_target_pairs={{0,64},{16,80},{32,96},{48,112},{64,0},{80,16},{96,32},{112,48},{1... | collective-permute-start | bytes 1572872 | tf_op jit(solution)/shard_map/scatter_x/ppermute | solution.py:30
  80.5 0.0 collective-permute-done.12.away_ref
  80.5 1.3 %core_sum_second.1 = bf16[64,4096]{1,0:T(8,128)(2,1)} custom-call(bf16[256,256]{1,0:T(8,128)(2,1)S(1)} %mine.1.coef_ref.mine_ref, bf16[256,4096]{1,0:T(8,128)(2,1)S(1)} %bitcast.19, bf16[128,4096]{1,0:T(8,128)(2,1)S(1)} %collective-permute-done.12.away_ref), custom_call_target="tpu_custom_call" | custom-call | flops 134217728 | bytes 3801088 | tf_op jit(solution)/shard_map/scatter_x/core_sum_second/pallas_call | solution.py:71
  81.8 2.5 %collective-permute-start.14 = (bf16[64,4096]{1,0:T(8,128)(2,1)}, bf16[64,4096]{1,0:T(8,128)(2,1)}, u32[]{:S(2)}, u32[]{:S(2)}) collective-permute-start(bf16[64,4096]{1,0:T(8,128)(2,1)} %core_sum_second.1), channel_id=1, source_target_pairs={{0,32},{16,48},{32,64},{48,80},{64,96},{80,112},{96,0},{112,16},{1... | collective-permute-start | bytes 1572872 | tf_op jit(solution)/shard_map/scatter_x/ppermute | solution.py:30
  84.3 2.3 %rest.1 = (bf16[16,2,4096]{2,1,0:T(2,128)(2,1)}, bf16[256,64]{1,0:T(8,128)(2,1)S(1)}, f32[256,1]{1,0:T(8,128)S(1)}, bf16[512,256]{1,0:T(8,128)(2,1)S(1)}, bf16[5...) custom-call(f32[256,256]{1,0:T(8,128)S(1)} %near.1.s0_ref.s_ref, f32[256,256]{1,0:T(8,128)S(1)} %get-tuple-element.31.s1_ref, ...), custom_call_target="tpu_custom_call" | custom-call | flops 268435456 | bytes 5704704 | tf_op jit(solution)/shard_map/rest/rest/pallas_call | solution.py:71
  86.6 0.0 copy-start.1
  86.6 1.0 copy-done.1
  87.6 0.7 copy-done.5
  88.3 0.7 copy-done.7
  89.0 9.5 %all-to-all-start.2 = ((bf16[16,2,4096]{2,1,0:T(2,128)(2,1)}), bf16[16,2,4096]{2,1,0:T(2,128)(2,1)S(1)}, u32[]{:S(2)}, u32[]{:S(2)}) async-start(bf16[16,2,4096]{2,1,0:T(2,128)(2,1)} %get-tuple-element.47), calls=%async_computation.2 | async-start | bytes 524288 | tf_op jit(solution)/shard_map/hard_back/all_to_all | solution.py:365
  98.4 0.7 reduce
  99.1 0.0 collective-permute-done.11.refs_1_
  99.1 0.0 collective-permute-done.13.refs_2_
  99.1 7.3 %collective-permute-done.14.refs_3_ = bf16[64,4096]{1,0:T(8,128)(2,1)} collective-permute-done((bf16[64,4096]{1,0:T(8,128)(2,1)}, bf16[64,4096]{1,0:T(8,128)(2,1)}, u32[]{:S(2)}, u32[]{:S(2)}) %collective-permute-start.14) | collective-permute-done | bytes 524320 | tf_op jit(solution)/shard_map/scatter_x/ppermute | solution.py:30
  106.5 1.2 copy-done.2
  107.7 1.7 %x_sum.1 = (f32[16,4096]{1,0:T(8,128)S(1)}, bf16[16,4096]{1,0:T(8,128)(2,1)S(1)}, bf16[16,4096]{1,0:T(8,128)(2,1)S(1)}, bf16[16,4096]{1,0:T(8,128)(2,1)S(1)}) custom-call(f32[64,4096]{1,0:T(8,128)S(1)} %copy-done.2, bf16[64,4096]{1,0:T(8,128)(2,1)} %collective-permute-done.11.refs_1_, bf16[64,4096]{1,0:T(8,128)(2,1)} %collective-permute-done.13.refs_2_, ...), custom_call_target="tpu_custom_call" | custom-call | flops 1048576 | bytes 3145728 | tf_op jit(solution)/shard_map/scatter_x/x_sum/pallas_call | solution.py:351
  109.4 4.0 %collective-permute-start.15 = (bf16[16,4096]{1,0:T(8,128)(2,1)S(1)}, bf16[16,4096]{1,0:T(8,128)(2,1)S(1)}, u32[]{:S(2)}, u32[]{:S(2)}) collective-permute-start(bf16[16,4096]{1,0:T(8,128)(2,1)S(1)} %get-tuple-element.43), channel_id=1, source_target_pairs={{0,384},{16,400},{32,416},{48,432},{64,448},{80,464},{96,480},{112... | collective-permute-start | bytes 393224 | tf_op jit(solution)/shard_map/scatter_z/ppermute | solution.py:30
  113.4 2.8 %collective-permute-start.16 = (bf16[16,4096]{1,0:T(8,128)(2,1)S(1)}, bf16[16,4096]{1,0:T(8,128)(2,1)S(1)}, u32[]{:S(2)}, u32[]{:S(2)}) collective-permute-start(bf16[16,4096]{1,0:T(8,128)(2,1)S(1)} %get-tuple-element.44), channel_id=1, source_target_pairs={{0,256},{16,272},{32,288},{48,304},{64,320},{80,336},{96,352},{112... | collective-permute-start | bytes 393224 | tf_op jit(solution)/shard_map/scatter_z/ppermute | solution.py:30
  116.2 3.4 %collective-permute-start.17 = (bf16[16,4096]{1,0:T(8,128)(2,1)S(1)}, bf16[16,4096]{1,0:T(8,128)(2,1)S(1)}, u32[]{:S(2)}, u32[]{:S(2)}) collective-permute-start(bf16[16,4096]{1,0:T(8,128)(2,1)S(1)} %get-tuple-element.45), channel_id=1, source_target_pairs={{0,128},{16,144},{32,160},{48,176},{64,192},{80,208},{96,224},{112... | collective-permute-start | bytes 393224 | tf_op jit(solution)/shard_map/scatter_z/ppermute | solution.py:30
  119.6 5.7 %query_grad.1 = bf16[1,256,4096]{2,1,0:T(8,128)(2,1)} custom-call(bf16[512,256]{1,0:T(8,128)(2,1)S(1)} %copy-done.6, bf16[512,256]{1,0:T(8,128)(2,1)S(1)} %copy-done.8, bf16[256,64]{1,0:T(8,128)(2,1)S(1)} %get-tuple-element.38.ch, bf16[64,4096]{1,0:T(8,128)(2,1)S(1)} %pad_maximum_fusion.refs_0_, bf16[64,4096]{1,0:T(8,128)(2,1)} %collective-permute-done.3.refs_1_, ...), custom_call_target="tpu_custom_call" | custom-call | flops 2281701376 | bytes 7118848 | tf_op jit(solution)/shard_map/d_query/query_grad/pallas_call | solution.py:71
  125.3 0.0 collective-permute-done.15
  125.3 1.6 %collective-permute-done.16 = bf16[16,4096]{1,0:T(8,128)(2,1)S(1)} collective-permute-done((bf16[16,4096]{1,0:T(8,128)(2,1)S(1)}, bf16[16,4096]{1,0:T(8,128)(2,1)S(1)}, u32[]{:S(2)}, u32[]{:S(2)}) %collective-permute-start.16) | collective-permute-done | bytes 131104 | tf_op jit(solution)/shard_map/scatter_z/ppermute | solution.py:30
  126.9 0.0 collective-permute-done.17
  126.9 0.7 fusion.13
  127.7 0.0 all-to-all-done.2
  127.7 0.1 reshape.341
  127.8 0.9 fusion
  (15 shorter events, 0.0 us)
Async XLA Ops:
  0.6 56.5 %copy-start = (bf16[1,256,4096]{2,1,0:T(8,128)(2,1)S(1)}, bf16[1,256,4096]{2,1,0:T(8,128)(2,1)}, u32[]{:S(2)}) copy-start(bf16[1,256,4096]{2,1,0:T(8,128)(2,1)} %param.5) | copy-start | bytes 6291460
  0.6 18.1 %collective-permute-start.2 = (bf16[16,4096]{1,0:T(8,128)(2,1)}, bf16[16,4096]{1,0:T(8,128)(2,1)S(1)}, u32[]{:S(2)}, u32[]{:S(2)}) collective-permute-start(bf16[16,4096]{1,0:T(8,128)(2,1)} %bitcast.26), channel_id=1, source_target_pairs={{0,384},{16,400},{32,416},{48,432},{64,448},{80,464},{96,480},{112... | collective-permute-start | bytes 393224 | tf_op jit(solution)/shard_map/gather_z/ppermute | solution.py:30
  7.9 10.9 %collective-permute-start.1 = (bf16[16,4096]{1,0:T(8,128)(2,1)}, bf16[16,4096]{1,0:T(8,128)(2,1)S(1)}, u32[]{:S(2)}, u32[]{:S(2)}) collective-permute-start(bf16[16,4096]{1,0:T(8,128)(2,1)} %bitcast.27), channel_id=1, source_target_pairs={{0,256},{16,272},{32,288},{48,304},{64,320},{80,336},{96,352},{112... | collective-permute-start | bytes 393224 | tf_op jit(solution)/shard_map/gather_z/ppermute | solution.py:30
  9.8 9.0 %collective-permute-start = (bf16[16,4096]{1,0:T(8,128)(2,1)}, bf16[16,4096]{1,0:T(8,128)(2,1)S(1)}, u32[]{:S(2)}, u32[]{:S(2)}) collective-permute-start(bf16[16,4096]{1,0:T(8,128)(2,1)} %bitcast.28), channel_id=1, source_target_pairs={{0,128},{16,144},{32,160},{48,176},{64,192},{80,208},{96,224},{112... | collective-permute-start | bytes 393224 | tf_op jit(solution)/shard_map/gather_z/ppermute | solution.py:30
  12.0 0.9 copy-start.3
  12.9 0.7 copy-start.4
  13.6 42.9 %copy-start.9 = (s32[1,256]{1,0:T(1,128)S(1)}, s32[1,256]{1,0:T(1,128)}, u32[]{:S(2)}) copy-start(s32[1,256]{1,0:T(1,128)} %param.7) | copy-start | bytes 3076
  14.6 13.7 %all-to-all-start = ((bf16[4,8,4224]{2,1,0:T(8,128)(2,1)}), bf16[4,8,4224]{2,1,0:T(8,128)(2,1)S(1)}, u32[]{:S(2)}, u32[]{:S(2)}) async-start(bf16[4,8,4224]{2,1,0:T(8,128)(2,1)} %bitcast.4), calls=%async_computation | async-start | bytes 540672 | tf_op jit(solution)/shard_map/hard_out/all_to_all | solution.py:56
  19.7 30.4 %collective-permute-start.4 = (bf16[64,4096]{1,0:T(8,128)(2,1)S(1)}, bf16[64,4096]{1,0:T(8,128)(2,1)}, u32[]{:S(2)}, u32[]{:S(2)}) collective-permute-start(bf16[64,4096]{1,0:T(8,128)(2,1)S(1)} %pad_maximum_fusion.refs_0_), channel_id=1, source_target_pairs={{0,64},{16,80},{32,96},{48,112},{64,0},{80,16},{96,32},{112,48},{1... | collective-permute-start | bytes 1572872 | tf_op jit(solution)/shard_map/gather_x/ppermute | solution.py:30
  26.1 26.0 %collective-permute-start.3 = (bf16[64,4096]{1,0:T(8,128)(2,1)S(1)}, bf16[64,4096]{1,0:T(8,128)(2,1)}, u32[]{:S(2)}, u32[]{:S(2)}) collective-permute-start(bf16[64,4096]{1,0:T(8,128)(2,1)S(1)} %pad_maximum_fusion.refs_0_), channel_id=1, source_target_pairs={{0,32},{16,48},{32,64},{48,80},{64,96},{80,112},{96,0},{112,16},{1... | collective-permute-start | bytes 1572872 | tf_op jit(solution)/shard_map/gather_x/ppermute | solution.py:30
  28.3 26.2 %collective-permute-start.5 = (bf16[64,4096]{1,0:T(8,128)(2,1)S(1)}, bf16[64,4096]{1,0:T(8,128)(2,1)}, u32[]{:S(2)}, u32[]{:S(2)}) collective-permute-start(bf16[64,4096]{1,0:T(8,128)(2,1)S(1)} %pad_maximum_fusion.refs_0_), channel_id=1, source_target_pairs={{0,96},{16,112},{32,0},{48,16},{64,32},{80,48},{96,64},{112,80},{1... | collective-permute-start | bytes 1572872 | tf_op jit(solution)/shard_map/gather_x/ppermute | solution.py:30
  33.5 29.2 %all-to-all-start.1 = ((bf16[4,8,4224]{2,1,0:T(8,128)(2,1)}), bf16[4,8,4224]{2,1,0:T(8,128)(2,1)S(1)}, u32[]{:S(2)}, u32[]{:S(2)}) async-start(bf16[4,8,4224]{2,1,0:T(8,128)(2,1)} %bitcast.6), calls=%async_computation.1 | async-start | bytes 540672 | tf_op jit(solution)/shard_map/hard_out/all_to_all | solution.py:56
  46.6 12.6 %collective-permute-start.6 = (bf16[64,4096]{1,0:T(8,128)(2,1)S(1)}, bf16[64,4096]{1,0:T(8,128)(2,1)}, u32[]{:S(2)}, u32[]{:S(2)}) collective-permute-start(bf16[64,4096]{1,0:T(8,128)(2,1)S(1)} %pad_maximum_fusion.refs_0_), channel_id=1, source_target_pairs={{0,16},{16,0},{32,48},{48,32},{64,80},{80,64},{96,112},{112,96},{1... | collective-permute-start | bytes 1572872 | tf_op jit(solution)/shard_map/gather_core/ppermute | solution.py:289
  50.1 12.6 %collective-permute-start.8 = (bf16[64,4096]{1,0:T(8,128)(2,1)}, bf16[64,4096]{1,0:T(8,128)(2,1)}, u32[]{:S(2)}, u32[]{:S(2)}) collective-permute-start(bf16[64,4096]{1,0:T(8,128)(2,1)} %collective-permute-done.4.refs_2_), channel_id=1, source_target_pairs={{0,16},{16,0},{32,48},{48,32},{64,80},{80,64},{96,112},{112,96},{1... | collective-permute-start | bytes 1572872 | tf_op jit(solution)/shard_map/gather_core/ppermute | solution.py:289
  52.1 10.6 %collective-permute-start.7 = (bf16[64,4096]{1,0:T(8,128)(2,1)}, bf16[64,4096]{1,0:T(8,128)(2,1)}, u32[]{:S(2)}, u32[]{:S(2)}) collective-permute-start(bf16[64,4096]{1,0:T(8,128)(2,1)} %collective-permute-done.3.refs_1_), channel_id=1, source_target_pairs={{0,16},{16,0},{32,48},{48,32},{64,80},{80,64},{96,112},{112,96},{1... | collective-permute-start | bytes 1572872 | tf_op jit(solution)/shard_map/gather_core/ppermute | solution.py:289
  54.5 8.2 %collective-permute-start.9 = (bf16[64,4096]{1,0:T(8,128)(2,1)}, bf16[64,4096]{1,0:T(8,128)(2,1)}, u32[]{:S(2)}, u32[]{:S(2)}) collective-permute-start(bf16[64,4096]{1,0:T(8,128)(2,1)} %collective-permute-done.5.refs_3_), channel_id=1, source_target_pairs={{0,16},{16,0},{32,48},{48,32},{64,80},{80,64},{96,112},{112,96},{1... | collective-permute-start | bytes 1572872 | tf_op jit(solution)/shard_map/gather_core/ppermute | solution.py:289
  66.6 7.7 %collective-permute-start.10 = (bf16[128,4096]{1,0:T(8,128)(2,1)S(1)}, bf16[128,4096]{1,0:T(8,128)(2,1)S(1)}, u32[]{:S(2)}, u32[]{:S(2)}) collective-permute-start(bf16[128,4096]{1,0:T(8,128)(2,1)S(1)} %get-tuple-element.29), channel_id=1, source_target_pairs={{0,16},{16,0},{32,48},{48,32},{64,80},{80,64},{96,112},{112,96},{1... | collective-permute-start | bytes 3145736 | tf_op jit(solution)/shard_map/scatter_core/ppermute | solution.py:319
  72.0 8.4 %collective-permute-start.12 = (bf16[128,4096]{1,0:T(8,128)(2,1)S(1)}, bf16[128,4096]{1,0:T(8,128)(2,1)S(1)}, u32[]{:S(2)}, u32[]{:S(2)}) collective-permute-start(bf16[128,4096]{1,0:T(8,128)(2,1)S(1)} %get-tuple-element.33), channel_id=1, source_target_pairs={{0,16},{16,0},{32,48},{48,32},{64,80},{80,64},{96,112},{112,96},{1... | collective-permute-start | bytes 3145736 | tf_op jit(solution)/shard_map/scatter_core/ppermute | solution.py:320
  75.8 23.4 %collective-permute-start.11 = (bf16[64,4096]{1,0:T(8,128)(2,1)}, bf16[64,4096]{1,0:T(8,128)(2,1)}, u32[]{:S(2)}, u32[]{:S(2)}) collective-permute-start(bf16[64,4096]{1,0:T(8,128)(2,1)} %get-tuple-element.30), channel_id=1, source_target_pairs={{0,96},{16,112},{32,0},{48,16},{64,32},{80,48},{96,64},{112,80},{1... | collective-permute-start | bytes 1572872 | tf_op jit(solution)/shard_map/scatter_x/ppermute | solution.py:30
  77.7 21.4 %collective-permute-start.13 = (bf16[64,4096]{1,0:T(8,128)(2,1)}, bf16[64,4096]{1,0:T(8,128)(2,1)}, u32[]{:S(2)}, u32[]{:S(2)}) collective-permute-start(bf16[64,4096]{1,0:T(8,128)(2,1)} %get-tuple-element.41), channel_id=1, source_target_pairs={{0,64},{16,80},{32,96},{48,112},{64,0},{80,16},{96,32},{112,48},{1... | collective-permute-start | bytes 1572872 | tf_op jit(solution)/shard_map/scatter_x/ppermute | solution.py:30
  81.8 24.7 %collective-permute-start.14 = (bf16[64,4096]{1,0:T(8,128)(2,1)}, bf16[64,4096]{1,0:T(8,128)(2,1)}, u32[]{:S(2)}, u32[]{:S(2)}) collective-permute-start(bf16[64,4096]{1,0:T(8,128)(2,1)} %core_sum_second.1), channel_id=1, source_target_pairs={{0,32},{16,48},{32,64},{48,80},{64,96},{80,112},{96,0},{112,16},{1... | collective-permute-start | bytes 1572872 | tf_op jit(solution)/shard_map/scatter_x/ppermute | solution.py:30
  86.6 1.0 copy-start.1
  87.6 0.7 copy-start.5
  88.3 0.7 copy-start.7
  89.0 30.6 %copy-start.6 = (bf16[512,256]{1,0:T(8,128)(2,1)S(1)}, bf16[512,256]{1,0:T(8,128)(2,1)}, u32[]{:S(2)}) copy-start(bf16[512,256]{1,0:T(8,128)(2,1)} %copy-done.5) | copy-start | bytes 786436
  89.0 30.6 %copy-start.8 = (bf16[512,256]{1,0:T(8,128)(2,1)S(1)}, bf16[512,256]{1,0:T(8,128)(2,1)}, u32[]{:S(2)}) copy-start(bf16[512,256]{1,0:T(8,128)(2,1)} %copy-done.7) | copy-start | bytes 786436
  89.0 38.7 %all-to-all-start.2 = ((bf16[16,2,4096]{2,1,0:T(2,128)(2,1)}), bf16[16,2,4096]{2,1,0:T(2,128)(2,1)S(1)}, u32[]{:S(2)}, u32[]{:S(2)}) async-start(bf16[16,2,4096]{2,1,0:T(2,128)(2,1)} %get-tuple-element.47), calls=%async_computation.2 | async-start | bytes 524288 | tf_op jit(solution)/shard_map/hard_back/all_to_all | solution.py:365
  106.5 1.2 copy-start.2
  109.4 15.9 %collective-permute-start.15 = (bf16[16,4096]{1,0:T(8,128)(2,1)S(1)}, bf16[16,4096]{1,0:T(8,128)(2,1)S(1)}, u32[]{:S(2)}, u32[]{:S(2)}) collective-permute-start(bf16[16,4096]{1,0:T(8,128)(2,1)S(1)} %get-tuple-element.43), channel_id=1, source_target_pairs={{0,384},{16,400},{32,416},{48,432},{64,448},{80,464},{96,480},{112... | collective-permute-start | bytes 393224 | tf_op jit(solution)/shard_map/scatter_z/ppermute | solution.py:30
  113.4 13.5 %collective-permute-start.16 = (bf16[16,4096]{1,0:T(8,128)(2,1)S(1)}, bf16[16,4096]{1,0:T(8,128)(2,1)S(1)}, u32[]{:S(2)}, u32[]{:S(2)}) collective-permute-start(bf16[16,4096]{1,0:T(8,128)(2,1)S(1)} %get-tuple-element.44), channel_id=1, source_target_pairs={{0,256},{16,272},{32,288},{48,304},{64,320},{80,336},{96,352},{112... | collective-permute-start | bytes 393224 | tf_op jit(solution)/shard_map/scatter_z/ppermute | solution.py:30
  116.2 10.8 %collective-permute-start.17 = (bf16[16,4096]{1,0:T(8,128)(2,1)S(1)}, bf16[16,4096]{1,0:T(8,128)(2,1)S(1)}, u32[]{:S(2)}, u32[]{:S(2)}) collective-permute-start(bf16[16,4096]{1,0:T(8,128)(2,1)S(1)} %get-tuple-element.45), channel_id=1, source_target_pairs={{0,128},{16,144},{32,160},{48,176},{64,192},{80,208},{96,224},{112... | collective-permute-start | bytes 393224 | tf_op jit(solution)/shard_map/scatter_z/ppermute | solution.py:30
